TPU v7x, 32 devices: a whole 2x2x4 slice. The times are simulated.
32 devices in a mesh: batch: 4 (over y, core), seq: 8 (over z, x).
Axes of the slice: x: 2, y: 2, z: 4, core: 2. Of those that a mesh axis runs over, the one named last changes fastest.
Arguments:
- tokens: bfloat16 [8, 32, 64, 768], P('batch', 'seq'), may hold values from -6 to 6
- cotangent: bfloat16 [8, 32, 64, 768], P('batch', 'seq'), may hold values from -6 to 6
- timestep: int32 [8], P('batch'), may hold values from 0 to 999
- class_ids: int32 [8], P('batch'), may hold values from 0 to 999
- heights: int32 [8], P('batch'), may hold values from 8 to 32, as said below
- widths: int32 [8], P('batch'), may hold values from 16 to 64, as said below
- time_weight: bfloat16 [256, 768], replicated, may hold values from -0.375 to 0.375
- class_table: bfloat16 [1000, 768], replicated, may hold values from -6 to 6
- ada_weight: bfloat16 [768, 4608], replicated, may hold values from -0.21875 to 0.21875
- ada_bias: float32 [4608], replicated, may hold values from -4 to 4
- conv_attn: bfloat16 [9, 768], replicated, may hold values from -2 to 2
- qkv_weight: bfloat16 [768, 2304], replicated, may hold values from -0.09375 to 0.09375
- proj_weight: bfloat16 [768, 768], replicated, may hold values from -1.75 to 1.75
- up_weight: bfloat16 [768, 3072], replicated, may hold values from -0.21875 to 0.21875
- conv_ffn: bfloat16 [9, 3072], replicated, may hold values from -2 to 2
- down_weight: bfloat16 [3072, 768], replicated, may hold values from -0.109375 to 0.109375
Outputs:
- layer_out: bfloat16 [8, 32, 64, 768], P('batch', 'seq')
- token_grad: float32 [8, 32, 64, 768], P('batch', 'seq')
- cond_grad: float32 [8, 768], P('batch')
- time_weight_grad: float32 [256, 768], P(None, ('batch', 'seq'))
- class_table_grad: float32 [1000, 768], P(None, ('batch', 'seq'))
- ada_weight_grad: float32 [768, 4608], P(('batch', 'seq'))
- ada_bias_grad: float32 [4608], P(('batch', 'seq'))
- conv_attn_grad: float32 [9, 768], P(None, ('batch', 'seq'))
- qkv_weight_grad: float32 [768, 2304], P(('batch', 'seq'))
- proj_weight_grad: float32 [768, 768], P(('batch', 'seq'))
- up_weight_grad: float32 [768, 3072], P(('batch', 'seq'))
- conv_ffn_grad: float32 [9, 3072], P(None, ('batch', 'seq'))
- down_weight_grad: float32 [3072, 768], P(None, ('batch', 'seq'))
Inputs may be any that keep to these rules, and one draw needn't show every extreme that they name: `heights`: some latent has all 32 rows valid. `widths`: some latent has all 64 columns valid.
All inputs are finite; a program needn't handle non-finite values.
Results may differ from a plain program's by a relative error of at most 0.025.
Values may be sent and summed in bfloat16 or wider, within the bound.
No kernel may reach another device: no remote copies, remote signals or barrier semaphores. Data moves between devices by JAX's collectives and lax.ppermute only.
A program may use at most 448 MiB of HBM per device.

v0:
```python
import math

import jax
import jax.numpy as jnp
from jax import lax
from jax.sharding import PartitionSpec as P

D = 768
HEADS = 12
HEAD_DIM = 64


HIGHEST = lax.Precision.HIGHEST


def extended(cells, sides, width):
    for axis, dim in sides:
        count = lax.axis_size(axis)
        ends = count - 1
        head = lax.slice_in_dim(cells, 0, width, axis=dim)
        tail = lax.slice_in_dim(cells, cells.shape[dim] - width, cells.shape[dim], axis=dim)
        cells = jnp.concatenate(
            [
                lax.ppermute(tail, axis, [(i, (i + 1) % count) for i in range(ends)]),
                cells,
                lax.ppermute(head, axis, [((i + 1) % count, i) for i in range(ends)]),
            ],
            axis=dim,
        )
    return cells


def pad_columns(values):
    return jnp.pad(values, ((0, 0), (0, 0), (1, 1), (0, 0)))


def shifted_sum(padded, kernel, extent_rows, extent_cols):
    summed = jnp.zeros((padded.shape[0], extent_rows, extent_cols, padded.shape[3]), jnp.float32)
    for offset in range(9):
        down_by = offset // 3
        right_by = offset % 3
        window = padded[
            :, down_by : down_by + extent_rows, right_by : right_by + extent_cols
        ].astype(jnp.float32)
        summed = summed + window * kernel[offset].astype(jnp.float32)
    return summed


def kernel_grad(padded, grad_out, extent_rows, extent_cols):
    grad_float = grad_out.astype(jnp.float32)
    collected = []
    for offset in range(9):
        down_by = offset // 3
        right_by = offset % 3
        window = padded[
            :, down_by : down_by + extent_rows, right_by : right_by + extent_cols
        ].astype(jnp.float32)
        collected.append(jnp.sum(window * grad_float, axis=(0, 1, 2)))
    return jnp.stack(collected)


def regroup(values):
    shape_in = values.shape
    parted = values.reshape(shape_in[0], shape_in[1] // 2, 2, shape_in[2] // 2, 2, shape_in[3])
    return parted.transpose(0, 2, 4, 1, 3, 5).reshape(
        shape_in[0], 4, shape_in[1] // 2 * (shape_in[2] // 2), shape_in[3]
    )


def ungroup(values, rows_in, cols_in):
    shape_in = values.shape
    parted = values.reshape(shape_in[0], 2, 2, rows_in // 2, cols_in // 2, shape_in[3])
    return parted.transpose(0, 3, 1, 4, 2, 5).reshape(shape_in[0], rows_in, cols_in, shape_in[3])


def normalize(values):
    centre = values - jnp.mean(values, axis=-1, keepdims=True)
    spread = jnp.mean(centre * centre, axis=-1, keepdims=True)
    scaled = lax.rsqrt(spread + 1e-06)
    return (centre * scaled, scaled)


def norm_back(grad_norm, normed, scaled):
    return scaled * (
        grad_norm
        - jnp.mean(grad_norm, axis=-1, keepdims=True)
        - normed * jnp.mean(grad_norm * normed, axis=-1, keepdims=True)
    )


def gelu_exact(values):
    return 0.5 * values * (1.0 + lax.erf(values * 0.7071067811865476))


def gelu_slope(values):
    normal_cdf = 0.5 * (1.0 + lax.erf(values * 0.7071067811865476))
    return normal_cdf + values * jnp.exp(-0.5 * values * values) * 0.3989422804014327


def shards(
    tokens,
    cotangent,
    timestep,
    class_ids,
    heights,
    widths,
    time_weight,
    class_table,
    ada_weight,
    ada_bias,
    conv_attn,
    qkv_weight,
    proj_weight,
    up_weight,
    conv_ffn,
    down_weight,
):
    latents_here = tokens.shape[0]
    rows_here = tokens.shape[1]
    grid_cols = tokens.shape[2]
    seq_count = lax.axis_size("seq")
    seq_place = lax.axis_index("seq")
    per_group = rows_here // 2 * (grid_cols // 2)
    blocks = latents_here * 4
    all_keys = seq_count * per_group
    factor = HEAD_DIM ** (-0.5)
    half_freq = time_weight.shape[0] // 2
    frequency = jnp.exp(-math.log(10000.0) * jnp.arange(half_freq, dtype=jnp.float32) / half_freq)
    angles = timestep.astype(jnp.float32)[:, None] * frequency[None, :]
    embedding = jnp.concatenate([jnp.cos(angles), jnp.sin(angles)], axis=1).astype(jnp.bfloat16)
    one_hot = (
        class_ids[:, None] == jnp.arange(class_table.shape[0], dtype=jnp.int32)[None, :]
    ).astype(jnp.bfloat16)
    condition = jnp.dot(embedding, time_weight, preferred_element_type=jnp.float32) + jnp.dot(
        one_hot, class_table, preferred_element_type=jnp.float32
    )
    logistic = jax.nn.sigmoid(condition)
    activated_cond = (condition * logistic).astype(jnp.bfloat16)
    modulate = jnp.dot(activated_cond, ada_weight, preferred_element_type=jnp.float32) + ada_bias
    pieces = modulate.reshape(latents_here, 6, 1, 1, D)
    shift_one = pieces[:, 0]
    scale_one = pieces[:, 1]
    gate_one = pieces[:, 2]
    shift_two = pieces[:, 3]
    scale_two = pieces[:, 4]
    gate_two = pieces[:, 5]
    row_global = seq_place * rows_here + jnp.arange(rows_here, dtype=jnp.int32)
    col_ids = jnp.arange(grid_cols, dtype=jnp.int32)
    usable = (
        (row_global[None, :, None] < heights[:, None, None])
        & (col_ids[None, None, :] < widths[:, None, None])
    ).astype(jnp.float32)[..., None]
    key_ids = jnp.arange(all_keys, dtype=jnp.int32)
    key_owner = key_ids // per_group
    inside = key_ids % per_group
    group_row = key_owner * (rows_here // 2) + inside // (grid_cols // 2)
    group_col = inside % (grid_cols // 2)
    group_ids = jnp.arange(4, dtype=jnp.int32)
    key_row = group_row[None, :] * 2 + (group_ids // 2)[:, None]
    key_col = group_col[None, :] * 2 + (group_ids % 2)[:, None]
    key_usable = (
        (key_row[None] < heights[:, None, None]) & (key_col[None] < widths[:, None, None])
    ).reshape(blocks, all_keys)
    source = tokens.astype(jnp.float32)
    normed_one, scaled_one = normalize(source)
    entered = ((normed_one * (1.0 + scale_one) + shift_one) * usable).astype(jnp.bfloat16)
    entered_pad = pad_columns(extended(entered, (("seq", 1),), 1))
    mixed_in = (
        entered.astype(jnp.float32) + shifted_sum(entered_pad, conv_attn, rows_here, grid_cols)
    ).astype(jnp.bfloat16)
    triple = jnp.einsum(
        "lrwd,de->lrwe", mixed_in, qkv_weight, preferred_element_type=jnp.float32
    ).astype(jnp.bfloat16)
    queries = regroup(triple[..., :D]).reshape(blocks, per_group, HEADS, HEAD_DIM)
    pairs_local = regroup(triple[..., D:])
    gathered = lax.all_gather(pairs_local, "seq", axis=2, tiled=True).reshape(
        blocks, all_keys, 2 * D
    )

    def attend(operands):
        block_q, block_kv, block_ok = operands
        keys_in = block_kv[:, :D].reshape(-1, HEADS, HEAD_DIM)
        values_in = block_kv[:, D:].reshape(-1, HEADS, HEAD_DIM)
        scores = (
            jnp.einsum("qhe,khe->hqk", block_q, keys_in, preferred_element_type=jnp.float32)
            * factor
        )
        scores = jnp.where(block_ok[None, None, :], scores, -1e30)
        row_peak = jnp.max(scores, axis=-1, keepdims=True)
        numerator = jnp.exp(scores - row_peak)
        summed = jnp.sum(numerator, axis=-1, keepdims=True)
        probability = numerator / summed
        upper_part = probability.astype(jnp.bfloat16)
        lower_part = (probability - upper_part.astype(jnp.float32)).astype(jnp.bfloat16)
        mixed_out = jnp.einsum(
            "hqk,khe->qhe", upper_part, values_in, preferred_element_type=jnp.float32
        )
        extra_out = jnp.einsum(
            "hqk,khe->qhe", lower_part, values_in, preferred_element_type=jnp.float32
        )
        return (
            mixed_out.reshape(-1, D),
            (mixed_out + extra_out).reshape(-1, D),
            (row_peak + jnp.log(summed))[..., 0],
        )

    attended, attended_full, log_total = lax.map(attend, (queries, gathered, key_usable))
    attended_tok = ungroup(
        attended.reshape(latents_here, 4, per_group, D).astype(jnp.bfloat16), rows_here, grid_cols
    )
    branch = jnp.einsum(
        "lrwd,de->lrwe", attended_tok, proj_weight, preferred_element_type=jnp.float32
    )
    after_attn = source + gate_one * branch
    normed_two, scaled_two = normalize(after_attn)
    entered_two = ((normed_two * (1.0 + scale_two) + shift_two) * usable).astype(jnp.bfloat16)
    raised = jnp.einsum(
        "lrwd,df->lrwf", entered_two, up_weight, preferred_element_type=jnp.float32
    ).astype(jnp.bfloat16)
    raised_pad = pad_columns(extended(raised, (("seq", 1),), 1))
    convolved = shifted_sum(raised_pad, conv_ffn, rows_here, grid_cols)
    activated = gelu_exact(convolved).astype(jnp.bfloat16)
    expanded = jnp.einsum(
        "lrwf,fd->lrwd", activated, down_weight, preferred_element_type=jnp.float32
    )
    output = (after_attn + gate_two * expanded).astype(jnp.bfloat16)
    grad_out = cotangent.astype(jnp.float32)
    grad_gate_two = jnp.sum(grad_out * expanded, axis=(1, 2))
    grad_expanded = (gate_two * grad_out).astype(jnp.bfloat16)
    down_grad = jnp.einsum(
        "lrwf,lrwd->fd", activated, grad_expanded, preferred_element_type=jnp.float32
    )
    grad_act = jnp.einsum(
        "lrwd,fd->lrwf", grad_expanded, down_weight, preferred_element_type=jnp.float32
    )
    grad_conv = (grad_act * gelu_slope(convolved)).astype(jnp.bfloat16)
    conv_ffn_grad = kernel_grad(raised_pad, grad_conv, rows_here, grid_cols)
    grad_conv_pad = pad_columns(extended(grad_conv, (("seq", 1),), 1))
    grad_raised = shifted_sum(grad_conv_pad, conv_ffn[::-1], rows_here, grid_cols).astype(
        jnp.bfloat16
    )
    up_grad = jnp.einsum(
        "lrwd,lrwf->df", entered_two, grad_raised, preferred_element_type=jnp.float32
    )
    grad_e2 = (
        jnp.einsum("lrwf,df->lrwd", grad_raised, up_weight, preferred_element_type=jnp.float32)
        * usable
    )
    grad_shift_two = jnp.sum(grad_e2, axis=(1, 2))
    grad_scale_two = jnp.sum(grad_e2 * normed_two, axis=(1, 2))
    grad_after = grad_out + norm_back(grad_e2 * (1.0 + scale_two), normed_two, scaled_two)
    grad_gate_one = jnp.sum(grad_after * branch, axis=(1, 2))
    grad_branch = (gate_one * grad_after).astype(jnp.bfloat16)
    proj_grad = jnp.einsum(
        "lrwd,lrwe->de", attended_tok, grad_branch, preferred_element_type=jnp.float32
    )
    grad_attended = jnp.einsum(
        "lrwe,de->lrwd", grad_branch, proj_weight, preferred_element_type=jnp.float32
    ).astype(jnp.bfloat16)
    grad_grouped = regroup(grad_attended).reshape(blocks, per_group, HEADS, HEAD_DIM)
    gathered_back = lax.all_gather(pairs_local, "seq", axis=2, tiled=True).reshape(
        blocks, all_keys, 2 * D
    )
    full_heads = attended_full.reshape(blocks, per_group, HEADS, HEAD_DIM)

    def attend_back(operands):
        block_q, block_kv, block_ok, block_lse, block_grad, block_full = operands
        keys_in = block_kv[:, :D].reshape(-1, HEADS, HEAD_DIM)
        values_in = block_kv[:, D:].reshape(-1, HEADS, HEAD_DIM)
        scores = (
            jnp.einsum("qhe,khe->hqk", block_q, keys_in, preferred_element_type=jnp.float32)
            * factor
        )
        scores = jnp.where(block_ok[None, None, :], scores, -1e30)
        probability = jnp.exp(scores - block_lse[..., None])
        grad_prob = jnp.einsum(
            "qhe,khe->hqk", block_grad, values_in, preferred_element_type=jnp.float32
        )
        row_delta = jnp.sum(block_grad.astype(jnp.float32) * block_full, axis=-1).T
        grad_scores = (probability * (grad_prob - row_delta[..., None])).astype(jnp.bfloat16)
        grad_query = (
            jnp.einsum("hqk,khe->qhe", grad_scores, keys_in, preferred_element_type=jnp.float32)
            * factor
        )
        return (grad_query.reshape(-1, D), grad_scores, probability.astype(jnp.bfloat16))

    grad_queries, score_grads, prob_store = lax.map(
        attend_back, (queries, gathered_back, key_usable, log_total, grad_grouped, full_heads)
    )
    grad_keys = (
        jnp.einsum("bhqk,bqhe->kbhe", score_grads, queries, preferred_element_type=jnp.float32)
        * factor
    )
    grad_values = jnp.einsum(
        "bhqk,bqhe->kbhe", prob_store, grad_grouped, preferred_element_type=jnp.float32
    )
    pair_sums = lax.psum_scatter(
        jnp.concatenate(
            [
                grad_keys.reshape(lax.axis_size("seq") * per_group, blocks, D),
                grad_values.reshape(lax.axis_size("seq") * per_group, blocks, D),
            ],
            axis=-1,
        ).astype(jnp.bfloat16),
        "seq",
        scatter_dimension=0,
        tiled=True,
    )
    pair_grads = pair_sums.transpose(1, 0, 2).reshape(latents_here, 4, per_group, 2 * D)
    query_grads = grad_queries.astype(jnp.bfloat16).reshape(latents_here, 4, per_group, D)
    grad_triple = ungroup(jnp.concatenate([query_grads, pair_grads], axis=-1), rows_here, grid_cols)
    qkv_grad = jnp.einsum(
        "lrwd,lrwe->de", mixed_in, grad_triple, preferred_element_type=jnp.float32
    )
    grad_mixed = jnp.einsum(
        "lrwe,de->lrwd", grad_triple, qkv_weight, preferred_element_type=jnp.float32
    ).astype(jnp.bfloat16)
    conv_attn_grad = kernel_grad(entered_pad, grad_mixed, rows_here, grid_cols)
    grad_mixed_pad = pad_columns(extended(grad_mixed, (("seq", 1),), 1))
    grad_entered = (
        grad_mixed.astype(jnp.float32)
        + shifted_sum(grad_mixed_pad, conv_attn[::-1], rows_here, grid_cols)
    ) * usable
    grad_shift_one = jnp.sum(grad_entered, axis=(1, 2))
    grad_scale_one = jnp.sum(grad_entered * normed_one, axis=(1, 2))
    token_grad = grad_after + norm_back(grad_entered * (1.0 + scale_one), normed_one, scaled_one)
    grad_pieces = jnp.stack(
        [
            grad_shift_one,
            grad_scale_one,
            grad_gate_one,
            grad_shift_two,
            grad_scale_two,
            grad_gate_two,
        ],
        axis=1,
    ).reshape(latents_here, 6 * D)
    ada_weight_grad = jnp.dot(
        activated_cond.astype(jnp.float32).T,
        grad_pieces,
        precision=HIGHEST,
        preferred_element_type=jnp.float32,
    )
    ada_bias_grad = jnp.sum(grad_pieces, axis=0)
    grad_silu = jnp.dot(
        grad_pieces,
        ada_weight.astype(jnp.float32).T,
        precision=HIGHEST,
        preferred_element_type=jnp.float32,
    )
    grad_condition = grad_silu * logistic * (1.0 + condition * (1.0 - logistic))
    time_grad = jnp.dot(
        embedding.astype(jnp.float32).T,
        grad_condition,
        precision=HIGHEST,
        preferred_element_type=jnp.float32,
    )
    class_grad = jnp.dot(
        one_hot.astype(jnp.float32).T,
        grad_condition,
        precision=HIGHEST,
        preferred_element_type=jnp.float32,
    )
    cond_grad = lax.psum(grad_condition, "seq")
    shares = (
        lax.psum_scatter(time_grad, ("batch", "seq"), scatter_dimension=1, tiled=True),
        lax.psum_scatter(class_grad, ("batch", "seq"), scatter_dimension=1, tiled=True),
        lax.psum_scatter(ada_weight_grad, ("batch", "seq"), scatter_dimension=0, tiled=True),
        lax.psum_scatter(ada_bias_grad, ("batch", "seq"), scatter_dimension=0, tiled=True),
        lax.psum_scatter(conv_attn_grad, ("batch", "seq"), scatter_dimension=1, tiled=True),
        lax.psum_scatter(qkv_grad, ("batch", "seq"), scatter_dimension=0, tiled=True),
        lax.psum_scatter(proj_grad, ("batch", "seq"), scatter_dimension=0, tiled=True),
        lax.psum_scatter(up_grad, ("batch", "seq"), scatter_dimension=0, tiled=True),
        lax.psum_scatter(conv_ffn_grad, ("batch", "seq"), scatter_dimension=1, tiled=True),
        lax.psum_scatter(down_grad, ("batch", "seq"), scatter_dimension=1, tiled=True),
    )
    return (
        output,
        token_grad,
        cond_grad,
        shares[0],
        shares[1],
        shares[2],
        shares[3],
        shares[4],
        shares[5],
        shares[6],
        shares[7],
        shares[8],
        shares[9],
    )


def solution(mesh):
    in_specs = (
        P("batch", "seq", None, None),
        P("batch", "seq", None, None),
        P("batch"),
        P("batch"),
        P("batch"),
        P("batch"),
        P(),
        P(),
        P(),
        P(),
        P(),
        P(),
        P(),
        P(),
        P(),
        P(),
    )
    out_specs = (
        P("batch", "seq", None, None),
        P("batch", "seq", None, None),
        P("batch", None),
        P(None, ("batch", "seq")),
        P(None, ("batch", "seq")),
        P(("batch", "seq"), None),
        P(("batch", "seq")),
        P(None, ("batch", "seq")),
        P(("batch", "seq"), None),
        P(("batch", "seq"), None),
        P(("batch", "seq"), None),
        P(None, ("batch", "seq")),
        P(None, ("batch", "seq")),
    )
    return jax.shard_map(shards, mesh=mesh, in_specs=in_specs, out_specs=out_specs, check_vma=False)
```

profile of v0, /device:TPU:0, one launch (start us, length us, event | category | flops | bytes accessed | tf_op | source)
XLA Modules:
  0.0 1881.0 jit_solution(4200168843573450520)
XLA Ops:
  76.1 158.2 %all-gather.2.cloned.1.call-done = bf16[2,4,512,1536]{3,2,1,0:T(8,128)(2,1)} async-done(((bf16[2,4,64,1536]{3,2,1,0:T(8,128)(2,1)}), bf16[2,4,512,1536]{3,2,1,0:T(8,128)(2,1)}) %all-gather.2.cloned.1.call-update) | async-done | bytes 12582928 | tf_op jit(solution)/shard_map/all_gather | solution.py:176
  234.3 16.6 copy.95
  251.8 77.9 %while.28 = (s32[]{:T(128)}, bf16[8,64,768]{2,1,0:T(8,128)(2,1)}, f32[8,64,768]{1,2,0:T(8,128)}, f32[8,12,64]{2,1,0:T(8,128)}, bf16[8,512,1536]{1,2,0:T(8,128)(2...) while((s32[]{:T(128)}, bf16[8,64,768]{2,1,0:T(8,128)(2,1)}, ...), condition=%wide.region_5.6_spmd, body=%wide.region_2.5_spmd.sunk | while | flops 156548352 | bytes 17635960 | solution.py:207
  346.1 31.7 %collective-permute-done.2 = bf16[2,1,64,3072]{3,2,1,0:T(8,128)(2,1)S(1)} collective-permute-done((bf16[2,1,64,3072]{3,2,1,0:T(8,128)(2,1)S(1)}, bf16[2,1,64,3072]{3,2,1,0:T(8,128)(2,1)S(1)}, u32[]{:S(2)}, u32[]{:S(2)}) %collective-permute-start.2) | collective-permute-done | bytes 786464 | tf_op jit(solution)/shard_map/ppermute | solution.py:24
  379.9 9.1 multiply_convert_fusion.2
  389.0 14.3 fusion.47
  413.2 29.9 %collective-permute-done.4 = bf16[2,1,64,3072]{3,2,1,0:T(8,128)(2,1)} collective-permute-done((bf16[2,1,64,3072]{3,2,1,0:T(8,128)(2,1)}, bf16[2,1,64,3072]{3,2,1,0:T(8,128)(2,1)}, u32[]{:S(2)}, u32[]{:S(2)}) %collective-permute-start.4) | collective-permute-done | bytes 786464 | tf_op jit(solution)/shard_map/ppermute | solution.py:24
  448.3 7.5 fusion.38
  480.0 147.9 %while.29 = (s32[]{:T(128)}, bf16[8,64,768]{2,1,0:T(8,128)(2,1)}, bf16[8,12,64,512]{3,2,1,0:T(8,128)(2,1)}, bf16[8,12,64,512]{3,2,1,0:T(8,128)(2,1)}, bf16[8,512...) while((s32[]{:T(128)}, bf16[8,64,768]{2,1,0:T(8,128)(2,1)}, ...), condition=%wide.region_12.13_spmd, body=%wide.region_10.12_spmd.sunk | while | flops 153992448 | bytes 23219384 | solution.py:287
  628.0 7.8 multiply_convert_fusion.1
  635.7 8.7 copy.109
  644.4 7.8 convolution_convert_fusion.1
  652.2 8.7 copy.110
  660.8 10.5 pad_maximum_fusion
  681.0 8.9 convolution_bitcast_fusion.3
  690.7 8.9 convolution_bitcast_fusion.1
  699.9 183.0 %reduce-scatter.13.cloned.1.call-done = bf16[64,8,1536]{2,0,1:T(8,128)(2,1)} async-done(((bf16[512,8,1536]{2,0,1:T(8,128)(2,1)}), bf16[64,8,1536]{2,0,1:T(8,128)(2,1)}) %reduce-scatter.13.cloned.1.call-update) | async-done | bytes 1572880 | tf_op jit(solution)/shard_map/reduce_scatter | solution.py:297
  894.4 8.1 fusion.102
  907.4 7.1 collective-permute-done.6
  920.0 7.8 fusion.114
  934.1 7.0 convolution_bitcast_fusion.2
  941.1 9.7 fusion.138
  950.9 33.4 %reduce-scatter.29.cloned.1.call-done = f32[96,9]{1,0:T(8,128)} async-done(((f32[3072,9]{1,0:T(8,128)}), f32[96,9]{1,0:T(8,128)}) %reduce-scatter.29.cloned.1.call-update) | async-done | bytes 3472
  1002.5 41.2 %all-reduce.6 = (f32[4608]{0:T(1024)}, f32[9,768]{1,0:T(8,128)}) all-reduce(f32[4608]{0:T(1024)} %reduce_sum.332, f32[9,768]{1,0:T(8,128)} %stack.97), channel_id=6, replica_groups=mesh['batch'=4,'seq'=8] {'batch','seq'}, use_global_device_ids=true, to_apply=%region_27.28.clone | all-reduce | flops 11520 | bytes 92160
  1045.1 21.2 %psum.7 = f32[2,768]{1,0:T(2,128)} all-reduce(f32[2,768]{1,0:T(2,128)S(1)} %copy-done.44), channel_id=1, replica_groups=mesh['batch'=4,'seq'=8] {'seq'}, use_global_device_ids=true, to_apply=%region_22.23 | all-reduce | flops 1536 | bytes 12288 | tf_op jit(solution)/shard_map/psum | solution.py:364
  1072.9 15.3 reduce-scatter.23.cloned.1.call-done
  1088.3 141.9 %reduce-scatter.27.cloned.1.call-done = f32[3072,24]{0,1:T(8,128)} async-done(((f32[3072,768]{0,1:T(8,128)}), f32[3072,24]{0,1:T(8,128)}) %reduce-scatter.27.cloned.1.call-update) | async-done | bytes 294928 | tf_op jit(solution)/shard_map/reduce_scatter | solution.py:375
  1230.2 141.1 %reduce-scatter.25.cloned.1.call-done = f32[24,3072]{1,0:T(8,128)} async-done(((f32[768,3072]{1,0:T(8,128)}), f32[24,3072]{1,0:T(8,128)}) %reduce-scatter.25.cloned.1.call-update) | async-done | bytes 294928 | tf_op jit(solution)/shard_map/reduce_scatter | solution.py:373
  1371.2 101.1 %reduce-scatter.15.cloned.1.call-done = f32[256,24]{0,1:T(8,128)} async-done(((f32[256,768]{0,1:T(8,128)}), f32[256,24]{0,1:T(8,128)}) %reduce-scatter.15.cloned.1.call-update) | async-done | bytes 24592 | tf_op jit(solution)/shard_map/reduce_scatter | solution.py:366
  1472.3 107.5 %reduce-scatter.17.cloned.1.call-done = f32[1000,24]{0,1:T(8,128)} async-done(((f32[1000,768]{0,1:T(8,128)}), f32[1000,24]{0,1:T(8,128)}) %reduce-scatter.17.cloned.1.call-update) | async-done | bytes 96016 | tf_op jit(solution)/shard_map/reduce_scatter | solution.py:367
  1579.8 125.3 %reduce-scatter.21.cloned.1.call-done = f32[24,2304]{1,0:T(8,128)} async-done(((f32[768,2304]{1,0:T(8,128)}), f32[24,2304]{1,0:T(8,128)}) %reduce-scatter.21.cloned.1.call-update) | async-done | bytes 221200 | tf_op jit(solution)/shard_map/reduce_scatter | solution.py:371
  1705.1 168.6 %reduce-scatter.19.cloned.1.call-done = f32[24,4608]{1,0:T(8,128)} async-done(((f32[768,4608]{1,0:T(8,128)}), f32[24,4608]{1,0:T(8,128)}) %reduce-scatter.19.cloned.1.call-update) | async-done | bytes 442384 | tf_op jit(solution)/shard_map/reduce_scatter | solution.py:368
  (571 shorter events, 416.3 us)
Async XLA Ops:
  7.2 36.1 %copy-start = (bf16[768,2304]{1,0:T(8,128)(2,1)S(1)}, bf16[768,2304]{1,0:T(8,128)(2,1)}, u32[]{:S(2)}) copy-start(bf16[768,2304]{1,0:T(8,128)(2,1)} %param.31) | copy-start | bytes 10616836
  7.2 227.1 %all-gather.2.cloned.1.call-start = ((), (), s32[]{:S(2)}) async-start(), calls=%async_computation.9 | async-start | bytes 14155776 | tf_op jit(solution)/shard_map/all_gather | solution.py:176
  27.0 9.1 collective-permute-start
  31.8 8.3 collective-permute-start.1
  55.4 827.5 %reduce-scatter.13.cloned.1.call-start = ((), (), s32[]{:S(2)}) async-start(), calls=%async_computation.10 | async-start | bytes 14155776 | tf_op jit(solution)/shard_map/reduce_scatter | solution.py:297
  59.9 271.8 %copy-start.49 = (f32[2,1,1,1,768]{4,0,1,3,2:T(2,128)}, f32[2,1,1,1,768]{4,0,1,3,2:T(2,128)S(1)}, u32[]{:S(2)}) copy-start(f32[2,1,1,1,768]{4,0,1,3,2:T(2,128)S(1)} %copy.188) | copy-start | bytes 18436
  342.1 35.7 %collective-permute-start.2 = (bf16[2,1,64,3072]{3,2,1,0:T(8,128)(2,1)S(1)}, bf16[2,1,64,3072]{3,2,1,0:T(8,128)(2,1)S(1)}, u32[]{:S(2)}, u32[]{:S(2)}) collective-permute-start(bf16[2,1,64,3072]{3,2,1,0:T(8,128)(2,1)S(1)} %get-tuple-element.293), channel_id=1, source_target_pairs={{0,1},{1,2},{2,3},{3,4},{4,5},{5,6},{6,7},{8,9},{9,10},{10,11},{11... | collective-permute-start | bytes 2359304 | tf_op jit(solution)/shard_map/ppermute | solution.py:24
  344.6 33.2 %collective-permute-start.3 = (bf16[2,1,64,3072]{3,2,1,0:T(8,128)(2,1)S(1)}, bf16[2,1,64,3072]{3,2,1,0:T(8,128)(2,1)S(1)}, u32[]{:S(2)}, u32[]{:S(2)}) collective-permute-start(bf16[2,1,64,3072]{3,2,1,0:T(8,128)(2,1)S(1)} %get-tuple-element.294), channel_id=1, source_target_pairs={{1,0},{2,1},{3,2},{4,3},{5,4},{6,5},{7,6},{9,8},{10,9},{11,10},{12... | collective-permute-start | bytes 2359304 | tf_op jit(solution)/shard_map/ppermute | solution.py:26
  345.9 43.1 %copy-start.82 = (f32[2,1,1,1,768]{4,0,1,3,2:T(2,128)}, f32[2,1,1,1,768]{4,0,1,3,2:T(2,128)S(1)}, u32[]{:S(2)}) copy-start(f32[2,1,1,1,768]{4,0,1,3,2:T(2,128)S(1)} %copy.187) | copy-start | bytes 18436
  346.0 33.8 %copy-start.25 = (f32[1,3072]{1,0:T(1,128)}, f32[1,3072]{1,0:T(1,128)S(1)}, u32[]{:S(2)}) copy-start(f32[1,3072]{1,0:T(1,128)S(1)} %get-tuple-element.304) | copy-start | bytes 36868
  406.1 37.0 %collective-permute-start.4 = (bf16[2,1,64,3072]{3,2,1,0:T(8,128)(2,1)}, bf16[2,1,64,3072]{3,2,1,0:T(8,128)(2,1)}, u32[]{:S(2)}, u32[]{:S(2)}) collective-permute-start(bf16[2,1,64,3072]{3,2,1,0:T(8,128)(2,1)} %get-tuple-element.291), channel_id=1, source_target_pairs={{0,1},{1,2},{2,3},{3,4},{4,5},{5,6},{6,7},{8,9},{9,10},{10,11},{11... | collective-permute-start | bytes 2359304 | tf_op jit(solution)/shard_map/ppermute | solution.py:24
  411.4 31.7 %collective-permute-start.5 = (bf16[2,1,64,3072]{3,2,1,0:T(8,128)(2,1)}, bf16[2,1,64,3072]{3,2,1,0:T(8,128)(2,1)}, u32[]{:S(2)}, u32[]{:S(2)}) collective-permute-start(bf16[2,1,64,3072]{3,2,1,0:T(8,128)(2,1)} %get-tuple-element.292), channel_id=1, source_target_pairs={{1,0},{2,1},{3,2},{4,3},{5,4},{6,5},{7,6},{9,8},{10,9},{11,10},{12... | collective-permute-start | bytes 2359304 | tf_op jit(solution)/shard_map/ppermute | solution.py:26
  413.1 35.0 %copy-start.6 = (bf16[2,4,64,3072]{3,2,1,0:T(8,128)(2,1)S(1)}, bf16[2,4,64,3072]{3,2,1,0:T(8,128)(2,1)}, u32[]{:S(2)}) copy-start(bf16[2,4,64,3072]{3,2,1,0:T(8,128)(2,1)} %copy-done.5) | copy-start | bytes 9437188
  413.1 35.0 %copy-start.26 = (f32[1,3072]{1,0:T(1,128)S(1)}, f32[1,3072]{1,0:T(1,128)}, u32[]{:S(2)}) copy-start(f32[1,3072]{1,0:T(1,128)} %copy-done.25) | copy-start | bytes 36868
  413.1 35.0 %copy-start.28 = (f32[1,3072]{1,0:T(1,128)S(1)}, f32[1,3072]{1,0:T(1,128)}, u32[]{:S(2)}) copy-start(f32[1,3072]{1,0:T(1,128)} %copy-done.27) | copy-start | bytes 36868
  413.1 35.0 %copy-start.30 = (f32[1,3072]{1,0:T(1,128)S(1)}, f32[1,3072]{1,0:T(1,128)}, u32[]{:S(2)}) copy-start(f32[1,3072]{1,0:T(1,128)} %copy-done.29) | copy-start | bytes 36868
  413.1 35.0 %copy-start.32 = (f32[1,3072]{1,0:T(1,128)S(1)}, f32[1,3072]{1,0:T(1,128)}, u32[]{:S(2)}) copy-start(f32[1,3072]{1,0:T(1,128)} %copy-done.31) | copy-start | bytes 36868
  413.2 35.0 %copy-start.34 = (f32[1,3072]{1,0:T(1,128)S(1)}, f32[1,3072]{1,0:T(1,128)}, u32[]{:S(2)}) copy-start(f32[1,3072]{1,0:T(1,128)} %copy-done.33) | copy-start | bytes 36868
  413.2 35.0 %copy-start.36 = (f32[1,3072]{1,0:T(1,128)S(1)}, f32[1,3072]{1,0:T(1,128)}, u32[]{:S(2)}) copy-start(f32[1,3072]{1,0:T(1,128)} %copy-done.35) | copy-start | bytes 36868
  413.2 35.0 %copy-start.38 = (f32[1,3072]{1,0:T(1,128)S(1)}, f32[1,3072]{1,0:T(1,128)}, u32[]{:S(2)}) copy-start(f32[1,3072]{1,0:T(1,128)} %copy-done.37) | copy-start | bytes 36868
  413.2 35.0 %copy-start.40 = (f32[1,3072]{1,0:T(1,128)S(1)}, f32[1,3072]{1,0:T(1,128)}, u32[]{:S(2)}) copy-start(f32[1,3072]{1,0:T(1,128)} %copy-done.39) | copy-start | bytes 36868
  671.4 312.9 %reduce-scatter.29.cloned.1.call-start = ((), (), s32[]{:S(2)}) async-start(), calls=%async_computation.18 | async-start | bytes 1622016
  677.0 411.2 %reduce-scatter.23.cloned.1.call-start = ((), (), s32[]{:S(2)}) async-start(), calls=%async_computation.15 | async-start | bytes 2433024 | tf_op jit(solution)/shard_map/reduce_scatter | solution.py:372
  681.0 549.2 %reduce-scatter.27.cloned.1.call-start = ((), (), s32[]{:S(2)}) async-start(), calls=%async_computation.17 | async-start | bytes 9732096 | tf_op jit(solution)/shard_map/reduce_scatter | solution.py:375
  690.0 681.3 %reduce-scatter.25.cloned.1.call-start = ((), (), s32[]{:S(2)}) async-start(), calls=%async_computation.16 | async-start | bytes 9732096 | tf_op jit(solution)/shard_map/reduce_scatter | solution.py:373
  699.6 772.7 %reduce-scatter.15.cloned.1.call-start = ((), (), s32[]{:S(2)}) async-start(), calls=%async_computation.11 | async-start | bytes 811008 | tf_op jit(solution)/shard_map/reduce_scatter | solution.py:366
  902.6 11.9 collective-permute-start.6
  906.1 8.4 collective-permute-start.7
  929.8 650.0 %reduce-scatter.17.cloned.1.call-start = ((), (), s32[]{:S(2)}) async-start(), calls=%async_computation.12 | async-start | bytes 3244032 | tf_op jit(solution)/shard_map/reduce_scatter | solution.py:367
  933.8 771.3 %reduce-scatter.21.cloned.1.call-start = ((), (), s32[]{:S(2)}) async-start(), calls=%async_computation.14 | async-start | bytes 7299072 | tf_op jit(solution)/shard_map/reduce_scatter | solution.py:371
  941.1 932.6 %reduce-scatter.19.cloned.1.call-start = ((), (), s32[]{:S(2)}) async-start(), calls=%async_computation.13 | async-start | bytes 14598144 | tf_op jit(solution)/shard_map/reduce_scatter | solution.py:368
  950.8 94.2 %copy-start.44 = (f32[2,768]{1,0:T(2,128)S(1)}, f32[2,768]{1,0:T(2,128)}, u32[]{:S(2)}) copy-start(f32[2,768]{1,0:T(2,128)} %copy-done.43) | copy-start | bytes 18436
  (107 other events, 817.1 us)
Sparse Core Ops, SparseCore 0:
  55.5 178.7 all-gather.1
  671.5 211.2 reduce-scatter.12
  888.1 96.1 reduce-scatter.28
  990.0 98.2 reduce-scatter.22
  1095.6 134.5 reduce-scatter.26
  1236.5 134.6 reduce-scatter.24
  1377.7 94.5 reduce-scatter.14
  1479.2 100.5 reduce-scatter.16
  1587.0 118.0 reduce-scatter.20
  1711.5 162.1 reduce-scatter.18
where the time goes:
time: 1890 us; the launch traced here: 1880 us
  waiting for transfers between devices  1250 us (66%)
  local copies, waits for them, and re-layouts  253 us (13%)
  matrix products  195 us (10%)
  other arithmetic  80.6 us (4%)
  blocking collectives  62.4 us (3%)
  starting transfers between devices  22.8 us (1%)
    reduce_scatter x1, waiting for transfers between devices, shards(): lax.psum_scatter(jnp.concatenate([grad_keys.reshape(lax.axis_size('seq')...  183 us
    reduce_scatter x1, waiting for transfers between devices, shards(): lax.psum_scatter(ada_weight_grad, ('batch', 'seq'), scatter_dimension=0,...  169 us
    all_gather x1, waiting for transfers between devices, shards(): lax.all_gather(pairs_local, 'seq', axis=2, tiled=True)  158 us
    reduce_scatter x1, waiting for transfers between devices, shards(): lax.psum_scatter(down_grad, ('batch', 'seq'), scatter_dimension=1, tiled=...  142 us
    reduce_scatter x1, waiting for transfers between devices, shards(): lax.psum_scatter(up_grad, ('batch', 'seq'), scatter_dimension=0, tiled=True)  141 us
    reduce_scatter x1, waiting for transfers between devices, shards(): lax.psum_scatter(qkv_grad, ('batch', 'seq'), scatter_dimension=0, tiled=T...  125 us
    reduce_scatter x1, waiting for transfers between devices, shards(): lax.psum_scatter(class_grad, ('batch', 'seq'), scatter_dimension=1, tiled...  107 us
    reduce_scatter x1, waiting for transfers between devices, shards(): lax.psum_scatter(time_grad, ('batch', 'seq'), scatter_dimension=1, tiled=...  101 us
  transfers between devices with their start and end apart: 18, of which 15 were waited for; matrix products, arithmetic and copies ran while one was open for 7% of the time, Pallas kernels for 0%

commit v1 on v0

v1 whole, which is shorter than its diff:
```python
import functools
import math

import jax
import jax.numpy as jnp
from jax import lax
from jax.experimental import pallas as pl
from jax.experimental.pallas import tpu as pltpu
from jax.sharding import PartitionSpec as P

D = 768
HEADS = 12
HEAD_DIM = 64
PAIR = 2 * HEAD_DIM
PAIRS = HEADS // 2
FF_BLOCK = 256
LANE_PARTS = D // 128
FACTOR = HEAD_DIM ** (-0.5)

F32 = jnp.float32
BF16 = jnp.bfloat16
HIGHEST = lax.Precision.HIGHEST
NN = (((1,), (0,)), ((), ()))
NT = (((1,), (1,)), ((), ()))
VMEM_LIMIT = 60 * 1024 * 1024


def mm(left, right, dims=NN):
    return lax.dot_general(left, right, dims, preferred_element_type=F32)


def shift_down(values):
    rows = lax.broadcasted_iota(jnp.int32, values.shape, 0)
    return jnp.where(rows == 0, 0.0, pltpu.roll(values, 1, 0))


def shift_up(values):
    count = values.shape[0]
    rows = lax.broadcasted_iota(jnp.int32, values.shape, 0)
    return jnp.where(rows == count - 1, 0.0, pltpu.roll(values, count - 1, 0))


def put_shifts(ref, row, parity, values):
    ref[row, 1 + parity] = values
    if parity == 0:
        ref[row, 3] = shift_up(values)
    else:
        ref[row, 0] = shift_down(values)


def normalize(values):
    centre = values - jnp.mean(values, axis=-1, keepdims=True)
    spread = jnp.mean(centre * centre, axis=-1, keepdims=True)
    scaled = lax.rsqrt(spread + 1e-06)
    return centre * scaled, scaled


def norm_back(grad_norm, normed, scaled):
    return scaled * (
        grad_norm
        - jnp.mean(grad_norm, axis=-1, keepdims=True)
        - normed * jnp.mean(grad_norm * normed, axis=-1, keepdims=True)
    )


def put_row(buf, row, values):
    for k in range(LANE_PARTS):
        buf[row, k] = values[:, 128 * k : 128 * (k + 1)]


def get_row(buf, row):
    return jnp.concatenate([buf[row, k] for k in range(LANE_PARTS)], axis=1)


def put_columns(buf, row, parity, values):
    for k in range(LANE_PARTS):
        buf[row, k, pl.ds(parity, values.shape[0], stride=2), :] = values[:, 128 * k : 128 * (k + 1)]


def get_columns(buf, row, parity):
    half = buf.shape[2] // 2
    return jnp.concatenate(
        [buf[row, k, pl.ds(parity, half, stride=2), :] for k in range(LANE_PARTS)], axis=1
    )


def usable_of(meta, latents, latent, row, parity, half):
    cols = 2 * lax.broadcasted_iota(jnp.int32, (half, 1), 0) + parity
    row_ok = jnp.logical_and(row >= 0, row < meta[latent])
    limit = jnp.where(row_ok, meta[latents + latent], 0)
    return (cols < limit).astype(F32)


def sum8(values):
    total = values[0:8]
    for start in range(8, values.shape[0], 8):
        total = total + values[start : start + 8]
    return total


def enter_kernel(meta, tok, top, bot, pieces, kern, out, buf, ent):
    latents = pl.num_programs(0)
    latent = pl.program_id(0)
    rows_here, cols = tok.shape[1], tok.shape[2]
    half = cols // 2
    row0 = meta[2 * latents]
    shift = pieces[0, 0:1, :]
    scale = 1.0 + pieces[0, 1:2, :]
    for rr in range(rows_here + 2):
        source = top[0, 0] if rr == 0 else bot[0, 0] if rr == rows_here + 1 else tok[0, rr - 1]
        put_row(buf, rr, source.astype(F32))
        for parity in range(2):
            normed, _ = normalize(get_columns(buf, rr, parity))
            ok = usable_of(meta, latents, latent, row0 + rr - 1, parity, half)
            put_shifts(ent, rr, parity, ((normed * scale + shift) * ok).astype(BF16).astype(F32))
    for row in range(rows_here):
        for parity in range(2):
            total = jnp.zeros((half, D), F32)
            for i in range(3):
                for j in range(3):
                    tap = 3 * i + j
                    total = total + ent[row + i, parity + j] * kern[tap : tap + 1, :]
            mixed = (ent[row + 1, 1 + parity] + total).astype(BF16)
            group = 2 * (row % 2) + parity
            out[0, group, (row // 2) * half : (row // 2 + 1) * half, :] = mixed


def enter(meta, tokens, top, bot, pieces, kern):
    latents, rows_here, cols, _ = tokens.shape
    half = cols // 2
    per_group = rows_here // 2 * half
    whole = lambda *shape: pl.BlockSpec(shape, lambda l, m: (l,) + (0,) * (len(shape) - 1))
    return pl.pallas_call(
        enter_kernel,
        out_shape=jax.ShapeDtypeStruct((latents, 4, per_group, D), BF16),
        grid_spec=pltpu.PrefetchScalarGridSpec(
            num_scalar_prefetch=1,
            grid=(latents,),
            in_specs=[
                whole(1, rows_here, cols, D),
                whole(1, 1, cols, D),
                whole(1, 1, cols, D),
                whole(1, 6, D),
                pl.BlockSpec((9, D), lambda l, m: (0, 0)),
            ],
            out_specs=whole(1, 4, per_group, D),
            scratch_shapes=[
                pltpu.VMEM((rows_here + 2, LANE_PARTS, cols, 128), F32),
                pltpu.VMEM((rows_here + 2, 4, half, D), F32),
            ],
        ),
        compiler_params=pltpu.CompilerParams(vmem_limit_bytes=VMEM_LIMIT),
        name="enter",
    )(meta, tokens, top, bot, pieces, kern)


def cot_kernel(meta, cot, top, bot, pieces, ge_out, get_out, cot_out, buf):
    rows_here, cols = cot.shape[1], cot.shape[2]
    half = cols // 2
    gate = pieces[0, 5:6, :]
    for rr in range(rows_here + 2):
        source = top[0, 0] if rr == 0 else bot[0, 0] if rr == rows_here + 1 else cot[0, rr - 1]
        put_row(buf, rr, source.astype(F32))
        for parity in range(2):
            values = get_columns(buf, rr, parity)
            scaled = (gate * values).astype(BF16)
            at = (2 * rr + parity) * half
            ge_out[0, at : at + half, :] = scaled
            if 1 <= rr <= rows_here:
                cot_out[0, at - cols : at - cols + half, :] = values.astype(BF16)
    inner = ge_out[0, cols : cols + rows_here * cols, :].astype(F32)
    get_out[0] = inner.T.astype(BF16)


def prepare_cot(meta, cotangent, top, bot, pieces):
    latents, rows_here, cols, _ = cotangent.shape
    whole = lambda *shape: pl.BlockSpec(shape, lambda l, m: (l,) + (0,) * (len(shape) - 1))
    own = rows_here * cols
    return pl.pallas_call(
        cot_kernel,
        out_shape=(
            jax.ShapeDtypeStruct((latents, own + 2 * cols, D), BF16),
            jax.ShapeDtypeStruct((latents, D, own), BF16),
            jax.ShapeDtypeStruct((latents, own, D), BF16),
        ),
        grid_spec=pltpu.PrefetchScalarGridSpec(
            num_scalar_prefetch=1,
            grid=(latents,),
            in_specs=[
                whole(1, rows_here, cols, D),
                whole(1, 1, cols, D),
                whole(1, 1, cols, D),
                whole(1, 6, D),
            ],
            out_specs=(whole(1, own + 2 * cols, D), whole(1, D, own), whole(1, own, D)),
            scratch_shapes=[pltpu.VMEM((rows_here + 2, LANE_PARTS, cols, 128), F32)],
        ),
        compiler_params=pltpu.CompilerParams(vmem_limit_bytes=VMEM_LIMIT),
        name="prepare_cot",
    )(meta, cotangent, top, bot, pieces)


def second_kernel(meta, att, tok, top2, top1, bot1, bot2, pieces, proj, e2_out, e2t_out, after_out, branch_out, buf, bran):
    latents = pl.num_programs(0)
    latent = pl.program_id(0)
    rows_here, cols = tok.shape[1], tok.shape[2]
    half = cols // 2
    row0 = meta[2 * latents]
    gate = pieces[0, 2:3, :]
    shift = pieces[0, 3:4, :]
    scale = 1.0 + pieces[0, 4:5, :]
    for group in range(4):
        bran[group] = mm(att[group], proj[...])
    for rr in range(rows_here + 4):
        at_row = rr - 2
        source = (
            top2[0, 0]
            if at_row == -2
            else top1[0, 0]
            if at_row == -1
            else bot1[0, 0]
            if at_row == rows_here
            else bot2[0, 0]
            if at_row == rows_here + 1
            else tok[0, at_row]
        )
        put_row(buf, rr, source.astype(F32))
        for parity in range(2):
            group = 2 * (rr % 2) + parity
            branch = bran[group, (rr // 2) * half : (rr // 2 + 1) * half, :]
            after = get_columns(buf, rr, parity) + gate * branch
            normed, _ = normalize(after)
            ok = usable_of(meta, latents, latent, row0 + at_row, parity, half)
            at = (2 * rr + parity) * half
            e2_out[0, at : at + half, :] = ((normed * scale + shift) * ok).astype(BF16)
            if 0 <= at_row < rows_here:
                own = at - 2 * cols
                after_out[0, own : own + half, :] = after
                branch_out[0, own : own + half, :] = branch
    inner = e2_out[0, 2 * cols : 2 * cols + rows_here * cols, :].astype(F32)
    e2t_out[0] = inner.T.astype(BF16)


def second(meta, attended, tokens, tops, bots, pieces, proj):
    latents, rows_here, cols, _ = tokens.shape
    half = cols // 2
    own = rows_here * cols
    wide = attended.shape[1]
    whole = lambda *shape: pl.BlockSpec(shape, lambda l, m: (l,) + (0,) * (len(shape) - 1))
    return pl.pallas_call(
        second_kernel,
        out_shape=(
            jax.ShapeDtypeStruct((latents, own + 4 * cols, D), BF16),
            jax.ShapeDtypeStruct((latents, D, own), BF16),
            jax.ShapeDtypeStruct((latents, own, D), F32),
            jax.ShapeDtypeStruct((latents, own, D), F32),
        ),
        grid_spec=pltpu.PrefetchScalarGridSpec(
            num_scalar_prefetch=1,
            grid=(latents,),
            in_specs=[
                whole(4, wide, D),
                whole(1, rows_here, cols, D),
                whole(1, 1, cols, D),
                whole(1, 1, cols, D),
                whole(1, 1, cols, D),
                whole(1, 1, cols, D),
                whole(1, 6, D),
                pl.BlockSpec((D, D), lambda l, m: (0, 0)),
            ],
            out_specs=(
                whole(1, own + 4 * cols, D),
                whole(1, D, own),
                whole(1, own, D),
                whole(1, own, D),
            ),
            scratch_shapes=[
                pltpu.VMEM((rows_here + 4, LANE_PARTS, cols, 128), F32),
                pltpu.VMEM((4, wide, D), F32),
            ],
        ),
        compiler_params=pltpu.CompilerParams(vmem_limit_bytes=VMEM_LIMIT),
        name="second",
    )(meta, attended, tokens, tops[1], tops[0], bots[0], bots[1], pieces, proj)


def ffn_kernel(e2, e2t, ge, get, up, down, kern, exp_out, ge2_out, down_out, up_out, kern_out, lifted, gact, gconv, act, graised, exp_acc, ge2_acc, down_acc, up_acc, kern_acc):
    step, latent = pl.program_id(0), pl.program_id(1)
    steps, latents = pl.num_programs(0), pl.num_programs(1)
    half = lifted.shape[2]
    rows_here = lifted.shape[0] - 4
    block = lifted.shape[3]

    raised = mm(e2[0], up[...]).astype(BF16).astype(F32)
    for rr in range(rows_here + 4):
        for parity in range(2):
            at = (2 * rr + parity) * half
            put_shifts(lifted, rr, parity, raised[at : at + half])
    gact[...] = mm(ge[0], down[...], NT)

    taps = [kern[t : t + 1, :] for t in range(9)]

    for rr in range(rows_here + 2):
        for parity in range(2):
            total = jnp.zeros((half, block), F32)
            for i in range(3):
                for j in range(3):
                    total = total + lifted[rr + i, parity + j] * taps[3 * i + j]
            cdf = 0.5 * (1.0 + lax.erf(total * 0.7071067811865476))
            bell = jnp.exp(-0.5 * total * total) * 0.3989422804014327
            at = (2 * rr + parity) * half
            if 1 <= rr <= rows_here:
                own = at - 2 * half
                act[own : own + half, :] = (total * cdf).astype(BF16)
            grad = gact[at : at + half, :] * (cdf + total * bell)
            put_shifts(gconv, rr, parity, grad.astype(BF16).astype(F32))

    sums = [jnp.zeros((8, block), F32) for _ in range(9)]
    for row in range(rows_here):
        for parity in range(2):
            total = jnp.zeros((half, block), F32)
            here = gconv[row + 1, 1 + parity]
            for i in range(3):
                for j in range(3):
                    total = total + gconv[row + 2 - i, parity + 2 - j] * taps[3 * i + j]
                    sums[3 * i + j] = sums[3 * i + j] + sum8(lifted[row + 1 + i, parity + j] * here)
            at = (2 * row + parity) * half
            graised[at : at + half, :] = total.astype(BF16)

    expanded = mm(act[...], down[...])
    grad_e2 = mm(graised[...], up[...], NT)
    down_part = mm(get[0], act[...])
    up_part = mm(e2t[0], graised[...])

    @pl.when(step == 0)
    def _():
        exp_acc[latent] = expanded
        ge2_acc[latent] = grad_e2

    @pl.when(step > 0)
    def _():
        exp_acc[latent] += expanded
        ge2_acc[latent] += grad_e2

    @pl.when(latent == 0)
    def _():
        down_acc[...] = down_part
        up_acc[...] = up_part
        for t in range(9):
            kern_acc[t] = sums[t]

    @pl.when(latent > 0)
    def _():
        down_acc[...] += down_part
        up_acc[...] += up_part
        for t in range(9):
            kern_acc[t] += sums[t]

    @pl.when(latent == latents - 1)
    def _():
        down_out[...] = down_acc[...].astype(BF16)
        up_out[...] = up_acc[...].astype(BF16)
        for t in range(9):
            kern_out[t : t + 1, :] = jnp.sum(kern_acc[t], axis=0, keepdims=True)

    @pl.when(step == steps - 1)
    def _():
        exp_out[latent] = exp_acc[latent]
        ge2_out[latent] = ge2_acc[latent]


def ffn(e2, e2t, ge, get, up, down, kern, cols):
    latents = e2.shape[0]
    half = cols // 2
    own = e2t.shape[2]
    rows_here = own // cols
    hidden = up.shape[1]
    steps = hidden // FF_BLOCK
    per_latent = lambda *shape: pl.BlockSpec((1,) + shape, lambda f, l: (l, 0, 0))
    return pl.pallas_call(
        ffn_kernel,
        out_shape=(
            jax.ShapeDtypeStruct((latents, own, D), F32),
            jax.ShapeDtypeStruct((latents, own, D), F32),
            jax.ShapeDtypeStruct((D, hidden), BF16),
            jax.ShapeDtypeStruct((D, hidden), BF16),
            jax.ShapeDtypeStruct((9, hidden), F32),
        ),
        grid=(steps, latents),
        in_specs=[
            per_latent(own + 4 * cols, D),
            per_latent(D, own),
            per_latent(own + 2 * cols, D),
            per_latent(D, own),
            pl.BlockSpec((D, FF_BLOCK), lambda f, l: (0, f)),
            pl.BlockSpec((FF_BLOCK, D), lambda f, l: (f, 0)),
            pl.BlockSpec((9, FF_BLOCK), lambda f, l: (0, f)),
        ],
        out_specs=(
            pl.BlockSpec((latents, own, D), lambda f, l: (0, 0, 0)),
            pl.BlockSpec((latents, own, D), lambda f, l: (0, 0, 0)),
            pl.BlockSpec((D, FF_BLOCK), lambda f, l: (0, f)),
            pl.BlockSpec((D, FF_BLOCK), lambda f, l: (0, f)),
            pl.BlockSpec((9, FF_BLOCK), lambda f, l: (0, f)),
        ),
        scratch_shapes=[
            pltpu.VMEM((rows_here + 4, 4, half, FF_BLOCK), F32),
            pltpu.VMEM((own + 2 * cols, FF_BLOCK), F32),
            pltpu.VMEM((rows_here + 2, 4, half, FF_BLOCK), F32),
            pltpu.VMEM((own, FF_BLOCK), BF16),
            pltpu.VMEM((own, FF_BLOCK), BF16),
            pltpu.VMEM((latents, own, D), F32),
            pltpu.VMEM((latents, own, D), F32),
            pltpu.VMEM((D, FF_BLOCK), F32),
            pltpu.VMEM((D, FF_BLOCK), F32),
            pltpu.VMEM((9, 8, FF_BLOCK), F32),
        ],
        compiler_params=pltpu.CompilerParams(vmem_limit_bytes=VMEM_LIMIT),
        name="ffn",
    )(e2, e2t, ge, get, up, down, kern)


def middle_kernel(meta, exp, ge2, after_in, branch_in, cot_in, pieces, proj, out, after_grad, gb_out, gatt_out, sums_out, buf):
    latents = pl.num_programs(0)
    latent = pl.program_id(0)
    rows_here, cols = out.shape[1], out.shape[2]
    half = cols // 2
    row0 = meta[2 * latents]
    gate_one = pieces[0, 2:3, :]
    scale = 1.0 + pieces[0, 4:5, :]
    gate_two = pieces[0, 5:6, :]
    sums = [jnp.zeros((8, D), F32) for _ in range(4)]
    for row in range(rows_here):
        for parity in range(2):
            at = (2 * row + parity) * half
            part = pl.ds(at, half)
            after = after_in[0, part, :]
            cot = cot_in[0, part, :].astype(F32)
            expanded = exp[0, part, :]
            put_columns(buf, row, parity, after + gate_two * expanded)
            normed, scaled = normalize(after)
            ok = usable_of(meta, latents, latent, row0 + row, parity, half)
            grad = ge2[0, part, :] * ok
            grad_after = cot + norm_back(grad * scale, normed, scaled)
            after_grad[0, part, :] = grad_after
            sums[0] = sums[0] + sum8(grad_after * branch_in[0, part, :])
            sums[1] = sums[1] + sum8(grad)
            sums[2] = sums[2] + sum8(grad * normed)
            sums[3] = sums[3] + sum8(cot * expanded)
            group = 2 * (row % 2) + parity
            to = pl.ds((row // 2) * half, half)
            gb_out[0, group, to, :] = (gate_one * grad_after).astype(BF16)
        out[0, row] = get_row(buf, row).astype(BF16)
    for k in range(4):
        sums_out[0, k : k + 1, :] = jnp.sum(sums[k], axis=0, keepdims=True)
    for group in range(4):
        gatt_out[0, group] = mm(gb_out[0, group], proj[...], NT).astype(BF16)


def middle(meta, exp, ge2, after, branch, cot, pieces, proj, rows_here, cols):
    latents, own, _ = exp.shape
    per_group = own // 4
    whole = lambda *shape: pl.BlockSpec(shape, lambda l, m: (l,) + (0,) * (len(shape) - 1))
    return pl.pallas_call(
        middle_kernel,
        out_shape=(
            jax.ShapeDtypeStruct((latents, rows_here, cols, D), BF16),
            jax.ShapeDtypeStruct((latents, own, D), F32),
            jax.ShapeDtypeStruct((latents, 4, per_group, D), BF16),
            jax.ShapeDtypeStruct((latents, 4, per_group, D), BF16),
            jax.ShapeDtypeStruct((latents, 4, D), F32),
        ),
        grid_spec=pltpu.PrefetchScalarGridSpec(
            num_scalar_prefetch=1,
            grid=(latents,),
            in_specs=[
                whole(1, own, D),
                whole(1, own, D),
                whole(1, own, D),
                whole(1, own, D),
                whole(1, own, D),
                whole(1, 6, D),
                pl.BlockSpec((D, D), lambda l, m: (0, 0)),
            ],
            out_specs=(
                whole(1, rows_here, cols, D),
                whole(1, own, D),
                whole(1, 4, per_group, D),
                whole(1, 4, per_group, D),
                whole(1, 4, D),
            ),
            scratch_shapes=[
                pltpu.VMEM((rows_here, LANE_PARTS, cols, 128), F32),
            ],
        ),
        compiler_params=pltpu.CompilerParams(vmem_limit_bytes=VMEM_LIMIT),
        name="middle",
    )(meta, exp, ge2, after, branch, cot, pieces, proj)


def leave_kernel(meta, gm, tok, top, bot, after_grad, pieces, kern, out, kern_out, sums_out, buf, ent, gmx, obuf):
    latents = pl.num_programs(0)
    latent = pl.program_id(0)
    rows_here, cols = tok.shape[1], tok.shape[2]
    half = cols // 2
    row0 = meta[2 * latents]
    shift = pieces[0, 0:1, :]
    scale = 1.0 + pieces[0, 1:2, :]
    taps = [kern[t : t + 1, :] for t in range(9)]
    for rr in range(rows_here + 2):
        source = top[0, 0] if rr == 0 else bot[0, 0] if rr == rows_here + 1 else tok[0, rr - 1]
        put_row(buf, rr, source.astype(F32))
        for parity in range(2):
            normed, _ = normalize(get_columns(buf, rr, parity))
            ok = usable_of(meta, latents, latent, row0 + rr - 1, parity, half)
            put_shifts(ent, rr, parity, ((normed * scale + shift) * ok).astype(BF16).astype(F32))
            group = 2 * ((rr + 1) % 2) + parity
            at = (rr // 2) * half
            put_shifts(gmx, rr, parity, gm[group, at : at + half, :].astype(F32))
    sums = [jnp.zeros((8, D), F32) for _ in range(2)]
    tap_sums = [jnp.zeros((8, D), F32) for _ in range(9)]
    for row in range(rows_here):
        for parity in range(2):
            here = gmx[row + 1, 1 + parity]
            total = here
            for i in range(3):
                for j in range(3):
                    t = 3 * i + j
                    total = total + gmx[row + 2 - i, parity + 2 - j] * taps[t]
                    tap_sums[t] = tap_sums[t] + sum8(ent[row + i, parity + j] * here)
            ok = usable_of(meta, latents, latent, row0 + row, parity, half)
            grad = total * ok
            normed, scaled = normalize(get_columns(buf, row + 1, parity))
            sums[0] = sums[0] + sum8(grad)
            sums[1] = sums[1] + sum8(grad * normed)
            at = (2 * row + parity) * half
            back = after_grad[0, at : at + half, :] + norm_back(grad * scale, normed, scaled)
            put_columns(obuf, row, parity, back)
        out[0, row] = get_row(obuf, row)
    for k in range(2):
        sums_out[0, k : k + 1, :] = jnp.sum(sums[k], axis=0, keepdims=True)
    for t in range(9):
        kern_out[0, t : t + 1, :] = jnp.sum(tap_sums[t], axis=0, keepdims=True)


def leave(meta, gm, tokens, top, bot, after_grad, pieces, kern):
    latents, rows_here, cols, _ = tokens.shape
    half = cols // 2
    own = rows_here * cols
    wide = gm.shape[1]
    whole = lambda *shape: pl.BlockSpec(shape, lambda l, m: (l,) + (0,) * (len(shape) - 1))
    return pl.pallas_call(
        leave_kernel,
        out_shape=(
            jax.ShapeDtypeStruct((latents, rows_here, cols, D), F32),
            jax.ShapeDtypeStruct((latents, 9, D), F32),
            jax.ShapeDtypeStruct((latents, 2, D), F32),
        ),
        grid_spec=pltpu.PrefetchScalarGridSpec(
            num_scalar_prefetch=1,
            grid=(latents,),
            in_specs=[
                whole(4, wide, D),
                whole(1, rows_here, cols, D),
                whole(1, 1, cols, D),
                whole(1, 1, cols, D),
                whole(1, own, D),
                whole(1, 6, D),
                pl.BlockSpec((9, D), lambda l, m: (0, 0)),
            ],
            out_specs=(whole(1, rows_here, cols, D), whole(1, 9, D), whole(1, 2, D)),
            scratch_shapes=[
                pltpu.VMEM((rows_here + 2, LANE_PARTS, cols, 128), F32),
                pltpu.VMEM((rows_here + 2, 4, half, D), F32),
                pltpu.VMEM((rows_here + 2, 4, half, D), F32),
                pltpu.VMEM((rows_here, LANE_PARTS, cols, 128), F32),
            ],
        ),
        compiler_params=pltpu.CompilerParams(vmem_limit_bytes=VMEM_LIMIT),
        name="leave",
    )(meta, gm, tokens, top, bot, after_grad, pieces, kern)


def pair_parts(values):
    lanes = lax.broadcasted_iota(jnp.int32, values.shape, 1)
    first = lanes < HEAD_DIM
    zero = jnp.zeros_like(values)
    return jnp.where(first, values, zero), jnp.where(first, zero, values)


def attend_kernel(mixed, wq, wk, wvt, bias, out, lse_out):
    tokens = mixed.shape[0]
    strips, window, _ = out.shape
    step = tokens // strips
    margin = (window - step) // 2
    m = mixed[...]
    query = (mm(m, wq[...]).astype(BF16) * FACTOR).astype(BF16)
    key = mm(m, wk[...]).astype(BF16)
    value_t = mm(wvt[...], m, NT).astype(BF16)
    keep = jnp.tile(bias[...], (1, tokens // 128))
    parts = []
    for e, key_e in enumerate(pair_parts(key)):
        scores = mm(key_e, query, NT) + keep
        peak = jnp.max(scores, axis=0, keepdims=True)
        raw = jnp.exp(scores - peak)
        total = jnp.sum(raw, axis=0, keepdims=True)
        prob = (raw * (1.0 / total)).astype(BF16)
        parts.append(mm(value_t[e * HEAD_DIM : (e + 1) * HEAD_DIM], prob))
        lse_out[0, e : e + 1, :] = peak + jnp.log(total)
    att = jnp.concatenate(parts, axis=0).T.astype(BF16)
    blank = jnp.zeros((margin, PAIR), BF16)
    for s in range(strips):
        low, high = s * step - margin, (s + 1) * step + margin
        if low < 0:
            out[s] = jnp.concatenate([blank, att[:high]], axis=0)
        elif high > tokens:
            out[s] = jnp.concatenate([att[low:], blank], axis=0)
        else:
            out[s] = att[low:high]


def attend(mixed, weight, weight_t, bias, strips, window):
    tokens = mixed.shape[0]
    return pl.pallas_call(
        attend_kernel,
        out_shape=(
            jax.ShapeDtypeStruct((strips, window, D), BF16),
            jax.ShapeDtypeStruct((PAIRS, 2, tokens), F32),
        ),
        grid=(PAIRS,),
        in_specs=[
            pl.BlockSpec((tokens, D), lambda p: (0, 0)),
            pl.BlockSpec((D, PAIR), lambda p: (0, p)),
            pl.BlockSpec((D, PAIR), lambda p: (0, PAIRS + p)),
            pl.BlockSpec((PAIR, D), lambda p: (2 * PAIRS + p, 0)),
            pl.BlockSpec((tokens, 128), lambda p: (0, 0)),
        ],
        out_specs=(
            pl.BlockSpec((strips, window, PAIR), lambda p: (0, 0, p)),
            pl.BlockSpec((1, 2, tokens), lambda p: (p, 0, 0)),
        ),
        compiler_params=pltpu.CompilerParams(vmem_limit_bytes=VMEM_LIMIT),
        name="attend",
    )(mixed, weight, weight, weight_t, bias)


def attend_back_kernel(offset, query, key, value, key_t, bias, lse, gatt, wq, wk, wv, dq_out, dk_out, dv_out, gm_out, acc):
    tokens = query.shape[0]
    strips, window, _ = gm_out.shape
    step = tokens // strips
    margin = window - step
    p = pl.program_id(0)
    q = query[...]
    keep = jnp.tile(bias[...], (1, tokens // 128))
    queries = pair_parts(q)
    keys = pair_parts(key[...])
    values = pair_parts(value[...])
    grads = pair_parts(gatt[...])
    dk = jnp.zeros((tokens, PAIR), F32)
    dv = jnp.zeros((tokens, PAIR), F32)
    parts = []
    for e in range(2):
        scores = mm(keys[e], q, NT) * FACTOR + keep
        prob = jnp.exp(scores - lse[0, e : e + 1, :])
        grad_prob = mm(values[e], gatt[...], NT)
        delta = jnp.sum(prob * grad_prob, axis=0, keepdims=True)
        grad_scores = (prob * (grad_prob - delta)).astype(BF16)
        dv = dv + mm(prob.astype(BF16), grads[e])
        dk = dk + mm(grad_scores, queries[e])
        parts.append(mm(key_t[e * HEAD_DIM : (e + 1) * HEAD_DIM], grad_scores))
    dq = (jnp.concatenate(parts, axis=0).T * FACTOR).astype(BF16)
    dk = (dk * FACTOR).astype(BF16)
    dv = dv.astype(BF16)
    dq_out[...] = dq
    dk_out[...] = dk
    dv_out[...] = dv
    total = mm(dq, wq[...], NT) + mm(dk, wk[...], NT) + mm(dv, wv[...], NT)

    @pl.when(p == 0)
    def _():
        acc[0:margin] = jnp.zeros((margin, D), F32)
        acc[margin + tokens :] = jnp.zeros((margin, D), F32)
        acc[margin : margin + tokens] = total

    @pl.when(p > 0)
    def _():
        acc[margin : margin + tokens] += total

    @pl.when(p == pl.num_programs(0) - 1)
    def _():
        for s in range(strips):
            start = pl.multiple_of(offset[0] + s * step, 8)
            gm_out[s] = acc[pl.ds(start, window), :].astype(BF16)


def attend_back(offset, triple, key_t, bias, lse, gatt, weight, strips, window):
    tokens = triple.shape[0]
    margin = window - tokens // strips
    part = lambda k: pl.BlockSpec((tokens, PAIR), lambda p, o: (0, k * PAIRS + p))
    slab = lambda k: pl.BlockSpec((D, PAIR), lambda p, o: (0, k * PAIRS + p))
    return pl.pallas_call(
        attend_back_kernel,
        out_shape=(
            jax.ShapeDtypeStruct((tokens, D), BF16),
            jax.ShapeDtypeStruct((tokens, D), BF16),
            jax.ShapeDtypeStruct((tokens, D), BF16),
            jax.ShapeDtypeStruct((strips, window, D), BF16),
        ),
        grid_spec=pltpu.PrefetchScalarGridSpec(
            num_scalar_prefetch=1,
            grid=(PAIRS,),
            in_specs=[
                part(0),
                part(1),
                part(2),
                pl.BlockSpec((PAIR, tokens), lambda p, o: (p, 0)),
                pl.BlockSpec((tokens, 128), lambda p, o: (0, 0)),
                pl.BlockSpec((1, 2, tokens), lambda p, o: (p, 0, 0)),
                part(0),
                slab(0),
                slab(1),
                slab(2),
            ],
            out_specs=(
                part(0),
                part(0),
                part(0),
                pl.BlockSpec((strips, window, D), lambda p, o: (0, 0, 0)),
            ),
            scratch_shapes=[pltpu.VMEM((tokens + 2 * margin, D), F32)],
        ),
        compiler_params=pltpu.CompilerParams(vmem_limit_bytes=VMEM_LIMIT),
        name="attend_back",
    )(offset, triple, triple, triple, key_t, bias, lse, gatt, weight, weight, weight)


def from_before(values, axis):
    count = lax.axis_size(axis)
    return lax.ppermute(values, axis, [(i, i + 1) for i in range(count - 1)])


def from_after(values, axis):
    count = lax.axis_size(axis)
    return lax.ppermute(values, axis, [(i + 1, i) for i in range(count - 1)])


def exchange(values, axis, bit):
    count = lax.axis_size(axis)
    return lax.ppermute(values, axis, [(i, i ^ bit) for i in range(count)])


def swap(values):
    return lax.all_to_all(values, "seq", 0, 0, tiled=False)


BITS = {"y": ("batch", 2), "c": ("batch", 1), "h": ("seq", 4), "l": ("seq", 2), "x": ("seq", 1)}
ORDER = "ychlx"


def halve(values, dims, bit):
    axis, mask = BITS[bit]
    mine = (lax.axis_index(axis) // mask) % 2
    at = dims.index(bit)
    send = lax.dynamic_index_in_dim(values, 1 - mine, at, keepdims=False)
    keep = lax.dynamic_index_in_dim(values, mine, at, keepdims=False)
    got = exchange(send, axis, mask)
    return keep.astype(F32) + got.astype(F32), dims.replace(bit, "")


def reduce_rows(values, order):
    shape = values.shape
    devices = lax.axis_size("batch") * lax.axis_size("seq")
    if lax.axis_size("batch") != 4 or lax.axis_size("seq") != 8:
        return lax.psum_scatter(values, ("batch", "seq"), scatter_dimension=0, tiled=True).astype(F32)
    values = values.reshape((2, 2, 2, 2, 2, shape[0] // devices, shape[1]))
    dims = ORDER
    for bit in order:
        values, dims = halve(values.astype(BF16), dims, bit)
    return values


def gather_seq(values):
    count = lax.axis_size("seq")
    me = lax.axis_index("seq")
    if count > 8:
        return lax.all_gather(values, "seq", axis=0)
    got = [values]
    for k in range(1, count):
        got.append(lax.ppermute(values, "seq", [(i, (i + k) % count) for i in range(count)]))
    back = jnp.stack(got[::-1])
    return lax.dynamic_slice_in_dim(jnp.concatenate([back, back]), (count - 1 - me) % count, count)


def attend_plain(mixed, weight, ok, heads):
    wide = heads * HEAD_DIM
    triple = mm(mixed, weight).astype(BF16)
    split = lambda k: triple[:, k * wide : (k + 1) * wide].reshape(-1, heads, HEAD_DIM)
    queries, keys, values = split(0), split(1), split(2)
    scores = jnp.einsum("qhe,khe->hqk", queries, keys, preferred_element_type=F32) * FACTOR
    scores = jnp.where(ok[None, None, :], scores, -1e30)
    prob = jax.nn.softmax(scores, axis=-1)
    out = jnp.einsum("hqk,khe->qhe", prob.astype(BF16), values, preferred_element_type=F32)
    return out.reshape(-1, wide).astype(BF16), (queries, keys, values, prob)


def attend_plain_back(saved, grad, weight):
    queries, keys, values, prob = saved
    heads = queries.shape[1]
    grad = grad.reshape(-1, heads, HEAD_DIM)
    grad_prob = jnp.einsum("qhe,khe->hqk", grad, values, preferred_element_type=F32)
    delta = jnp.sum(prob * grad_prob, axis=-1, keepdims=True)
    grad_scores = (prob * (grad_prob - delta)).astype(BF16)
    dq = jnp.einsum("hqk,khe->qhe", grad_scores, keys, preferred_element_type=F32) * FACTOR
    dk = jnp.einsum("hqk,qhe->khe", grad_scores, queries, preferred_element_type=F32) * FACTOR
    dv = jnp.einsum("hqk,qhe->khe", prob.astype(BF16), grad, preferred_element_type=F32)
    flat = lambda v: v.reshape(v.shape[0], -1).astype(BF16)
    grads = jnp.concatenate([flat(dq), flat(dk), flat(dv)], axis=1)
    return grads, mm(grads, weight, NT)


def shards(
    tokens,
    cotangent,
    timestep,
    class_ids,
    heights,
    widths,
    time_weight,
    class_table,
    ada_weight,
    ada_bias,
    conv_attn,
    qkv_weight,
    proj_weight,
    up_weight,
    conv_ffn,
    down_weight,
):
    latents, rows_here, cols, _ = tokens.shape
    half = cols // 2
    seq_count = lax.axis_size("seq")
    seq_place = lax.axis_index("seq")
    batch_count = lax.axis_size("batch")
    batch_place = lax.axis_index("batch")
    devices = batch_count * seq_count
    blocks = latents * 4
    share = seq_count // blocks
    per_group = rows_here // 2 * half
    group_tokens = seq_count * per_group

    first, last = tokens[:, :1], tokens[:, rows_here - 1 :]
    top = from_before(last, "seq")
    bot = from_after(first, "seq")
    top_two = from_before(tokens[:, rows_here - 2 : rows_here - 1], "seq")
    bot_two = from_after(tokens[:, 1:2], "seq")
    cot_top = from_before(cotangent[:, rows_here - 1 :], "seq")
    cot_bot = from_after(cotangent[:, :1], "seq")

    half_freq = time_weight.shape[0] // 2
    frequency = jnp.exp(-math.log(10000.0) * jnp.arange(half_freq, dtype=F32) / half_freq)
    angles = timestep.astype(F32)[:, None] * frequency[None, :]
    embedding = jnp.concatenate([jnp.cos(angles), jnp.sin(angles)], axis=1).astype(BF16)
    one_hot = (
        class_ids[:, None] == jnp.arange(class_table.shape[0], dtype=jnp.int32)[None, :]
    ).astype(BF16)
    condition = mm(embedding, time_weight) + mm(one_hot, class_table)
    logistic = jax.nn.sigmoid(condition)
    activated_cond = (condition * logistic).astype(BF16)
    pieces = (mm(activated_cond, ada_weight) + ada_bias).reshape(latents, 6, D)
    meta = jnp.concatenate(
        [heights, widths, jnp.reshape(seq_place * rows_here, (1,))]
    ).astype(jnp.int32)
    kern_attn = conv_attn.astype(F32)
    kern_ffn = conv_ffn.astype(F32)

    mixed = enter(meta, tokens, top, bot, pieces, kern_attn)
    sent = mixed.reshape(blocks, 1, per_group, D)
    sent = jnp.broadcast_to(sent, (blocks, share, per_group, D)).reshape(seq_count, per_group, D)
    grouped = swap(sent).reshape(group_tokens, D)

    my_block = seq_place // share
    my_latent = my_block // 4
    my_a = (my_block // 2) % 2
    my_b = my_block % 2
    places = jnp.arange(group_tokens, dtype=jnp.int32)
    key_row = places // half * 2 + my_a
    key_col = places % half * 2 + my_b
    height = lax.dynamic_index_in_dim(heights, my_latent, 0, keepdims=False)
    width = lax.dynamic_index_in_dim(widths, my_latent, 0, keepdims=False)
    key_ok = (key_row < height) & (key_col < width)

    margin = half
    window = per_group + 2 * margin
    if share == 1:
        bias = jnp.broadcast_to(jnp.where(key_ok, 0.0, -1e30)[:, None], (group_tokens, 128))
        weight_t = qkv_weight.T
        windows, lse = attend(grouped, qkv_weight, weight_t, bias, seq_count, window)
        attended = swap(windows)
    else:
        heads = HEADS // share
        wide = heads * HEAD_DIM
        chunk = seq_place % share
        thirds = qkv_weight.reshape(D, 3, share, wide)
        my_weight = lax.dynamic_index_in_dim(thirds, chunk, 2, keepdims=False).reshape(D, 3 * wide)
        att, saved = attend_plain(grouped, my_weight, key_ok, heads)
        att = jnp.pad(att, ((margin, margin), (0, 0)))
        windows = jnp.stack(
            [att[s * per_group : s * per_group + window] for s in range(seq_count)]
        )
        attended = swap(windows).reshape(blocks, share, window, wide)
        attended = attended.transpose(0, 2, 1, 3).reshape(blocks, window, D)

    ge, get, cot_split = prepare_cot(meta, cotangent, cot_top, cot_bot, pieces)
    e2, e2t, after_attn, branch = second(
        meta, attended, tokens, (top, top_two), (bot, bot_two), pieces, proj_weight
    )
    expanded, grad_e2, down_grad, up_grad, conv_ffn_part = ffn(
        e2, e2t, ge, get, up_weight, down_weight, kern_ffn, cols
    )
    output, grad_after, grad_branch, grad_attended, mid_sums = middle(
        meta, expanded, grad_e2, after_attn, branch, cot_split, pieces, proj_weight, rows_here, cols
    )

    att_own = attended[:, margin : margin + per_group].reshape(blocks * per_group, D)
    flat_branch = grad_branch.reshape(blocks * per_group, D)
    proj_grad = mm(att_own, flat_branch, (((0,), (0,)), ((), ()))).astype(BF16)
    tall = per_group + margin
    if share == 1:
        gatt = swap(grad_attended.reshape(seq_count, per_group, D)).reshape(group_tokens, D)
        triple = mm(grouped, qkv_weight).astype(BF16)
        key_t = mm(weight_t[D : 2 * D], grouped, NT).astype(BF16)
        offset = jnp.reshape(margin * (1 - my_a), (1,)).astype(jnp.int32)
        dq, dk, dv, gm_windows = attend_back(
            offset, triple, key_t, bias, lse, gatt, qkv_weight, seq_count, tall
        )
        gm = swap(gm_windows)
        grad_triple = jnp.concatenate([dq, dk, dv], axis=1)
        qkv_grad = mm(grouped, grad_triple, (((0,), (0,)), ((), ()))).astype(BF16)
    else:
        sent = grad_attended.reshape(blocks, per_group, share, wide).transpose(0, 2, 1, 3)
        gatt = swap(sent.reshape(seq_count, per_group, wide)).reshape(group_tokens, wide)
        grad_triple, gm_part = attend_plain_back(saved, gatt, my_weight)
        base = jnp.pad(gm_part.astype(BF16), ((margin, margin), (0, 0)))
        base = lax.dynamic_slice_in_dim(base, margin * (1 - my_a), group_tokens + margin)
        gm_windows = jnp.stack(
            [base[s * per_group : s * per_group + tall] for s in range(seq_count)]
        )
        gm = swap(gm_windows).reshape(blocks, share, tall, D)
        gm = jnp.sum(gm.astype(F32), axis=1).astype(BF16)
        own_grad = mm(grouped, grad_triple, (((0,), (0,)), ((), ()))).astype(BF16)
        spread = jnp.zeros((D, 3, share, wide), BF16)
        qkv_grad = lax.dynamic_update_index_in_dim(
            spread, own_grad.reshape(D, 3, wide), chunk, 2
        ).reshape(D, 3 * D)

    token_grad, conv_attn_part, end_sums = leave(
        meta, gm, tokens, top, bot, grad_after, pieces, kern_attn
    )

    down_rows = reduce_rows(down_grad, "cyxlh")
    up_rows = reduce_rows(up_grad, "cxlyh")
    proj_rows = reduce_rows(proj_grad, "clhyx")
    qkv_rows = reduce_rows(qkv_grad, "clyhx")

    ffn_rows = conv_ffn_part.reshape(9 * conv_ffn_part.shape[1] // D, D)
    early = jnp.sum(
        gather_seq(jnp.concatenate([mid_sums.reshape(latents * 4, D), ffn_rows])), axis=0
    )
    late = jnp.sum(
        gather_seq(
            jnp.concatenate([end_sums.reshape(latents * 2, D), jnp.sum(conv_attn_part, axis=0)])
        ),
        axis=0,
    )
    early_all = lax.all_gather(early, "batch", axis=0)
    late_all = lax.all_gather(late, "batch", axis=0)
    total = batch_count * latents
    mid_all = early_all[:, : latents * 4].reshape(total, 4, D)
    end_all = late_all[:, : latents * 2].reshape(total, 2, D)
    grad_pieces = jnp.concatenate([end_all, mid_all], axis=1).reshape(total, 6 * D)
    conv_ffn_grad = jnp.sum(early_all[:, latents * 4 :], axis=0).reshape(9, -1)
    conv_attn_grad = jnp.sum(late_all[:, latents * 2 :], axis=0)

    here = batch_place * seq_count + seq_place
    own_cols = D // devices
    conditions = lax.all_gather(
        jnp.concatenate([condition, embedding.astype(F32)], axis=1), "batch", axis=0
    ).reshape(total, -1)
    ids_all = lax.all_gather(class_ids, "batch", axis=0).reshape(total)
    embedding_all = conditions[:, D:]
    condition_all = conditions[:, :D]
    logistic_all = jax.nn.sigmoid(condition_all)
    activated_all = (condition_all * logistic_all).astype(BF16).astype(F32)
    grad_silu = lax.dot_general(
        grad_pieces, ada_weight.astype(F32), NT, precision=HIGHEST, preferred_element_type=F32
    )
    cond_all = grad_silu * logistic_all * (1.0 + condition_all * (1.0 - logistic_all))
    cond_grad = lax.dynamic_slice_in_dim(cond_all, batch_place * latents, latents)
    cond_cols = lax.dynamic_slice_in_dim(cond_all, here * own_cols, own_cols, axis=1)
    act_cols = lax.dynamic_slice_in_dim(activated_all, here * own_cols, own_cols, axis=1)
    outer = lambda left, right: lax.dot_general(
        left, right, (((0,), (0,)), ((), ())), precision=HIGHEST, preferred_element_type=F32
    )
    hot_all = (ids_all[:, None] == jnp.arange(class_table.shape[0], dtype=jnp.int32)[None, :]).astype(F32)
    bias_grad = jnp.sum(grad_pieces, axis=0)
    bias_cols = 6 * D // devices
    hidden_cols = conv_ffn.shape[1] // devices
    return (
        output,
        token_grad,
        cond_grad,
        outer(embedding_all, cond_cols),
        outer(hot_all, cond_cols),
        outer(act_cols, grad_pieces),
        lax.dynamic_slice_in_dim(bias_grad, here * bias_cols, bias_cols),
        lax.dynamic_slice_in_dim(conv_attn_grad, here * own_cols, own_cols, axis=1),
        qkv_rows,
        proj_rows,
        up_rows,
        lax.dynamic_slice_in_dim(conv_ffn_grad, here * hidden_cols, hidden_cols, axis=1),
        down_rows.T,
    )


def solution(mesh):
    strips = P("batch", "seq", None, None)
    in_specs = (strips, strips) + (P("batch"),) * 4 + (P(),) * 10
    both = ("batch", "seq")
    out_specs = (
        strips,
        strips,
        P("batch", None),
        P(None, both),
        P(None, both),
        P(both, None),
        P(both),
        P(None, both),
        P(both, None),
        P(both, None),
        P(both, None),
        P(None, both),
        P(None, both),
    )
    return jax.shard_map(shards, mesh=mesh, in_specs=in_specs, out_specs=out_specs, check_vma=False)
```

time: 1890 us -> 460 us (0.24)
  waiting for transfers between devices: 1250 us -> 81 us
  local copies, waits for them, and re-layouts: 253 us -> 57.4 us
  matrix products: 195 us -> 31.5 us
  Pallas kernels: 0 us -> 121 us
  starting transfers between devices: 22.8 us -> 97.7 us
  other arithmetic: 80.6 us -> 23.2 us
  blocking collectives: 62.4 us -> 39 us
    reduce_scatter x8 -> x0, waiting for transfers between devices: 984 us -> none  [the longest x1 183 us: shards(): lax.psum_scatter(jnp.concatenate([grad_keys.reshape(lax.axis_size('seq')...]
    dot_general x69 -> x11, matrix products: 195 us -> 31.5 us  [the longest x7 19.1 us: mm(): return lax.dot_general(left, right, dims, preferred_element_type=F32)]
    all_gather x1 -> x0, waiting for transfers between devices: 158 us -> none  [shards(): lax.all_gather(pairs_local, 'seq', axis=2, tiled=True)]
    pallas_call x0 -> x8, Pallas kernels: none -> 121 us  [the longest x1 53.5 us: ffn(): pl.pallas_call(ffn_kernel, out_shape=(jax.ShapeDtypeStruct((latents, own,...]
    dynamic_update_slice x40 -> x0, local copies, waits for them, and re-layouts: 58.4 us -> none  [shards(): lax.map(attend, (queries, gathered, key_usable))]
    ppermute x8 -> x40, starting transfers between devices: 21.7 us -> 78.9 us  [the longest x14 35.7 us: gather_seq(): lax.ppermute(values, 'seq', [(i, (i + k) % count) for i in range(count)])]
    reshape x10 -> x7, local copies, waits for them, and re-layouts: 42.1 us -> 4.56 us  [the longest x1 1.55 us: shards(): pieces = (mm(activated_cond, ada_weight) + ada_bias).reshape(latents, 6, D)]
    unnamed x1, blocking collectives: 41.2 us -> 5.56 us
  transfers between devices with their start and end apart: 18 -> 44, of which waited for: 15 -> 14; matrix products, arithmetic and copies ran while one was open for 7% -> 23% of each run, Pallas kernels for 0% -> 7%
where the time goes in v1:
time: 460 us; the launch traced here: 453 us
  Pallas kernels  121 us (26%)
  starting transfers between devices  97.7 us (21%)
  waiting for transfers between devices  81 us (18%)
  local copies, waits for them, and re-layouts  57.4 us (12%)
  blocking collectives  39 us (8%)
  matrix products  31.5 us (7%)
  other arithmetic  23.2 us (5%)
    pallas_call x1, Pallas kernels, ffn(): pl.pallas_call(ffn_kernel, out_shape=(jax.ShapeDtypeStruct((latents, own,...  53.5 us
    ppermute x20, waiting for transfers between devices, exchange(): return lax.ppermute(values, axis, [(i, i ^ bit) for i in range(count)])  48.9 us
    ppermute x14, starting transfers between devices, gather_seq(): lax.ppermute(values, 'seq', [(i, (i + k) % count) for i in range(count)])  35.7 us
    all_to_all x4, waiting for transfers between devices, swap(): return lax.all_to_all(values, 'seq', 0, 0, tiled=False)  24.1 us
    ppermute x20, starting transfers between devices, exchange(): return lax.ppermute(values, axis, [(i, i ^ bit) for i in range(count)])  22.6 us
    pallas_call x1, Pallas kernels, attend_back(): pl.pallas_call(attend_back_kernel, out_shape=(jax.ShapeDtypeStruct((token...  20.3 us
    all_gather x1, blocking collectives, shards(): late_all = lax.all_gather(late, 'batch', axis=0)  19.9 us
    unnamed x60, local copies, waits for them, and re-layouts  19.2 us
  transfers between devices with their start and end apart: 44, of which 14 were waited for; matrix products, arithmetic and copies ran while one was open for 23% of the time, Pallas kernels for 7%

profile of v1, /device:TPU:0, one launch (start us, length us, event | category | flops | bytes accessed | tf_op | source)
XLA Modules:
  0.0 453.0 jit_solution(5192092275900163953)
XLA Ops:
  4.2 6.2 %collective-permute-start = (bf16[2,1,64,768]{3,2,1,0:T(8,128)(2,1)}, bf16[2,1,64,768]{3,2,1,0:T(8,128)(2,1)}, u32[]{:S(2)}, u32[]{:S(2)}) collective-permute-start(bf16[2,1,64,768]{3,2,1,0:T(8,128)(2,1)} %get-tuple-element.78), channel_id=1, source_target_pairs={{0,1},{1,2},{2,3},{3,4},{4,5},{5,6},{6,7},{8,9},{9,10},{10,11},{11... | collective-permute-start | bytes 589832 | tf_op jit(solution)/shard_map/ppermute | solution.py:739
  13.3 4.7 %convolution_add_fusion = f32[2,4608]{1,0:T(2,128)} fusion(bf16[768,4608]{1,0:T(8,128)(2,1)} %param.24, f32[4608]{0:T(1024)S(1)} %copy-done.15, f32[2,768]{1,0:T(2,128)S(1)} %convolution_add_fusion.1), kind=kOutput, calls=%fused_computation | convolution fusion | flops 14172672 | bytes 7139328 | tf_op jit(solution)/shard_map/dot_general | solution.py:29
  22.1 5.1 %enter.1 = bf16[2,4,64,768]{3,2,1,0:T(8,128)(2,1)} custom-call(s32[5]{0:T(128)} %pad_add_fusion.meta, bf16[2,4,64,768]{3,2,1,0:T(8,128)(2,1)} %tok.5, bf16[2,1,64,768]{3,2,1,0:T(8,128)(2,1)} %collective-permute-done.top.top1, bf16[2,1,64,768]{3,2,1,0:T(8,128)(2,1)} %collective-permute-done.1.bot.bot1, f32[2,6,768]{2,1,0:T(8,128)} %reshape.165.pieces, ...), custom_call_target="tpu_custom_call" | custom-call | tf_op jit(solution)/shard_map/enter/pallas_call | solution.py:133
  27.2 5.5 %all-to-all-start = ((bf16[8,64,768]{2,1,0:T(8,128)(2,1)}), bf16[8,64,768]{2,1,0:T(8,128)(2,1)}, u32[]{:S(2)}, u32[]{:S(2)}) async-start(bf16[8,64,768]{2,1,0:T(8,128)(2,1)} %bitcast.188), calls=%async_computation | async-start | bytes 1572864 | tf_op jit(solution)/shard_map/all_to_all | solution.py:753
  40.1 12.4 %all-to-all-done = bf16[8,64,768]{2,1,0:T(8,128)(2,1)} async-done(((bf16[8,64,768]{2,1,0:T(8,128)(2,1)}), bf16[8,64,768]{2,1,0:T(8,128)(2,1)}, u32[]{:S(2)}, u32[]{:S(2)}) %all-to-all-start) | async-done | bytes 786464 | tf_op jit(solution)/shard_map/all_to_all | solution.py:753
  53.4 14.4 %attend.1 = (bf16[8,128,768]{2,1,0:T(8,128)(2,1)}, f32[6,2,512]{2,1,0:T(2,128)}) custom-call(bf16[512,768]{1,0:T(8,128)(2,1)} %bitcast.2.mixed, bf16[768,2304]{1,0:T(8,128)(2,1)} %wv.1, bf16[768,2304]{1,0:T(8,128)(2,1)} %wv.1, bf16[2304,768]{1,0:T(8,128)(2,1)} %bitcast.182, f32[512,128]{1,0:T(8,128)} %broadcast_in_dim.12.bias), custom_call_target="tpu_custom_call" | custom-call | tf_op jit(solution)/shard_map/attend/pallas_call | solution.py:624
  67.7 4.6 %all-to-all-start.1 = ((bf16[8,128,768]{2,1,0:T(8,128)(2,1)}), bf16[8,128,768]{2,1,0:T(8,128)(2,1)}, u32[]{:S(2)}, u32[]{:S(2)}) async-start(bf16[8,128,768]{2,1,0:T(8,128)(2,1)} %get-tuple-element.39), calls=%async_computation.1 | async-start | bytes 3145728 | tf_op jit(solution)/shard_map/all_to_all | solution.py:753
  75.4 5.2 %collective-permute-start.4 = (bf16[2,1,64,768]{3,2,1,0:T(8,128)(2,1)}, bf16[2,1,64,768]{3,2,1,0:T(8,128)(2,1)}, u32[]{:S(2)}, u32[]{:S(2)}) collective-permute-start(bf16[2,1,64,768]{3,2,1,0:T(8,128)(2,1)} %get-tuple-element.74), channel_id=1, source_target_pairs={{0,1},{1,2},{2,3},{3,4},{4,5},{5,6},{6,7},{8,9},{9,10},{10,11},{11... | collective-permute-start | bytes 589832 | tf_op jit(solution)/shard_map/ppermute | solution.py:739
  85.6 5.4 %collective-permute-start.2 = (bf16[2,1,64,768]{3,2,1,0:T(8,128)(2,1)}, bf16[2,1,64,768]{3,2,1,0:T(8,128)(2,1)}, u32[]{:S(2)}, u32[]{:S(2)}) collective-permute-start(bf16[2,1,64,768]{3,2,1,0:T(8,128)(2,1)} %get-tuple-element.76), channel_id=1, source_target_pairs={{0,1},{1,2},{2,3},{3,4},{4,5},{5,6},{6,7},{8,9},{9,10},{10,11},{11... | collective-permute-start | bytes 589832 | tf_op jit(solution)/shard_map/ppermute | solution.py:739
  91.0 5.6 %all-reduce = s32[8]{0:T(128)} all-reduce(s32[8]{0:T(128)} %dynamic-update-slice), channel_id=5, replica_groups=mesh['batch'=4,'seq'=8] {'batch'}, use_global_device_ids=true, to_apply=%add | all-reduce | flops 8 | bytes 64
  96.5 5.8 %all-gather.6 = f32[4,2,1024]{2,1,0:T(2,128)} all-gather(f32[1,2,1024]{2,1,0:T(2,128)S(1)} %maximum_bitcast_fusion), channel_id=4, replica_groups=mesh['batch'=4,'seq'=8] {'batch'}, dimensions={0}, use_global_device_ids=true | all-gather | bytes 40960 | tf_op jit(solution)/shard_map/all_gather | solution.py:986
  110.3 4.6 %convolution_convert_fusion.1.query.key.value = bf16[512,2304]{1,0:T(8,128)(2,1)} fusion(bf16[512,768]{1,0:T(8,128)(2,1)} %bitcast.2.mixed, bf16[768,2304]{1,0:T(8,128)(2,1)S(1)} %copy-done.3), kind=kOutput, calls=%fused_computation.6 | convolution fusion | flops 1813118976 | bytes 6684672 | tf_op jit(solution)/shard_map/dot_general | solution.py:29
  118.1 6.6 %second.1 = (bf16[2,512,768]{2,1,0:T(8,128)(2,1)}, bf16[2,768,256]{2,1,0:T(8,128)(2,1)}, f32[2,256,768]{2,1,0:T(8,128)}, f32[2,256,768]{2,1,0:T(8,128)}) custom-call(s32[5]{0:T(128)} %pad_add_fusion.meta, bf16[8,128,768]{2,1,0:T(8,128)(2,1)} %all-to-all-done.1.att, bf16[2,4,64,768]{3,2,1,0:T(8,128)(2,1)} %tok.5, ...), custom_call_target="tpu_custom_call" | custom-call | tf_op jit(solution)/shard_map/second/pallas_call | solution.py:250
  124.7 53.5 %ffn.1 = (f32[2,256,768]{2,1,0:T(8,128)}, f32[2,256,768]{2,1,0:T(8,128)}, bf16[768,3072]{1,0:T(8,128)(2,1)}, bf16[768,3072]{1,0:T(8,128)(2,1)}, f32[9,3072]{1,0:T(8,128)}) custom-call(bf16[2,512,768]{2,1,0:T(8,128)(2,1)} %get-tuple-element.40.e2, bf16[2,768,256]{2,1,0:T(8,128)(2,1)} %get-tuple-element.41.e2t, bf16[2,384,768]{2,1,0:T(8,128)(2,1)} %get-tuple-element.42.ge, ...), custom_call_target="tpu_custom_call" | custom-call | tf_op jit(solution)/shard_map/ffn/pallas_call | solution.py:380
  178.2 8.7 %middle.1 = (bf16[2,4,64,768]{3,2,1,0:T(8,128)(2,1)}, f32[2,256,768]{2,1,0:T(8,128)}, bf16[2,4,64,768]{3,2,1,0:T(8,128)(2,1)}, bf16[2,4,64,768]{3,2,1,0:T(8,128)(2,1)}, f32[2,4,768]{2,1,0:T(4,128)}) custom-call(s32[5]{0:T(128)} %pad_add_fusion.meta, f32[2,256,768]{2,1,0:T(8,128)} %get-tuple-element.44.exp, f32[2,256,768]{2,1,0:T(8,128)} %get-tuple-element.45.ge2, ...), custom_call_target="tpu_custom_call" | custom-call | tf_op jit(solution)/shard_map/middle/pallas_call | solution.py:464
  190.1 8.1 %collective-permute-start.18 = (f32[44,768]{1,0:T(8,128)S(1)}, f32[44,768]{1,0:T(8,128)}, u32[]{:S(2)}, u32[]{:S(2)}) collective-permute-start(f32[44,768]{1,0:T(8,128)S(1)} %constant_dynamic-update-slice_fusion), channel_id=1, source_target_pairs={{0,2},{1,3},{2,4},{3,5},{4,6},{5,7},{6,0},{7,1},{8,10},{9,11},{10,... | collective-permute-start | bytes 405512 | tf_op jit(solution)/shard_map/ppermute | solution.py:789
  201.4 3.9 all-to-all-start.2
  207.9 5.0 %constant_dynamic-slice_fusion.2 = (bf16[2,1,2,2,2,24,3072]{6,5,4,3,2,1,0:T(8,128)(2,1)S(1)}, bf16[2,1,2,2,2,24,3072]{6,5,4,3,2,1,0:T(8,128)(2,1)S(1)}, bf16[2,1...) fusion(bf16[2,2,2,2,2,24,3072]{6,5,4,3,2,1,0:T(8,128)(2,1)S(1)} %bitcast.184, ...), kind=kLoop, calls=%fused_computation.109 | loop fusion | bytes 18874376 | tf_op jit(solution)/shard_map/jit(dynamic_index_in_dim)/dynamic_slice | solution.py:765
  223.9 8.2 %collective-permute-start.15 = (f32[44,768]{1,0:T(8,128)S(1)}, f32[44,768]{1,0:T(8,128)S(1)}, u32[]{:S(2)}, u32[]{:S(2)}) collective-permute-start(f32[44,768]{1,0:T(8,128)S(1)} %constant_dynamic-update-slice_fusion), channel_id=1, source_target_pairs={{0,5},{1,6},{2,7},{3,0},{4,1},{5,2},{6,3},{7,4},{8,13},{9,14},{10,... | collective-permute-start | bytes 405512 | tf_op jit(solution)/shard_map/ppermute | solution.py:789
  232.1 5.0 %collective-permute-done.15 = f32[44,768]{1,0:T(8,128)S(1)} collective-permute-done((f32[44,768]{1,0:T(8,128)S(1)}, f32[44,768]{1,0:T(8,128)S(1)}, u32[]{:S(2)}, u32[]{:S(2)}) %collective-permute-start.15) | collective-permute-done | bytes 135200 | tf_op jit(solution)/shard_map/ppermute | solution.py:789
  247.5 7.6 %collective-permute-done.26 = bf16[2,2,2,24,768]{4,3,2,0,1:T(8,128)(2,1)S(1)} collective-permute-done((bf16[2,2,2,24,768]{4,3,2,0,1:T(8,128)(2,1)S(1)}, bf16[2,2,2,24,768]{4,3,2,0,1:T(8,128)(2,1)S(1)}, u32[]{:S(2)}, u32[]{:S(2)}) %collective-permute-start.26) | collective-permute-done | bytes 294944 | tf_op jit(solution)/shard_map/ppermute | solution.py:749
  256.4 7.8 %all-gather.5 = f32[4,44,768]{2,1,0:T(8,128)S(1)} all-gather(f32[1,44,768]{2,1,0:T(8,128)S(1)} %bitcast.194), channel_id=3, replica_groups=mesh['batch'=4,'seq'=8] {'batch'}, dimensions={0}, use_global_device_ids=true | all-gather | bytes 675840 | tf_op jit(solution)/shard_map/all_gather | solution.py:975
  276.8 20.3 %attend_back.1 = (bf16[512,768]{1,0:T(8,128)(2,1)}, bf16[512,768]{1,0:T(8,128)(2,1)}, bf16[512,768]{1,0:T(8,128)(2,1)}, bf16[8,96,768]{2,1,0:T(8,128)(2,1)}) custom-call(s32[1]{0:T(128)} %bitcast.6.offset, bf16[512,2304]{1,0:T(8,128)(2,1)} %convolution_convert_fusion.1.query.key.value, bf16[512,2304]{1,0:T(8,128)(2,1)} %convolution_convert_fusion.1.query.key.value, ...), custom_call_target="tpu_custom_call" | custom-call | tf_op jit(solution)/shard_map/attend_back/pallas_call | solution.py:701
  297.1 4.9 %all-to-all-start.3 = ((bf16[8,96,768]{2,1,0:T(8,128)(2,1)}), bf16[8,96,768]{2,1,0:T(8,128)(2,1)}, u32[]{:S(2)}, u32[]{:S(2)}) async-start(bf16[8,96,768]{2,1,0:T(8,128)(2,1)} %get-tuple-element.52), calls=%async_computation.3 | async-start | bytes 2359296 | tf_op jit(solution)/shard_map/all_to_all | solution.py:753
  318.3 11.7 %all-to-all-done.3.gm = bf16[8,96,768]{2,1,0:T(8,128)(2,1)} async-done(((bf16[8,96,768]{2,1,0:T(8,128)(2,1)}), bf16[8,96,768]{2,1,0:T(8,128)(2,1)}, u32[]{:S(2)}, u32[]{:S(2)}) %all-to-all-start.3) | async-done | bytes 1179680 | tf_op jit(solution)/shard_map/all_to_all | solution.py:753
  330.0 8.6 %leave.1 = (f32[2,4,64,768]{3,2,1,0:T(8,128)}, f32[2,9,768]{2,1,0:T(8,128)}, f32[2,2,768]{2,1,0:T(2,128)}) custom-call(s32[5]{0:T(128)} %pad_add_fusion.meta, bf16[8,96,768]{2,1,0:T(8,128)(2,1)} %all-to-all-done.3.gm, bf16[2,4,64,768]{3,2,1,0:T(8,128)(2,1)} %tok.5, bf16[2,1,64,768]{3,2,1,0:T(8,128)(2,1)} %collective-permute-done.top.top1, ...), custom_call_target="tpu_custom_call" | custom-call | tf_op jit(solution)/shard_map/leave/pallas_call | solution.py:552
  361.9 19.9 %all-gather.4 = f32[4,13,768]{2,1,0:T(8,128)S(1)} all-gather(f32[1,13,768]{2,1,0:T(8,128)S(1)} %bitcast.196), channel_id=2, replica_groups=mesh['batch'=4,'seq'=8] {'batch'}, dimensions={0}, use_global_device_ids=true | all-gather | bytes 199680 | tf_op jit(solution)/shard_map/all_gather | solution.py:976
  383.3 7.9 %fusion.16 = f32[8,768]{1,0:T(8,128)S(1)} fusion(f32[8,4608]{1,0:T(8,128)S(1)} %bitcast.189, bf16[768,4608]{1,0:T(8,128)(2,1)} %param.24, f32[8,1024]{1,0:T(8,128)} %reshape.218), kind=kOutput, calls=%fused_computation.40 | convolution fusion | flops 339787776 | bytes 7274496 | tf_op jit(solution)/shard_map/dot_general | solution.py:994
  403.5 10.4 %collective-permute-done.32 = bf16[2,2,24,3072]{3,2,1,0:T(8,128)(2,1)S(1)} collective-permute-done((bf16[2,2,24,3072]{3,2,1,0:T(8,128)(2,1)S(1)}, bf16[2,2,24,3072]{3,2,1,0:T(8,128)(2,1)S(1)}, u32[]{:S(2)}, u32[]{:S(2)}) %collective-permute-start.32) | collective-permute-done | bytes 589856 | tf_op jit(solution)/shard_map/ppermute | solution.py:749
  417.7 4.9 %collective-permute-done.33 = bf16[2,24,3072]{2,1,0:T(8,128)(2,1)S(1)} collective-permute-done((bf16[2,24,3072]{2,1,0:T(8,128)(2,1)S(1)}, bf16[2,24,3072]{2,1,0:T(8,128)(2,1)S(1)}, u32[]{:S(2)}, u32[]{:S(2)}) %collective-permute-start.33) | collective-permute-done | bytes 294944 | tf_op jit(solution)/shard_map/ppermute | solution.py:749
  428.0 12.1 %collective-permute-done.34 = bf16[24,3072]{1,0:T(8,128)(2,1)S(1)} collective-permute-done((bf16[24,3072]{1,0:T(8,128)(2,1)S(1)}, bf16[24,3072]{1,0:T(8,128)(2,1)S(1)}, u32[]{:S(2)}, u32[]{:S(2)}) %collective-permute-start.34) | collective-permute-done | bytes 147488 | tf_op jit(solution)/shard_map/ppermute | solution.py:749
  440.8 6.1 %collective-permute-done.23 = bf16[2,24,2304]{2,1,0:T(8,128)(2,1)S(1)} collective-permute-done((bf16[2,24,2304]{2,1,0:T(8,128)(2,1)S(1)}, bf16[2,24,2304]{2,1,0:T(8,128)(2,1)S(1)}, u32[]{:S(2)}, u32[]{:S(2)}) %collective-permute-start.23) | collective-permute-done | bytes 221216 | tf_op jit(solution)/shard_map/ppermute | solution.py:749
  (230 shorter events, 150.3 us)
Async XLA Ops:
  2.9 19.3 %collective-permute-start.1 = (bf16[2,1,64,768]{3,2,1,0:T(8,128)(2,1)}, bf16[2,1,64,768]{3,2,1,0:T(8,128)(2,1)}, u32[]{:S(2)}, u32[]{:S(2)}) collective-permute-start(bf16[2,1,64,768]{3,2,1,0:T(8,128)(2,1)} %get-tuple-element.77), channel_id=1, source_target_pairs={{1,0},{2,1},{3,2},{4,3},{5,4},{6,5},{7,6},{9,8},{10,9},{11,10},{12... | collective-permute-start | bytes 589832 | tf_op jit(solution)/shard_map/ppermute | solution.py:744
  4.2 18.0 %collective-permute-start = (bf16[2,1,64,768]{3,2,1,0:T(8,128)(2,1)}, bf16[2,1,64,768]{3,2,1,0:T(8,128)(2,1)}, u32[]{:S(2)}, u32[]{:S(2)}) collective-permute-start(bf16[2,1,64,768]{3,2,1,0:T(8,128)(2,1)} %get-tuple-element.78), channel_id=1, source_target_pairs={{0,1},{1,2},{2,3},{3,4},{4,5},{5,6},{6,7},{8,9},{9,10},{10,11},{11... | collective-permute-start | bytes 589832 | tf_op jit(solution)/shard_map/ppermute | solution.py:739
  27.2 25.3 %all-to-all-start = ((bf16[8,64,768]{2,1,0:T(8,128)(2,1)}), bf16[8,64,768]{2,1,0:T(8,128)(2,1)}, u32[]{:S(2)}, u32[]{:S(2)}) async-start(bf16[8,64,768]{2,1,0:T(8,128)(2,1)} %bitcast.188), calls=%async_computation | async-start | bytes 1572864 | tf_op jit(solution)/shard_map/all_to_all | solution.py:753
  67.7 50.3 %all-to-all-start.1 = ((bf16[8,128,768]{2,1,0:T(8,128)(2,1)}), bf16[8,128,768]{2,1,0:T(8,128)(2,1)}, u32[]{:S(2)}, u32[]{:S(2)}) async-start(bf16[8,128,768]{2,1,0:T(8,128)(2,1)} %get-tuple-element.39), calls=%async_computation.1 | async-start | bytes 3145728 | tf_op jit(solution)/shard_map/all_to_all | solution.py:753
  74.1 32.6 %collective-permute-start.5 = (bf16[2,1,64,768]{3,2,1,0:T(8,128)(2,1)}, bf16[2,1,64,768]{3,2,1,0:T(8,128)(2,1)}, u32[]{:S(2)}, u32[]{:S(2)}) collective-permute-start(bf16[2,1,64,768]{3,2,1,0:T(8,128)(2,1)} %get-tuple-element.73), channel_id=1, source_target_pairs={{1,0},{2,1},{3,2},{4,3},{5,4},{6,5},{7,6},{9,8},{10,9},{11,10},{12... | collective-permute-start | bytes 589832 | tf_op jit(solution)/shard_map/ppermute | solution.py:744
  75.4 31.3 %collective-permute-start.4 = (bf16[2,1,64,768]{3,2,1,0:T(8,128)(2,1)}, bf16[2,1,64,768]{3,2,1,0:T(8,128)(2,1)}, u32[]{:S(2)}, u32[]{:S(2)}) collective-permute-start(bf16[2,1,64,768]{3,2,1,0:T(8,128)(2,1)} %get-tuple-element.74), channel_id=1, source_target_pairs={{0,1},{1,2},{2,3},{3,4},{4,5},{5,6},{6,7},{8,9},{9,10},{10,11},{11... | collective-permute-start | bytes 589832 | tf_op jit(solution)/shard_map/ppermute | solution.py:739
  80.6 37.4 %collective-permute-start.3 = (bf16[2,1,64,768]{3,2,1,0:T(8,128)(2,1)}, bf16[2,1,64,768]{3,2,1,0:T(8,128)(2,1)}, u32[]{:S(2)}, u32[]{:S(2)}) collective-permute-start(bf16[2,1,64,768]{3,2,1,0:T(8,128)(2,1)} %get-tuple-element.75), channel_id=1, source_target_pairs={{1,0},{2,1},{3,2},{4,3},{5,4},{6,5},{7,6},{9,8},{10,9},{11,10},{12... | collective-permute-start | bytes 589832 | tf_op jit(solution)/shard_map/ppermute | solution.py:744
  85.6 32.5 %collective-permute-start.2 = (bf16[2,1,64,768]{3,2,1,0:T(8,128)(2,1)}, bf16[2,1,64,768]{3,2,1,0:T(8,128)(2,1)}, u32[]{:S(2)}, u32[]{:S(2)}) collective-permute-start(bf16[2,1,64,768]{3,2,1,0:T(8,128)(2,1)} %get-tuple-element.76), channel_id=1, source_target_pairs={{0,1},{1,2},{2,3},{3,4},{4,5},{5,6},{6,7},{8,9},{9,10},{10,11},{11... | collective-permute-start | bytes 589832 | tf_op jit(solution)/shard_map/ppermute | solution.py:739
  187.8 52.8 %collective-permute-start.19 = (f32[44,768]{1,0:T(8,128)S(1)}, f32[44,768]{1,0:T(8,128)S(1)}, u32[]{:S(2)}, u32[]{:S(2)}) collective-permute-start(f32[44,768]{1,0:T(8,128)S(1)} %constant_dynamic-update-slice_fusion), channel_id=1, source_target_pairs={{0,1},{1,2},{2,3},{3,4},{4,5},{5,6},{6,7},{7,0},{8,9},{9,10},{10,1... | collective-permute-start | bytes 405512 | tf_op jit(solution)/shard_map/ppermute | solution.py:789
  190.1 49.6 %collective-permute-start.18 = (f32[44,768]{1,0:T(8,128)S(1)}, f32[44,768]{1,0:T(8,128)}, u32[]{:S(2)}, u32[]{:S(2)}) collective-permute-start(f32[44,768]{1,0:T(8,128)S(1)} %constant_dynamic-update-slice_fusion), channel_id=1, source_target_pairs={{0,2},{1,3},{2,4},{3,5},{4,6},{5,7},{6,0},{7,1},{8,10},{9,11},{10,... | collective-permute-start | bytes 405512 | tf_op jit(solution)/shard_map/ppermute | solution.py:789
  198.2 40.5 %collective-permute-start.17 = (f32[44,768]{1,0:T(8,128)S(1)}, f32[44,768]{1,0:T(8,128)}, u32[]{:S(2)}, u32[]{:S(2)}) collective-permute-start(f32[44,768]{1,0:T(8,128)S(1)} %constant_dynamic-update-slice_fusion), channel_id=1, source_target_pairs={{0,3},{1,4},{2,5},{3,6},{4,7},{5,0},{6,1},{7,2},{8,11},{9,12},{10,... | collective-permute-start | bytes 405512 | tf_op jit(solution)/shard_map/ppermute | solution.py:789
  198.2 39.0 %collective-permute-start.16 = (f32[44,768]{1,0:T(8,128)S(1)}, f32[44,768]{1,0:T(8,128)}, u32[]{:S(2)}, u32[]{:S(2)}) collective-permute-start(f32[44,768]{1,0:T(8,128)S(1)} %constant_dynamic-update-slice_fusion), channel_id=1, source_target_pairs={{0,4},{1,5},{2,6},{3,7},{4,0},{5,1},{6,2},{7,3},{8,12},{9,13},{10,... | collective-permute-start | bytes 405512 | tf_op jit(solution)/shard_map/ppermute | solution.py:789
  198.2 18.0 %collective-permute-start.13 = (f32[44,768]{1,0:T(8,128)S(1)}, f32[44,768]{1,0:T(8,128)}, u32[]{:S(2)}, u32[]{:S(2)}) collective-permute-start(f32[44,768]{1,0:T(8,128)S(1)} %constant_dynamic-update-slice_fusion), channel_id=1, source_target_pairs={{0,7},{1,0},{2,1},{3,2},{4,3},{5,4},{6,5},{7,6},{8,15},{9,8},{10,9... | collective-permute-start | bytes 405512 | tf_op jit(solution)/shard_map/ppermute | solution.py:789
  201.4 74.5 %all-to-all-start.2 = ((bf16[8,64,768]{2,1,0:T(8,128)(2,1)}), bf16[8,64,768]{2,1,0:T(8,128)(2,1)S(1)}, u32[]{:S(2)}, u32[]{:S(2)}) async-start(bf16[8,64,768]{2,1,0:T(8,128)(2,1)} %bitcast.192), calls=%async_computation.2 | async-start | bytes 1572864 | tf_op jit(solution)/shard_map/all_to_all | solution.py:753
  223.9 13.2 %collective-permute-start.15 = (f32[44,768]{1,0:T(8,128)S(1)}, f32[44,768]{1,0:T(8,128)S(1)}, u32[]{:S(2)}, u32[]{:S(2)}) collective-permute-start(f32[44,768]{1,0:T(8,128)S(1)} %constant_dynamic-update-slice_fusion), channel_id=1, source_target_pairs={{0,5},{1,6},{2,7},{3,0},{4,1},{5,2},{6,3},{7,4},{8,13},{9,14},{10,... | collective-permute-start | bytes 405512 | tf_op jit(solution)/shard_map/ppermute | solution.py:789
  237.1 71.3 %collective-permute-start.30 = (bf16[2,2,2,2,24,3072]{5,4,1,0,2,3:T(8,128)(2,1)}, bf16[2,2,2,2,24,3072]{5,4,1,0,2,3:T(8,128)(2,1)}, u32[]{:S(2)}, u32[]{:S(2)}) collective-permute-start(bf16[2,2,2,2,24,3072]{5,4,1,0,2,3:T(8,128)(2,1)} %bitcast.179), channel_id=1, source_target_pairs={{0,8},{8,0},{16,24},{24,16},{1,9},{9,1},{17,25},{25,17},{2,10},{10... | collective-permute-start | bytes 7077896 | tf_op jit(solution)/shard_map/ppermute | solution.py:749
  238.6 74.6 %collective-permute-start.35 = (bf16[2,2,2,2,24,3072]{5,4,1,2,3,0:T(8,128)(2,1)}, bf16[2,2,2,2,24,3072]{5,4,1,2,3,0:T(8,128)(2,1)}, u32[]{:S(2)}, u32[]{:S(2)}) collective-permute-start(bf16[2,2,2,2,24,3072]{5,4,1,2,3,0:T(8,128)(2,1)} %bitcast.178), channel_id=1, source_target_pairs={{0,8},{8,0},{16,24},{24,16},{1,9},{9,1},{17,25},{25,17},{2,10},{10... | collective-permute-start | bytes 7077896 | tf_op jit(solution)/shard_map/ppermute | solution.py:749
  244.6 10.5 %collective-permute-start.26 = (bf16[2,2,2,24,768]{4,3,2,0,1:T(8,128)(2,1)S(1)}, bf16[2,2,2,24,768]{4,3,2,0,1:T(8,128)(2,1)S(1)}, u32[]{:S(2)}, u32[]{:S(2)}) collective-permute-start(bf16[2,2,2,24,768]{4,3,2,0,1:T(8,128)(2,1)S(1)} %dynamic-slice_bitcast_fusion.8), channel_id=1, source_target_pairs={{0,2},{1,3},{2,0},{3,1},{4,6},{5,7},{6,4},{7,5},{8,10},{9,11},{10,... | collective-permute-start | bytes 884744 | tf_op jit(solution)/shard_map/ppermute | solution.py:749
  255.2 9.8 %collective-permute-start.27 = (bf16[2,2,24,768]{3,2,1,0:T(8,128)(2,1)S(1)}, bf16[2,2,24,768]{3,2,1,0:T(8,128)(2,1)S(1)}, u32[]{:S(2)}, u32[]{:S(2)}) collective-permute-start(bf16[2,2,24,768]{3,2,1,0:T(8,128)(2,1)S(1)} %dynamic-slice_bitcast_fusion.12), channel_id=1, source_target_pairs={{0,4},{1,5},{2,6},{3,7},{4,0},{5,1},{6,2},{7,3},{8,12},{9,13},{10,... | collective-permute-start | bytes 442376 | tf_op jit(solution)/shard_map/ppermute | solution.py:749
  297.1 32.9 %all-to-all-start.3 = ((bf16[8,96,768]{2,1,0:T(8,128)(2,1)}), bf16[8,96,768]{2,1,0:T(8,128)(2,1)}, u32[]{:S(2)}, u32[]{:S(2)}) async-start(bf16[8,96,768]{2,1,0:T(8,128)(2,1)} %get-tuple-element.52), calls=%async_computation.3 | async-start | bytes 2359296 | tf_op jit(solution)/shard_map/all_to_all | solution.py:753
  308.4 33.1 %collective-permute-start.20 = (bf16[2,2,2,2,24,2304]{5,4,3,1,0,2:T(8,128)(2,1)}, bf16[2,2,2,2,24,2304]{5,4,3,1,0,2:T(8,128)(2,1)}, u32[]{:S(2)}, u32[]{:S(2)}) collective-permute-start(bf16[2,2,2,2,24,2304]{5,4,3,1,0,2:T(8,128)(2,1)} %bitcast.180), channel_id=1, source_target_pairs={{0,8},{8,0},{16,24},{24,16},{1,9},{9,1},{17,25},{25,17},{2,10},{10... | collective-permute-start | bytes 5308424 | tf_op jit(solution)/shard_map/ppermute | solution.py:749
  341.5 9.6 %collective-permute-start.11 = (f32[13,768]{1,0:T(8,128)S(1)}, f32[13,768]{1,0:T(8,128)S(1)}, u32[]{:S(2)}, u32[]{:S(2)}) collective-permute-start(f32[13,768]{1,0:T(8,128)S(1)} %pad_maximum_fusion.1), channel_id=1, source_target_pairs={{0,2},{1,3},{2,4},{3,5},{4,6},{5,7},{6,0},{7,1},{8,10},{9,11},{10,... | collective-permute-start | bytes 119816 | tf_op jit(solution)/shard_map/ppermute | solution.py:789
  343.5 9.8 %collective-permute-start.10 = (f32[13,768]{1,0:T(8,128)S(1)}, f32[13,768]{1,0:T(8,128)S(1)}, u32[]{:S(2)}, u32[]{:S(2)}) collective-permute-start(f32[13,768]{1,0:T(8,128)S(1)} %pad_maximum_fusion.1), channel_id=1, source_target_pairs={{0,3},{1,4},{2,5},{3,6},{4,7},{5,0},{6,1},{7,2},{8,11},{9,12},{10,... | collective-permute-start | bytes 119816 | tf_op jit(solution)/shard_map/ppermute | solution.py:789
  353.3 43.0 %collective-permute-start.31 = (bf16[2,2,2,24,3072]{4,3,1,0,2:T(8,128)(2,1)}, bf16[2,2,2,24,3072]{4,3,1,0,2:T(8,128)(2,1)}, u32[]{:S(2)}, u32[]{:S(2)}) collective-permute-start(bf16[2,2,2,24,3072]{4,3,1,0,2:T(8,128)(2,1)} %dynamic-slice_bitcast_fusion.1), channel_id=1, source_target_pairs={{0,1},{1,0},{2,3},{3,2},{4,5},{5,4},{6,7},{7,6},{8,9},{9,8},{10,11... | collective-permute-start | bytes 3538952 | tf_op jit(solution)/shard_map/ppermute | solution.py:749
  354.7 44.5 %collective-permute-start.36 = (bf16[2,2,2,24,3072]{4,3,0,1,2:T(8,128)(2,1)}, bf16[2,2,2,24,3072]{4,3,0,1,2:T(8,128)(2,1)}, u32[]{:S(2)}, u32[]{:S(2)}) collective-permute-start(bf16[2,2,2,24,3072]{4,3,0,1,2:T(8,128)(2,1)} %dynamic-slice_bitcast_fusion), channel_id=1, source_target_pairs={{0,16},{8,24},{16,0},{24,8},{1,17},{9,25},{17,1},{25,9},{2,18},{10... | collective-permute-start | bytes 3538952 | tf_op jit(solution)/shard_map/ppermute | solution.py:749
  356.4 45.7 %collective-permute-start.21 = (bf16[2,2,2,24,2304]{4,3,2,1,0:T(8,128)(2,1)}, bf16[2,2,2,24,2304]{4,3,2,1,0:T(8,128)(2,1)S(1)}, u32[]{:S(2)}, u32[]{:S(2)}) collective-permute-start(bf16[2,2,2,24,2304]{4,3,2,1,0:T(8,128)(2,1)} %dynamic-slice_bitcast_fusion.2), channel_id=1, source_target_pairs={{0,2},{1,3},{2,0},{3,1},{4,6},{5,7},{6,4},{7,5},{8,10},{9,11},{10,... | collective-permute-start | bytes 2654216 | tf_op jit(solution)/shard_map/ppermute | solution.py:749
  398.2 15.6 %collective-permute-start.32 = (bf16[2,2,24,3072]{3,2,1,0:T(8,128)(2,1)S(1)}, bf16[2,2,24,3072]{3,2,1,0:T(8,128)(2,1)S(1)}, u32[]{:S(2)}, u32[]{:S(2)}) collective-permute-start(bf16[2,2,24,3072]{3,2,1,0:T(8,128)(2,1)S(1)} %dynamic-slice_bitcast_fusion.4), channel_id=1, source_target_pairs={{0,2},{1,3},{2,0},{3,1},{4,6},{5,7},{6,4},{7,5},{8,10},{9,11},{10,... | collective-permute-start | bytes 1769480 | tf_op jit(solution)/shard_map/ppermute | solution.py:749
  400.9 15.4 %collective-permute-start.37 = (bf16[2,2,24,3072]{3,2,0,1:T(8,128)(2,1)S(1)}, bf16[2,2,24,3072]{3,2,0,1:T(8,128)(2,1)S(1)}, u32[]{:S(2)}, u32[]{:S(2)}) collective-permute-start(bf16[2,2,24,3072]{3,2,0,1:T(8,128)(2,1)S(1)} %dynamic-slice_bitcast_fusion.3), channel_id=1, source_target_pairs={{0,1},{1,0},{2,3},{3,2},{4,5},{5,4},{6,7},{7,6},{8,9},{9,8},{10,11... | collective-permute-start | bytes 1769480 | tf_op jit(solution)/shard_map/ppermute | solution.py:749
  402.4 24.5 %collective-permute-start.22 = (bf16[2,2,24,2304]{3,2,1,0:T(8,128)(2,1)S(1)}, bf16[2,2,24,2304]{3,2,1,0:T(8,128)(2,1)S(1)}, u32[]{:S(2)}, u32[]{:S(2)}) collective-permute-start(bf16[2,2,24,2304]{3,2,1,0:T(8,128)(2,1)S(1)} %dynamic-slice_bitcast_fusion.5), channel_id=1, source_target_pairs={{0,16},{8,24},{16,0},{24,8},{1,17},{9,25},{17,1},{25,9},{2,18},{10... | collective-permute-start | bytes 1327112 | tf_op jit(solution)/shard_map/ppermute | solution.py:749
  422.7 17.4 %collective-permute-start.34 = (bf16[24,3072]{1,0:T(8,128)(2,1)S(1)}, bf16[24,3072]{1,0:T(8,128)(2,1)S(1)}, u32[]{:S(2)}, u32[]{:S(2)}) collective-permute-start(bf16[24,3072]{1,0:T(8,128)(2,1)S(1)} %dynamic-slice_bitcast_fusion.11), channel_id=1, source_target_pairs={{0,4},{1,5},{2,6},{3,7},{4,0},{5,1},{6,2},{7,3},{8,12},{9,13},{10,... | collective-permute-start | bytes 442376 | tf_op jit(solution)/shard_map/ppermute | solution.py:749
  424.8 23.0 %collective-permute-start.39 = (bf16[24,3072]{1,0:T(8,128)(2,1)S(1)}, bf16[24,3072]{1,0:T(8,128)(2,1)S(1)}, u32[]{:S(2)}, u32[]{:S(2)}) collective-permute-start(bf16[24,3072]{1,0:T(8,128)(2,1)S(1)} %dynamic-slice_bitcast_fusion.10), channel_id=1, source_target_pairs={{0,4},{1,5},{2,6},{3,7},{4,0},{5,1},{6,2},{7,3},{8,12},{9,13},{10,... | collective-permute-start | bytes 442376 | tf_op jit(solution)/shard_map/ppermute | solution.py:749
  427.0 19.9 %collective-permute-start.23 = (bf16[2,24,2304]{2,1,0:T(8,128)(2,1)S(1)}, bf16[2,24,2304]{2,1,0:T(8,128)(2,1)S(1)}, u32[]{:S(2)}, u32[]{:S(2)}) collective-permute-start(bf16[2,24,2304]{2,1,0:T(8,128)(2,1)S(1)} %dynamic-slice_bitcast_fusion.9), channel_id=1, source_target_pairs={{0,4},{1,5},{2,6},{3,7},{4,0},{5,1},{6,2},{7,3},{8,12},{9,13},{10,... | collective-permute-start | bytes 663560 | tf_op jit(solution)/shard_map/ppermute | solution.py:749
  (31 other events, 336.6 us)

commit v2 on v1

--- a/solution.py
+++ b/solution.py
@@ -284,140 +284,171 @@
     )(meta, attended, tokens, tops[1], tops[0], bots[0], bots[1], pieces, proj)
 
 
-def ffn_kernel(e2, e2t, ge, get, up, down, kern, exp_out, ge2_out, down_out, up_out, kern_out, lifted, gact, gconv, act, graised, exp_acc, ge2_acc, down_acc, up_acc, kern_acc):
-    step, latent = pl.program_id(0), pl.program_id(1)
-    steps, latents = pl.num_programs(0), pl.num_programs(1)
-    half = lifted.shape[2]
-    rows_here = lifted.shape[0] - 4
-    block = lifted.shape[3]
-
-    raised = mm(e2[0], up[...]).astype(BF16).astype(F32)
-    for rr in range(rows_here + 4):
+def normal_parts(values):
+    density = jnp.exp(-0.5 * values * values) * 0.3989422804014327
+    t = 1.0 / (1.0 + 0.2316419 * jnp.abs(values))
+    series = t * (
+        0.319381530
+        + t * (-0.356563782 + t * (1.781477937 + t * (-1.821255978 + t * 1.330274429)))
+    )
+    tail = density * series
+    return jnp.where(values > 0.0, 1.0 - tail, tail), density
+
+
+def ffn_kernel(core, e2, e2t, ge, get, up, down, kern_in, exp_out, ge2_out, send_out, keep_out, kern_out, *scratch):
+    latents = e2.shape[0]
+    lifted, gact, gconv, act, graised = [scratch[k * latents : (k + 1) * latents] for k in range(5)]
+    down_acc, up_acc = scratch[5 * latents :]
+    step = pl.program_id(0)
+    half = lifted[0].shape[2]
+    rows_here = lifted[0].shape[0] - 4
+    block = lifted[0].shape[3]
+    taps = [kern_in[t : t + 1, :].astype(F32) for t in range(9)]
+    sums = [jnp.zeros((8, block), F32) for _ in range(9)]
+    rows_per = 4
+
+    def lift(latent, part):
+        size = rows_per * 2 * half
+        raised = mm(e2[latent, part * size : (part + 1) * size], up[...])
+        raised = raised.astype(BF16).astype(F32)
+        for k in range(rows_per):
+            for parity in range(2):
+                at = (2 * k + parity) * half
+                put_shifts(lifted[latent], part * rows_per + k, parity, raised[at : at + half])
+
+    def pull(latent, part):
+        size = gact[latent].shape[0] // 2
+        at = part * size
+        gact[latent][at : at + size] = mm(ge[latent, at : at + size], down[...], NT)
+
+    def bend(latent, rr):
         for parity in range(2):
-            at = (2 * rr + parity) * half
-            put_shifts(lifted, rr, parity, raised[at : at + half])
-    gact[...] = mm(ge[0], down[...], NT)
-
-    taps = [kern[t : t + 1, :] for t in range(9)]
-
-    for rr in range(rows_here + 2):
-        for parity in range(2):
-            total = jnp.zeros((half, block), F32)
+            total = None
             for i in range(3):
                 for j in range(3):
-                    total = total + lifted[rr + i, parity + j] * taps[3 * i + j]
-            cdf = 0.5 * (1.0 + lax.erf(total * 0.7071067811865476))
-            bell = jnp.exp(-0.5 * total * total) * 0.3989422804014327
+                    term = lifted[latent][rr + i, parity + j] * taps[3 * i + j]
+                    total = term if total is None else total + term
+            cdf, density = normal_parts(total)
             at = (2 * rr + parity) * half
             if 1 <= rr <= rows_here:
                 own = at - 2 * half
-                act[own : own + half, :] = (total * cdf).astype(BF16)
-            grad = gact[at : at + half, :] * (cdf + total * bell)
-            put_shifts(gconv, rr, parity, grad.astype(BF16).astype(F32))
-
-    sums = [jnp.zeros((8, block), F32) for _ in range(9)]
-    for row in range(rows_here):
+                act[latent][own : own + half, :] = (total * cdf).astype(BF16)
+            grad = gact[latent][at : at + half, :] * (cdf + total * density)
+            put_shifts(gconv[latent], rr, parity, grad.astype(BF16).astype(F32))
+
+    def unbend(latent, row):
         for parity in range(2):
-            total = jnp.zeros((half, block), F32)
-            here = gconv[row + 1, 1 + parity]
+            total = None
+            here = gconv[latent][row + 1, 1 + parity]
             for i in range(3):
                 for j in range(3):
-                    total = total + gconv[row + 2 - i, parity + 2 - j] * taps[3 * i + j]
-                    sums[3 * i + j] = sums[3 * i + j] + sum8(lifted[row + 1 + i, parity + j] * here)
+                    t = 3 * i + j
+                    term = gconv[latent][row + 2 - i, parity + 2 - j] * taps[t]
+                    total = term if total is None else total + term
+                    sums[t] = sums[t] + sum8(lifted[latent][row + 1 + i, parity + j] * here)
             at = (2 * row + parity) * half
-            graised[at : at + half, :] = total.astype(BF16)
-
-    expanded = mm(act[...], down[...])
-    grad_e2 = mm(graised[...], up[...], NT)
-    down_part = mm(get[0], act[...])
-    up_part = mm(e2t[0], graised[...])
+            graised[latent][at : at + half, :] = total.astype(BF16)
+
+    def gather(latent, part):
+        cut = slice(part * 256, (part + 1) * 256)
+        if part == 0:
+            exp_out[latent] += mm(act[latent][...], down[...])
+        elif part == 1:
+            ge2_out[latent] += mm(graised[latent][...], up[...], NT)
+        elif part == 2:
+            value = mm(get[latent], act[latent][...])
+            down_acc[...] = value if latent == 0 else down_acc[...] + value
+        else:
+            value = mm(e2t[latent], graised[latent][...])
+            up_acc[...] = value if latent == 0 else up_acc[...] + value
 
     @pl.when(step == 0)
     def _():
-        exp_acc[latent] = expanded
-        ge2_acc[latent] = grad_e2
-
-    @pl.when(step > 0)
-    def _():
-        exp_acc[latent] += expanded
-        ge2_acc[latent] += grad_e2
-
-    @pl.when(latent == 0)
-    def _():
-        down_acc[...] = down_part
-        up_acc[...] = up_part
-        for t in range(9):
-            kern_acc[t] = sums[t]
-
-    @pl.when(latent > 0)
-    def _():
-        down_acc[...] += down_part
-        up_acc[...] += up_part
-        for t in range(9):
-            kern_acc[t] += sums[t]
-
-    @pl.when(latent == latents - 1)
-    def _():
-        down_out[...] = down_acc[...].astype(BF16)
-        up_out[...] = up_acc[...].astype(BF16)
-        for t in range(9):
-            kern_out[t : t + 1, :] = jnp.sum(kern_acc[t], axis=0, keepdims=True)
-
-    @pl.when(step == steps - 1)
-    def _():
-        exp_out[latent] = exp_acc[latent]
-        ge2_out[latent] = ge2_acc[latent]
-
-
-def ffn(e2, e2t, ge, get, up, down, kern, cols):
+        exp_out[...] = jnp.zeros_like(exp_out)
+        ge2_out[...] = jnp.zeros_like(ge2_out)
+
+    lifts = (rows_here + 4) // rows_per
+    for part in range(lifts):
+        lift(0, part)
+    for part in range(2):
+        pull(0, part)
+    for latent in range(latents):
+        more = []
+        if latent + 1 < latents:
+            more += [functools.partial(lift, latent + 1, part) for part in range(lifts)]
+            more += [functools.partial(pull, latent + 1, part) for part in range(2)]
+        if latent > 0:
+            more += [functools.partial(gather, latent - 1, part) for part in range(4)]
+        work = [functools.partial(bend, latent, rr) for rr in range(rows_here + 2)]
+        work += [functools.partial(unbend, latent, row) for row in range(rows_here)]
+        for k, unit in enumerate(work):
+            if k < len(more):
+                more[k]()
+            unit()
+        for unit in more[len(work) :]:
+            unit()
+    for part in range(4):
+        gather(latents - 1, part)
+
+    size = down_acc.shape[0] // 4
+    for which, acc in enumerate((down_acc, up_acc)):
+        for y in range(2):
+            mine = pl.multiple_of((2 * y + core[0]) * size, 8)
+            other = pl.multiple_of((2 * y + 1 - core[0]) * size, 8)
+            keep_out[which, y] = acc[pl.ds(mine, size), :].astype(BF16)
+            send_out[which, y] = acc[pl.ds(other, size), :].astype(BF16)
+    for t in range(9):
+        kern_out[t : t + 1, :] = jnp.sum(sums[t], axis=0, keepdims=True)
+
+
+def ffn(core, e2, e2t, ge, get, up, down, kern, cols):
     latents = e2.shape[0]
     half = cols // 2
     own = e2t.shape[2]
     rows_here = own // cols
     hidden = up.shape[1]
-    steps = hidden // FF_BLOCK
-    per_latent = lambda *shape: pl.BlockSpec((1,) + shape, lambda f, l: (l, 0, 0))
+    fixed = lambda *shape: pl.BlockSpec(shape, lambda f, c: (0,) * len(shape))
+    parts = jax.ShapeDtypeStruct((2, 2, D // 4, hidden), BF16)
+    parts_spec = pl.BlockSpec((2, 2, D // 4, FF_BLOCK), lambda f, c: (0, 0, 0, f))
+    each = lambda *args: [pltpu.VMEM(*args)] * latents
     return pl.pallas_call(
         ffn_kernel,
         out_shape=(
             jax.ShapeDtypeStruct((latents, own, D), F32),
             jax.ShapeDtypeStruct((latents, own, D), F32),
-            jax.ShapeDtypeStruct((D, hidden), BF16),
-            jax.ShapeDtypeStruct((D, hidden), BF16),
+            parts,
+            parts,
             jax.ShapeDtypeStruct((9, hidden), F32),
         ),
-        grid=(steps, latents),
-        in_specs=[
-            per_latent(own + 4 * cols, D),
-            per_latent(D, own),
-            per_latent(own + 2 * cols, D),
-            per_latent(D, own),
-            pl.BlockSpec((D, FF_BLOCK), lambda f, l: (0, f)),
-            pl.BlockSpec((FF_BLOCK, D), lambda f, l: (f, 0)),
-            pl.BlockSpec((9, FF_BLOCK), lambda f, l: (0, f)),
-        ],
-        out_specs=(
-            pl.BlockSpec((latents, own, D), lambda f, l: (0, 0, 0)),
-            pl.BlockSpec((latents, own, D), lambda f, l: (0, 0, 0)),
-            pl.BlockSpec((D, FF_BLOCK), lambda f, l: (0, f)),
-            pl.BlockSpec((D, FF_BLOCK), lambda f, l: (0, f)),
-            pl.BlockSpec((9, FF_BLOCK), lambda f, l: (0, f)),
-        ),
-        scratch_shapes=[
-            pltpu.VMEM((rows_here + 4, 4, half, FF_BLOCK), F32),
-            pltpu.VMEM((own + 2 * cols, FF_BLOCK), F32),
-            pltpu.VMEM((rows_here + 2, 4, half, FF_BLOCK), F32),
-            pltpu.VMEM((own, FF_BLOCK), BF16),
-            pltpu.VMEM((own, FF_BLOCK), BF16),
-            pltpu.VMEM((latents, own, D), F32),
-            pltpu.VMEM((latents, own, D), F32),
-            pltpu.VMEM((D, FF_BLOCK), F32),
-            pltpu.VMEM((D, FF_BLOCK), F32),
-            pltpu.VMEM((9, 8, FF_BLOCK), F32),
-        ],
+        grid_spec=pltpu.PrefetchScalarGridSpec(
+            num_scalar_prefetch=1,
+            grid=(hidden // FF_BLOCK,),
+            in_specs=[
+                fixed(latents, own + 4 * cols, D),
+                fixed(latents, D, own),
+                fixed(latents, own + 2 * cols, D),
+                fixed(latents, D, own),
+                pl.BlockSpec((D, FF_BLOCK), lambda f, c: (0, f)),
+                pl.BlockSpec((FF_BLOCK, D), lambda f, c: (f, 0)),
+                pl.BlockSpec((9, FF_BLOCK), lambda f, c: (0, f)),
+            ],
+            out_specs=(
+                fixed(latents, own, D),
+                fixed(latents, own, D),
+                parts_spec,
+                parts_spec,
+                pl.BlockSpec((9, FF_BLOCK), lambda f, c: (0, f)),
+            ),
+            scratch_shapes=each((rows_here + 4, 4, half, FF_BLOCK), F32)
+            + each((own + 2 * cols, FF_BLOCK), F32)
+            + each((rows_here + 2, 4, half, FF_BLOCK), F32)
+            + each((own, FF_BLOCK), BF16)
+            + each((own, FF_BLOCK), BF16)
+            + [pltpu.VMEM((D, FF_BLOCK), F32), pltpu.VMEM((D, FF_BLOCK), F32)],
+        ),
         compiler_params=pltpu.CompilerParams(vmem_limit_bytes=VMEM_LIMIT),
         name="ffn",
-    )(e2, e2t, ge, get, up, down, kern)
+    )(core, e2, e2t, ge, get, up, down, kern)
 
 
 def middle_kernel(meta, exp, ge2, after_in, branch_in, cot_in, pieces, proj, out, after_grad, gb_out, gatt_out, sums_out, buf):
@@ -744,11 +775,6 @@
     return lax.ppermute(values, axis, [(i + 1, i) for i in range(count - 1)])
 
 
-def exchange(values, axis, bit):
-    count = lax.axis_size(axis)
-    return lax.ppermute(values, axis, [(i, i ^ bit) for i in range(count)])
-
-
 def swap(values):
     return lax.all_to_all(values, "seq", 0, 0, tiled=False)
 
@@ -757,38 +783,61 @@
 ORDER = "ychlx"
 
 
-def halve(values, dims, bit):
+def blocks_of(values):
+    return values.reshape(values.shape[:-2] + (2, 2, 2, 2, 2, values.shape[-2] // 32, values.shape[-1]))
+
+
+def split(values, dims, bit):
     axis, mask = BITS[bit]
     mine = (lax.axis_index(axis) // mask) % 2
-    at = dims.index(bit)
+    at = values.ndim - 2 - len(dims) + dims.index(bit)
     send = lax.dynamic_index_in_dim(values, 1 - mine, at, keepdims=False)
     keep = lax.dynamic_index_in_dim(values, mine, at, keepdims=False)
-    got = exchange(send, axis, mask)
-    return keep.astype(F32) + got.astype(F32), dims.replace(bit, "")
-
-
-def reduce_rows(values, order):
-    shape = values.shape
-    devices = lax.axis_size("batch") * lax.axis_size("seq")
-    if lax.axis_size("batch") != 4 or lax.axis_size("seq") != 8:
-        return lax.psum_scatter(values, ("batch", "seq"), scatter_dimension=0, tiled=True).astype(F32)
-    values = values.reshape((2, 2, 2, 2, 2, shape[0] // devices, shape[1]))
-    dims = ORDER
+    return send, keep, dims.replace(bit, "")
+
+
+def hop(values, bit):
+    axis, mask = BITS[bit]
+    count = lax.axis_size(axis)
+    return lax.ppermute(values, axis, [(i, i ^ mask) for i in range(count)])
+
+
+def add(keep, got):
+    return keep.astype(F32) + got.astype(F32)
+
+
+def after(values, *others):
+    return lax.optimization_barrier((values,) + others)[0]
+
+
+def reduce_rest(values, dims, order):
     for bit in order:
-        values, dims = halve(values.astype(BF16), dims, bit)
+        send, keep, dims = split(values.astype(BF16), dims, bit)
+        values = add(keep, hop(send, bit))
     return values
 
 
-def gather_seq(values):
-    count = lax.axis_size("seq")
-    me = lax.axis_index("seq")
-    if count > 8:
-        return lax.all_gather(values, "seq", axis=0)
-    got = [values]
-    for k in range(1, count):
-        got.append(lax.ppermute(values, "seq", [(i, (i + k) % count) for i in range(count)]))
-    back = jnp.stack(got[::-1])
-    return lax.dynamic_slice_in_dim(jnp.concatenate([back, back]), (count - 1 - me) % count, count)
+def scatter_rows(values):
+    return lax.psum_scatter(values, ("batch", "seq"), scatter_dimension=0, tiled=True).astype(F32)
+
+
+def sum_and_gather(common, sliced):
+    seq_count, batch_count = lax.axis_size("seq"), lax.axis_size("batch")
+    rows, cols = sliced.shape
+    mine = cols // (seq_count * batch_count)
+    parts = sliced.reshape(rows, batch_count, seq_count, mine).transpose(2, 1, 0, 3).reshape(seq_count, -1)
+    flat = common.reshape(1, -1)
+    whole = jnp.concatenate([jnp.broadcast_to(flat, (seq_count, flat.shape[1])), parts], axis=1)
+    pad = -whole.shape[1] % 1024
+    whole = jnp.pad(whole, ((0, 0), (0, pad))).reshape(seq_count, -1, 128)
+    summed = jnp.sum(swap(whole), axis=0)
+    gathered = lax.all_gather(summed, "batch", axis=0).reshape(batch_count, -1)
+    common_all = gathered[:, : flat.shape[1]].reshape((batch_count,) + common.shape)
+    parts_all = jnp.sum(gathered[:, flat.shape[1] : flat.shape[1] + parts.shape[1]], axis=0)
+    own = lax.dynamic_index_in_dim(
+        parts_all.reshape(batch_count, rows, mine), lax.axis_index("batch"), 0, keepdims=False
+    )
+    return common_all, own
 
 
 def attend_plain(mixed, weight, ok, heads):
@@ -871,7 +920,7 @@
         [heights, widths, jnp.reshape(seq_place * rows_here, (1,))]
     ).astype(jnp.int32)
     kern_attn = conv_attn.astype(F32)
-    kern_ffn = conv_ffn.astype(F32)
+    core = jnp.reshape(batch_place % 2, (1,)).astype(jnp.int32)
 
     mixed = enter(meta, tokens, top, bot, pieces, kern_attn)
     sent = mixed.reshape(blocks, 1, per_group, D)
@@ -911,12 +960,26 @@
         attended = attended.transpose(0, 2, 1, 3).reshape(blocks, window, D)
 
     ge, get, cot_split = prepare_cot(meta, cotangent, cot_top, cot_bot, pieces)
+    conditions = lax.all_gather(
+        jnp.concatenate([condition, embedding.astype(F32), class_ids.astype(F32)[:, None]], axis=1),
+        "batch",
+        axis=0,
+    )
+    if share == 1:
+        triple = mm(grouped, qkv_weight).astype(BF16)
+        key_t = mm(weight_t[D : 2 * D], grouped, NT).astype(BF16)
+        attended, ge, triple, key_t, conditions = lax.optimization_barrier(
+            (attended, ge, triple, key_t, conditions)
+        )
     e2, e2t, after_attn, branch = second(
         meta, attended, tokens, (top, top_two), (bot, bot_two), pieces, proj_weight
     )
-    expanded, grad_e2, down_grad, up_grad, conv_ffn_part = ffn(
-        e2, e2t, ge, get, up_weight, down_weight, kern_ffn, cols
-    )
+    expanded, grad_e2, send_c, keep_c, conv_ffn_part = ffn(
+        core, e2, e2t, ge, get, up_weight, down_weight, conv_ffn, cols
+    )
+    halving = batch_count == 4 and seq_count == 8
+    if halving:
+        got_c = hop(send_c, "c")
     output, grad_after, grad_branch, grad_attended, mid_sums = middle(
         meta, expanded, grad_e2, after_attn, branch, cot_split, pieces, proj_weight, rows_here, cols
     )
@@ -924,18 +987,31 @@
     att_own = attended[:, margin : margin + per_group].reshape(blocks * per_group, D)
     flat_branch = grad_branch.reshape(blocks * per_group, D)
     proj_grad = mm(att_own, flat_branch, (((0,), (0,)), ((), ()))).astype(BF16)
+    hidden = conv_ffn.shape[1]
+    own_hidden = hidden // devices
+    side = conv_ffn_part.reshape(9, devices, own_hidden).transpose(1, 0, 2).reshape(devices, -1)
+    side_rows = D // devices
+    side_cols = -(-9 * own_hidden // (128 * side_rows)) * 128
+    side = jnp.pad(side, ((0, 0), (0, side_rows * side_cols - 9 * own_hidden)))
+    side = side.reshape(D, side_cols).astype(BF16)
     tall = per_group + margin
     if share == 1:
         gatt = swap(grad_attended.reshape(seq_count, per_group, D)).reshape(group_tokens, D)
-        triple = mm(grouped, qkv_weight).astype(BF16)
-        key_t = mm(weight_t[D : 2 * D], grouped, NT).astype(BF16)
+        if halving:
+            keep_c = after(keep_c, grad_attended)
+            sums = add(keep_c, got_c).astype(BF16).reshape(2, 2, 2, 2, 2, D // devices, hidden)
+            send_a, keep_a, dims_a = split(sums[0], "yhlx", "y")
+            send_b, keep_b, dims_b = split(sums[1], "yhlx", "x")
+            gatt, send_a, send_b = lax.optimization_barrier((gatt, send_a, send_b))
+            got_a, got_b = hop(send_a, "y"), hop(send_b, "x")
         offset = jnp.reshape(margin * (1 - my_a), (1,)).astype(jnp.int32)
         dq, dk, dv, gm_windows = attend_back(
             offset, triple, key_t, bias, lse, gatt, qkv_weight, seq_count, tall
         )
         gm = swap(gm_windows)
-        grad_triple = jnp.concatenate([dq, dk, dv], axis=1)
-        qkv_grad = mm(grouped, grad_triple, (((0,), (0,)), ((), ()))).astype(BF16)
+        turned = (((0,), (0,)), ((), ()))
+        rest_one = mm(grouped, jnp.concatenate([dq, dk], axis=1), turned).astype(BF16)
+        rest_two = jnp.concatenate([mm(grouped, dv, turned).astype(BF16), proj_grad, side], axis=1)
     else:
         sent = grad_attended.reshape(blocks, per_group, share, wide).transpose(0, 2, 1, 3)
         gatt = swap(sent.reshape(seq_count, per_group, wide)).reshape(group_tokens, wide)
@@ -952,49 +1028,68 @@
         qkv_grad = lax.dynamic_update_index_in_dim(
             spread, own_grad.reshape(D, 3, wide), chunk, 2
         ).reshape(D, 3 * D)
+        rest_one = qkv_grad[:, : 2 * D]
+        rest_two = jnp.concatenate([qkv_grad[:, 2 * D :], proj_grad, side], axis=1)
+
+    if halving:
+        keep_a, keep_b = after(keep_a, gm_windows), after(keep_b, gm_windows)
+        send_a, keep_a, dims_a = split(add(keep_a, got_a).astype(BF16), dims_a, "x")
+        send_b, keep_b, dims_b = split(add(keep_b, got_b).astype(BF16), dims_b, "y")
+        got_a, got_b = hop(send_a, "x"), hop(send_b, "y")
+        send_one, keep_one, dims_one = split(blocks_of(rest_one), ORDER, "c")
+        send_two, keep_two, dims_two = split(blocks_of(rest_two), ORDER, "c")
+        got_one, got_two = hop(send_one, "c"), hop(send_two, "c")
+        send_one, keep_one, dims_one = split(add(keep_one, got_one).astype(BF16), dims_one, "y")
+        send_two, keep_two, dims_two = split(add(keep_two, got_two).astype(BF16), dims_two, "x")
+        got_one, got_two = hop(send_one, "y"), hop(send_two, "x")
+    total = batch_count * latents
+
+    here = batch_place * seq_count + seq_place
+    own_cols = D // devices
+    conditions = conditions.reshape(total, -1)
+    condition_all = conditions[:, :D]
+    embedding_all = conditions[:, D : D + embedding.shape[1]]
+    ids_all = conditions[:, -1].astype(jnp.int32)
+    logistic_all = jax.nn.sigmoid(condition_all)
+    activated_all = (condition_all * logistic_all).astype(BF16).astype(F32)
+    slope_all = logistic_all * (1.0 + condition_all * (1.0 - logistic_all))
+
+    def back_through(grads):
+        high = lax.reduce_precision(grads, 8, 7)
+        middle_term = lax.reduce_precision(grads - high, 8, 7)
+        low = grads - high - middle_term
+        product = mm(jnp.concatenate([high, middle_term, low]).astype(BF16), ada_weight, NT)
+        return product[:total] + product[total : 2 * total] + product[2 * total :]
 
     token_grad, conv_attn_part, end_sums = leave(
         meta, gm, tokens, top, bot, grad_after, pieces, kern_attn
     )
 
-    down_rows = reduce_rows(down_grad, "cyxlh")
-    up_rows = reduce_rows(up_grad, "cxlyh")
-    proj_rows = reduce_rows(proj_grad, "clhyx")
-    qkv_rows = reduce_rows(qkv_grad, "clyhx")
-
-    ffn_rows = conv_ffn_part.reshape(9 * conv_ffn_part.shape[1] // D, D)
-    early = jnp.sum(
-        gather_seq(jnp.concatenate([mid_sums.reshape(latents * 4, D), ffn_rows])), axis=0
-    )
-    late = jnp.sum(
-        gather_seq(
-            jnp.concatenate([end_sums.reshape(latents * 2, D), jnp.sum(conv_attn_part, axis=0)])
-        ),
-        axis=0,
-    )
-    early_all = lax.all_gather(early, "batch", axis=0)
-    late_all = lax.all_gather(late, "batch", axis=0)
-    total = batch_count * latents
-    mid_all = early_all[:, : latents * 4].reshape(total, 4, D)
-    end_all = late_all[:, : latents * 2].reshape(total, 2, D)
-    grad_pieces = jnp.concatenate([end_all, mid_all], axis=1).reshape(total, 6 * D)
-    conv_ffn_grad = jnp.sum(early_all[:, latents * 4 :], axis=0).reshape(9, -1)
-    conv_attn_grad = jnp.sum(late_all[:, latents * 2 :], axis=0)
-
-    here = batch_place * seq_count + seq_place
-    own_cols = D // devices
-    conditions = lax.all_gather(
-        jnp.concatenate([condition, embedding.astype(F32)], axis=1), "batch", axis=0
-    ).reshape(total, -1)
-    ids_all = lax.all_gather(class_ids, "batch", axis=0).reshape(total)
-    embedding_all = conditions[:, D:]
-    condition_all = conditions[:, :D]
-    logistic_all = jax.nn.sigmoid(condition_all)
-    activated_all = (condition_all * logistic_all).astype(BF16).astype(F32)
-    grad_silu = lax.dot_general(
-        grad_pieces, ada_weight.astype(F32), NT, precision=HIGHEST, preferred_element_type=F32
-    )
-    cond_all = grad_silu * logistic_all * (1.0 + condition_all * (1.0 - logistic_all))
+    all_sums, conv_attn_grad = sum_and_gather(
+        jnp.concatenate([end_sums, mid_sums], axis=1), jnp.sum(conv_attn_part, axis=0)
+    )
+    if halving:
+        pair = jnp.stack([add(keep_a, got_a), add(keep_b, got_b)])
+        pair = reduce_rest(pair, dims_a, "lh")
+        down_rows, up_rows = pair[0], pair[1]
+        send_one, keep_one, dims_one = split(add(keep_one, got_one).astype(BF16), dims_one, "x")
+        send_two, keep_two, dims_two = split(add(keep_two, got_two).astype(BF16), dims_two, "y")
+        got_one, got_two = hop(send_one, "x"), hop(send_two, "y")
+        rest_rows = jnp.concatenate([add(keep_one, got_one), add(keep_two, got_two)], axis=-1)
+        rest_rows = reduce_rest(rest_rows, dims_one, "lh")
+    else:
+        whole = jnp.stack([keep_c, send_c])
+        whole = jnp.where(core[0] == 0, whole, whole[::-1]).transpose(1, 2, 0, 3, 4)
+        whole = whole.reshape(2, D, hidden)
+        down_rows, up_rows = scatter_rows(whole[0]), scatter_rows(whole[1])
+        rest_rows = scatter_rows(jnp.concatenate([rest_one, rest_two], axis=1))
+    qkv_rows = rest_rows[:, : 3 * D]
+    proj_rows = rest_rows[:, 3 * D : 4 * D]
+    conv_ffn_grad = rest_rows[:, 4 * D :].reshape(-1)[: 9 * own_hidden].reshape(9, own_hidden)
+
+    grad_pieces = all_sums.reshape(total, 6 * D)
+    grad_silu = back_through(grad_pieces)
+    cond_all = grad_silu * slope_all
     cond_grad = lax.dynamic_slice_in_dim(cond_all, batch_place * latents, latents)
     cond_cols = lax.dynamic_slice_in_dim(cond_all, here * own_cols, own_cols, axis=1)
     act_cols = lax.dynamic_slice_in_dim(activated_all, here * own_cols, own_cols, axis=1)
@@ -1002,9 +1097,10 @@
         left, right, (((0,), (0,)), ((), ())), precision=HIGHEST, preferred_element_type=F32
     )
     hot_all = (ids_all[:, None] == jnp.arange(class_table.shape[0], dtype=jnp.int32)[None, :]).astype(F32)
-    bias_grad = jnp.sum(grad_pieces, axis=0)
     bias_cols = 6 * D // devices
-    hidden_cols = conv_ffn.shape[1] // devices
+    bias_grad = jnp.sum(
+        lax.dynamic_slice_in_dim(grad_pieces, here * bias_cols, bias_cols, axis=1), axis=0
+    )
     return (
         output,
         token_grad,
@@ -1012,12 +1108,12 @@
         outer(embedding_all, cond_cols),
         outer(hot_all, cond_cols),
         outer(act_cols, grad_pieces),
-        lax.dynamic_slice_in_dim(bias_grad, here * bias_cols, bias_cols),
-        lax.dynamic_slice_in_dim(conv_attn_grad, here * own_cols, own_cols, axis=1),
+        bias_grad,
+        conv_attn_grad,
         qkv_rows,
         proj_rows,
         up_rows,
-        lax.dynamic_slice_in_dim(conv_ffn_grad, here * hidden_cols, hidden_cols, axis=1),
+        conv_ffn_grad,
         down_rows.T,
     )
 

time: 460 us -> 372 us (0.81); the launches traced: 453 us -> 370 us
  blocking collectives: 39 us -> 11.3 us
  starting transfers between devices: 97.7 us -> 75.2 us
  local copies, waits for them, and re-layouts: 57.4 us -> 36 us
  Pallas kernels: 121 us -> 109 us
  waiting for transfers between devices: 81 us -> 85.9 us
    ppermute x34 -> x15, starting transfers between devices: 58.3 us -> 16.2 us  [hop(): return lax.ppermute(values, axis, [(i, i ^ mask) for i in range(count)])]
    all_gather x3 -> x2, blocking collectives: 33.5 us -> 11.3 us  [the longest x1 5.82 us: shards(): lax.all_gather(jnp.concatenate([condition, embedding.astype(F32), class_i...]
    all_to_all x4 -> x5, starting transfers between devices: 18.8 us -> 38.4 us  [swap(): return lax.all_to_all(values, 'seq', 0, 0, tiled=False)]
    unnamed x60 -> x45, local copies, waits for them, and re-layouts: 19.2 us -> 5.37 us
    pallas_call x1, Pallas kernels: 53.5 us -> 42.2 us  [ffn(): pl.pallas_call(ffn_kernel, out_shape=(jax.ShapeDtypeStruct((latents, own,...]
    dot_general x1 -> x0, matrix products: 7.9 us -> none  [shards(): lax.dot_general(grad_pieces, ada_weight.astype(F32), NT, precision=HIGHES...]
    dynamic_slice x10 -> x8, local copies, waits for them, and re-layouts: 13.8 us -> 7.26 us  [the longest x5 3.87 us: split(): keep = lax.dynamic_index_in_dim(values, mine, at, keepdims=False)]
    dot_general x7 -> x9, matrix products: 19.1 us -> 24.6 us  [mm(): return lax.dot_general(left, right, dims, preferred_element_type=F32)]
  transfers between devices with their start and end apart: 44 -> 26, of which waited for: 14 -> 10; matrix products, arithmetic and copies ran while one was open for 23% -> 20% of each run, Pallas kernels for 7% -> 6%
where the time goes in v2:
time: 372 us; the launch traced here: 370 us
  Pallas kernels  109 us (29%)
  waiting for transfers between devices  85.9 us (23%)
  starting transfers between devices  75.2 us (20%)
  local copies, waits for them, and re-layouts  36 us (10%)
  matrix products  27.7 us (7%)
  other arithmetic  23.4 us (6%)
  blocking collectives  11.3 us (3%)
    ppermute x15, waiting for transfers between devices, hop(): return lax.ppermute(values, axis, [(i, i ^ mask) for i in range(count)])  57.3 us
    pallas_call x1, Pallas kernels, ffn(): pl.pallas_call(ffn_kernel, out_shape=(jax.ShapeDtypeStruct((latents, own,...  42.2 us
    all_to_all x5, starting transfers between devices, swap(): return lax.all_to_all(values, 'seq', 0, 0, tiled=False)  38.4 us
    all_to_all x5, waiting for transfers between devices, swap(): return lax.all_to_all(values, 'seq', 0, 0, tiled=False)  28.2 us
    dot_general x9, matrix products, mm(): return lax.dot_general(left, right, dims, preferred_element_type=F32)  24.6 us
    pallas_call x1, Pallas kernels, attend_back(): pl.pallas_call(attend_back_kernel, out_shape=(jax.ShapeDtypeStruct((token...  20.3 us
    ppermute x3, starting transfers between devices, from_before(): return lax.ppermute(values, axis, [(i, i + 1) for i in range(count - 1)])  16.8 us
    ppermute x15, starting transfers between devices, hop(): return lax.ppermute(values, axis, [(i, i ^ mask) for i in range(count)])  16.2 us
  transfers between devices with their start and end apart: 26, of which 10 were waited for; matrix products, arithmetic and copies ran while one was open for 20% of the time, Pallas kernels for 6%

profile of v2, /device:TPU:0, one launch (start us, length us, event | category | flops | bytes accessed | tf_op | source)
XLA Modules:
  0.0 370.4 jit_solution(15893570683883794673)
XLA Ops:
  4.2 6.2 %collective-permute-start = (bf16[2,1,64,768]{3,2,1,0:T(8,128)(2,1)}, bf16[2,1,64,768]{3,2,1,0:T(8,128)(2,1)}, u32[]{:S(2)}, u32[]{:S(2)}) collective-permute-start(bf16[2,1,64,768]{3,2,1,0:T(8,128)(2,1)} %get-tuple-element.98), channel_id=1, source_target_pairs={{0,1},{1,2},{2,3},{3,4},{4,5},{5,6},{6,7},{8,9},{9,10},{10,11},{11... | collective-permute-start | bytes 589832 | tf_op jit(solution)/shard_map/ppermute | solution.py:770
  11.1 4.0 %convolution_add_fusion = f32[2,4608]{1,0:T(2,128)S(1)} fusion(bf16[768,4608]{1,0:T(8,128)(2,1)} %param.24, f32[4608]{0:T(1024)S(1)} %copy-done.16, f32[2,768]{1,0:T(2,128)S(1)} %convolution_add_fusion.1), kind=kOutput, calls=%fused_computation.1 | convolution fusion | flops 14172672 | bytes 7139328 | tf_op jit(solution)/shard_map/dot_general | solution.py:29
  17.3 5.2 %enter.1 = bf16[2,4,64,768]{3,2,1,0:T(8,128)(2,1)} custom-call(s32[5]{0:T(128)} %pad_add_fusion.meta, bf16[2,4,64,768]{3,2,1,0:T(8,128)(2,1)} %tok.5, bf16[2,1,64,768]{3,2,1,0:T(8,128)(2,1)} %collective-permute-done.top.top1, bf16[2,1,64,768]{3,2,1,0:T(8,128)(2,1)} %collective-permute-done.1.bot.bot1, f32[2,6,768]{2,1,0:T(8,128)} %reshape.160.pieces, ...), custom_call_target="tpu_custom_call" | custom-call | tf_op jit(solution)/shard_map/enter/pallas_call | solution.py:133
  22.5 5.8 %all-to-all-start = ((bf16[8,64,768]{2,1,0:T(8,128)(2,1)}), bf16[8,64,768]{2,1,0:T(8,128)(2,1)}, u32[]{:S(2)}, u32[]{:S(2)}) async-start(bf16[8,64,768]{2,1,0:T(8,128)(2,1)} %bitcast.144), calls=%async_computation | async-start | bytes 1572864 | tf_op jit(solution)/shard_map/all_to_all | solution.py:779
  30.8 3.6 copy.66
  35.7 13.0 %all-to-all-done = bf16[8,64,768]{2,1,0:T(8,128)(2,1)} async-done(((bf16[8,64,768]{2,1,0:T(8,128)(2,1)}), bf16[8,64,768]{2,1,0:T(8,128)(2,1)}, u32[]{:S(2)}, u32[]{:S(2)}) %all-to-all-start) | async-done | bytes 786464 | tf_op jit(solution)/shard_map/all_to_all | solution.py:779
  49.5 14.4 %attend.1 = (bf16[8,128,768]{2,1,0:T(8,128)(2,1)}, f32[6,2,512]{2,1,0:T(2,128)}) custom-call(bf16[512,768]{1,0:T(8,128)(2,1)} %bitcast.3.mixed, bf16[768,2304]{1,0:T(8,128)(2,1)} %wv.1, bf16[768,2304]{1,0:T(8,128)(2,1)} %wv.1, bf16[2304,768]{1,0:T(8,128)(2,1)} %bitcast.135, f32[512,128]{1,0:T(8,128)} %broadcast_in_dim.18.bias), custom_call_target="tpu_custom_call" | custom-call | tf_op jit(solution)/shard_map/attend/pallas_call | solution.py:655
  63.8 4.6 %all-to-all-start.1 = ((bf16[8,128,768]{2,1,0:T(8,128)(2,1)}), bf16[8,128,768]{2,1,0:T(8,128)(2,1)}, u32[]{:S(2)}, u32[]{:S(2)}) async-start(bf16[8,128,768]{2,1,0:T(8,128)(2,1)} %get-tuple-element.50), calls=%async_computation.1 | async-start | bytes 3145728 | tf_op jit(solution)/shard_map/all_to_all | solution.py:779
  71.5 5.2 %collective-permute-start.2 = (bf16[2,1,64,768]{3,2,1,0:T(8,128)(2,1)}, bf16[2,1,64,768]{3,2,1,0:T(8,128)(2,1)}, u32[]{:S(2)}, u32[]{:S(2)}) collective-permute-start(bf16[2,1,64,768]{3,2,1,0:T(8,128)(2,1)} %get-tuple-element.100), channel_id=1, source_target_pairs={{0,1},{1,2},{2,3},{3,4},{4,5},{5,6},{6,7},{8,9},{9,10},{10,11},{11... | collective-permute-start | bytes 589832 | tf_op jit(solution)/shard_map/ppermute | solution.py:770
  78.0 5.3 %collective-permute-start.4 = (bf16[2,1,64,768]{3,2,1,0:T(8,128)(2,1)}, bf16[2,1,64,768]{3,2,1,0:T(8,128)(2,1)}, u32[]{:S(2)}, u32[]{:S(2)}) collective-permute-start(bf16[2,1,64,768]{3,2,1,0:T(8,128)(2,1)} %get-tuple-element.96), channel_id=1, source_target_pairs={{0,1},{1,2},{2,3},{3,4},{4,5},{5,6},{6,7},{8,9},{9,10},{10,11},{11... | collective-permute-start | bytes 589832 | tf_op jit(solution)/shard_map/ppermute | solution.py:770
  86.5 5.8 %all-gather.2 = f32[4,2,1025]{2,1,0:T(2,128)} all-gather(f32[1,2,1025]{2,1,0:T(2,128)S(1)} %maximum_bitcast_fusion), channel_id=2, replica_groups=mesh['batch'=4,'seq'=8] {'batch'}, dimensions={0}, use_global_device_ids=true | all-gather | bytes 41000 | tf_op jit(solution)/shard_map/all_gather | solution.py:963
  92.3 3.6 prepare_cot.1
  95.9 4.5 %convolution_convert_fusion.query.key.value = bf16[512,2304]{1,0:T(8,128)(2,1)} fusion(bf16[512,768]{1,0:T(8,128)(2,1)} %bitcast.3.mixed, bf16[768,2304]{1,0:T(8,128)(2,1)S(1)} %copy-done.3), kind=kOutput, calls=%fused_computation.2 | convolution fusion | flops 1813118976 | bytes 6684672 | tf_op jit(solution)/shard_map/dot_general | solution.py:29
  103.6 3.2 all-to-all-done.1.att
  106.9 6.6 %second.1 = (bf16[2,512,768]{2,1,0:T(8,128)(2,1)}, bf16[2,768,256]{2,1,0:T(8,128)(2,1)}, f32[2,256,768]{2,1,0:T(8,128)}, f32[2,256,768]{2,1,0:T(8,128)}) custom-call(s32[5]{0:T(128)} %pad_add_fusion.meta, bf16[8,128,768]{2,1,0:T(8,128)(2,1)} %all-to-all-done.1.att, bf16[2,4,64,768]{3,2,1,0:T(8,128)(2,1)} %tok.5, ...), custom_call_target="tpu_custom_call" | custom-call | tf_op jit(solution)/shard_map/second/pallas_call | solution.py:250
  113.4 42.2 %ffn.1 = (f32[2,256,768]{2,1,0:T(8,128)}, f32[2,256,768]{2,1,0:T(8,128)}, bf16[2,2,192,3072]{3,2,1,0:T(8,128)(2,1)}, bf16[2,2,192,3072]{3,2,1,0:T(8,128)(2,1)}, f32[9,3072]{1,0:T(8,128)}) custom-call(s32[1]{0:T(128)} %bitcast.1.core, bf16[2,512,768]{2,1,0:T(8,128)(2,1)} %get-tuple-element.53.e2, bf16[2,768,256]{2,1,0:T(8,128)(2,1)} %get-tuple-element.54.e2t, ...), custom_call_target="tpu_custom_call" | custom-call | tf_op jit(solution)/shard_map/ffn/pallas_call | solution.py:414
  155.9 8.5 %middle.1 = (bf16[2,4,64,768]{3,2,1,0:T(8,128)(2,1)}, f32[2,256,768]{2,1,0:T(8,128)}, bf16[2,4,64,768]{3,2,1,0:T(8,128)(2,1)}, bf16[2,4,64,768]{3,2,1,0:T(8,128)(2,1)}, f32[2,4,768]{2,1,0:T(4,128)}) custom-call(s32[5]{0:T(128)} %pad_add_fusion.meta, f32[2,256,768]{2,1,0:T(8,128)} %get-tuple-element.57.exp, f32[2,256,768]{2,1,0:T(8,128)} %get-tuple-element.58.ge2, ...), custom_call_target="tpu_custom_call" | custom-call | tf_op jit(solution)/shard_map/middle/pallas_call | solution.py:495
  164.4 18.3 %all-to-all-start.2 = ((bf16[8,64,768]{2,1,0:T(8,128)(2,1)}), bf16[8,64,768]{2,1,0:T(8,128)(2,1)S(1)}, u32[]{:S(2)}, u32[]{:S(2)}) async-start(bf16[8,64,768]{2,1,0:T(8,128)(2,1)} %bitcast.148), calls=%async_computation.2 | async-start | bytes 1572864 | tf_op jit(solution)/shard_map/all_to_all | solution.py:779
  182.7 5.7 %add_convert_fusion = bf16[2,2,192,3072]{3,2,1,0:T(8,128)(2,1)S(1)} fusion(bf16[2,2,192,3072]{3,2,1,0:T(8,128)(2,1)} %collective-permute-done.6, bf16[2,2,192,3072]{3,2,1,0:T(8,128)(2,1)} %get-tuple-element.68), kind=kLoop, calls=%fused_computation | loop fusion | flops 9437184 | bytes 14155776 | tf_op jit(solution)/shard_map/convert_element_type | solution.py:1002
  191.3 12.0 %all-to-all-done.2 = bf16[8,64,768]{2,1,0:T(8,128)(2,1)S(1)} async-done(((bf16[8,64,768]{2,1,0:T(8,128)(2,1)}), bf16[8,64,768]{2,1,0:T(8,128)(2,1)S(1)}, u32[]{:S(2)}, u32[]{:S(2)}) %all-to-all-start.2) | async-done | bytes 786464 | tf_op jit(solution)/shard_map/all_to_all | solution.py:779
  204.3 20.3 %attend_back.1 = (bf16[512,768]{1,0:T(8,128)(2,1)}, bf16[512,768]{1,0:T(8,128)(2,1)}, bf16[512,768]{1,0:T(8,128)(2,1)}, bf16[8,96,768]{2,1,0:T(8,128)(2,1)}) custom-call(s32[1]{0:T(128)} %bitcast.10.offset, bf16[512,2304]{1,0:T(8,128)(2,1)} %convolution_convert_fusion.query.key.value, bf16[512,2304]{1,0:T(8,128)(2,1)} %convolution_convert_fusion.query.key.value, ...), custom_call_target="tpu_custom_call" | custom-call | tf_op jit(solution)/shard_map/attend_back/pallas_call | solution.py:732
  235.7 4.5 %all-to-all-start.3 = ((bf16[8,96,768]{2,1,0:T(8,128)(2,1)}), bf16[8,96,768]{2,1,0:T(8,128)(2,1)}, u32[]{:S(2)}, u32[]{:S(2)}) async-start(bf16[8,96,768]{2,1,0:T(8,128)(2,1)} %get-tuple-element.71), calls=%async_computation.3 | async-start | bytes 2359296 | tf_op jit(solution)/shard_map/all_to_all | solution.py:779
  248.0 3.3 copy.76
  255.4 13.9 %collective-permute-done.15 = bf16[2,2,2,24,3072]{4,3,0,1,2:T(8,128)(2,1)} collective-permute-done((bf16[2,2,2,24,3072]{4,3,0,1,2:T(8,128)(2,1)}, bf16[2,2,2,24,3072]{4,3,0,1,2:T(8,128)(2,1)}, u32[]{:S(2)}, u32[]{:S(2)}) %collective-permute-start.15) | collective-permute-done | bytes 1179680 | tf_op jit(solution)/shard_map/ppermute | solution.py:802
  272.8 12.0 %collective-permute-done.17 = bf16[2,2,2,24,3072]{4,3,1,2,0:T(8,128)(2,1)S(1)} collective-permute-done((bf16[2,2,2,24,3072]{4,3,1,2,0:T(8,128)(2,1)}, bf16[2,2,2,24,3072]{4,3,1,2,0:T(8,128)(2,1)S(1)}, u32[]{:S(2)}, u32[]{:S(2)}) %collective-permute-start.17) | collective-permute-done | bytes 1179680 | tf_op jit(solution)/shard_map/ppermute | solution.py:802
  289.1 8.2 %collective-permute-done.16 = bf16[2,2,24,3072]{3,2,0,1:T(8,128)(2,1)S(1)} collective-permute-done((bf16[2,2,24,3072]{3,2,0,1:T(8,128)(2,1)S(1)}, bf16[2,2,24,3072]{3,2,0,1:T(8,128)(2,1)S(1)}, u32[]{:S(2)}, u32[]{:S(2)}) %collective-permute-start.16) | collective-permute-done | bytes 589856 | tf_op jit(solution)/shard_map/ppermute | solution.py:802
  303.2 7.9 %collective-permute-done.11 = bf16[2,2,2,24,1664]{4,3,2,1,0:T(8,128)(2,1)S(1)} collective-permute-done((bf16[2,2,2,24,1664]{4,3,2,1,0:T(8,128)(2,1)S(1)}, bf16[2,2,2,24,1664]{4,3,2,1,0:T(8,128)(2,1)S(1)}, u32[]{:S(2)}, u32[]{:S(2)}) %collective-permute-start.11) | collective-permute-done | bytes 639008 | tf_op jit(solution)/shard_map/ppermute | solution.py:802
  312.5 8.7 %leave.1 = (f32[2,4,64,768]{3,2,1,0:T(8,128)}, f32[2,9,768]{2,1,0:T(8,128)}, f32[2,2,768]{2,1,0:T(2,128)}) custom-call(s32[5]{0:T(128)} %pad_add_fusion.meta, bf16[8,96,768]{2,1,0:T(8,128)(2,1)} %all-to-all-done.3.gm, bf16[2,4,64,768]{3,2,1,0:T(8,128)(2,1)} %tok.5, bf16[2,1,64,768]{3,2,1,0:T(8,128)(2,1)} %collective-permute-done.top.top1, ...), custom_call_target="tpu_custom_call" | custom-call | tf_op jit(solution)/shard_map/leave/pallas_call | solution.py:583
  324.0 5.3 %all-to-all-start.4 = ((f32[8,80,128]{2,1,0:T(8,128)}), f32[8,80,128]{2,1,0:T(8,128)S(1)}, u32[]{:S(2)}, u32[]{:S(2)}) async-start(f32[8,80,128]{2,1,0:T(8,128)} %bitcast.133), calls=%async_computation.4 | async-start | bytes 655360 | tf_op jit(solution)/shard_map/all_to_all | solution.py:779
  336.2 13.7 %collective-permute-done.13 = bf16[2,24,3200]{2,1,0:T(8,128)(2,1)S(1)} collective-permute-done((bf16[2,24,3200]{2,1,0:T(8,128)(2,1)S(1)}, bf16[2,24,3200]{2,1,0:T(8,128)(2,1)S(1)}, u32[]{:S(2)}, u32[]{:S(2)}) %collective-permute-start.13) | collective-permute-done | bytes 307232 | tf_op jit(solution)/shard_map/ppermute | solution.py:802
  350.7 5.5 %all-gather.1 = f32[320,128]{1,0:T(8,128)S(1)} all-gather(f32[80,128]{1,0:T(8,128)S(1)} %reduce_sum.37), channel_id=3, replica_groups=mesh['batch'=4,'seq'=8] {'batch'}, dimensions={0}, use_global_device_ids=true | all-gather | bytes 204800 | tf_op jit(solution)/shard_map/all_gather | solution.py:834
  356.5 4.9 %fusion.25 = f32[24,768]{1,0:T(8,128)S(1)} fusion(bf16[768,4608]{1,0:T(8,128)(2,1)} %param.24, bf16[8,4608]{1,0:T(8,128)(2,1)S(1)} %get-tuple-element.104, bf16[8,4608]{1,0:T(8,128)(2,1)S(1)} %get-tuple-element.105, bf16[8,4608]{1,0:T(8,128)(2,1)S(1)} %get-tuple-element.103), kind=kOutput, calls=%fused_computation.75 | convolution fusion | flops 170532864 | bytes 7372800 | tf_op jit(solution)/shard_map/dot_general | solution.py:29
  (175 shorter events, 83.2 us)
Async XLA Ops:
  2.9 14.1 %collective-permute-start.1 = (bf16[2,1,64,768]{3,2,1,0:T(8,128)(2,1)}, bf16[2,1,64,768]{3,2,1,0:T(8,128)(2,1)}, u32[]{:S(2)}, u32[]{:S(2)}) collective-permute-start(bf16[2,1,64,768]{3,2,1,0:T(8,128)(2,1)} %get-tuple-element.97), channel_id=1, source_target_pairs={{1,0},{2,1},{3,2},{4,3},{5,4},{6,5},{7,6},{9,8},{10,9},{11,10},{12... | collective-permute-start | bytes 589832 | tf_op jit(solution)/shard_map/ppermute | solution.py:775
  4.2 13.1 %collective-permute-start = (bf16[2,1,64,768]{3,2,1,0:T(8,128)(2,1)}, bf16[2,1,64,768]{3,2,1,0:T(8,128)(2,1)}, u32[]{:S(2)}, u32[]{:S(2)}) collective-permute-start(bf16[2,1,64,768]{3,2,1,0:T(8,128)(2,1)} %get-tuple-element.98), channel_id=1, source_target_pairs={{0,1},{1,2},{2,3},{3,4},{4,5},{5,6},{6,7},{8,9},{9,10},{10,11},{11... | collective-permute-start | bytes 589832 | tf_op jit(solution)/shard_map/ppermute | solution.py:770
  17.1 13.7 %copy-start.2 = (bf16[768,2304]{1,0:T(8,128)(2,1)S(1)}, bf16[768,2304]{1,0:T(8,128)(2,1)}, u32[]{:S(2)}) copy-start(bf16[768,2304]{1,0:T(8,128)(2,1)} %wv.1) | copy-start | bytes 10616836
  22.5 26.1 %all-to-all-start = ((bf16[8,64,768]{2,1,0:T(8,128)(2,1)}), bf16[8,64,768]{2,1,0:T(8,128)(2,1)}, u32[]{:S(2)}, u32[]{:S(2)}) async-start(bf16[8,64,768]{2,1,0:T(8,128)(2,1)} %bitcast.144), calls=%async_computation | async-start | bytes 1572864 | tf_op jit(solution)/shard_map/all_to_all | solution.py:779
  63.8 32.1 %copy-start.3 = (bf16[768,2304]{1,0:T(8,128)(2,1)S(1)}, bf16[768,2304]{1,0:T(8,128)(2,1)}, u32[]{:S(2)}) copy-start(bf16[768,2304]{1,0:T(8,128)(2,1)} %wv.1) | copy-start | bytes 10616836
  63.8 43.0 %all-to-all-start.1 = ((bf16[8,128,768]{2,1,0:T(8,128)(2,1)}), bf16[8,128,768]{2,1,0:T(8,128)(2,1)}, u32[]{:S(2)}, u32[]{:S(2)}) async-start(bf16[8,128,768]{2,1,0:T(8,128)(2,1)} %get-tuple-element.50), calls=%async_computation.1 | async-start | bytes 3145728 | tf_op jit(solution)/shard_map/all_to_all | solution.py:779
  70.2 22.1 %collective-permute-start.3 = (bf16[2,1,64,768]{3,2,1,0:T(8,128)(2,1)}, bf16[2,1,64,768]{3,2,1,0:T(8,128)(2,1)}, u32[]{:S(2)}, u32[]{:S(2)}) collective-permute-start(bf16[2,1,64,768]{3,2,1,0:T(8,128)(2,1)} %get-tuple-element.99), channel_id=1, source_target_pairs={{1,0},{2,1},{3,2},{4,3},{5,4},{6,5},{7,6},{9,8},{10,9},{11,10},{12... | collective-permute-start | bytes 589832 | tf_op jit(solution)/shard_map/ppermute | solution.py:775
  71.5 20.8 %collective-permute-start.2 = (bf16[2,1,64,768]{3,2,1,0:T(8,128)(2,1)}, bf16[2,1,64,768]{3,2,1,0:T(8,128)(2,1)}, u32[]{:S(2)}, u32[]{:S(2)}) collective-permute-start(bf16[2,1,64,768]{3,2,1,0:T(8,128)(2,1)} %get-tuple-element.100), channel_id=1, source_target_pairs={{0,1},{1,2},{2,3},{3,4},{4,5},{5,6},{6,7},{8,9},{9,10},{10,11},{11... | collective-permute-start | bytes 589832 | tf_op jit(solution)/shard_map/ppermute | solution.py:770
  76.7 30.1 %collective-permute-start.5 = (bf16[2,1,64,768]{3,2,1,0:T(8,128)(2,1)}, bf16[2,1,64,768]{3,2,1,0:T(8,128)(2,1)}, u32[]{:S(2)}, u32[]{:S(2)}) collective-permute-start(bf16[2,1,64,768]{3,2,1,0:T(8,128)(2,1)} %get-tuple-element.95), channel_id=1, source_target_pairs={{1,0},{2,1},{3,2},{4,3},{5,4},{6,5},{7,6},{9,8},{10,9},{11,10},{12... | collective-permute-start | bytes 589832 | tf_op jit(solution)/shard_map/ppermute | solution.py:775
  78.0 28.8 %collective-permute-start.4 = (bf16[2,1,64,768]{3,2,1,0:T(8,128)(2,1)}, bf16[2,1,64,768]{3,2,1,0:T(8,128)(2,1)}, u32[]{:S(2)}, u32[]{:S(2)}) collective-permute-start(bf16[2,1,64,768]{3,2,1,0:T(8,128)(2,1)} %get-tuple-element.96), channel_id=1, source_target_pairs={{0,1},{1,2},{2,3},{3,4},{4,5},{5,6},{6,7},{8,9},{9,10},{10,11},{11... | collective-permute-start | bytes 589832 | tf_op jit(solution)/shard_map/ppermute | solution.py:770
  113.4 42.4 %copy-start.11 = (f32[4,2,1025]{2,1,0:T(2,128)S(1)}, f32[4,2,1025]{2,1,0:T(2,128)}, u32[]{:S(2)}) copy-start(f32[4,2,1025]{2,1,0:T(2,128)} %all-gather.2) | copy-start | bytes 98404
  155.6 27.0 %collective-permute-start.6 = (bf16[2,2,192,3072]{3,2,1,0:T(8,128)(2,1)}, bf16[2,2,192,3072]{3,2,1,0:T(8,128)(2,1)}, u32[]{:S(2)}, u32[]{:S(2)}) collective-permute-start(bf16[2,2,192,3072]{3,2,1,0:T(8,128)(2,1)} %get-tuple-element.69), channel_id=1, source_target_pairs={{0,8},{8,0},{16,24},{24,16},{1,9},{9,1},{17,25},{25,17},{2,10},{10... | collective-permute-start | bytes 14155784 | tf_op jit(solution)/shard_map/ppermute | solution.py:802
  155.9 74.1 %copy-start.12 = (f32[8,1025]{1,0:T(8,128)}, f32[8,1025]{1,0:T(8,128)S(1)}, u32[]{:S(2)}) copy-start(f32[8,1025]{1,0:T(8,128)S(1)} %reshape.169) | copy-start | bytes 98404
  164.4 38.9 %all-to-all-start.2 = ((bf16[8,64,768]{2,1,0:T(8,128)(2,1)}), bf16[8,64,768]{2,1,0:T(8,128)(2,1)S(1)}, u32[]{:S(2)}, u32[]{:S(2)}) async-start(bf16[8,64,768]{2,1,0:T(8,128)(2,1)} %bitcast.148), calls=%async_computation.2 | async-start | bytes 1572864 | tf_op jit(solution)/shard_map/all_to_all | solution.py:779
  230.0 23.1 %collective-permute-start.7 = (bf16[2,2,2,2,24,1536]{5,4,2,1,3,0:T(8,128)(2,1)}, bf16[2,2,2,2,24,1536]{5,4,2,1,3,0:T(8,128)(2,1)}, u32[]{:S(2)}, u32[]{:S(2)}) collective-permute-start(bf16[2,2,2,2,24,1536]{5,4,2,1,3,0:T(8,128)(2,1)} %bitcast.130), channel_id=1, source_target_pairs={{0,8},{8,0},{16,24},{24,16},{1,9},{9,1},{17,25},{25,17},{2,10},{10... | collective-permute-start | bytes 3538952 | tf_op jit(solution)/shard_map/ppermute | solution.py:802
  235.7 76.9 %all-to-all-start.3 = ((bf16[8,96,768]{2,1,0:T(8,128)(2,1)}), bf16[8,96,768]{2,1,0:T(8,128)(2,1)}, u32[]{:S(2)}, u32[]{:S(2)}) async-start(bf16[8,96,768]{2,1,0:T(8,128)(2,1)} %get-tuple-element.71), calls=%async_computation.3 | async-start | bytes 2359296 | tf_op jit(solution)/shard_map/all_to_all | solution.py:779
  240.2 29.1 %collective-permute-start.15 = (bf16[2,2,2,24,3072]{4,3,0,1,2:T(8,128)(2,1)}, bf16[2,2,2,24,3072]{4,3,0,1,2:T(8,128)(2,1)}, u32[]{:S(2)}, u32[]{:S(2)}) collective-permute-start(bf16[2,2,2,24,3072]{4,3,0,1,2:T(8,128)(2,1)} %bitcast.147), channel_id=1, source_target_pairs={{0,16},{8,24},{16,0},{24,8},{1,17},{9,25},{17,1},{25,9},{2,18},{10... | collective-permute-start | bytes 3538952 | tf_op jit(solution)/shard_map/ppermute | solution.py:802
  251.3 33.4 %collective-permute-start.17 = (bf16[2,2,2,24,3072]{4,3,1,2,0:T(8,128)(2,1)}, bf16[2,2,2,24,3072]{4,3,1,2,0:T(8,128)(2,1)S(1)}, u32[]{:S(2)}, u32[]{:S(2)}) collective-permute-start(bf16[2,2,2,24,3072]{4,3,1,2,0:T(8,128)(2,1)} %bitcast.146), channel_id=1, source_target_pairs={{0,1},{1,0},{2,3},{3,2},{4,5},{5,4},{6,7},{7,6},{8,9},{9,8},{10,11... | collective-permute-start | bytes 3538952 | tf_op jit(solution)/shard_map/ppermute | solution.py:802
  253.0 32.7 %collective-permute-start.10 = (bf16[2,2,2,2,24,1664]{5,4,3,2,1,0:T(8,128)(2,1)S(1)}, bf16[2,2,2,2,24,1664]{5,4,3,2,1,0:T(8,128)(2,1)S(1)}, u32[]{:S(2)}, u32[]{:S(2)}) collective-permute-start(bf16[2,2,2,2,24,1664]{5,4,3,2,1,0:T(8,128)(2,1)S(1)} %dynamic-slice_bitcast_fusion), channel_id=1, source_target_pairs={{0,8},{8,0},{16,24},{24,16},{1,9},{9,1},{17,25},{25,17},{2,10},{10... | collective-permute-start | bytes 3833864 | tf_op jit(solution)/shard_map/ppermute | solution.py:802
  253.1 16.2 %copy-start.6 = (bf16[1,2,2,2,24,3072]{5,4,1,2,3,0:T(8,128)(2,1)S(1)}, bf16[1,2,2,2,24,3072]{5,4,1,2,3,0:T(8,128)(2,1)}, u32[]{:S(2)}) copy-start(bf16[1,2,2,2,24,3072]{5,4,1,2,3,0:T(8,128)(2,1)} %copy.93) | copy-start | bytes 3538948
  254.9 29.8 %copy-start.5 = (bf16[2,2,2,1,24,3072]{5,4,1,2,0,3:T(8,128)(2,1)S(1)}, bf16[2,2,2,1,24,3072]{5,4,1,2,0,3:T(8,128)(2,1)}, u32[]{:S(2)}) copy-start(bf16[2,2,2,1,24,3072]{5,4,1,2,0,3:T(8,128)(2,1)} %copy.92) | copy-start | bytes 3538948
  254.9 31.3 %collective-permute-start.8 = (bf16[2,2,2,24,1536]{4,3,1,0,2:T(8,128)(2,1)S(1)}, bf16[2,2,2,24,1536]{4,3,1,0,2:T(8,128)(2,1)S(1)}, u32[]{:S(2)}, u32[]{:S(2)}) collective-permute-start(bf16[2,2,2,24,1536]{4,3,1,0,2:T(8,128)(2,1)S(1)} %dynamic-slice_bitcast_fusion.4), channel_id=1, source_target_pairs={{0,16},{8,24},{16,0},{24,8},{1,17},{9,25},{17,1},{25,9},{2,18},{10... | collective-permute-start | bytes 1769480 | tf_op jit(solution)/shard_map/ppermute | solution.py:802
  271.1 26.3 %collective-permute-start.16 = (bf16[2,2,24,3072]{3,2,0,1:T(8,128)(2,1)S(1)}, bf16[2,2,24,3072]{3,2,0,1:T(8,128)(2,1)S(1)}, u32[]{:S(2)}, u32[]{:S(2)}) collective-permute-start(bf16[2,2,24,3072]{3,2,0,1:T(8,128)(2,1)S(1)} %dynamic-slice_bitcast_fusion.3), channel_id=1, source_target_pairs={{0,1},{1,0},{2,3},{3,2},{4,5},{5,4},{6,7},{7,6},{8,9},{9,8},{10,11... | collective-permute-start | bytes 1769480 | tf_op jit(solution)/shard_map/ppermute | solution.py:802
  285.2 14.0 %collective-permute-start.18 = (bf16[2,2,24,3072]{3,2,0,1:T(8,128)(2,1)S(1)}, bf16[2,2,24,3072]{3,2,0,1:T(8,128)(2,1)S(1)}, u32[]{:S(2)}, u32[]{:S(2)}) collective-permute-start(bf16[2,2,24,3072]{3,2,0,1:T(8,128)(2,1)S(1)} %dynamic-slice_bitcast_fusion.2), channel_id=1, source_target_pairs={{0,16},{8,24},{16,0},{24,8},{1,17},{9,25},{17,1},{25,9},{2,18},{10... | collective-permute-start | bytes 1769480 | tf_op jit(solution)/shard_map/ppermute | solution.py:802
  286.1 24.9 %collective-permute-start.11 = (bf16[2,2,2,24,1664]{4,3,2,1,0:T(8,128)(2,1)S(1)}, bf16[2,2,2,24,1664]{4,3,2,1,0:T(8,128)(2,1)S(1)}, u32[]{:S(2)}, u32[]{:S(2)}) collective-permute-start(bf16[2,2,2,24,1664]{4,3,2,1,0:T(8,128)(2,1)S(1)} %dynamic-slice_bitcast_fusion.1), channel_id=1, source_target_pairs={{0,1},{1,0},{2,3},{3,2},{4,5},{5,4},{6,7},{7,6},{8,9},{9,8},{10,11... | collective-permute-start | bytes 1916936 | tf_op jit(solution)/shard_map/ppermute | solution.py:802
  287.1 42.2 %collective-permute-start.9 = (bf16[2,2,24,1536]{3,2,1,0:T(8,128)(2,1)}, bf16[2,2,24,1536]{3,2,1,0:T(8,128)(2,1)}, u32[]{:S(2)}, u32[]{:S(2)}) collective-permute-start(bf16[2,2,24,1536]{3,2,1,0:T(8,128)(2,1)} %dynamic-slice_bitcast_fusion.7), channel_id=1, source_target_pairs={{0,1},{1,0},{2,3},{3,2},{4,5},{5,4},{6,7},{7,6},{8,9},{9,8},{10,11... | collective-permute-start | bytes 884744 | tf_op jit(solution)/shard_map/ppermute | solution.py:802
  300.2 33.3 %collective-permute-start.19 = (bf16[2,2,24,3072]{3,2,0,1:T(8,128)(2,1)}, bf16[2,2,24,3072]{3,2,0,1:T(8,128)(2,1)S(1)}, u32[]{:S(2)}, u32[]{:S(2)}) collective-permute-start(bf16[2,2,24,3072]{3,2,0,1:T(8,128)(2,1)} %fusion.17), channel_id=1, source_target_pairs={{0,2},{1,3},{2,0},{3,1},{4,6},{5,7},{6,4},{7,5},{8,10},{9,11},{10,... | collective-permute-start | bytes 1769480 | tf_op jit(solution)/shard_map/ppermute | solution.py:802
  312.0 18.4 %collective-permute-start.12 = (bf16[2,2,24,1664]{3,2,1,0:T(8,128)(2,1)}, bf16[2,2,24,1664]{3,2,1,0:T(8,128)(2,1)}, u32[]{:S(2)}, u32[]{:S(2)}) collective-permute-start(bf16[2,2,24,1664]{3,2,1,0:T(8,128)(2,1)} %dynamic-slice_bitcast_fusion.5), channel_id=1, source_target_pairs={{0,16},{8,24},{16,0},{24,8},{1,17},{9,25},{17,1},{25,9},{2,18},{10... | collective-permute-start | bytes 958472 | tf_op jit(solution)/shard_map/ppermute | solution.py:802
  324.0 26.6 %all-to-all-start.4 = ((f32[8,80,128]{2,1,0:T(8,128)}), f32[8,80,128]{2,1,0:T(8,128)S(1)}, u32[]{:S(2)}, u32[]{:S(2)}) async-start(f32[8,80,128]{2,1,0:T(8,128)} %bitcast.133), calls=%async_computation.4 | async-start | bytes 655360 | tf_op jit(solution)/shard_map/all_to_all | solution.py:779
  331.5 18.4 %collective-permute-start.13 = (bf16[2,24,3200]{2,1,0:T(8,128)(2,1)S(1)}, bf16[2,24,3200]{2,1,0:T(8,128)(2,1)S(1)}, u32[]{:S(2)}, u32[]{:S(2)}) collective-permute-start(bf16[2,24,3200]{2,1,0:T(8,128)(2,1)S(1)} %fusion.22), channel_id=1, source_target_pairs={{0,2},{1,3},{2,0},{3,1},{4,6},{5,7},{6,4},{7,5},{8,10},{9,11},{10,... | collective-permute-start | bytes 921608 | tf_op jit(solution)/shard_map/ppermute | solution.py:802
  333.7 32.7 %collective-permute-start.20 = (bf16[2,24,3072]{2,1,0:T(8,128)(2,1)S(1)}, bf16[2,24,3072]{2,1,0:T(8,128)(2,1)}, u32[]{:S(2)}, u32[]{:S(2)}) collective-permute-start(bf16[2,24,3072]{2,1,0:T(8,128)(2,1)S(1)} %dynamic-slice_bitcast_fusion.6), channel_id=1, source_target_pairs={{0,4},{1,5},{2,6},{3,7},{4,0},{5,1},{6,2},{7,3},{8,12},{9,13},{10,... | collective-permute-start | bytes 884744 | tf_op jit(solution)/shard_map/ppermute | solution.py:802
  350.6 17.7 %collective-permute-start.14 = (bf16[24,3200]{1,0:T(8,128)(2,1)}, bf16[24,3200]{1,0:T(8,128)(2,1)S(1)}, u32[]{:S(2)}, u32[]{:S(2)}) collective-permute-start(bf16[24,3200]{1,0:T(8,128)(2,1)} %dynamic-slice_bitcast_fusion.8), channel_id=1, source_target_pairs={{0,4},{1,5},{2,6},{3,7},{4,0},{5,1},{6,2},{7,3},{8,12},{9,13},{10,... | collective-permute-start | bytes 460808 | tf_op jit(solution)/shard_map/ppermute | solution.py:802
  (15 other events, 92.7 us)

commit v3 on v2

--- a/solution.py
+++ b/solution.py
@@ -150,6 +150,7 @@
             ],
         ),
         compiler_params=pltpu.CompilerParams(vmem_limit_bytes=VMEM_LIMIT),
+        cost_estimate=pl.CostEstimate(flops=6_000_000_000, bytes_accessed=4_000_000, transcendentals=0),
         name="enter",
     )(meta, tokens, top, bot, pieces, kern)
 
@@ -196,6 +197,7 @@
             scratch_shapes=[pltpu.VMEM((rows_here + 2, LANE_PARTS, cols, 128), F32)],
         ),
         compiler_params=pltpu.CompilerParams(vmem_limit_bytes=VMEM_LIMIT),
+        cost_estimate=pl.CostEstimate(flops=4_000_000_000, bytes_accessed=4_000_000, transcendentals=0),
         name="prepare_cot",
     )(meta, cotangent, top, bot, pieces)
 
@@ -280,6 +282,7 @@
             ],
         ),
         compiler_params=pltpu.CompilerParams(vmem_limit_bytes=VMEM_LIMIT),
+        cost_estimate=pl.CostEstimate(flops=7_000_000_000, bytes_accessed=4_000_000, transcendentals=0),
         name="second",
     )(meta, attended, tokens, tops[1], tops[0], bots[0], bots[1], pieces, proj)
 
@@ -447,6 +450,7 @@
             + [pltpu.VMEM((D, FF_BLOCK), F32), pltpu.VMEM((D, FF_BLOCK), F32)],
         ),
         compiler_params=pltpu.CompilerParams(vmem_limit_bytes=VMEM_LIMIT),
+        cost_estimate=pl.CostEstimate(flops=48_000_000_000, bytes_accessed=4_000_000, transcendentals=0),
         name="ffn",
     )(core, e2, e2t, ge, get, up, down, kern)
 
@@ -525,6 +529,7 @@
             ],
         ),
         compiler_params=pltpu.CompilerParams(vmem_limit_bytes=VMEM_LIMIT),
+        cost_estimate=pl.CostEstimate(flops=10_000_000_000, bytes_accessed=4_000_000, transcendentals=0),
         name="middle",
     )(meta, exp, ge2, after, branch, cot, pieces, proj)
 
@@ -608,6 +613,7 @@
             ],
         ),
         compiler_params=pltpu.CompilerParams(vmem_limit_bytes=VMEM_LIMIT),
+        cost_estimate=pl.CostEstimate(flops=10_000_000_000, bytes_accessed=4_000_000, transcendentals=0),
         name="leave",
     )(meta, gm, tokens, top, bot, after_grad, pieces, kern)
 
@@ -671,11 +677,12 @@
             pl.BlockSpec((1, 2, tokens), lambda p: (p, 0, 0)),
         ),
         compiler_params=pltpu.CompilerParams(vmem_limit_bytes=VMEM_LIMIT),
+        cost_estimate=pl.CostEstimate(flops=16_000_000_000, bytes_accessed=4_000_000, transcendentals=0),
         name="attend",
     )(mixed, weight, weight, weight_t, bias)
 
 
-def attend_back_kernel(offset, query, key, value, key_t, bias, lse, gatt, wq, wk, wv, dq_out, dk_out, dv_out, gm_out, acc):
+def attend_back_kernel(offset, query, key, value, key_t, bias, lse, gatt, wq, wk, wv, mixed_t, send_out, keep_out, gm_out, acc, part):
     tokens = query.shape[0]
     strips, window, _ = gm_out.shape
     step = tokens // strips
@@ -702,9 +709,14 @@
     dq = (jnp.concatenate(parts, axis=0).T * FACTOR).astype(BF16)
     dk = (dk * FACTOR).astype(BF16)
     dv = dv.astype(BF16)
-    dq_out[...] = dq
-    dk_out[...] = dk
-    dv_out[...] = dv
+    size = D // 4
+    for k, grad in enumerate((dq, dk, dv)):
+        part[k] = mm(mixed_t[...], grad)
+        for y in range(2):
+            mine = pl.multiple_of((2 * y + offset[1]) * size, 8)
+            other = pl.multiple_of((2 * y + 1 - offset[1]) * size, 8)
+            keep_out[k, y] = part[k, pl.ds(mine, size), :].astype(BF16)
+            send_out[k, y] = part[k, pl.ds(other, size), :].astype(BF16)
     total = mm(dq, wq[...], NT) + mm(dk, wk[...], NT) + mm(dv, wv[...], NT)
 
     @pl.when(p == 0)
@@ -724,17 +736,18 @@
             gm_out[s] = acc[pl.ds(start, window), :].astype(BF16)
 
 
-def attend_back(offset, triple, key_t, bias, lse, gatt, weight, strips, window):
+def attend_back(offset, triple, key_t, bias, lse, gatt, weight, mixed_t, strips, window):
     tokens = triple.shape[0]
     margin = window - tokens // strips
     part = lambda k: pl.BlockSpec((tokens, PAIR), lambda p, o: (0, k * PAIRS + p))
     slab = lambda k: pl.BlockSpec((D, PAIR), lambda p, o: (0, k * PAIRS + p))
+    parts = jax.ShapeDtypeStruct((3, 2, D // 4, D), BF16)
+    parts_spec = pl.BlockSpec((3, 2, D // 4, PAIR), lambda p, o: (0, 0, 0, p))
     return pl.pallas_call(
         attend_back_kernel,
         out_shape=(
-            jax.ShapeDtypeStruct((tokens, D), BF16),
-            jax.ShapeDtypeStruct((tokens, D), BF16),
-            jax.ShapeDtypeStruct((tokens, D), BF16),
+            parts,
+            parts,
             jax.ShapeDtypeStruct((strips, window, D), BF16),
         ),
         grid_spec=pltpu.PrefetchScalarGridSpec(
@@ -751,18 +764,22 @@
                 slab(0),
                 slab(1),
                 slab(2),
+                pl.BlockSpec((D, tokens), lambda p, o: (0, 0)),
             ],
             out_specs=(
-                part(0),
-                part(0),
-                part(0),
+                parts_spec,
+                parts_spec,
                 pl.BlockSpec((strips, window, D), lambda p, o: (0, 0, 0)),
             ),
-            scratch_shapes=[pltpu.VMEM((tokens + 2 * margin, D), F32)],
+            scratch_shapes=[
+                pltpu.VMEM((tokens + 2 * margin, D), F32),
+                pltpu.VMEM((3, D, PAIR), F32),
+            ],
         ),
         compiler_params=pltpu.CompilerParams(vmem_limit_bytes=VMEM_LIMIT),
+        cost_estimate=pl.CostEstimate(flops=23_000_000_000, bytes_accessed=4_000_000, transcendentals=0),
         name="attend_back",
-    )(offset, triple, triple, triple, key_t, bias, lse, gatt, weight, weight, weight)
+    )(offset, triple, triple, triple, key_t, bias, lse, gatt, weight, weight, weight, mixed_t)
 
 
 def from_before(values, axis):
@@ -823,20 +840,24 @@
 
 def sum_and_gather(common, sliced):
     seq_count, batch_count = lax.axis_size("seq"), lax.axis_size("batch")
-    rows, cols = sliced.shape
-    mine = cols // (seq_count * batch_count)
-    parts = sliced.reshape(rows, batch_count, seq_count, mine).transpose(2, 1, 0, 3).reshape(seq_count, -1)
+    batch_place = lax.axis_index("batch")
     flat = common.reshape(1, -1)
-    whole = jnp.concatenate([jnp.broadcast_to(flat, (seq_count, flat.shape[1])), parts], axis=1)
-    pad = -whole.shape[1] % 1024
-    whole = jnp.pad(whole, ((0, 0), (0, pad))).reshape(seq_count, -1, 128)
+    pieces = [jnp.broadcast_to(flat, (seq_count, flat.shape[1]))]
+    for values in sliced:
+        cut = values.reshape(values.shape[0], batch_count, seq_count, -1).transpose(2, 1, 0, 3)
+        pieces.append(cut.reshape(seq_count, -1))
+    whole = jnp.concatenate(pieces, axis=1)
+    whole = jnp.pad(whole, ((0, 0), (0, -whole.shape[1] % 1024))).reshape(seq_count, -1, 128)
     summed = jnp.sum(swap(whole), axis=0)
     gathered = lax.all_gather(summed, "batch", axis=0).reshape(batch_count, -1)
     common_all = gathered[:, : flat.shape[1]].reshape((batch_count,) + common.shape)
-    parts_all = jnp.sum(gathered[:, flat.shape[1] : flat.shape[1] + parts.shape[1]], axis=0)
-    own = lax.dynamic_index_in_dim(
-        parts_all.reshape(batch_count, rows, mine), lax.axis_index("batch"), 0, keepdims=False
-    )
+    at = flat.shape[1]
+    own = []
+    for values, piece in zip(sliced, pieces[1:]):
+        part = jnp.sum(gathered[:, at : at + piece.shape[1]], axis=0)
+        part = part.reshape(batch_count, values.shape[0], -1)
+        own.append(lax.dynamic_index_in_dim(part, batch_place, 0, keepdims=False))
+        at += piece.shape[1]
     return common_all, own
 
 
@@ -900,10 +921,6 @@
     first, last = tokens[:, :1], tokens[:, rows_here - 1 :]
     top = from_before(last, "seq")
     bot = from_after(first, "seq")
-    top_two = from_before(tokens[:, rows_here - 2 : rows_here - 1], "seq")
-    bot_two = from_after(tokens[:, 1:2], "seq")
-    cot_top = from_before(cotangent[:, rows_here - 1 :], "seq")
-    cot_bot = from_after(cotangent[:, :1], "seq")
 
     half_freq = time_weight.shape[0] // 2
     frequency = jnp.exp(-math.log(10000.0) * jnp.arange(half_freq, dtype=F32) / half_freq)
@@ -927,6 +944,13 @@
     sent = jnp.broadcast_to(sent, (blocks, share, per_group, D)).reshape(seq_count, per_group, D)
     grouped = swap(sent).reshape(group_tokens, D)
 
+    weight_t = qkv_weight.T
+    low_rows = jnp.stack([tokens[:, rows_here - 2 : rows_here - 1], cotangent[:, rows_here - 1 :]])
+    high_rows = jnp.stack([tokens[:, 1:2], cotangent[:, :1]])
+    low_rows, high_rows, grouped = lax.optimization_barrier((low_rows, high_rows, grouped))
+    top_two, cot_top = from_before(low_rows, "seq")
+    bot_two, cot_bot = from_after(high_rows, "seq")
+
     my_block = seq_place // share
     my_latent = my_block // 4
     my_a = (my_block // 2) % 2
@@ -942,8 +966,10 @@
     window = per_group + 2 * margin
     if share == 1:
         bias = jnp.broadcast_to(jnp.where(key_ok, 0.0, -1e30)[:, None], (group_tokens, 128))
-        weight_t = qkv_weight.T
         windows, lse = attend(grouped, qkv_weight, weight_t, bias, seq_count, window)
+        windows, top_two, bot_two, cot_top, cot_bot = lax.optimization_barrier(
+            (windows, top_two, bot_two, cot_top, cot_bot)
+        )
         attended = swap(windows)
     else:
         heads = HEADS // share
@@ -968,8 +994,9 @@
     if share == 1:
         triple = mm(grouped, qkv_weight).astype(BF16)
         key_t = mm(weight_t[D : 2 * D], grouped, NT).astype(BF16)
-        attended, ge, triple, key_t, conditions = lax.optimization_barrier(
-            (attended, ge, triple, key_t, conditions)
+        grouped_t = grouped.T
+        attended, ge, triple, key_t, grouped_t, conditions = lax.optimization_barrier(
+            (attended, ge, triple, key_t, grouped_t, conditions)
         )
     e2, e2t, after_attn, branch = second(
         meta, attended, tokens, (top, top_two), (bot, bot_two), pieces, proj_weight
@@ -984,16 +1011,10 @@
         meta, expanded, grad_e2, after_attn, branch, cot_split, pieces, proj_weight, rows_here, cols
     )
 
-    att_own = attended[:, margin : margin + per_group].reshape(blocks * per_group, D)
+    att_own = after(attended, grad_attended)[:, margin : margin + per_group]
+    att_own = att_own.reshape(blocks * per_group, D)
     flat_branch = grad_branch.reshape(blocks * per_group, D)
-    proj_grad = mm(att_own, flat_branch, (((0,), (0,)), ((), ()))).astype(BF16)
     hidden = conv_ffn.shape[1]
-    own_hidden = hidden // devices
-    side = conv_ffn_part.reshape(9, devices, own_hidden).transpose(1, 0, 2).reshape(devices, -1)
-    side_rows = D // devices
-    side_cols = -(-9 * own_hidden // (128 * side_rows)) * 128
-    side = jnp.pad(side, ((0, 0), (0, side_rows * side_cols - 9 * own_hidden)))
-    side = side.reshape(D, side_cols).astype(BF16)
     tall = per_group + margin
     if share == 1:
         gatt = swap(grad_attended.reshape(seq_count, per_group, D)).reshape(group_tokens, D)
@@ -1002,16 +1023,20 @@
             sums = add(keep_c, got_c).astype(BF16).reshape(2, 2, 2, 2, 2, D // devices, hidden)
             send_a, keep_a, dims_a = split(sums[0], "yhlx", "y")
             send_b, keep_b, dims_b = split(sums[1], "yhlx", "x")
-            gatt, send_a, send_b = lax.optimization_barrier((gatt, send_a, send_b))
+            late_branch = after(flat_branch, got_c)
+            proj_grad = mm(att_own, late_branch, (((0,), (0,)), ((), ()))).astype(BF16)
+            send_p, keep_p, _ = split(blocks_of(proj_grad), ORDER, "c")
+            got_p = hop(send_p, "c")
+            gatt, send_a, send_b, send_p = lax.optimization_barrier((gatt, send_a, send_b, send_p))
             got_a, got_b = hop(send_a, "y"), hop(send_b, "x")
-        offset = jnp.reshape(margin * (1 - my_a), (1,)).astype(jnp.int32)
-        dq, dk, dv, gm_windows = attend_back(
-            offset, triple, key_t, bias, lse, gatt, qkv_weight, seq_count, tall
+        offset = jnp.stack([margin * (1 - my_a), batch_place % 2]).astype(jnp.int32)
+        send_r, keep_r, gm_windows = attend_back(
+            offset, triple, key_t, bias, lse, gatt, qkv_weight, grouped_t, seq_count, tall
         )
         gm = swap(gm_windows)
-        turned = (((0,), (0,)), ((), ()))
-        rest_one = mm(grouped, jnp.concatenate([dq, dk], axis=1), turned).astype(BF16)
-        rest_two = jnp.concatenate([mm(grouped, dv, turned).astype(BF16), proj_grad, side], axis=1)
+        if halving:
+            gm_windows, got_a, got_b = lax.optimization_barrier((gm_windows, got_a, got_b))
+        gm = swap(gm_windows)
     else:
         sent = grad_attended.reshape(blocks, per_group, share, wide).transpose(0, 2, 1, 3)
         gatt = swap(sent.reshape(seq_count, per_group, wide)).reshape(group_tokens, wide)
@@ -1028,19 +1053,20 @@
         qkv_grad = lax.dynamic_update_index_in_dim(
             spread, own_grad.reshape(D, 3, wide), chunk, 2
         ).reshape(D, 3 * D)
-        rest_one = qkv_grad[:, : 2 * D]
-        rest_two = jnp.concatenate([qkv_grad[:, 2 * D :], proj_grad, side], axis=1)
+        proj_grad = mm(att_own, flat_branch, (((0,), (0,)), ((), ()))).astype(BF16)
+        rest = jnp.concatenate([qkv_grad, proj_grad], axis=1)
 
     if halving:
-        keep_a, keep_b = after(keep_a, gm_windows), after(keep_b, gm_windows)
+        got_r = hop(send_r, "c")
+        keep_a, keep_b = after(keep_a, keep_r), after(keep_b, keep_r)
         send_a, keep_a, dims_a = split(add(keep_a, got_a).astype(BF16), dims_a, "x")
         send_b, keep_b, dims_b = split(add(keep_b, got_b).astype(BF16), dims_b, "y")
+        sums = add(keep_r, got_r).astype(BF16).reshape(3, 2, 2, 2, 2, D // devices, D)
+        sums_p = add(keep_p, got_p).astype(BF16)
+        send_one, keep_one, dims_one = split(sums[:2], "yhlx", "y")
+        send_two, keep_two, dims_two = split(jnp.stack([sums[2], sums_p]), "yhlx", "x")
+        gm = after(gm, send_a, send_b)
         got_a, got_b = hop(send_a, "x"), hop(send_b, "y")
-        send_one, keep_one, dims_one = split(blocks_of(rest_one), ORDER, "c")
-        send_two, keep_two, dims_two = split(blocks_of(rest_two), ORDER, "c")
-        got_one, got_two = hop(send_one, "c"), hop(send_two, "c")
-        send_one, keep_one, dims_one = split(add(keep_one, got_one).astype(BF16), dims_one, "y")
-        send_two, keep_two, dims_two = split(add(keep_two, got_two).astype(BF16), dims_two, "x")
         got_one, got_two = hop(send_one, "y"), hop(send_two, "x")
     total = batch_count * latents
 
@@ -1065,27 +1091,35 @@
         meta, gm, tokens, top, bot, grad_after, pieces, kern_attn
     )
 
-    all_sums, conv_attn_grad = sum_and_gather(
-        jnp.concatenate([end_sums, mid_sums], axis=1), jnp.sum(conv_attn_part, axis=0)
+    all_sums, (conv_attn_grad, conv_ffn_grad) = sum_and_gather(
+        jnp.concatenate([end_sums, mid_sums], axis=1),
+        (jnp.sum(conv_attn_part, axis=0), conv_ffn_part),
     )
     if halving:
+        keep_a, keep_b, keep_one, keep_two, end_sums = lax.optimization_barrier(
+            (keep_a, keep_b, keep_one, keep_two, end_sums)
+        )
         pair = jnp.stack([add(keep_a, got_a), add(keep_b, got_b)])
         pair = reduce_rest(pair, dims_a, "lh")
         down_rows, up_rows = pair[0], pair[1]
         send_one, keep_one, dims_one = split(add(keep_one, got_one).astype(BF16), dims_one, "x")
         send_two, keep_two, dims_two = split(add(keep_two, got_two).astype(BF16), dims_two, "y")
         got_one, got_two = hop(send_one, "x"), hop(send_two, "y")
-        rest_rows = jnp.concatenate([add(keep_one, got_one), add(keep_two, got_two)], axis=-1)
+        rest_rows = jnp.concatenate([add(keep_one, got_one), add(keep_two, got_two)])
         rest_rows = reduce_rest(rest_rows, dims_one, "lh")
     else:
         whole = jnp.stack([keep_c, send_c])
         whole = jnp.where(core[0] == 0, whole, whole[::-1]).transpose(1, 2, 0, 3, 4)
         whole = whole.reshape(2, D, hidden)
         down_rows, up_rows = scatter_rows(whole[0]), scatter_rows(whole[1])
-        rest_rows = scatter_rows(jnp.concatenate([rest_one, rest_two], axis=1))
-    qkv_rows = rest_rows[:, : 3 * D]
-    proj_rows = rest_rows[:, 3 * D : 4 * D]
-    conv_ffn_grad = rest_rows[:, 4 * D :].reshape(-1)[: 9 * own_hidden].reshape(9, own_hidden)
+        if share == 1:
+            rest = jnp.stack([keep_r, send_r])
+            rest = jnp.where(core[0] == 0, rest, rest[::-1]).transpose(2, 0, 3, 1, 4).reshape(D, -1)
+            proj_grad = mm(att_own, flat_branch, (((0,), (0,)), ((), ()))).astype(BF16)
+            rest = jnp.concatenate([rest, proj_grad], axis=1)
+        rest_rows = scatter_rows(rest).reshape(own_cols, 4, D).transpose(1, 0, 2)
+    qkv_rows = jnp.concatenate([rest_rows[0], rest_rows[1], rest_rows[2]], axis=1)
+    proj_rows = rest_rows[3]
 
     grad_pieces = all_sums.reshape(total, 6 * D)
     grad_silu = back_through(grad_pieces)

time: 372 us -> 334 us (0.90)
  starting transfers between devices: 75.2 us -> 51.9 us
  waiting for transfers between devices: 85.9 us -> 77.2 us
  matrix products: 27.7 us -> 19.9 us
  local copies, waits for them, and re-layouts: 36 us -> 30.7 us
  Pallas kernels: 109 us -> 114 us
    ppermute x15, waiting for transfers between devices: 57.3 us -> 22.4 us  [hop(): return lax.ppermute(values, axis, [(i, i ^ mask) for i in range(count)])]
    all_to_all x5, waiting for transfers between devices: 28.2 us -> 54.5 us  [swap(): return lax.all_to_all(values, 'seq', 0, 0, tiled=False)]
    all_to_all x5, starting transfers between devices: 38.4 us -> 25.3 us  [swap(): return lax.all_to_all(values, 'seq', 0, 0, tiled=False)]
    ppermute x3 -> x2, starting transfers between devices: 16.8 us -> 8.1 us  [from_before(): return lax.ppermute(values, axis, [(i, i + 1) for i in range(count - 1)])]
    dot_general x9 -> x7, matrix products: 24.6 us -> 16.9 us  [mm(): return lax.dot_general(left, right, dims, preferred_element_type=F32)]
    slice x8 -> x6, local copies, waits for them, and re-layouts: 8.12 us -> 1.49 us  [the longest x1 1.4 us: shards(): first, last = (tokens[:, :1], tokens[:, rows_here - 1:])]
    squeeze x1 -> x7, local copies, waits for them, and re-layouts: 0.6 us -> 6.21 us  [the longest x4 4.36 us: split(): keep = lax.dynamic_index_in_dim(values, mine, at, keepdims=False)]
    unnamed x45 -> x55, local copies, waits for them, and re-layouts: 5.37 us -> 10.9 us
  transfers between devices with their start and end apart: 26 -> 24, of which waited for: 10 -> 10; matrix products, arithmetic and copies ran while one was open for 20% -> 20% of each run, Pallas kernels for 6% -> 18%
where the time goes in v3:
time: 334 us; the launch traced here: 331 us
  Pallas kernels  114 us (34%)
  waiting for transfers between devices  77.2 us (23%)
  starting transfers between devices  51.9 us (16%)
  local copies, waits for them, and re-layouts  30.7 us (9%)
  other arithmetic  24.3 us (7%)
  matrix products  19.9 us (6%)
  blocking collectives  11.1 us (3%)
    all_to_all x5, waiting for transfers between devices, swap(): return lax.all_to_all(values, 'seq', 0, 0, tiled=False)  54.5 us
    pallas_call x1, Pallas kernels, ffn(): pl.pallas_call(ffn_kernel, out_shape=(jax.ShapeDtypeStruct((latents, own,...  42.3 us
    all_to_all x5, starting transfers between devices, swap(): return lax.all_to_all(values, 'seq', 0, 0, tiled=False)  25.3 us
    pallas_call x1, Pallas kernels, attend_back(): pl.pallas_call(attend_back_kernel, out_shape=(parts, parts, jax.ShapeDtyp...  25.2 us
    ppermute x15, waiting for transfers between devices, hop(): return lax.ppermute(values, axis, [(i, i ^ mask) for i in range(count)])  22.4 us
    dot_general x7, matrix products, mm(): return lax.dot_general(left, right, dims, preferred_element_type=F32)  16.9 us
    ppermute x15, starting transfers between devices, hop(): return lax.ppermute(values, axis, [(i, i ^ mask) for i in range(count)])  16 us
    pallas_call x1, Pallas kernels, attend(): pl.pallas_call(attend_kernel, out_shape=(jax.ShapeDtypeStruct((strips, wi...  14.4 us
  transfers between devices with their start and end apart: 24, of which 10 were waited for; matrix products, arithmetic and copies ran while one was open for 20% of the time, Pallas kernels for 18%

profile of v3, /device:TPU:0, one launch (start us, length us, event | category | flops | bytes accessed | tf_op | source)
XLA Modules:
  0.0 330.6 jit_solution(2568666722018276217)
XLA Ops:
  2.1 4.9 %collective-permute-start = (bf16[2,1,64,768]{3,2,1,0:T(8,128)(2,1)S(1)}, bf16[2,1,64,768]{3,2,1,0:T(8,128)(2,1)S(1)}, u32[]{:S(2)}, u32[]{:S(2)}) collective-permute-start(bf16[2,1,64,768]{3,2,1,0:T(8,128)(2,1)S(1)} %get-tuple-element.139), channel_id=1, source_target_pairs={{0,1},{1,2},{2,3},{3,4},{4,5},{5,6},{6,7},{8,9},{9,10},{10,11},{11... | collective-permute-start | bytes 589832 | tf_op jit(solution)/shard_map/ppermute | solution.py:787
  9.0 4.0 %convolution_add_fusion = f32[2,4608]{1,0:T(2,128)S(1)} fusion(bf16[768,4608]{1,0:T(8,128)(2,1)} %param.24, f32[4608]{0:T(1024)S(1)} %copy-done.17, f32[2,768]{1,0:T(2,128)S(1)} %convolution_add_fusion.1), kind=kOutput, calls=%fused_computation.1 | convolution fusion | flops 14172672 | bytes 7139328 | tf_op jit(solution)/shard_map/dot_general | solution.py:29
  16.3 5.1 %enter.1 = bf16[2,4,64,768]{3,2,1,0:T(8,128)(2,1)} custom-call(s32[5]{0:T(128)} %pad_add_fusion.meta, bf16[2,4,64,768]{3,2,1,0:T(8,128)(2,1)} %tok.5, bf16[2,1,64,768]{3,2,1,0:T(8,128)(2,1)} %copy-done.22, bf16[2,1,64,768]{3,2,1,0:T(8,128)(2,1)} %copy-done.23, f32[2,6,768]{2,1,0:T(8,128)} %reshape.142.pieces, f32[9,768]{1,0:T(8,128)} %convert_element_type.183.kern), custom_call_target="tpu_custom_call" | custom-call | flops 6000000000 | bytes 4000000 | tf_op jit(solution)/shard_map/enter/pallas_call | solution.py:133
  21.3 7.0 %all-to-all-start = ((bf16[8,64,768]{2,1,0:T(8,128)(2,1)}), bf16[8,64,768]{2,1,0:T(8,128)(2,1)S(1)}, u32[]{:S(2)}, u32[]{:S(2)}) async-start(bf16[8,64,768]{2,1,0:T(8,128)(2,1)} %bitcast.183), calls=%async_computation | async-start | bytes 1572864 | tf_op jit(solution)/shard_map/all_to_all | solution.py:796
  29.5 5.8 %copy.106 = bf16[768,2304]{0,1:T(8,128)(2,1)} copy(bf16[768,2304]{1,0:T(8,128)(2,1)} %wv.1) | data formatting | bytes 7077888 | tf_op args[11]
  36.7 11.5 %all-to-all-done = bf16[8,64,768]{2,1,0:T(8,128)(2,1)S(1)} async-done(((bf16[8,64,768]{2,1,0:T(8,128)(2,1)}), bf16[8,64,768]{2,1,0:T(8,128)(2,1)S(1)}, u32[]{:S(2)}, u32[]{:S(2)}) %all-to-all-start) | async-done | bytes 786464 | tf_op jit(solution)/shard_map/all_to_all | solution.py:796
  48.2 3.2 collective-permute-start.2
  53.6 14.4 %attend.1 = (bf16[8,128,768]{2,1,0:T(8,128)(2,1)}, f32[6,2,512]{2,1,0:T(2,128)}) custom-call(bf16[512,768]{1,0:T(8,128)(2,1)} %bitcast.173, bf16[768,2304]{1,0:T(8,128)(2,1)} %wv.1, bf16[768,2304]{1,0:T(8,128)(2,1)} %wv.1, bf16[2304,768]{1,0:T(8,128)(2,1)} %bitcast.170, f32[512,128]{1,0:T(8,128)} %broadcast_in_dim.18.bias), custom_call_target="tpu_custom_call" | custom-call | flops 16000000000 | bytes 4000000 | tf_op jit(solution)/shard_map/attend/pallas_call | solution.py:661
  69.6 4.9 %all-to-all-start.1 = ((bf16[8,128,768]{2,1,0:T(8,128)(2,1)}), bf16[8,128,768]{2,1,0:T(8,128)(2,1)S(1)}, u32[]{:S(2)}, u32[]{:S(2)}) async-start(bf16[8,128,768]{2,1,0:T(8,128)(2,1)} %get-tuple-element.72), calls=%async_computation.1 | async-start | bytes 3145728 | tf_op jit(solution)/shard_map/all_to_all | solution.py:796
  74.7 5.4 %all-gather.2 = f32[4,2,1025]{2,1,0:T(2,128)S(1)} all-gather(f32[1,2,1025]{2,1,0:T(2,128)S(1)} %maximum_bitcast_fusion), channel_id=2, replica_groups=mesh['batch'=4,'seq'=8] {'batch'}, dimensions={0}, use_global_device_ids=true | all-gather | bytes 41000 | tf_op jit(solution)/shard_map/all_gather | solution.py:989
  81.2 3.2 fusion.key_t
  84.4 3.4 %convolution_convert_fusion.query.key.value = bf16[512,2304]{1,0:T(8,128)(2,1)} fusion(bf16[512,768]{1,0:T(8,128)(2,1)S(1)} %bitcast.176, bf16[768,2304]{1,0:T(8,128)(2,1)S(1)} %copy-done.3), kind=kOutput, calls=%fused_computation.2 | convolution fusion | flops 1813118976 | bytes 6684672 | tf_op jit(solution)/shard_map/dot_general | solution.py:29
  87.8 3.6 %prepare_cot.1 = (bf16[2,384,768]{2,1,0:T(8,128)(2,1)}, bf16[2,768,256]{2,1,0:T(8,128)(2,1)}, bf16[2,256,768]{2,1,0:T(8,128)(2,1)}) custom-call(s32[5]{0:T(128)} %pad_add_fusion.meta, bf16[2,4,64,768]{3,2,1,0:T(8,128)(2,1)} %cot.1, bf16[2,1,64,768]{3,2,1,0:T(8,128)(2,1)} %bitcast.187, bf16[2,1,64,768]{3,2,1,0:T(8,128)(2,1)} %bitcast.188, ...), custom_call_target="tpu_custom_call" | custom-call | flops 4000000000 | bytes 4000000 | tf_op jit(solution)/shard_map/prepare_cot/pallas_call | solution.py:180
  91.4 19.8 %all-to-all-done.1.att = bf16[8,128,768]{2,1,0:T(8,128)(2,1)S(1)} async-done(((bf16[8,128,768]{2,1,0:T(8,128)(2,1)}), bf16[8,128,768]{2,1,0:T(8,128)(2,1)S(1)}, u32[]{:S(2)}, u32[]{:S(2)}) %all-to-all-start.1) | async-done | bytes 1572896 | tf_op jit(solution)/shard_map/all_to_all | solution.py:796
  112.3 6.6 %second.1 = (bf16[2,512,768]{2,1,0:T(8,128)(2,1)}, bf16[2,768,256]{2,1,0:T(8,128)(2,1)}, f32[2,256,768]{2,1,0:T(8,128)}, f32[2,256,768]{2,1,0:T(8,128)}) custom-call(s32[5]{0:T(128)} %pad_add_fusion.meta, bf16[8,128,768]{2,1,0:T(8,128)(2,1)} %copy-done.4, bf16[2,4,64,768]{3,2,1,0:T(8,128)(2,1)} %tok.5, bf16[2,1,64,768]{3,2,1,0:T(8,128)(2,1)} %get-tuple-element.77.top2, ...), custom_call_target="tpu_custom_call" | custom-call | flops 7000000000 | bytes 4000000 | tf_op jit(solution)/shard_map/second/pallas_call | solution.py:252
  118.9 42.3 %ffn.1 = (f32[2,256,768]{2,1,0:T(8,128)}, f32[2,256,768]{2,1,0:T(8,128)}, bf16[2,2,192,3072]{3,2,1,0:T(8,128)(2,1)}, bf16[2,2,192,3072]{3,2,1,0:T(8,128)(2,1)}, f32[9,3072]{1,0:T(8,128)}) custom-call(s32[1]{0:T(128)} %bitcast.1.core, bf16[2,512,768]{2,1,0:T(8,128)(2,1)} %get-tuple-element.79.e2, bf16[2,768,256]{2,1,0:T(8,128)(2,1)} %get-tuple-element.80.e2t, ...), custom_call_target="tpu_custom_call" | custom-call | flops 48000000000 | bytes 4000000 | tf_op jit(solution)/shard_map/ffn/pallas_call | solution.py:417
  161.9 8.5 %middle.1 = (bf16[2,4,64,768]{3,2,1,0:T(8,128)(2,1)}, f32[2,256,768]{2,1,0:T(8,128)}, bf16[2,4,64,768]{3,2,1,0:T(8,128)(2,1)}, bf16[2,4,64,768]{3,2,1,0:T(8,128)(2,1)}, f32[2,4,768]{2,1,0:T(4,128)}) custom-call(s32[5]{0:T(128)} %pad_add_fusion.meta, f32[2,256,768]{2,1,0:T(8,128)} %get-tuple-element.83.exp, f32[2,256,768]{2,1,0:T(8,128)} %get-tuple-element.84.ge2, ...), custom_call_target="tpu_custom_call" | custom-call | flops 10000000000 | bytes 4000000 | tf_op jit(solution)/shard_map/middle/pallas_call | solution.py:499
  170.4 3.9 %all-to-all-start.2 = ((bf16[8,64,768]{2,1,0:T(8,128)(2,1)}), bf16[8,64,768]{2,1,0:T(8,128)(2,1)S(1)}, u32[]{:S(2)}, u32[]{:S(2)}) async-start(bf16[8,64,768]{2,1,0:T(8,128)(2,1)} %bitcast.185), calls=%async_computation.2 | async-start | bytes 1572864 | tf_op jit(solution)/shard_map/all_to_all | solution.py:796
  178.2 5.7 %add_convert_fusion = bf16[2,2,192,3072]{3,2,1,0:T(8,128)(2,1)S(1)} fusion(bf16[2,2,192,3072]{3,2,1,0:T(8,128)(2,1)} %collective-permute-done.4, bf16[2,2,192,3072]{3,2,1,0:T(8,128)(2,1)} %get-tuple-element.94), kind=kLoop, calls=%fused_computation | loop fusion | flops 9437184 | bytes 14155776 | tf_op jit(solution)/shard_map/convert_element_type | solution.py:1023
  186.7 8.3 %all-to-all-done.2 = bf16[8,64,768]{2,1,0:T(8,128)(2,1)S(1)} async-done(((bf16[8,64,768]{2,1,0:T(8,128)(2,1)}), bf16[8,64,768]{2,1,0:T(8,128)(2,1)S(1)}, u32[]{:S(2)}, u32[]{:S(2)}) %all-to-all-start.2) | async-done | bytes 786464 | tf_op jit(solution)/shard_map/all_to_all | solution.py:796
  198.0 25.2 %attend_back.1 = (bf16[3,2,192,768]{3,2,1,0:T(8,128)(2,1)}, bf16[3,2,192,768]{3,2,1,0:T(8,128)(2,1)}, bf16[8,96,768]{2,1,0:T(8,128)(2,1)}) custom-call(s32[2]{0:T(128)} %pad_add_fusion.1.offset, bf16[512,2304]{1,0:T(8,128)(2,1)} %convolution_convert_fusion.query.key.value, bf16[512,2304]{1,0:T(8,128)(2,1)} %convolution_convert_fusion.query.key.value, ...), custom_call_target="tpu_custom_call" | custom-call | flops 23000000512 | bytes 4000000 | tf_op jit(solution)/shard_map/attend_back/pallas_call | solution.py:746
  224.7 4.5 %all-to-all-start.3 = ((bf16[8,96,768]{2,1,0:T(8,128)(2,1)}), bf16[8,96,768]{2,1,0:T(8,128)(2,1)}, u32[]{:S(2)}, u32[]{:S(2)}) async-start(bf16[8,96,768]{2,1,0:T(8,128)(2,1)} %get-tuple-element.104), calls=%async_computation.3 | async-start | bytes 2359296 | tf_op jit(solution)/shard_map/all_to_all | solution.py:796
  236.8 1.9 add_convert_fusion.1
  243.7 14.9 %all-to-all-done.3.gm = bf16[8,96,768]{2,1,0:T(8,128)(2,1)} async-done(((bf16[8,96,768]{2,1,0:T(8,128)(2,1)}), bf16[8,96,768]{2,1,0:T(8,128)(2,1)}, u32[]{:S(2)}, u32[]{:S(2)}) %all-to-all-start.3) | async-done | bytes 1179680 | tf_op jit(solution)/shard_map/all_to_all | solution.py:796
  258.5 8.5 %leave.1 = (f32[2,4,64,768]{3,2,1,0:T(8,128)}, f32[2,9,768]{2,1,0:T(8,128)}, f32[2,2,768]{2,1,0:T(2,128)}) custom-call(s32[5]{0:T(128)} %pad_add_fusion.meta, bf16[8,96,768]{2,1,0:T(8,128)(2,1)} %all-to-all-done.3.gm, bf16[2,4,64,768]{3,2,1,0:T(8,128)(2,1)} %tok.5, bf16[2,1,64,768]{3,2,1,0:T(8,128)(2,1)} %copy-done.22, bf16[2,1,64,768]{3,2,1,0:T(8,128)(2,1)} %copy-done.23, ...), custom_call_target="tpu_custom_call" | custom-call | flops 10000000000 | bytes 4000000 | tf_op jit(solution)/shard_map/leave/pallas_call | solution.py:588
  273.3 3.6 %collective-permute-done.10 = bf16[2,2,2,24,768]{4,3,0,1,2:T(8,128)(2,1)S(1)} collective-permute-done((bf16[2,2,2,24,768]{4,3,0,1,2:T(8,128)(2,1)S(1)}, bf16[2,2,2,24,768]{4,3,0,1,2:T(8,128)(2,1)S(1)}, u32[]{:S(2)}, u32[]{:S(2)}) %collective-permute-start.10) | collective-permute-done | bytes 294944 | tf_op jit(solution)/shard_map/ppermute | solution.py:819
  277.0 1.9 collective-permute-done.12
  284.1 4.9 %all-to-all-start.4 = ((f32[8,112,128]{2,1,0:T(8,128)}), f32[8,112,128]{2,1,0:T(8,128)S(1)}, u32[]{:S(2)}, u32[]{:S(2)}) async-start(f32[8,112,128]{2,1,0:T(8,128)} %bitcast.164), calls=%async_computation.4 | async-start | bytes 917504 | tf_op jit(solution)/shard_map/all_to_all | solution.py:796
  291.1 2.8 collective-permute-start.14
  293.9 15.8 %collective-permute-done.17 = bf16[2,2,24,3072]{3,2,1,0:T(8,128)(2,1)S(1)} collective-permute-done((bf16[2,2,24,3072]{3,2,1,0:T(8,128)(2,1)}, bf16[2,2,24,3072]{3,2,1,0:T(8,128)(2,1)S(1)}, u32[]{:S(2)}, u32[]{:S(2)}) %collective-permute-start.17) | collective-permute-done | bytes 589856 | tf_op jit(solution)/shard_map/ppermute | solution.py:819
  313.0 5.7 %all-gather.1 = f32[448,128]{1,0:T(8,128)S(1)} all-gather(f32[112,128]{1,0:T(8,128)S(1)} %reduce_sum.46), channel_id=3, replica_groups=mesh['batch'=4,'seq'=8] {'batch'}, dimensions={0}, use_global_device_ids=true | all-gather | bytes 286720 | tf_op jit(solution)/shard_map/all_gather | solution.py:852
  319.0 4.9 %fusion.20 = f32[24,768]{1,0:T(8,128)S(1)} fusion(bf16[768,4608]{1,0:T(8,128)(2,1)} %param.24, bf16[8,4608]{1,0:T(8,128)(2,1)S(1)} %get-tuple-element.154, bf16[8,4608]{1,0:T(8,128)(2,1)S(1)} %get-tuple-element.155, bf16[8,4608]{1,0:T(8,128)(2,1)S(1)} %get-tuple-element.153), kind=kOutput, calls=%fused_computation.75 | convolution fusion | flops 170532864 | bytes 7372800 | tf_op jit(solution)/shard_map/dot_general | solution.py:29
  (180 shorter events, 63.1 us)
Async XLA Ops:
  0.6 8.0 %copy-start = (bf16[1000,768]{1,0:T(8,128)(2,1)S(1)}, bf16[1000,768]{1,0:T(8,128)(2,1)}, u32[]{:S(2)}) copy-start(bf16[1000,768]{1,0:T(8,128)(2,1)} %param.23) | copy-start | bytes 4608004
  0.7 7.6 %copy-start.24 = (s32[2]{0:T(128)S(1)}, s32[2]{0:T(128)}, u32[]{:S(2)}) copy-start(s32[2]{0:T(128)} %param.18) | copy-start | bytes 28
  0.7 7.7 %copy-start.11 = (bf16[256,768]{1,0:T(8,128)(2,1)S(1)}, bf16[256,768]{1,0:T(8,128)(2,1)}, u32[]{:S(2)}) copy-start(bf16[256,768]{1,0:T(8,128)(2,1)} %param.22) | copy-start | bytes 1179652
  0.7 7.9 %copy-start.19 = (s32[2]{0:T(128)S(1)}, s32[2]{0:T(128)}, u32[]{:S(2)}) copy-start(s32[2]{0:T(128)} %param.19) | copy-start | bytes 28
  0.7 8.3 %copy-start.17 = (f32[4608]{0:T(1024)S(1)}, f32[4608]{0:T(1024)}, u32[]{:S(2)}) copy-start(f32[4608]{0:T(1024)} %param.25) | copy-start | bytes 55300
  2.1 12.8 %collective-permute-start = (bf16[2,1,64,768]{3,2,1,0:T(8,128)(2,1)S(1)}, bf16[2,1,64,768]{3,2,1,0:T(8,128)(2,1)S(1)}, u32[]{:S(2)}, u32[]{:S(2)}) collective-permute-start(bf16[2,1,64,768]{3,2,1,0:T(8,128)(2,1)S(1)} %get-tuple-element.139), channel_id=1, source_target_pairs={{0,1},{1,2},{2,3},{3,4},{4,5},{5,6},{6,7},{8,9},{9,10},{10,11},{11... | collective-permute-start | bytes 589832 | tf_op jit(solution)/shard_map/ppermute | solution.py:787
  7.0 8.3 %collective-permute-start.1 = (bf16[2,1,64,768]{3,2,1,0:T(8,128)(2,1)S(1)}, bf16[2,1,64,768]{3,2,1,0:T(8,128)(2,1)S(1)}, u32[]{:S(2)}, u32[]{:S(2)}) collective-permute-start(bf16[2,1,64,768]{3,2,1,0:T(8,128)(2,1)S(1)} %get-tuple-element.137), channel_id=1, source_target_pairs={{1,0},{2,1},{3,2},{4,3},{5,4},{6,5},{7,6},{9,8},{10,9},{11,10},{12... | collective-permute-start | bytes 589832 | tf_op jit(solution)/shard_map/ppermute | solution.py:792
  21.3 26.9 %all-to-all-start = ((bf16[8,64,768]{2,1,0:T(8,128)(2,1)}), bf16[8,64,768]{2,1,0:T(8,128)(2,1)S(1)}, u32[]{:S(2)}, u32[]{:S(2)}) async-start(bf16[8,64,768]{2,1,0:T(8,128)(2,1)} %bitcast.183), calls=%async_computation | async-start | bytes 1572864 | tf_op jit(solution)/shard_map/all_to_all | solution.py:796
  29.5 7.1 %copy-start.12 = (bf16[2,4,64,768]{3,2,1,0:T(8,128)(2,1)S(1)}, bf16[2,4,64,768]{3,2,1,0:T(8,128)(2,1)}, u32[]{:S(2)}) copy-start(bf16[2,4,64,768]{3,2,1,0:T(8,128)(2,1)} %cot.1) | copy-start | bytes 2359300
  48.2 19.8 %collective-permute-start.2 = (bf16[2,2,1,64,768]{4,3,1,2,0:T(8,128)(2,1)S(1)}, bf16[2,2,1,64,768]{4,3,1,2,0:T(8,128)(2,1)S(1)}, u32[]{:S(2)}, u32[]{:S(2)}) collective-permute-start(bf16[2,2,1,64,768]{4,3,1,2,0:T(8,128)(2,1)S(1)} %get-tuple-element.70), channel_id=1, source_target_pairs={{0,1},{1,2},{2,3},{3,4},{4,5},{5,6},{6,7},{8,9},{9,10},{10,11},{11... | collective-permute-start | bytes 1179656 | tf_op jit(solution)/shard_map/ppermute | solution.py:787
  51.5 17.3 %collective-permute-start.3 = (bf16[2,2,1,64,768]{4,3,1,2,0:T(8,128)(2,1)S(1)}, bf16[2,2,1,64,768]{4,3,1,2,0:T(8,128)(2,1)S(1)}, u32[]{:S(2)}, u32[]{:S(2)}) collective-permute-start(bf16[2,2,1,64,768]{4,3,1,2,0:T(8,128)(2,1)S(1)} %get-tuple-element.71), channel_id=1, source_target_pairs={{1,0},{2,1},{3,2},{4,3},{5,4},{6,5},{7,6},{9,8},{10,9},{11,10},{12... | collective-permute-start | bytes 1179656 | tf_op jit(solution)/shard_map/ppermute | solution.py:792
  69.6 10.5 %copy-start.6 = (bf16[8,64,768]{2,1,0:T(8,128)(2,1)S(1)}, bf16[8,64,768]{2,1,0:T(8,128)(2,1)}, u32[]{:S(2)}) copy-start(bf16[8,64,768]{2,1,0:T(8,128)(2,1)} %copy-done.5) | copy-start | bytes 2359300
  69.6 41.6 %all-to-all-start.1 = ((bf16[8,128,768]{2,1,0:T(8,128)(2,1)}), bf16[8,128,768]{2,1,0:T(8,128)(2,1)S(1)}, u32[]{:S(2)}, u32[]{:S(2)}) async-start(bf16[8,128,768]{2,1,0:T(8,128)(2,1)} %get-tuple-element.72), calls=%async_computation.1 | async-start | bytes 3145728 | tf_op jit(solution)/shard_map/all_to_all | solution.py:796
  161.2 14.4 %collective-permute-start.4 = (bf16[2,2,192,3072]{3,2,1,0:T(8,128)(2,1)}, bf16[2,2,192,3072]{3,2,1,0:T(8,128)(2,1)}, u32[]{:S(2)}, u32[]{:S(2)}) collective-permute-start(bf16[2,2,192,3072]{3,2,1,0:T(8,128)(2,1)} %get-tuple-element.95), channel_id=1, source_target_pairs={{0,8},{8,0},{16,24},{24,16},{1,9},{9,1},{17,25},{25,17},{2,10},{10... | collective-permute-start | bytes 14155784 | tf_op jit(solution)/shard_map/ppermute | solution.py:819
  170.4 24.6 %all-to-all-start.2 = ((bf16[8,64,768]{2,1,0:T(8,128)(2,1)}), bf16[8,64,768]{2,1,0:T(8,128)(2,1)S(1)}, u32[]{:S(2)}, u32[]{:S(2)}) async-start(bf16[8,64,768]{2,1,0:T(8,128)(2,1)} %bitcast.185), calls=%async_computation.2 | async-start | bytes 1572864 | tf_op jit(solution)/shard_map/all_to_all | solution.py:796
  177.8 45.4 %collective-permute-start.8 = (bf16[2,2,2,2,24,768]{5,4,3,2,1,0:T(8,128)(2,1)}, bf16[2,2,2,2,24,768]{5,4,3,2,1,0:T(8,128)(2,1)}, u32[]{:S(2)}, u32[]{:S(2)}) collective-permute-start(bf16[2,2,2,2,24,768]{5,4,3,2,1,0:T(8,128)(2,1)} %dynamic-slice_bitcast_fusion.8), channel_id=1, source_target_pairs={{0,8},{8,0},{16,24},{24,16},{1,9},{9,1},{17,25},{25,17},{2,10},{10... | collective-permute-start | bytes 1769480 | tf_op jit(solution)/shard_map/ppermute | solution.py:819
  195.0 29.6 %collective-permute-start.5 = (bf16[2,2,2,24,3072]{4,3,2,1,0:T(8,128)(2,1)}, bf16[2,2,2,24,3072]{4,3,2,1,0:T(8,128)(2,1)}, u32[]{:S(2)}, u32[]{:S(2)}) collective-permute-start(bf16[2,2,2,24,3072]{4,3,2,1,0:T(8,128)(2,1)} %get-tuple-element.102), channel_id=1, source_target_pairs={{0,16},{8,24},{16,0},{24,8},{1,17},{9,25},{17,1},{25,9},{2,18},{10... | collective-permute-start | bytes 3538952 | tf_op jit(solution)/shard_map/ppermute | solution.py:819
  196.6 28.1 %collective-permute-start.6 = (bf16[2,2,2,24,3072]{4,3,2,1,0:T(8,128)(2,1)}, bf16[2,2,2,24,3072]{4,3,2,1,0:T(8,128)(2,1)}, u32[]{:S(2)}, u32[]{:S(2)}) collective-permute-start(bf16[2,2,2,24,3072]{4,3,2,1,0:T(8,128)(2,1)} %get-tuple-element.103), channel_id=1, source_target_pairs={{0,1},{1,0},{2,3},{3,2},{4,5},{5,4},{6,7},{7,6},{8,9},{9,8},{10,11... | collective-permute-start | bytes 3538952 | tf_op jit(solution)/shard_map/ppermute | solution.py:819
  223.2 13.3 %collective-permute-start.7 = (bf16[3,2,192,768]{3,2,1,0:T(8,128)(2,1)}, bf16[3,2,192,768]{3,2,1,0:T(8,128)(2,1)}, u32[]{:S(2)}, u32[]{:S(2)}) collective-permute-start(bf16[3,2,192,768]{3,2,1,0:T(8,128)(2,1)} %get-tuple-element.118), channel_id=1, source_target_pairs={{0,8},{8,0},{16,24},{24,16},{1,9},{9,1},{17,25},{25,17},{2,10},{10... | collective-permute-start | bytes 5308424 | tf_op jit(solution)/shard_map/ppermute | solution.py:819
  224.7 33.8 %all-to-all-start.3 = ((bf16[8,96,768]{2,1,0:T(8,128)(2,1)}), bf16[8,96,768]{2,1,0:T(8,128)(2,1)}, u32[]{:S(2)}, u32[]{:S(2)}) async-start(bf16[8,96,768]{2,1,0:T(8,128)(2,1)} %get-tuple-element.104), calls=%async_computation.3 | async-start | bytes 2359296 | tf_op jit(solution)/shard_map/all_to_all | solution.py:796
  231.9 38.9 %collective-permute-start.15 = (bf16[2,2,24,3072]{3,2,1,0:T(8,128)(2,1)}, bf16[2,2,24,3072]{3,2,1,0:T(8,128)(2,1)}, u32[]{:S(2)}, u32[]{:S(2)}) collective-permute-start(bf16[2,2,24,3072]{3,2,1,0:T(8,128)(2,1)} %get-tuple-element.136), channel_id=1, source_target_pairs={{0,1},{1,0},{2,3},{3,2},{4,5},{5,4},{6,7},{7,6},{8,9},{9,8},{10,11... | collective-permute-start | bytes 1769480 | tf_op jit(solution)/shard_map/ppermute | solution.py:819
  236.0 36.1 %collective-permute-start.16 = (bf16[2,2,24,3072]{3,2,1,0:T(8,128)(2,1)}, bf16[2,2,24,3072]{3,2,1,0:T(8,128)(2,1)}, u32[]{:S(2)}, u32[]{:S(2)}) collective-permute-start(bf16[2,2,24,3072]{3,2,1,0:T(8,128)(2,1)} %get-tuple-element.134), channel_id=1, source_target_pairs={{0,16},{8,24},{16,0},{24,8},{1,17},{9,25},{17,1},{25,9},{2,18},{10... | collective-permute-start | bytes 1769480 | tf_op jit(solution)/shard_map/ppermute | solution.py:819
  240.9 26.2 %collective-permute-start.9 = (bf16[2,2,2,2,24,768]{5,4,0,1,2,3:T(8,128)(2,1)}, bf16[2,2,2,2,24,768]{5,4,0,1,2,3:T(8,128)(2,1)}, u32[]{:S(2)}, u32[]{:S(2)}) collective-permute-start(bf16[2,2,2,2,24,768]{5,4,0,1,2,3:T(8,128)(2,1)} %bitcast.161), channel_id=1, source_target_pairs={{0,16},{8,24},{16,0},{24,8},{1,17},{9,25},{17,1},{25,9},{2,18},{10... | collective-permute-start | bytes 1769480 | tf_op jit(solution)/shard_map/ppermute | solution.py:819
  243.2 26.8 %collective-permute-start.11 = (bf16[2,2,2,2,24,768]{5,4,0,2,3,1:T(8,128)(2,1)}, bf16[2,2,2,2,24,768]{5,4,0,2,3,1:T(8,128)(2,1)S(1)}, u32[]{:S(2)}, u32[]{:S(2)}) collective-permute-start(bf16[2,2,2,2,24,768]{5,4,0,2,3,1:T(8,128)(2,1)} %bitcast.160), channel_id=1, source_target_pairs={{0,1},{1,0},{2,3},{3,2},{4,5},{5,4},{6,7},{7,6},{8,9},{9,8},{10,11... | collective-permute-start | bytes 1769480 | tf_op jit(solution)/shard_map/ppermute | solution.py:819
  268.3 8.6 %collective-permute-start.10 = (bf16[2,2,2,24,768]{4,3,0,1,2:T(8,128)(2,1)S(1)}, bf16[2,2,2,24,768]{4,3,0,1,2:T(8,128)(2,1)S(1)}, u32[]{:S(2)}, u32[]{:S(2)}) collective-permute-start(bf16[2,2,2,24,768]{4,3,0,1,2:T(8,128)(2,1)S(1)} %dynamic-slice_bitcast_fusion.11), channel_id=1, source_target_pairs={{0,1},{1,0},{2,3},{3,2},{4,5},{5,4},{6,7},{7,6},{8,9},{9,8},{10,11... | collective-permute-start | bytes 884744 | tf_op jit(solution)/shard_map/ppermute | solution.py:819
  270.2 8.7 %collective-permute-start.12 = (bf16[2,2,2,24,768]{4,3,0,1,2:T(8,128)(2,1)S(1)}, bf16[2,2,2,24,768]{4,3,0,1,2:T(8,128)(2,1)S(1)}, u32[]{:S(2)}, u32[]{:S(2)}) collective-permute-start(bf16[2,2,2,24,768]{4,3,0,1,2:T(8,128)(2,1)S(1)} %dynamic-slice_bitcast_fusion.10), channel_id=1, source_target_pairs={{0,16},{8,24},{16,0},{24,8},{1,17},{9,25},{17,1},{25,9},{2,18},{10... | collective-permute-start | bytes 884744 | tf_op jit(solution)/shard_map/ppermute | solution.py:819
  279.7 10.3 %collective-permute-start.13 = (bf16[4,2,24,768]{3,2,0,1:T(8,128)(2,1)}, bf16[4,2,24,768]{3,2,0,1:T(8,128)(2,1)}, u32[]{:S(2)}, u32[]{:S(2)}) collective-permute-start(bf16[4,2,24,768]{3,2,0,1:T(8,128)(2,1)} %fusion.17), channel_id=1, source_target_pairs={{0,2},{1,3},{2,0},{3,1},{4,6},{5,7},{6,4},{7,5},{8,10},{9,11},{10,... | collective-permute-start | bytes 884744 | tf_op jit(solution)/shard_map/ppermute | solution.py:819
  282.1 27.6 %collective-permute-start.17 = (bf16[2,2,24,3072]{3,2,1,0:T(8,128)(2,1)}, bf16[2,2,24,3072]{3,2,1,0:T(8,128)(2,1)S(1)}, u32[]{:S(2)}, u32[]{:S(2)}) collective-permute-start(bf16[2,2,24,3072]{3,2,1,0:T(8,128)(2,1)} %fusion.8), channel_id=1, source_target_pairs={{0,2},{1,3},{2,0},{3,1},{4,6},{5,7},{6,4},{7,5},{8,10},{9,11},{10,... | collective-permute-start | bytes 1769480 | tf_op jit(solution)/shard_map/ppermute | solution.py:819
  284.1 28.8 %all-to-all-start.4 = ((f32[8,112,128]{2,1,0:T(8,128)}), f32[8,112,128]{2,1,0:T(8,128)S(1)}, u32[]{:S(2)}, u32[]{:S(2)}) async-start(f32[8,112,128]{2,1,0:T(8,128)} %bitcast.164), calls=%async_computation.4 | async-start | bytes 917504 | tf_op jit(solution)/shard_map/all_to_all | solution.py:796
  291.1 20.5 %collective-permute-start.14 = (bf16[4,24,768]{2,1,0:T(8,128)(2,1)S(1)}, bf16[4,24,768]{2,1,0:T(8,128)(2,1)S(1)}, u32[]{:S(2)}, u32[]{:S(2)}) collective-permute-start(bf16[4,24,768]{2,1,0:T(8,128)(2,1)S(1)} %dynamic-slice_bitcast_fusion.12), channel_id=1, source_target_pairs={{0,4},{1,5},{2,6},{3,7},{4,0},{5,1},{6,2},{7,3},{8,12},{9,13},{10,... | collective-permute-start | bytes 442376 | tf_op jit(solution)/shard_map/ppermute | solution.py:819
  309.9 19.8 %collective-permute-start.18 = (bf16[2,24,3072]{2,1,0:T(8,128)(2,1)S(1)}, bf16[2,24,3072]{2,1,0:T(8,128)(2,1)S(1)}, u32[]{:S(2)}, u32[]{:S(2)}) collective-permute-start(bf16[2,24,3072]{2,1,0:T(8,128)(2,1)S(1)} %dynamic-slice_bitcast_fusion.9), channel_id=1, source_target_pairs={{0,4},{1,5},{2,6},{3,7},{4,0},{5,1},{6,2},{7,3},{8,12},{9,13},{10,... | collective-permute-start | bytes 884744 | tf_op jit(solution)/shard_map/ppermute | solution.py:819
  324.9 5.7 %copy-start.1 = (bf16[1000,768]{1,0:T(8,128)(2,1)S(1)}, bf16[1000,768]{1,0:T(8,128)(2,1)}, u32[]{:S(2)}) copy-start(bf16[1000,768]{1,0:T(8,128)(2,1)} %param.23) | copy-start | bytes 4608004
  (20 other events, 60.8 us)

commit v4 on v3

--- a/solution.py
+++ b/solution.py
@@ -155,54 +155,42 @@
     )(meta, tokens, top, bot, pieces, kern)
 
 
-def cot_kernel(meta, cot, top, bot, pieces, ge_out, get_out, cot_out, buf):
+def cot_kernel(cot, pieces, ge_out, get_out, cot_out, buf):
     rows_here, cols = cot.shape[1], cot.shape[2]
     half = cols // 2
     gate = pieces[0, 5:6, :]
-    for rr in range(rows_here + 2):
-        source = top[0, 0] if rr == 0 else bot[0, 0] if rr == rows_here + 1 else cot[0, rr - 1]
-        put_row(buf, rr, source.astype(F32))
+    for row in range(rows_here):
+        put_row(buf, row, cot[0, row].astype(F32))
         for parity in range(2):
-            values = get_columns(buf, rr, parity)
-            scaled = (gate * values).astype(BF16)
-            at = (2 * rr + parity) * half
-            ge_out[0, at : at + half, :] = scaled
-            if 1 <= rr <= rows_here:
-                cot_out[0, at - cols : at - cols + half, :] = values.astype(BF16)
-    inner = ge_out[0, cols : cols + rows_here * cols, :].astype(F32)
-    get_out[0] = inner.T.astype(BF16)
-
-
-def prepare_cot(meta, cotangent, top, bot, pieces):
+            values = get_columns(buf, row, parity)
+            at = (2 * row + parity) * half
+            ge_out[0, at : at + half, :] = (gate * values).astype(BF16)
+            cot_out[0, at : at + half, :] = values.astype(BF16)
+    get_out[0] = ge_out[0].astype(F32).T.astype(BF16)
+
+
+def prepare_cot(cotangent, pieces):
     latents, rows_here, cols, _ = cotangent.shape
-    whole = lambda *shape: pl.BlockSpec(shape, lambda l, m: (l,) + (0,) * (len(shape) - 1))
+    whole = lambda *shape: pl.BlockSpec(shape, lambda l: (l,) + (0,) * (len(shape) - 1))
     own = rows_here * cols
     return pl.pallas_call(
         cot_kernel,
         out_shape=(
-            jax.ShapeDtypeStruct((latents, own + 2 * cols, D), BF16),
+            jax.ShapeDtypeStruct((latents, own, D), BF16),
             jax.ShapeDtypeStruct((latents, D, own), BF16),
             jax.ShapeDtypeStruct((latents, own, D), BF16),
         ),
-        grid_spec=pltpu.PrefetchScalarGridSpec(
-            num_scalar_prefetch=1,
-            grid=(latents,),
-            in_specs=[
-                whole(1, rows_here, cols, D),
-                whole(1, 1, cols, D),
-                whole(1, 1, cols, D),
-                whole(1, 6, D),
-            ],
-            out_specs=(whole(1, own + 2 * cols, D), whole(1, D, own), whole(1, own, D)),
-            scratch_shapes=[pltpu.VMEM((rows_here + 2, LANE_PARTS, cols, 128), F32)],
-        ),
+        grid=(latents,),
+        in_specs=[whole(1, rows_here, cols, D), whole(1, 6, D)],
+        out_specs=(whole(1, own, D), whole(1, D, own), whole(1, own, D)),
+        scratch_shapes=[pltpu.VMEM((rows_here, LANE_PARTS, cols, 128), F32)],
         compiler_params=pltpu.CompilerParams(vmem_limit_bytes=VMEM_LIMIT),
         cost_estimate=pl.CostEstimate(flops=4_000_000_000, bytes_accessed=4_000_000, transcendentals=0),
         name="prepare_cot",
-    )(meta, cotangent, top, bot, pieces)
-
-
-def second_kernel(meta, att, tok, top2, top1, bot1, bot2, pieces, proj, e2_out, e2t_out, after_out, branch_out, buf, bran):
+    )(cotangent, pieces)
+
+
+def second_kernel(meta, att, tok, top, bot, pieces, proj, e2_out, e2t_out, after_out, branch_out, buf, bran):
     latents = pl.num_programs(0)
     latent = pl.program_id(0)
     rows_here, cols = tok.shape[1], tok.shape[2]
@@ -213,47 +201,34 @@
     scale = 1.0 + pieces[0, 4:5, :]
     for group in range(4):
         bran[group] = mm(att[group], proj[...])
-    for rr in range(rows_here + 4):
-        at_row = rr - 2
-        source = (
-            top2[0, 0]
-            if at_row == -2
-            else top1[0, 0]
-            if at_row == -1
-            else bot1[0, 0]
-            if at_row == rows_here
-            else bot2[0, 0]
-            if at_row == rows_here + 1
-            else tok[0, at_row]
-        )
+    for rr in range(rows_here + 2):
+        source = top[0, 0] if rr == 0 else bot[0, 0] if rr == rows_here + 1 else tok[0, rr - 1]
         put_row(buf, rr, source.astype(F32))
         for parity in range(2):
-            group = 2 * (rr % 2) + parity
+            group = 2 * ((rr + 1) % 2) + parity
             branch = bran[group, (rr // 2) * half : (rr // 2 + 1) * half, :]
             after = get_columns(buf, rr, parity) + gate * branch
             normed, _ = normalize(after)
-            ok = usable_of(meta, latents, latent, row0 + at_row, parity, half)
+            ok = usable_of(meta, latents, latent, row0 + rr - 1, parity, half)
             at = (2 * rr + parity) * half
             e2_out[0, at : at + half, :] = ((normed * scale + shift) * ok).astype(BF16)
-            if 0 <= at_row < rows_here:
-                own = at - 2 * cols
+            if 1 <= rr <= rows_here:
+                own = at - cols
                 after_out[0, own : own + half, :] = after
                 branch_out[0, own : own + half, :] = branch
-    inner = e2_out[0, 2 * cols : 2 * cols + rows_here * cols, :].astype(F32)
-    e2t_out[0] = inner.T.astype(BF16)
-
-
-def second(meta, attended, tokens, tops, bots, pieces, proj):
+    e2t_out[0] = e2_out[0].astype(F32).T.astype(BF16)
+
+
+def second(meta, attended, tokens, top, bot, pieces, proj):
     latents, rows_here, cols, _ = tokens.shape
-    half = cols // 2
     own = rows_here * cols
     wide = attended.shape[1]
     whole = lambda *shape: pl.BlockSpec(shape, lambda l, m: (l,) + (0,) * (len(shape) - 1))
     return pl.pallas_call(
         second_kernel,
         out_shape=(
-            jax.ShapeDtypeStruct((latents, own + 4 * cols, D), BF16),
-            jax.ShapeDtypeStruct((latents, D, own), BF16),
+            jax.ShapeDtypeStruct((latents, own + 2 * cols, D), BF16),
+            jax.ShapeDtypeStruct((latents, D, own + 2 * cols), BF16),
             jax.ShapeDtypeStruct((latents, own, D), F32),
             jax.ShapeDtypeStruct((latents, own, D), F32),
         ),
@@ -265,30 +240,28 @@
                 whole(1, rows_here, cols, D),
                 whole(1, 1, cols, D),
                 whole(1, 1, cols, D),
-                whole(1, 1, cols, D),
-                whole(1, 1, cols, D),
                 whole(1, 6, D),
                 pl.BlockSpec((D, D), lambda l, m: (0, 0)),
             ],
             out_specs=(
-                whole(1, own + 4 * cols, D),
-                whole(1, D, own),
+                whole(1, own + 2 * cols, D),
+                whole(1, D, own + 2 * cols),
                 whole(1, own, D),
                 whole(1, own, D),
             ),
             scratch_shapes=[
-                pltpu.VMEM((rows_here + 4, LANE_PARTS, cols, 128), F32),
+                pltpu.VMEM((rows_here + 2, LANE_PARTS, cols, 128), F32),
                 pltpu.VMEM((4, wide, D), F32),
             ],
         ),
         compiler_params=pltpu.CompilerParams(vmem_limit_bytes=VMEM_LIMIT),
         cost_estimate=pl.CostEstimate(flops=7_000_000_000, bytes_accessed=4_000_000, transcendentals=0),
         name="second",
-    )(meta, attended, tokens, tops[1], tops[0], bots[0], bots[1], pieces, proj)
+    )(meta, attended, tokens, top, bot, pieces, proj)
 
 
 def normal_parts(values):
-    density = jnp.exp(-0.5 * values * values) * 0.3989422804014327
+    density = jnp.exp2(values * values * -0.7213475204444817 - 1.3257480647361592)
     t = 1.0 / (1.0 + 0.2316419 * jnp.abs(values))
     series = t * (
         0.319381530
@@ -304,94 +277,113 @@
     down_acc, up_acc = scratch[5 * latents :]
     step = pl.program_id(0)
     half = lifted[0].shape[2]
-    rows_here = lifted[0].shape[0] - 4
+    rows_here = gconv[0].shape[0]
     block = lifted[0].shape[3]
-    taps = [kern_in[t : t + 1, :].astype(F32) for t in range(9)]
-    sums = [jnp.zeros((8, block), F32) for _ in range(9)]
-    rows_per = 4
+    chunks = block // 128
+    lanes = [slice(c * 128, (c + 1) * 128) for c in range(chunks)]
+    taps = [[kern_in[t : t + 1, cut].astype(F32) for t in range(9)] for cut in lanes]
+    sums = [[jnp.zeros((8, 128), F32) for _ in range(9)] for _ in range(chunks)]
+    lift_rows = 3
+
+    def put(ref, row, parity, cut, values):
+        ref[row, 1 + parity, :, cut] = values
+        if parity == 0:
+            ref[row, 3, :, cut] = shift_up(values)
+        else:
+            ref[row, 0, :, cut] = shift_down(values)
 
     def lift(latent, part):
-        size = rows_per * 2 * half
+        size = lift_rows * 2 * half
         raised = mm(e2[latent, part * size : (part + 1) * size], up[...])
-        raised = raised.astype(BF16).astype(F32)
-        for k in range(rows_per):
+        for k in range(lift_rows):
             for parity in range(2):
                 at = (2 * k + parity) * half
-                put_shifts(lifted[latent], part * rows_per + k, parity, raised[at : at + half])
-
-    def pull(latent, part):
-        size = gact[latent].shape[0] // 2
-        at = part * size
-        gact[latent][at : at + size] = mm(ge[latent, at : at + size], down[...], NT)
-
-    def bend(latent, rr):
+                for cut in lanes:
+                    put(lifted[latent], part * lift_rows + k, parity, cut, raised[at : at + half, cut])
+
+    def pull(latent):
+        gact[latent][...] = mm(ge[latent], down[...], NT)
+
+    def bend(latent, row, c):
+        cut = lanes[c]
         for parity in range(2):
             total = None
             for i in range(3):
                 for j in range(3):
-                    term = lifted[latent][rr + i, parity + j] * taps[3 * i + j]
+                    term = lifted[latent][row + i, parity + j, :, cut] * taps[c][3 * i + j]
                     total = term if total is None else total + term
             cdf, density = normal_parts(total)
-            at = (2 * rr + parity) * half
-            if 1 <= rr <= rows_here:
-                own = at - 2 * half
-                act[latent][own : own + half, :] = (total * cdf).astype(BF16)
-            grad = gact[latent][at : at + half, :] * (cdf + total * density)
-            put_shifts(gconv[latent], rr, parity, grad.astype(BF16).astype(F32))
-
-    def unbend(latent, row):
+            at = (2 * row + parity) * half
+            act[latent][at : at + half, cut] = (total * cdf).astype(BF16)
+            grad = gact[latent][at : at + half, cut] * (cdf + total * density)
+            put(gconv[latent], row, parity, cut, grad)
+
+    def unbend(latent, rr, c):
+        cut = lanes[c]
         for parity in range(2):
             total = None
-            here = gconv[latent][row + 1, 1 + parity]
             for i in range(3):
+                row = rr - i
+                if not 0 <= row < rows_here:
+                    continue
                 for j in range(3):
-                    t = 3 * i + j
-                    term = gconv[latent][row + 2 - i, parity + 2 - j] * taps[t]
+                    term = gconv[latent][row, parity + 2 - j, :, cut] * taps[c][3 * i + j]
                     total = term if total is None else total + term
-                    sums[t] = sums[t] + sum8(lifted[latent][row + 1 + i, parity + j] * here)
-            at = (2 * row + parity) * half
-            graised[latent][at : at + half, :] = total.astype(BF16)
-
-    def gather(latent, part):
-        cut = slice(part * 256, (part + 1) * 256)
-        if part == 0:
-            exp_out[latent] += mm(act[latent][...], down[...])
-        elif part == 1:
-            ge2_out[latent] += mm(graised[latent][...], up[...], NT)
-        elif part == 2:
-            value = mm(get[latent], act[latent][...])
-            down_acc[...] = value if latent == 0 else down_acc[...] + value
-        else:
-            value = mm(e2t[latent], graised[latent][...])
-            up_acc[...] = value if latent == 0 else up_acc[...] + value
+            at = (2 * rr + parity) * half
+            graised[latent][at : at + half, cut] = total.astype(BF16)
+            if rr < rows_here:
+                here = gconv[latent][rr, 1 + parity, :, cut]
+                for i in range(3):
+                    for j in range(3):
+                        t = 3 * i + j
+                        part = lifted[latent][rr + i, parity + j, :, cut] * here
+                        sums[c][t] = sums[c][t] + sum8(part)
+
+    def expand(latent):
+        exp_out[latent] += mm(act[latent][...], down[...])
+
+    def lower(latent):
+        ge2_out[latent] += mm(graised[latent][...], up[...], NT)
+
+    def weigh_down(latent):
+        value = mm(get[latent], act[latent][...])
+        down_acc[...] = value if latent == 0 else down_acc[...] + value
+
+    def weigh_up(latent):
+        value = mm(e2t[latent], graised[latent][...])
+        up_acc[...] = value if latent == 0 else up_acc[...] + value
 
     @pl.when(step == 0)
     def _():
         exp_out[...] = jnp.zeros_like(exp_out)
         ge2_out[...] = jnp.zeros_like(ge2_out)
 
-    lifts = (rows_here + 4) // rows_per
-    for part in range(lifts):
-        lift(0, part)
-    for part in range(2):
-        pull(0, part)
+    def mix(work, more):
+        stride = max(1, len(work) // max(1, len(more)))
+        for k, unit in enumerate(work):
+            if k % stride == 0 and k // stride < len(more):
+                more[k // stride]()
+            unit()
+        for unit in more[-(-len(work) // stride) :]:
+            unit()
+
+    part = functools.partial
+    lifts = (rows_here + 2) // lift_rows
+    for k in range(lifts):
+        lift(0, k)
+    pull(0)
     for latent in range(latents):
-        more = []
+        bends = [part(bend, latent, row, c) for c in range(chunks) for row in range(rows_here)]
+        unbends = [part(unbend, latent, rr, c) for c in range(chunks) for rr in range(rows_here + 2)]
+        first, then = [], [part(expand, latent), part(weigh_down, latent)]
+        if latent > 0:
+            first += [part(lower, latent - 1), part(weigh_up, latent - 1)]
         if latent + 1 < latents:
-            more += [functools.partial(lift, latent + 1, part) for part in range(lifts)]
-            more += [functools.partial(pull, latent + 1, part) for part in range(2)]
-        if latent > 0:
-            more += [functools.partial(gather, latent - 1, part) for part in range(4)]
-        work = [functools.partial(bend, latent, rr) for rr in range(rows_here + 2)]
-        work += [functools.partial(unbend, latent, row) for row in range(rows_here)]
-        for k, unit in enumerate(work):
-            if k < len(more):
-                more[k]()
-            unit()
-        for unit in more[len(work) :]:
-            unit()
-    for part in range(4):
-        gather(latents - 1, part)
+            first += [part(lift, latent + 1, k) for k in range(lifts)] + [part(pull, latent + 1)]
+        mix(bends, first)
+        mix(unbends, then)
+    lower(latents - 1)
+    weigh_up(latents - 1)
 
     size = down_acc.shape[0] // 4
     for which, acc in enumerate((down_acc, up_acc)):
@@ -400,14 +392,15 @@
             other = pl.multiple_of((2 * y + 1 - core[0]) * size, 8)
             keep_out[which, y] = acc[pl.ds(mine, size), :].astype(BF16)
             send_out[which, y] = acc[pl.ds(other, size), :].astype(BF16)
-    for t in range(9):
-        kern_out[t : t + 1, :] = jnp.sum(sums[t], axis=0, keepdims=True)
+    for c, cut in enumerate(lanes):
+        for t in range(9):
+            kern_out[t : t + 1, cut] = jnp.sum(sums[c][t], axis=0, keepdims=True)
 
 
 def ffn(core, e2, e2t, ge, get, up, down, kern, cols):
-    latents = e2.shape[0]
+    latents, wide, _ = e2.shape
     half = cols // 2
-    own = e2t.shape[2]
+    own = ge.shape[1]
     rows_here = own // cols
     hidden = up.shape[1]
     fixed = lambda *shape: pl.BlockSpec(shape, lambda f, c: (0,) * len(shape))
@@ -418,7 +411,7 @@
         ffn_kernel,
         out_shape=(
             jax.ShapeDtypeStruct((latents, own, D), F32),
-            jax.ShapeDtypeStruct((latents, own, D), F32),
+            jax.ShapeDtypeStruct((latents, wide, D), F32),
             parts,
             parts,
             jax.ShapeDtypeStruct((9, hidden), F32),
@@ -427,9 +420,9 @@
             num_scalar_prefetch=1,
             grid=(hidden // FF_BLOCK,),
             in_specs=[
-                fixed(latents, own + 4 * cols, D),
-                fixed(latents, D, own),
-                fixed(latents, own + 2 * cols, D),
+                fixed(latents, wide, D),
+                fixed(latents, D, wide),
+                fixed(latents, own, D),
                 fixed(latents, D, own),
                 pl.BlockSpec((D, FF_BLOCK), lambda f, c: (0, f)),
                 pl.BlockSpec((FF_BLOCK, D), lambda f, c: (f, 0)),
@@ -437,80 +430,118 @@
             ],
             out_specs=(
                 fixed(latents, own, D),
-                fixed(latents, own, D),
+                fixed(latents, wide, D),
                 parts_spec,
                 parts_spec,
                 pl.BlockSpec((9, FF_BLOCK), lambda f, c: (0, f)),
             ),
-            scratch_shapes=each((rows_here + 4, 4, half, FF_BLOCK), F32)
-            + each((own + 2 * cols, FF_BLOCK), F32)
-            + each((rows_here + 2, 4, half, FF_BLOCK), F32)
+            scratch_shapes=each((rows_here + 2, 4, half, FF_BLOCK), F32)
+            + each((own, FF_BLOCK), F32)
+            + each((rows_here, 4, half, FF_BLOCK), F32)
             + each((own, FF_BLOCK), BF16)
-            + each((own, FF_BLOCK), BF16)
+            + each((wide, FF_BLOCK), BF16)
             + [pltpu.VMEM((D, FF_BLOCK), F32), pltpu.VMEM((D, FF_BLOCK), F32)],
         ),
         compiler_params=pltpu.CompilerParams(vmem_limit_bytes=VMEM_LIMIT),
-        cost_estimate=pl.CostEstimate(flops=48_000_000_000, bytes_accessed=4_000_000, transcendentals=0),
+        cost_estimate=pl.CostEstimate(flops=35_000_000_000, bytes_accessed=4_000_000, transcendentals=0),
         name="ffn",
     )(core, e2, e2t, ge, get, up, down, kern)
 
 
-def middle_kernel(meta, exp, ge2, after_in, branch_in, cot_in, pieces, proj, out, after_grad, gb_out, gatt_out, sums_out, buf):
+def output_kernel(exp, after_in, cot_in, pieces, out, sum_out, buf):
+    rows_here, cols = out.shape[1], out.shape[2]
+    half = cols // 2
+    gate = pieces[0, 5:6, :]
+    total = jnp.zeros((8, D), F32)
+    for row in range(rows_here):
+        for parity in range(2):
+            part = pl.ds((2 * row + parity) * half, half)
+            expanded = exp[0, part, :]
+            put_columns(buf, row, parity, after_in[0, part, :] + gate * expanded)
+            total = total + sum8(cot_in[0, part, :].astype(F32) * expanded)
+        out[0, row] = get_row(buf, row).astype(BF16)
+    sum_out[0] = jnp.sum(total, axis=0, keepdims=True)
+
+
+def finish_output(exp, after, cot, pieces, rows_here, cols):
+    latents, own, _ = exp.shape
+    whole = lambda *shape: pl.BlockSpec(shape, lambda l: (l,) + (0,) * (len(shape) - 1))
+    return pl.pallas_call(
+        output_kernel,
+        out_shape=(
+            jax.ShapeDtypeStruct((latents, rows_here, cols, D), BF16),
+            jax.ShapeDtypeStruct((latents, 1, D), F32),
+        ),
+        grid=(latents,),
+        in_specs=[whole(1, own, D), whole(1, own, D), whole(1, own, D), whole(1, 6, D)],
+        out_specs=(whole(1, rows_here, cols, D), whole(1, 1, D)),
+        scratch_shapes=[pltpu.VMEM((rows_here, LANE_PARTS, cols, 128), F32)],
+        compiler_params=pltpu.CompilerParams(vmem_limit_bytes=VMEM_LIMIT),
+        cost_estimate=pl.CostEstimate(flops=5_000_000_000, bytes_accessed=4_000_000, transcendentals=0),
+        name="finish_output",
+    )(exp, after, cot, pieces)
+
+
+def middle_kernel(meta, ge2, low, high, after_in, branch_in, cot_in, pieces, proj, after_grad, gb_out, gatt_out, sums_out):
     latents = pl.num_programs(0)
     latent = pl.program_id(0)
-    rows_here, cols = out.shape[1], out.shape[2]
+    own = after_in.shape[1]
+    cols = low.shape[1]
+    rows_here = own // cols
     half = cols // 2
     row0 = meta[2 * latents]
     gate_one = pieces[0, 2:3, :]
     scale = 1.0 + pieces[0, 4:5, :]
-    gate_two = pieces[0, 5:6, :]
-    sums = [jnp.zeros((8, D), F32) for _ in range(4)]
+    sums = [jnp.zeros((8, D), F32) for _ in range(3)]
     for row in range(rows_here):
         for parity in range(2):
             at = (2 * row + parity) * half
             part = pl.ds(at, half)
+            side = pl.ds(parity * half, half)
             after = after_in[0, part, :]
             cot = cot_in[0, part, :].astype(F32)
-            expanded = exp[0, part, :]
-            put_columns(buf, row, parity, after + gate_two * expanded)
             normed, scaled = normalize(after)
             ok = usable_of(meta, latents, latent, row0 + row, parity, half)
-            grad = ge2[0, part, :] * ok
+            grad = ge2[0, pl.ds(at + cols, half), :]
+            if row == 0:
+                grad = grad + low[0, side, :].astype(F32)
+            if row == rows_here - 1:
+                grad = grad + high[0, side, :].astype(F32)
+            grad = grad * ok
             grad_after = cot + norm_back(grad * scale, normed, scaled)
             after_grad[0, part, :] = grad_after
             sums[0] = sums[0] + sum8(grad_after * branch_in[0, part, :])
             sums[1] = sums[1] + sum8(grad)
             sums[2] = sums[2] + sum8(grad * normed)
-            sums[3] = sums[3] + sum8(cot * expanded)
             group = 2 * (row % 2) + parity
             to = pl.ds((row // 2) * half, half)
             gb_out[0, group, to, :] = (gate_one * grad_after).astype(BF16)
-        out[0, row] = get_row(buf, row).astype(BF16)
-    for k in range(4):
+    for k in range(3):
         sums_out[0, k : k + 1, :] = jnp.sum(sums[k], axis=0, keepdims=True)
     for group in range(4):
         gatt_out[0, group] = mm(gb_out[0, group], proj[...], NT).astype(BF16)
 
 
-def middle(meta, exp, ge2, after, branch, cot, pieces, proj, rows_here, cols):
-    latents, own, _ = exp.shape
+def middle(meta, ge2, low, high, after, branch, cot, pieces, proj):
+    latents, own, _ = after.shape
+    wide, cols = ge2.shape[1], low.shape[1]
     per_group = own // 4
     whole = lambda *shape: pl.BlockSpec(shape, lambda l, m: (l,) + (0,) * (len(shape) - 1))
     return pl.pallas_call(
         middle_kernel,
         out_shape=(
-            jax.ShapeDtypeStruct((latents, rows_here, cols, D), BF16),
             jax.ShapeDtypeStruct((latents, own, D), F32),
             jax.ShapeDtypeStruct((latents, 4, per_group, D), BF16),
             jax.ShapeDtypeStruct((latents, 4, per_group, D), BF16),
-            jax.ShapeDtypeStruct((latents, 4, D), F32),
+            jax.ShapeDtypeStruct((latents, 3, D), F32),
         ),
         grid_spec=pltpu.PrefetchScalarGridSpec(
             num_scalar_prefetch=1,
             grid=(latents,),
             in_specs=[
-                whole(1, own, D),
-                whole(1, own, D),
+                whole(1, wide, D),
+                whole(1, cols, D),
+                whole(1, cols, D),
                 whole(1, own, D),
                 whole(1, own, D),
                 whole(1, own, D),
@@ -518,23 +549,19 @@
                 pl.BlockSpec((D, D), lambda l, m: (0, 0)),
             ],
             out_specs=(
-                whole(1, rows_here, cols, D),
                 whole(1, own, D),
                 whole(1, 4, per_group, D),
                 whole(1, 4, per_group, D),
-                whole(1, 4, D),
+                whole(1, 3, D),
             ),
-            scratch_shapes=[
-                pltpu.VMEM((rows_here, LANE_PARTS, cols, 128), F32),
-            ],
         ),
         compiler_params=pltpu.CompilerParams(vmem_limit_bytes=VMEM_LIMIT),
-        cost_estimate=pl.CostEstimate(flops=10_000_000_000, bytes_accessed=4_000_000, transcendentals=0),
+        cost_estimate=pl.CostEstimate(flops=8_000_000_000, bytes_accessed=4_000_000, transcendentals=0),
         name="middle",
-    )(meta, exp, ge2, after, branch, cot, pieces, proj)
-
-
-def leave_kernel(meta, gm, tok, top, bot, after_grad, pieces, kern, out, kern_out, sums_out, buf, ent, gmx, obuf):
+    )(meta, ge2, low, high, after, branch, cot, pieces, proj)
+
+
+def leave_kernel(meta, gm, tok, top, bot, after_grad, pieces, kern, out, kern_out, sums_out, buf, ent, gmx, obuf, nbuf, sbuf):
     latents = pl.num_programs(0)
     latent = pl.program_id(0)
     rows_here, cols = tok.shape[1], tok.shape[2]
@@ -547,7 +574,10 @@
         source = top[0, 0] if rr == 0 else bot[0, 0] if rr == rows_here + 1 else tok[0, rr - 1]
         put_row(buf, rr, source.astype(F32))
         for parity in range(2):
-            normed, _ = normalize(get_columns(buf, rr, parity))
+            normed, scaled = normalize(get_columns(buf, rr, parity))
+            if 1 <= rr <= rows_here:
+                nbuf[rr - 1, parity] = normed
+                sbuf[rr - 1, parity] = jnp.broadcast_to(scaled, (half, 128))
             ok = usable_of(meta, latents, latent, row0 + rr - 1, parity, half)
             put_shifts(ent, rr, parity, ((normed * scale + shift) * ok).astype(BF16).astype(F32))
             group = 2 * ((rr + 1) % 2) + parity
@@ -566,7 +596,7 @@
                     tap_sums[t] = tap_sums[t] + sum8(ent[row + i, parity + j] * here)
             ok = usable_of(meta, latents, latent, row0 + row, parity, half)
             grad = total * ok
-            normed, scaled = normalize(get_columns(buf, row + 1, parity))
+            normed, scaled = nbuf[row, parity], sbuf[row, parity, :, 0:1]
             sums[0] = sums[0] + sum8(grad)
             sums[1] = sums[1] + sum8(grad * normed)
             at = (2 * row + parity) * half
@@ -610,6 +640,8 @@
                 pltpu.VMEM((rows_here + 2, 4, half, D), F32),
                 pltpu.VMEM((rows_here + 2, 4, half, D), F32),
                 pltpu.VMEM((rows_here, LANE_PARTS, cols, 128), F32),
+                pltpu.VMEM((rows_here, 2, half, D), F32),
+                pltpu.VMEM((rows_here, 2, half, 128), F32),
             ],
         ),
         compiler_params=pltpu.CompilerParams(vmem_limit_bytes=VMEM_LIMIT),
@@ -625,61 +657,62 @@
     return jnp.where(first, values, zero), jnp.where(first, zero, values)
 
 
-def attend_kernel(mixed, wq, wk, wvt, bias, out, lse_out):
+def attend_kernel(offset, mixed, wq, wk, wvt, bias, out, lse_out, padded):
     tokens = mixed.shape[0]
     strips, window, _ = out.shape
     step = tokens // strips
-    margin = (window - step) // 2
+    margin = window - step
     m = mixed[...]
     query = (mm(m, wq[...]).astype(BF16) * FACTOR).astype(BF16)
     key = mm(m, wk[...]).astype(BF16)
     value_t = mm(wvt[...], m, NT).astype(BF16)
     keep = jnp.tile(bias[...], (1, tokens // 128))
+    scores = [mm(key_e, query, NT) + keep for key_e in pair_parts(key)]
     parts = []
-    for e, key_e in enumerate(pair_parts(key)):
-        scores = mm(key_e, query, NT) + keep
-        peak = jnp.max(scores, axis=0, keepdims=True)
-        raw = jnp.exp(scores - peak)
+    for e in range(2):
+        peak = jnp.max(scores[e], axis=0, keepdims=True)
+        raw = jnp.exp(scores[e] - peak)
         total = jnp.sum(raw, axis=0, keepdims=True)
         prob = (raw * (1.0 / total)).astype(BF16)
         parts.append(mm(value_t[e * HEAD_DIM : (e + 1) * HEAD_DIM], prob))
         lse_out[0, e : e + 1, :] = peak + jnp.log(total)
-    att = jnp.concatenate(parts, axis=0).T.astype(BF16)
-    blank = jnp.zeros((margin, PAIR), BF16)
+    padded[0:margin] = jnp.zeros((margin, PAIR), F32)
+    padded[margin + tokens :] = jnp.zeros((margin, PAIR), F32)
+    padded[margin : margin + tokens] = jnp.concatenate(parts, axis=0).T
     for s in range(strips):
-        low, high = s * step - margin, (s + 1) * step + margin
-        if low < 0:
-            out[s] = jnp.concatenate([blank, att[:high]], axis=0)
-        elif high > tokens:
-            out[s] = jnp.concatenate([att[low:], blank], axis=0)
-        else:
-            out[s] = att[low:high]
-
-
-def attend(mixed, weight, weight_t, bias, strips, window):
+        start = pl.multiple_of(offset[0] + s * step, 8)
+        out[s] = padded[pl.ds(start, window), :].astype(BF16)
+
+
+def attend(offset, mixed, weight, weight_t, bias, strips, window):
     tokens = mixed.shape[0]
+    margin = window - tokens // strips
     return pl.pallas_call(
         attend_kernel,
         out_shape=(
             jax.ShapeDtypeStruct((strips, window, D), BF16),
             jax.ShapeDtypeStruct((PAIRS, 2, tokens), F32),
         ),
-        grid=(PAIRS,),
-        in_specs=[
-            pl.BlockSpec((tokens, D), lambda p: (0, 0)),
-            pl.BlockSpec((D, PAIR), lambda p: (0, p)),
-            pl.BlockSpec((D, PAIR), lambda p: (0, PAIRS + p)),
-            pl.BlockSpec((PAIR, D), lambda p: (2 * PAIRS + p, 0)),
-            pl.BlockSpec((tokens, 128), lambda p: (0, 0)),
-        ],
-        out_specs=(
-            pl.BlockSpec((strips, window, PAIR), lambda p: (0, 0, p)),
-            pl.BlockSpec((1, 2, tokens), lambda p: (p, 0, 0)),
+        grid_spec=pltpu.PrefetchScalarGridSpec(
+            num_scalar_prefetch=1,
+            grid=(PAIRS,),
+            in_specs=[
+                pl.BlockSpec((tokens, D), lambda p, o: (0, 0)),
+                pl.BlockSpec((D, PAIR), lambda p, o: (0, p)),
+                pl.BlockSpec((D, PAIR), lambda p, o: (0, PAIRS + p)),
+                pl.BlockSpec((PAIR, D), lambda p, o: (2 * PAIRS + p, 0)),
+                pl.BlockSpec((tokens, 128), lambda p, o: (0, 0)),
+            ],
+            out_specs=(
+                pl.BlockSpec((strips, window, PAIR), lambda p, o: (0, 0, p)),
+                pl.BlockSpec((1, 2, tokens), lambda p, o: (p, 0, 0)),
+            ),
+            scratch_shapes=[pltpu.VMEM((tokens + 2 * margin, PAIR), F32)],
         ),
         compiler_params=pltpu.CompilerParams(vmem_limit_bytes=VMEM_LIMIT),
         cost_estimate=pl.CostEstimate(flops=16_000_000_000, bytes_accessed=4_000_000, transcendentals=0),
         name="attend",
-    )(mixed, weight, weight, weight_t, bias)
+    )(offset, mixed, weight, weight, weight_t, bias)
 
 
 def attend_back_kernel(offset, query, key, value, key_t, bias, lse, gatt, wq, wk, wv, mixed_t, send_out, keep_out, gm_out, acc, part):
@@ -694,30 +727,30 @@
     keys = pair_parts(key[...])
     values = pair_parts(value[...])
     grads = pair_parts(gatt[...])
-    dk = jnp.zeros((tokens, PAIR), F32)
-    dv = jnp.zeros((tokens, PAIR), F32)
-    parts = []
+    scores = [mm(keys[e], q, NT) for e in range(2)]
+    grad_probs = [mm(values[e], gatt[...], NT) for e in range(2)]
+    parts, probs, grad_scores = [], [], []
     for e in range(2):
-        scores = mm(keys[e], q, NT) * FACTOR + keep
-        prob = jnp.exp(scores - lse[0, e : e + 1, :])
-        grad_prob = mm(values[e], gatt[...], NT)
-        delta = jnp.sum(prob * grad_prob, axis=0, keepdims=True)
-        grad_scores = (prob * (grad_prob - delta)).astype(BF16)
-        dv = dv + mm(prob.astype(BF16), grads[e])
-        dk = dk + mm(grad_scores, queries[e])
-        parts.append(mm(key_t[e * HEAD_DIM : (e + 1) * HEAD_DIM], grad_scores))
-    dq = (jnp.concatenate(parts, axis=0).T * FACTOR).astype(BF16)
-    dk = (dk * FACTOR).astype(BF16)
-    dv = dv.astype(BF16)
+        prob = jnp.exp(scores[e] * FACTOR + keep - lse[0, e : e + 1, :])
+        delta = jnp.sum(prob * grad_probs[e], axis=0, keepdims=True)
+        probs.append(prob.astype(BF16))
+        grad_scores.append((prob * (grad_probs[e] - delta)).astype(BF16))
+        parts.append(mm(key_t[e * HEAD_DIM : (e + 1) * HEAD_DIM], grad_scores[e]))
+    dv = mm(jnp.concatenate(probs, axis=1), jnp.concatenate(grads, axis=0))
+    dk = mm(jnp.concatenate(grad_scores, axis=1), jnp.concatenate(queries, axis=0))
+    dq = jnp.concatenate(parts, axis=0).T * FACTOR
+    dk = dk * FACTOR
+    all_three = jnp.concatenate([dq.astype(BF16), dk.astype(BF16), dv.astype(BF16)], axis=1)
+    part[...] = mm(mixed_t[...], all_three)
     size = D // 4
-    for k, grad in enumerate((dq, dk, dv)):
-        part[k] = mm(mixed_t[...], grad)
-        for y in range(2):
-            mine = pl.multiple_of((2 * y + offset[1]) * size, 8)
-            other = pl.multiple_of((2 * y + 1 - offset[1]) * size, 8)
-            keep_out[k, y] = part[k, pl.ds(mine, size), :].astype(BF16)
-            send_out[k, y] = part[k, pl.ds(other, size), :].astype(BF16)
-    total = mm(dq, wq[...], NT) + mm(dk, wk[...], NT) + mm(dv, wv[...], NT)
+    for y in range(2):
+        mine = pl.multiple_of((2 * y + offset[1]) * size, 8)
+        other = pl.multiple_of((2 * y + 1 - offset[1]) * size, 8)
+        for k in range(3):
+            cut = slice(k * PAIR, (k + 1) * PAIR)
+            keep_out[k, y] = part[pl.ds(mine, size), cut].astype(BF16)
+            send_out[k, y] = part[pl.ds(other, size), cut].astype(BF16)
+    total = mm(all_three, jnp.concatenate([wq[...], wk[...], wv[...]], axis=1), NT)
 
     @pl.when(p == 0)
     def _():
@@ -773,7 +806,7 @@
             ),
             scratch_shapes=[
                 pltpu.VMEM((tokens + 2 * margin, D), F32),
-                pltpu.VMEM((3, D, PAIR), F32),
+                pltpu.VMEM((D, 3 * PAIR), F32),
             ],
         ),
         compiler_params=pltpu.CompilerParams(vmem_limit_bytes=VMEM_LIMIT),
@@ -859,6 +892,13 @@
         own.append(lax.dynamic_index_in_dim(part, batch_place, 0, keepdims=False))
         at += piece.shape[1]
     return common_all, own
+
+
+def windows_of(values, offset, margin, strips):
+    step = values.shape[0] // strips
+    padded = jnp.pad(values, ((margin, margin), (0, 0)))
+    base = lax.dynamic_slice_in_dim(padded, offset, values.shape[0] + margin)
+    return jnp.stack([base[s * step : s * step + step + margin] for s in range(strips)])
 
 
 def attend_plain(mixed, weight, ok, heads):
@@ -945,11 +985,6 @@
     grouped = swap(sent).reshape(group_tokens, D)
 
     weight_t = qkv_weight.T
-    low_rows = jnp.stack([tokens[:, rows_here - 2 : rows_here - 1], cotangent[:, rows_here - 1 :]])
-    high_rows = jnp.stack([tokens[:, 1:2], cotangent[:, :1]])
-    low_rows, high_rows, grouped = lax.optimization_barrier((low_rows, high_rows, grouped))
-    top_two, cot_top = from_before(low_rows, "seq")
-    bot_two, cot_bot = from_after(high_rows, "seq")
 
     my_block = seq_place // share
     my_latent = my_block // 4
@@ -963,13 +998,11 @@
     key_ok = (key_row < height) & (key_col < width)
 
     margin = half
-    window = per_group + 2 * margin
+    tall = per_group + margin
+    offset = jnp.stack([margin * (1 - my_a), batch_place % 2]).astype(jnp.int32)
     if share == 1:
         bias = jnp.broadcast_to(jnp.where(key_ok, 0.0, -1e30)[:, None], (group_tokens, 128))
-        windows, lse = attend(grouped, qkv_weight, weight_t, bias, seq_count, window)
-        windows, top_two, bot_two, cot_top, cot_bot = lax.optimization_barrier(
-            (windows, top_two, bot_two, cot_top, cot_bot)
-        )
+        windows, lse = attend(offset, grouped, qkv_weight, weight_t, bias, seq_count, tall)
         attended = swap(windows)
     else:
         heads = HEADS // share
@@ -978,14 +1011,11 @@
         thirds = qkv_weight.reshape(D, 3, share, wide)
         my_weight = lax.dynamic_index_in_dim(thirds, chunk, 2, keepdims=False).reshape(D, 3 * wide)
         att, saved = attend_plain(grouped, my_weight, key_ok, heads)
-        att = jnp.pad(att, ((margin, margin), (0, 0)))
-        windows = jnp.stack(
-            [att[s * per_group : s * per_group + window] for s in range(seq_count)]
-        )
-        attended = swap(windows).reshape(blocks, share, window, wide)
-        attended = attended.transpose(0, 2, 1, 3).reshape(blocks, window, D)
-
-    ge, get, cot_split = prepare_cot(meta, cotangent, cot_top, cot_bot, pieces)
+        windows = windows_of(att, offset[0], margin, seq_count)
+        attended = swap(windows).reshape(blocks, share, tall, wide)
+        attended = attended.transpose(0, 2, 1, 3).reshape(blocks, tall, D)
+
+    ge, get, cot_split = prepare_cot(cotangent, pieces)
     conditions = lax.all_gather(
         jnp.concatenate([condition, embedding.astype(F32), class_ids.astype(F32)[:, None]], axis=1),
         "batch",
@@ -999,7 +1029,7 @@
             (attended, ge, triple, key_t, grouped_t, conditions)
         )
     e2, e2t, after_attn, branch = second(
-        meta, attended, tokens, (top, top_two), (bot, bot_two), pieces, proj_weight
+        meta, attended, tokens, top, bot, pieces, proj_weight
     )
     expanded, grad_e2, send_c, keep_c, conv_ffn_part = ffn(
         core, e2, e2t, ge, get, up_weight, down_weight, conv_ffn, cols
@@ -1007,15 +1037,18 @@
     halving = batch_count == 4 and seq_count == 8
     if halving:
         got_c = hop(send_c, "c")
-    output, grad_after, grad_branch, grad_attended, mid_sums = middle(
-        meta, expanded, grad_e2, after_attn, branch, cot_split, pieces, proj_weight, rows_here, cols
+    low = from_before(grad_e2[:, cols * (rows_here + 1) :].astype(BF16), "seq")
+    high = from_after(grad_e2[:, :cols].astype(BF16), "seq")
+    output, gate_sums = finish_output(expanded, after_attn, cot_split, pieces, rows_here, cols)
+    grad_after, grad_branch, grad_attended, mid_sums = middle(
+        meta, grad_e2, low, high, after_attn, branch, cot_split, pieces, proj_weight
     )
 
-    att_own = after(attended, grad_attended)[:, margin : margin + per_group]
-    att_own = att_own.reshape(blocks * per_group, D)
+    att_all = after(attended, grad_attended)
+    starts = [margin * ((k // 2) % 2) for k in range(blocks)]
+    att_own = jnp.concatenate([att_all[k, at : at + per_group] for k, at in enumerate(starts)])
     flat_branch = grad_branch.reshape(blocks * per_group, D)
     hidden = conv_ffn.shape[1]
-    tall = per_group + margin
     if share == 1:
         gatt = swap(grad_attended.reshape(seq_count, per_group, D)).reshape(group_tokens, D)
         if halving:
@@ -1029,7 +1062,6 @@
             got_p = hop(send_p, "c")
             gatt, send_a, send_b, send_p = lax.optimization_barrier((gatt, send_a, send_b, send_p))
             got_a, got_b = hop(send_a, "y"), hop(send_b, "x")
-        offset = jnp.stack([margin * (1 - my_a), batch_place % 2]).astype(jnp.int32)
         send_r, keep_r, gm_windows = attend_back(
             offset, triple, key_t, bias, lse, gatt, qkv_weight, grouped_t, seq_count, tall
         )
@@ -1041,11 +1073,7 @@
         sent = grad_attended.reshape(blocks, per_group, share, wide).transpose(0, 2, 1, 3)
         gatt = swap(sent.reshape(seq_count, per_group, wide)).reshape(group_tokens, wide)
         grad_triple, gm_part = attend_plain_back(saved, gatt, my_weight)
-        base = jnp.pad(gm_part.astype(BF16), ((margin, margin), (0, 0)))
-        base = lax.dynamic_slice_in_dim(base, margin * (1 - my_a), group_tokens + margin)
-        gm_windows = jnp.stack(
-            [base[s * per_group : s * per_group + tall] for s in range(seq_count)]
-        )
+        gm_windows = windows_of(gm_part.astype(BF16), offset[0], margin, seq_count)
         gm = swap(gm_windows).reshape(blocks, share, tall, D)
         gm = jnp.sum(gm.astype(F32), axis=1).astype(BF16)
         own_grad = mm(grouped, grad_triple, (((0,), (0,)), ((), ()))).astype(BF16)
@@ -1092,7 +1120,7 @@
     )
 
     all_sums, (conv_attn_grad, conv_ffn_grad) = sum_and_gather(
-        jnp.concatenate([end_sums, mid_sums], axis=1),
+        jnp.concatenate([end_sums, mid_sums, gate_sums], axis=1),
         (jnp.sum(conv_attn_part, axis=0), conv_ffn_part),
     )
     if halving:

time: 334 us -> 328 us (0.982)
  waiting for transfers between devices: 77.2 us -> 71.1 us
  Pallas kernels: 114 us -> 109 us
    all_to_all x5, waiting for transfers between devices: 54.5 us -> 47 us  [swap(): return lax.all_to_all(values, 'seq', 0, 0, tiled=False)]
    pallas_call x2 -> x3, Pallas kernels: 12.1 us -> 14.1 us  [the longest x1 8.37 us: middle(): pl.pallas_call(middle_kernel, out_shape=(jax.ShapeDtypeStruct((latents, o...]
    unnamed x55 -> x64, local copies, waits for them, and re-layouts: 10.9 us -> 12.5 us
  transfers between devices with their start and end apart: 24 -> 24, of which waited for: 10 -> 12; matrix products, arithmetic and copies ran while one was open for 20% -> 21% of each run, Pallas kernels for 18% -> 14%
where the time goes in v4:
time: 328 us; the launch traced here: 325 us
  Pallas kernels  109 us (33%)
  waiting for transfers between devices  71.1 us (22%)
  starting transfers between devices  54.6 us (17%)
  local copies, waits for them, and re-layouts  30.6 us (9%)
  other arithmetic  25.9 us (8%)
  matrix products  20.9 us (6%)
  blocking collectives  11.1 us (3%)
    all_to_all x5, waiting for transfers between devices, swap(): return lax.all_to_all(values, 'seq', 0, 0, tiled=False)  47 us
    pallas_call x1, Pallas kernels, ffn(): pl.pallas_call(ffn_kernel, out_shape=(jax.ShapeDtypeStruct((latents, own,...  39.6 us
    all_to_all x5, starting transfers between devices, swap(): return lax.all_to_all(values, 'seq', 0, 0, tiled=False)  25.6 us
    pallas_call x1, Pallas kernels, attend_back(): pl.pallas_call(attend_back_kernel, out_shape=(parts, parts, jax.ShapeDtyp...  21.9 us
    ppermute x15, waiting for transfers between devices, hop(): return lax.ppermute(values, axis, [(i, i ^ mask) for i in range(count)])  20.8 us
    ppermute x15, starting transfers between devices, hop(): return lax.ppermute(values, axis, [(i, i ^ mask) for i in range(count)])  18.2 us
    dot_general x7, matrix products, mm(): return lax.dot_general(left, right, dims, preferred_element_type=F32)  17.8 us
    pallas_call x1, Pallas kernels, attend(): pl.pallas_call(attend_kernel, out_shape=(jax.ShapeDtypeStruct((strips, wi...  13.8 us
  transfers between devices with their start and end apart: 24, of which 12 were waited for; matrix products, arithmetic and copies ran while one was open for 21% of the time, Pallas kernels for 14%

profile of v4, /device:TPU:0, one launch (start us, length us, event | category | flops | bytes accessed | tf_op | source)
XLA Modules:
  0.0 324.8 jit_solution(13179345400257653084)
XLA Ops:
  1.8 4.9 %collective-permute-start = (bf16[2,1,64,768]{3,2,1,0:T(8,128)(2,1)S(1)}, bf16[2,1,64,768]{3,2,1,0:T(8,128)(2,1)S(1)}, u32[]{:S(2)}, u32[]{:S(2)}) collective-permute-start(bf16[2,1,64,768]{3,2,1,0:T(8,128)(2,1)S(1)} %get-tuple-element.126), channel_id=1, source_target_pairs={{0,1},{1,2},{2,3},{3,4},{4,5},{5,6},{6,7},{8,9},{9,10},{10,11},{11... | collective-permute-start | bytes 589832 | tf_op jit(solution)/shard_map/ppermute | solution.py:820
  10.4 4.0 %convolution_add_fusion = f32[2,4608]{1,0:T(2,128)S(1)} fusion(bf16[768,4608]{1,0:T(8,128)(2,1)} %param.24, f32[4608]{0:T(1024)S(1)} %copy-done.16, f32[2,768]{1,0:T(2,128)S(1)} %convolution_add_fusion.1), kind=kOutput, calls=%fused_computation.1 | convolution fusion | flops 14172672 | bytes 7139328 | tf_op jit(solution)/shard_map/dot_general | solution.py:29
  17.6 5.1 %enter.1 = bf16[2,4,64,768]{3,2,1,0:T(8,128)(2,1)} custom-call(s32[5]{0:T(128)} %pad_add_fusion.meta, bf16[2,4,64,768]{3,2,1,0:T(8,128)(2,1)} %tok.5, bf16[2,1,64,768]{3,2,1,0:T(8,128)(2,1)} %copy-done.22, bf16[2,1,64,768]{3,2,1,0:T(8,128)(2,1)} %copy-done.23, f32[2,6,768]{2,1,0:T(8,128)} %reshape.139.pieces, f32[9,768]{1,0:T(8,128)} %convert_element_type.185.kern), custom_call_target="tpu_custom_call" | custom-call | flops 6000000000 | bytes 4000000 | tf_op jit(solution)/shard_map/enter/pallas_call | solution.py:133
  22.7 7.0 %all-to-all-start = ((bf16[8,64,768]{2,1,0:T(8,128)(2,1)}), bf16[8,64,768]{2,1,0:T(8,128)(2,1)S(1)}, u32[]{:S(2)}, u32[]{:S(2)}) async-start(bf16[8,64,768]{2,1,0:T(8,128)(2,1)} %bitcast.171), calls=%async_computation | async-start | bytes 1572864 | tf_op jit(solution)/shard_map/all_to_all | solution.py:829
  30.8 5.7 %copy.78 = bf16[768,2304]{0,1:T(8,128)(2,1)} copy(bf16[768,2304]{1,0:T(8,128)(2,1)} %wv.1) | data formatting | bytes 7077888 | tf_op args[11]
  38.5 10.9 %all-to-all-done = bf16[8,64,768]{2,1,0:T(8,128)(2,1)S(1)} async-done(((bf16[8,64,768]{2,1,0:T(8,128)(2,1)}), bf16[8,64,768]{2,1,0:T(8,128)(2,1)S(1)}, u32[]{:S(2)}, u32[]{:S(2)}) %all-to-all-start) | async-done | bytes 786464 | tf_op jit(solution)/shard_map/all_to_all | solution.py:829
  50.3 13.8 %attend.1 = (bf16[8,96,768]{2,1,0:T(8,128)(2,1)}, f32[6,2,512]{2,1,0:T(2,128)}) custom-call(s32[2]{0:T(128)} %pad_add_fusion.1.offset, bf16[512,768]{1,0:T(8,128)(2,1)} %bitcast.161, bf16[768,2304]{1,0:T(8,128)(2,1)} %wv.1, bf16[768,2304]{1,0:T(8,128)(2,1)} %wv.1, bf16[2304,768]{1,0:T(8,128)(2,1)} %bitcast.159, f32[512,128]{1,0:T(8,128)} %broadcast_in_dim.18.bias), custom_call_target="tpu_custom_call" | custom-call | flops 16000000000 | bytes 4000000 | tf_op jit(solution)/shard_map/attend/pallas_call | solution.py:690
  64.1 3.6 %all-to-all-start.1 = ((bf16[8,96,768]{2,1,0:T(8,128)(2,1)}), bf16[8,96,768]{2,1,0:T(8,128)(2,1)S(1)}, u32[]{:S(2)}, u32[]{:S(2)}) async-start(bf16[8,96,768]{2,1,0:T(8,128)(2,1)} %get-tuple-element.61), calls=%async_computation.1 | async-start | bytes 2359296 | tf_op jit(solution)/shard_map/all_to_all | solution.py:829
  67.8 5.4 %all-gather.2 = f32[4,2,1025]{2,1,0:T(2,128)S(1)} all-gather(f32[1,2,1025]{2,1,0:T(2,128)S(1)} %maximum_bitcast_fusion), channel_id=2, replica_groups=mesh['batch'=4,'seq'=8] {'batch'}, dimensions={0}, use_global_device_ids=true | all-gather | bytes 41000 | tf_op jit(solution)/shard_map/all_gather | solution.py:1019
  73.2 2.6 prepare_cot.1
  77.1 3.1 fusion.key_t
  80.2 3.4 %convolution_convert_fusion.query.key.value = bf16[512,2304]{1,0:T(8,128)(2,1)} fusion(bf16[512,768]{1,0:T(8,128)(2,1)S(1)} %bitcast.164, bf16[768,2304]{1,0:T(8,128)(2,1)S(1)} %copy-done.3), kind=kOutput, calls=%fused_computation.2 | convolution fusion | flops 1813118976 | bytes 6684672 | tf_op jit(solution)/shard_map/dot_general | solution.py:29
  83.6 12.8 %all-to-all-done.1.att = bf16[8,96,768]{2,1,0:T(8,128)(2,1)S(1)} async-done(((bf16[8,96,768]{2,1,0:T(8,128)(2,1)}), bf16[8,96,768]{2,1,0:T(8,128)(2,1)S(1)}, u32[]{:S(2)}, u32[]{:S(2)}) %all-to-all-start.1) | async-done | bytes 1179680 | tf_op jit(solution)/shard_map/all_to_all | solution.py:829
  97.4 6.5 %second.1 = (bf16[2,384,768]{2,1,0:T(8,128)(2,1)}, bf16[2,768,384]{2,1,0:T(8,128)(2,1)}, f32[2,256,768]{2,1,0:T(8,128)}, f32[2,256,768]{2,1,0:T(8,128)}) custom-call(s32[5]{0:T(128)} %pad_add_fusion.meta, bf16[8,96,768]{2,1,0:T(8,128)(2,1)} %copy-done.4, bf16[2,4,64,768]{3,2,1,0:T(8,128)(2,1)} %tok.5, bf16[2,1,64,768]{3,2,1,0:T(8,128)(2,1)} %copy-done.22, ...), custom_call_target="tpu_custom_call" | custom-call | flops 7000000000 | bytes 4000000 | tf_op jit(solution)/shard_map/second/pallas_call | solution.py:227
  103.9 39.6 %ffn.1 = (f32[2,256,768]{2,1,0:T(8,128)}, f32[2,384,768]{2,1,0:T(8,128)}, bf16[2,2,192,3072]{3,2,1,0:T(8,128)(2,1)}, bf16[2,2,192,3072]{3,2,1,0:T(8,128)(2,1)}, f32[9,3072]{1,0:T(8,128)}) custom-call(s32[1]{0:T(128)} %bitcast.core, bf16[2,384,768]{2,1,0:T(8,128)(2,1)} %get-tuple-element.64.e2, bf16[2,768,384]{2,1,0:T(8,128)(2,1)} %get-tuple-element.65.e2t, ...), custom_call_target="tpu_custom_call" | custom-call | flops 35000000512 | bytes 4000000 | tf_op jit(solution)/shard_map/ffn/pallas_call | solution.py:410
  145.6 3.4 %collective-permute-start.2 = (bf16[2,64,768]{2,1,0:T(8,128)(2,1)S(1)}, bf16[2,64,768]{2,1,0:T(8,128)(2,1)S(1)}, u32[]{:S(2)}, u32[]{:S(2)}) collective-permute-start(bf16[2,64,768]{2,1,0:T(8,128)(2,1)S(1)} %get-tuple-element.124), channel_id=1, source_target_pairs={{0,1},{1,2},{2,3},{3,4},{4,5},{5,6},{6,7},{8,9},{9,10},{10,11},{11... | collective-permute-start | bytes 589832 | tf_op jit(solution)/shard_map/ppermute | solution.py:820
  150.2 3.1 finish_output.1
  154.5 3.3 %collective-permute-done.2.low = bf16[2,64,768]{2,1,0:T(8,128)(2,1)S(1)} collective-permute-done((bf16[2,64,768]{2,1,0:T(8,128)(2,1)S(1)}, bf16[2,64,768]{2,1,0:T(8,128)(2,1)S(1)}, u32[]{:S(2)}, u32[]{:S(2)}) %collective-permute-start.2) | collective-permute-done | bytes 196640 | tf_op jit(solution)/shard_map/ppermute | solution.py:820
  158.5 8.4 %middle.1 = (f32[2,256,768]{2,1,0:T(8,128)}, bf16[2,4,64,768]{3,2,1,0:T(8,128)(2,1)}, bf16[2,4,64,768]{3,2,1,0:T(8,128)(2,1)}, f32[2,3,768]{2,1,0:T(4,128)}) custom-call(s32[5]{0:T(128)} %pad_add_fusion.meta, f32[2,384,768]{2,1,0:T(8,128)} %get-tuple-element.75.ge2, bf16[2,64,768]{2,1,0:T(8,128)(2,1)} %copy-done.24, bf16[2,64,768]{2,1,0:T(8,128)(2,1)} %copy-done.25, ...), custom_call_target="tpu_custom_call" | custom-call | flops 8000000000 | bytes 4000000 | tf_op jit(solution)/shard_map/middle/pallas_call | solution.py:530
  166.9 5.0 %all-to-all-start.2 = ((bf16[8,64,768]{2,1,0:T(8,128)(2,1)}), bf16[8,64,768]{2,1,0:T(8,128)(2,1)S(1)}, u32[]{:S(2)}, u32[]{:S(2)}) async-start(bf16[8,64,768]{2,1,0:T(8,128)(2,1)} %bitcast.173), calls=%async_computation.2 | async-start | bytes 1572864 | tf_op jit(solution)/shard_map/all_to_all | solution.py:829
  174.8 5.7 %add_convert_fusion = bf16[2,2,192,3072]{3,2,1,0:T(8,128)(2,1)S(1)} fusion(bf16[2,2,192,3072]{3,2,1,0:T(8,128)(2,1)} %collective-permute-done.4, bf16[2,2,192,3072]{3,2,1,0:T(8,128)(2,1)} %get-tuple-element.79), kind=kLoop, calls=%fused_computation | loop fusion | flops 9437184 | bytes 14155776 | tf_op jit(solution)/shard_map/convert_element_type | solution.py:1056
  183.3 9.0 %all-to-all-done.2 = bf16[8,64,768]{2,1,0:T(8,128)(2,1)S(1)} async-done(((bf16[8,64,768]{2,1,0:T(8,128)(2,1)}), bf16[8,64,768]{2,1,0:T(8,128)(2,1)S(1)}, u32[]{:S(2)}, u32[]{:S(2)}) %all-to-all-start.2) | async-done | bytes 786464 | tf_op jit(solution)/shard_map/all_to_all | solution.py:829
  195.3 21.9 %attend_back.1 = (bf16[3,2,192,768]{3,2,1,0:T(8,128)(2,1)}, bf16[3,2,192,768]{3,2,1,0:T(8,128)(2,1)}, bf16[8,96,768]{2,1,0:T(8,128)(2,1)}) custom-call(s32[2]{0:T(128)} %pad_add_fusion.1.offset, bf16[512,2304]{1,0:T(8,128)(2,1)} %convolution_convert_fusion.query.key.value, bf16[512,2304]{1,0:T(8,128)(2,1)} %convolution_convert_fusion.query.key.value, ...), custom_call_target="tpu_custom_call" | custom-call | flops 23000000512 | bytes 4000000 | tf_op jit(solution)/shard_map/attend_back/pallas_call | solution.py:779
  220.5 4.8 %all-to-all-start.3 = ((bf16[8,96,768]{2,1,0:T(8,128)(2,1)}), bf16[8,96,768]{2,1,0:T(8,128)(2,1)}, u32[]{:S(2)}, u32[]{:S(2)}) async-start(bf16[8,96,768]{2,1,0:T(8,128)(2,1)} %get-tuple-element.89), calls=%async_computation.3 | async-start | bytes 2359296 | tf_op jit(solution)/shard_map/all_to_all | solution.py:829
  239.0 14.3 %all-to-all-done.3.gm = bf16[8,96,768]{2,1,0:T(8,128)(2,1)} async-done(((bf16[8,96,768]{2,1,0:T(8,128)(2,1)}), bf16[8,96,768]{2,1,0:T(8,128)(2,1)}, u32[]{:S(2)}, u32[]{:S(2)}) %all-to-all-start.3) | async-done | bytes 1179680 | tf_op jit(solution)/shard_map/all_to_all | solution.py:829
  253.3 8.3 %leave.1 = (f32[2,4,64,768]{3,2,1,0:T(8,128)}, f32[2,9,768]{2,1,0:T(8,128)}, f32[2,2,768]{2,1,0:T(2,128)}) custom-call(s32[5]{0:T(128)} %pad_add_fusion.meta, bf16[8,96,768]{2,1,0:T(8,128)(2,1)} %all-to-all-done.3.gm, bf16[2,4,64,768]{3,2,1,0:T(8,128)(2,1)} %tok.5, bf16[2,1,64,768]{3,2,1,0:T(8,128)(2,1)} %copy-done.22, bf16[2,1,64,768]{3,2,1,0:T(8,128)(2,1)} %copy-done.23, ...), custom_call_target="tpu_custom_call" | custom-call | flops 10000000000 | bytes 4000000 | tf_op jit(solution)/shard_map/leave/pallas_call | solution.py:618
  278.5 5.3 %all-to-all-start.4 = ((f32[8,112,128]{2,1,0:T(8,128)}), f32[8,112,128]{2,1,0:T(8,128)S(1)}, u32[]{:S(2)}, u32[]{:S(2)}) async-start(f32[8,112,128]{2,1,0:T(8,128)} %bitcast.153), calls=%async_computation.4 | async-start | bytes 917504 | tf_op jit(solution)/shard_map/all_to_all | solution.py:829
  285.3 3.4 %collective-permute-start.14 = (bf16[4,24,768]{2,1,0:T(8,128)(2,1)S(1)}, bf16[4,24,768]{2,1,0:T(8,128)(2,1)S(1)}, u32[]{:S(2)}, u32[]{:S(2)}) collective-permute-start(bf16[4,24,768]{2,1,0:T(8,128)(2,1)S(1)} %dynamic-slice_bitcast_fusion.12), channel_id=1, source_target_pairs={{0,4},{1,5},{2,6},{3,7},{4,0},{5,1},{6,2},{7,3},{8,12},{9,13},{10,... | collective-permute-start | bytes 442376 | tf_op jit(solution)/shard_map/ppermute | solution.py:852
  288.6 13.0 %collective-permute-done.17 = bf16[2,2,24,3072]{3,2,1,0:T(8,128)(2,1)S(1)} collective-permute-done((bf16[2,2,24,3072]{3,2,1,0:T(8,128)(2,1)}, bf16[2,2,24,3072]{3,2,1,0:T(8,128)(2,1)S(1)}, u32[]{:S(2)}, u32[]{:S(2)}) %collective-permute-start.17) | collective-permute-done | bytes 589856 | tf_op jit(solution)/shard_map/ppermute | solution.py:852
  301.8 3.9 %collective-permute-start.18 = (bf16[2,24,3072]{2,1,0:T(8,128)(2,1)S(1)}, bf16[2,24,3072]{2,1,0:T(8,128)(2,1)S(1)}, u32[]{:S(2)}, u32[]{:S(2)}) collective-permute-start(bf16[2,24,3072]{2,1,0:T(8,128)(2,1)S(1)} %dynamic-slice_bitcast_fusion.9), channel_id=1, source_target_pairs={{0,4},{1,5},{2,6},{3,7},{4,0},{5,1},{6,2},{7,3},{8,12},{9,13},{10,... | collective-permute-start | bytes 884744 | tf_op jit(solution)/shard_map/ppermute | solution.py:852
  307.2 5.7 %all-gather.1 = f32[448,128]{1,0:T(8,128)S(1)} all-gather(f32[112,128]{1,0:T(8,128)S(1)} %reduce_sum.46), channel_id=3, replica_groups=mesh['batch'=4,'seq'=8] {'batch'}, dimensions={0}, use_global_device_ids=true | all-gather | bytes 286720 | tf_op jit(solution)/shard_map/all_gather | solution.py:885
  313.2 4.9 %fusion.20 = f32[24,768]{1,0:T(8,128)S(1)} fusion(bf16[768,4608]{1,0:T(8,128)(2,1)} %param.24, bf16[8,4608]{1,0:T(8,128)(2,1)S(1)} %get-tuple-element.134, bf16[8,4608]{1,0:T(8,128)(2,1)S(1)} %get-tuple-element.135, bf16[8,4608]{1,0:T(8,128)(2,1)S(1)} %get-tuple-element.133), kind=kOutput, calls=%fused_computation.73 | convolution fusion | flops 170532864 | bytes 7372800 | tf_op jit(solution)/shard_map/dot_general | solution.py:29
  (186 shorter events, 71.7 us)
Async XLA Ops:
  0.6 9.3 %copy-start = (bf16[1000,768]{1,0:T(8,128)(2,1)S(1)}, bf16[1000,768]{1,0:T(8,128)(2,1)}, u32[]{:S(2)}) copy-start(bf16[1000,768]{1,0:T(8,128)(2,1)} %param.23) | copy-start | bytes 4608004
  0.7 9.3 %copy-start.19 = (s32[2]{0:T(128)S(1)}, s32[2]{0:T(128)}, u32[]{:S(2)}) copy-start(s32[2]{0:T(128)} %param.19) | copy-start | bytes 28
  0.7 9.7 %copy-start.16 = (f32[4608]{0:T(1024)S(1)}, f32[4608]{0:T(1024)}, u32[]{:S(2)}) copy-start(f32[4608]{0:T(1024)} %param.25) | copy-start | bytes 55300
  1.8 14.4 %collective-permute-start = (bf16[2,1,64,768]{3,2,1,0:T(8,128)(2,1)S(1)}, bf16[2,1,64,768]{3,2,1,0:T(8,128)(2,1)S(1)}, u32[]{:S(2)}, u32[]{:S(2)}) collective-permute-start(bf16[2,1,64,768]{3,2,1,0:T(8,128)(2,1)S(1)} %get-tuple-element.126), channel_id=1, source_target_pairs={{0,1},{1,2},{2,3},{3,4},{4,5},{5,6},{6,7},{8,9},{9,10},{10,11},{11... | collective-permute-start | bytes 589832 | tf_op jit(solution)/shard_map/ppermute | solution.py:820
  6.7 9.6 %collective-permute-start.1 = (bf16[2,1,64,768]{3,2,1,0:T(8,128)(2,1)S(1)}, bf16[2,1,64,768]{3,2,1,0:T(8,128)(2,1)S(1)}, u32[]{:S(2)}, u32[]{:S(2)}) collective-permute-start(bf16[2,1,64,768]{3,2,1,0:T(8,128)(2,1)S(1)} %get-tuple-element.125), channel_id=1, source_target_pairs={{1,0},{2,1},{3,2},{4,3},{5,4},{6,5},{7,6},{9,8},{10,9},{11,10},{12... | collective-permute-start | bytes 589832 | tf_op jit(solution)/shard_map/ppermute | solution.py:825
  10.3 4.7 %copy-start.14 = (bf16[9,768]{1,0:T(8,128)(2,1)S(1)}, bf16[9,768]{1,0:T(8,128)(2,1)}, u32[]{:S(2)}) copy-start(bf16[9,768]{1,0:T(8,128)(2,1)} %param.26) | copy-start | bytes 41476
  10.3 5.4 %copy-start.20 = (s32[2]{0:T(128)S(1)}, s32[2]{0:T(128)}, u32[]{:S(2)}) copy-start(s32[2]{0:T(128)} %param.21) | copy-start | bytes 28
  10.4 5.3 %copy-start.21 = (s32[2]{0:T(128)S(1)}, s32[2]{0:T(128)}, u32[]{:S(2)}) copy-start(s32[2]{0:T(128)} %param.20) | copy-start | bytes 28
  22.7 26.6 %all-to-all-start = ((bf16[8,64,768]{2,1,0:T(8,128)(2,1)}), bf16[8,64,768]{2,1,0:T(8,128)(2,1)S(1)}, u32[]{:S(2)}, u32[]{:S(2)}) async-start(bf16[8,64,768]{2,1,0:T(8,128)(2,1)} %bitcast.171), calls=%async_computation | async-start | bytes 1572864 | tf_op jit(solution)/shard_map/all_to_all | solution.py:829
  64.1 32.3 %all-to-all-start.1 = ((bf16[8,96,768]{2,1,0:T(8,128)(2,1)}), bf16[8,96,768]{2,1,0:T(8,128)(2,1)S(1)}, u32[]{:S(2)}, u32[]{:S(2)}) async-start(bf16[8,96,768]{2,1,0:T(8,128)(2,1)} %get-tuple-element.61), calls=%async_computation.1 | async-start | bytes 2359296 | tf_op jit(solution)/shard_map/all_to_all | solution.py:829
  143.5 28.5 %collective-permute-start.4 = (bf16[2,2,192,3072]{3,2,1,0:T(8,128)(2,1)}, bf16[2,2,192,3072]{3,2,1,0:T(8,128)(2,1)}, u32[]{:S(2)}, u32[]{:S(2)}) collective-permute-start(bf16[2,2,192,3072]{3,2,1,0:T(8,128)(2,1)} %get-tuple-element.80), channel_id=1, source_target_pairs={{0,8},{8,0},{16,24},{24,16},{1,9},{9,1},{17,25},{25,17},{2,10},{10... | collective-permute-start | bytes 14155784 | tf_op jit(solution)/shard_map/ppermute | solution.py:852
  145.6 12.2 %collective-permute-start.2 = (bf16[2,64,768]{2,1,0:T(8,128)(2,1)S(1)}, bf16[2,64,768]{2,1,0:T(8,128)(2,1)S(1)}, u32[]{:S(2)}, u32[]{:S(2)}) collective-permute-start(bf16[2,64,768]{2,1,0:T(8,128)(2,1)S(1)} %get-tuple-element.124), channel_id=1, source_target_pairs={{0,1},{1,2},{2,3},{3,4},{4,5},{5,6},{6,7},{8,9},{9,10},{10,11},{11... | collective-permute-start | bytes 589832 | tf_op jit(solution)/shard_map/ppermute | solution.py:820
  148.9 8.9 %collective-permute-start.3 = (bf16[2,64,768]{2,1,0:T(8,128)(2,1)S(1)}, bf16[2,64,768]{2,1,0:T(8,128)(2,1)S(1)}, u32[]{:S(2)}, u32[]{:S(2)}) collective-permute-start(bf16[2,64,768]{2,1,0:T(8,128)(2,1)S(1)} %get-tuple-element.123), channel_id=1, source_target_pairs={{1,0},{2,1},{3,2},{4,3},{5,4},{6,5},{7,6},{9,8},{10,9},{11,10},{12... | collective-permute-start | bytes 589832 | tf_op jit(solution)/shard_map/ppermute | solution.py:825
  166.9 5.0 %copy-start.5 = (bf16[8,96,768]{2,1,0:T(8,128)(2,1)S(1)}, bf16[8,96,768]{2,1,0:T(8,128)(2,1)}, u32[]{:S(2)}) copy-start(bf16[8,96,768]{2,1,0:T(8,128)(2,1)} %copy-done.4) | copy-start | bytes 3538948
  166.9 25.4 %all-to-all-start.2 = ((bf16[8,64,768]{2,1,0:T(8,128)(2,1)}), bf16[8,64,768]{2,1,0:T(8,128)(2,1)S(1)}, u32[]{:S(2)}, u32[]{:S(2)}) async-start(bf16[8,64,768]{2,1,0:T(8,128)(2,1)} %bitcast.173), calls=%async_computation.2 | async-start | bytes 1572864 | tf_op jit(solution)/shard_map/all_to_all | solution.py:829
  173.8 6.7 %copy-start.9 = (bf16[768,768]{1,0:T(8,128)(2,1)}, bf16[768,768]{1,0:T(8,128)(2,1)S(1)}, u32[]{:S(2)}) copy-start(bf16[768,768]{1,0:T(8,128)(2,1)S(1)} %convolution_convert_fusion.1) | copy-start | bytes 3538948
  174.8 42.4 %collective-permute-start.8 = (bf16[2,2,2,2,24,768]{5,4,3,2,1,0:T(8,128)(2,1)}, bf16[2,2,2,2,24,768]{5,4,3,2,1,0:T(8,128)(2,1)}, u32[]{:S(2)}, u32[]{:S(2)}) collective-permute-start(bf16[2,2,2,2,24,768]{5,4,3,2,1,0:T(8,128)(2,1)} %dynamic-slice_bitcast_fusion.8), channel_id=1, source_target_pairs={{0,8},{8,0},{16,24},{24,16},{1,9},{9,1},{17,25},{25,17},{2,10},{10... | collective-permute-start | bytes 1769480 | tf_op jit(solution)/shard_map/ppermute | solution.py:852
  192.3 26.9 %collective-permute-start.5 = (bf16[2,2,2,24,3072]{4,3,2,1,0:T(8,128)(2,1)}, bf16[2,2,2,24,3072]{4,3,2,1,0:T(8,128)(2,1)}, u32[]{:S(2)}, u32[]{:S(2)}) collective-permute-start(bf16[2,2,2,24,3072]{4,3,2,1,0:T(8,128)(2,1)} %get-tuple-element.87), channel_id=1, source_target_pairs={{0,16},{8,24},{16,0},{24,8},{1,17},{9,25},{17,1},{25,9},{2,18},{10... | collective-permute-start | bytes 3538952 | tf_op jit(solution)/shard_map/ppermute | solution.py:852
  193.9 26.6 %collective-permute-start.6 = (bf16[2,2,2,24,3072]{4,3,2,1,0:T(8,128)(2,1)}, bf16[2,2,2,24,3072]{4,3,2,1,0:T(8,128)(2,1)}, u32[]{:S(2)}, u32[]{:S(2)}) collective-permute-start(bf16[2,2,2,24,3072]{4,3,2,1,0:T(8,128)(2,1)} %get-tuple-element.88), channel_id=1, source_target_pairs={{0,1},{1,0},{2,3},{3,2},{4,5},{5,4},{6,7},{7,6},{8,9},{9,8},{10,11... | collective-permute-start | bytes 3538952 | tf_op jit(solution)/shard_map/ppermute | solution.py:852
  217.2 15.0 %collective-permute-start.7 = (bf16[3,2,192,768]{3,2,1,0:T(8,128)(2,1)}, bf16[3,2,192,768]{3,2,1,0:T(8,128)(2,1)}, u32[]{:S(2)}, u32[]{:S(2)}) collective-permute-start(bf16[3,2,192,768]{3,2,1,0:T(8,128)(2,1)} %get-tuple-element.104), channel_id=1, source_target_pairs={{0,8},{8,0},{16,24},{24,16},{1,9},{9,1},{17,25},{25,17},{2,10},{10... | collective-permute-start | bytes 5308424 | tf_op jit(solution)/shard_map/ppermute | solution.py:852
  220.5 32.8 %all-to-all-start.3 = ((bf16[8,96,768]{2,1,0:T(8,128)(2,1)}), bf16[8,96,768]{2,1,0:T(8,128)(2,1)}, u32[]{:S(2)}, u32[]{:S(2)}) async-start(bf16[8,96,768]{2,1,0:T(8,128)(2,1)} %get-tuple-element.89), calls=%async_computation.3 | async-start | bytes 2359296 | tf_op jit(solution)/shard_map/all_to_all | solution.py:829
  228.7 38.0 %collective-permute-start.15 = (bf16[2,2,24,3072]{3,2,1,0:T(8,128)(2,1)}, bf16[2,2,24,3072]{3,2,1,0:T(8,128)(2,1)}, u32[]{:S(2)}, u32[]{:S(2)}) collective-permute-start(bf16[2,2,24,3072]{3,2,1,0:T(8,128)(2,1)} %get-tuple-element.122), channel_id=1, source_target_pairs={{0,1},{1,0},{2,3},{3,2},{4,5},{5,4},{6,7},{7,6},{8,9},{9,8},{10,11... | collective-permute-start | bytes 1769480 | tf_op jit(solution)/shard_map/ppermute | solution.py:852
  231.7 36.3 %collective-permute-start.16 = (bf16[2,2,24,3072]{3,2,1,0:T(8,128)(2,1)}, bf16[2,2,24,3072]{3,2,1,0:T(8,128)(2,1)}, u32[]{:S(2)}, u32[]{:S(2)}) collective-permute-start(bf16[2,2,24,3072]{3,2,1,0:T(8,128)(2,1)} %get-tuple-element.120), channel_id=1, source_target_pairs={{0,16},{8,24},{16,0},{24,8},{1,17},{9,25},{17,1},{25,9},{2,18},{10... | collective-permute-start | bytes 1769480 | tf_op jit(solution)/shard_map/ppermute | solution.py:852
  236.5 25.0 %collective-permute-start.9 = (bf16[2,2,2,2,24,768]{5,4,0,1,2,3:T(8,128)(2,1)}, bf16[2,2,2,2,24,768]{5,4,0,1,2,3:T(8,128)(2,1)}, u32[]{:S(2)}, u32[]{:S(2)}) collective-permute-start(bf16[2,2,2,2,24,768]{5,4,0,1,2,3:T(8,128)(2,1)} %bitcast.150), channel_id=1, source_target_pairs={{0,16},{8,24},{16,0},{24,8},{1,17},{9,25},{17,1},{25,9},{2,18},{10... | collective-permute-start | bytes 1769480 | tf_op jit(solution)/shard_map/ppermute | solution.py:852
  239.0 26.9 %collective-permute-start.11 = (bf16[2,2,2,2,24,768]{5,4,0,2,3,1:T(8,128)(2,1)}, bf16[2,2,2,2,24,768]{5,4,0,2,3,1:T(8,128)(2,1)S(1)}, u32[]{:S(2)}, u32[]{:S(2)}) collective-permute-start(bf16[2,2,2,2,24,768]{5,4,0,2,3,1:T(8,128)(2,1)} %bitcast.149), channel_id=1, source_target_pairs={{0,1},{1,0},{2,3},{3,2},{4,5},{5,4},{6,7},{7,6},{8,9},{9,8},{10,11... | collective-permute-start | bytes 1769480 | tf_op jit(solution)/shard_map/ppermute | solution.py:852
  262.8 8.5 %collective-permute-start.10 = (bf16[2,2,2,24,768]{4,3,0,1,2:T(8,128)(2,1)S(1)}, bf16[2,2,2,24,768]{4,3,0,1,2:T(8,128)(2,1)S(1)}, u32[]{:S(2)}, u32[]{:S(2)}) collective-permute-start(bf16[2,2,2,24,768]{4,3,0,1,2:T(8,128)(2,1)S(1)} %dynamic-slice_bitcast_fusion.11), channel_id=1, source_target_pairs={{0,1},{1,0},{2,3},{3,2},{4,5},{5,4},{6,7},{7,6},{8,9},{9,8},{10,11... | collective-permute-start | bytes 884744 | tf_op jit(solution)/shard_map/ppermute | solution.py:852
  266.0 7.1 %collective-permute-start.12 = (bf16[2,2,2,24,768]{4,3,0,1,2:T(8,128)(2,1)S(1)}, bf16[2,2,2,24,768]{4,3,0,1,2:T(8,128)(2,1)S(1)}, u32[]{:S(2)}, u32[]{:S(2)}) collective-permute-start(bf16[2,2,2,24,768]{4,3,0,1,2:T(8,128)(2,1)S(1)} %dynamic-slice_bitcast_fusion.10), channel_id=1, source_target_pairs={{0,16},{8,24},{16,0},{24,8},{1,17},{9,25},{17,1},{25,9},{2,18},{10... | collective-permute-start | bytes 884744 | tf_op jit(solution)/shard_map/ppermute | solution.py:852
  274.0 10.3 %collective-permute-start.13 = (bf16[4,2,24,768]{3,2,0,1:T(8,128)(2,1)}, bf16[4,2,24,768]{3,2,0,1:T(8,128)(2,1)}, u32[]{:S(2)}, u32[]{:S(2)}) collective-permute-start(bf16[4,2,24,768]{3,2,0,1:T(8,128)(2,1)} %fusion.17), channel_id=1, source_target_pairs={{0,2},{1,3},{2,0},{3,1},{4,6},{5,7},{6,4},{7,5},{8,10},{9,11},{10,... | collective-permute-start | bytes 884744 | tf_op jit(solution)/shard_map/ppermute | solution.py:852
  276.6 25.0 %collective-permute-start.17 = (bf16[2,2,24,3072]{3,2,1,0:T(8,128)(2,1)}, bf16[2,2,24,3072]{3,2,1,0:T(8,128)(2,1)S(1)}, u32[]{:S(2)}, u32[]{:S(2)}) collective-permute-start(bf16[2,2,24,3072]{3,2,1,0:T(8,128)(2,1)} %fusion.8), channel_id=1, source_target_pairs={{0,2},{1,3},{2,0},{3,1},{4,6},{5,7},{6,4},{7,5},{8,10},{9,11},{10,... | collective-permute-start | bytes 1769480 | tf_op jit(solution)/shard_map/ppermute | solution.py:852
  278.5 28.6 %all-to-all-start.4 = ((f32[8,112,128]{2,1,0:T(8,128)}), f32[8,112,128]{2,1,0:T(8,128)S(1)}, u32[]{:S(2)}, u32[]{:S(2)}) async-start(f32[8,112,128]{2,1,0:T(8,128)} %bitcast.153), calls=%async_computation.4 | async-start | bytes 917504 | tf_op jit(solution)/shard_map/all_to_all | solution.py:829
  285.3 20.4 %collective-permute-start.14 = (bf16[4,24,768]{2,1,0:T(8,128)(2,1)S(1)}, bf16[4,24,768]{2,1,0:T(8,128)(2,1)S(1)}, u32[]{:S(2)}, u32[]{:S(2)}) collective-permute-start(bf16[4,24,768]{2,1,0:T(8,128)(2,1)S(1)} %dynamic-slice_bitcast_fusion.12), channel_id=1, source_target_pairs={{0,4},{1,5},{2,6},{3,7},{4,0},{5,1},{6,2},{7,3},{8,12},{9,13},{10,... | collective-permute-start | bytes 442376 | tf_op jit(solution)/shard_map/ppermute | solution.py:852
  301.8 22.1 %collective-permute-start.18 = (bf16[2,24,3072]{2,1,0:T(8,128)(2,1)S(1)}, bf16[2,24,3072]{2,1,0:T(8,128)(2,1)S(1)}, u32[]{:S(2)}, u32[]{:S(2)}) collective-permute-start(bf16[2,24,3072]{2,1,0:T(8,128)(2,1)S(1)} %dynamic-slice_bitcast_fusion.9), channel_id=1, source_target_pairs={{0,4},{1,5},{2,6},{3,7},{4,0},{5,1},{6,2},{7,3},{8,12},{9,13},{10,... | collective-permute-start | bytes 884744 | tf_op jit(solution)/shard_map/ppermute | solution.py:852
  (20 other events, 40.0 us)

commit v5 on v4

--- a/solution.py
+++ b/solution.py
@@ -12,7 +12,8 @@
 HEADS = 12
 HEAD_DIM = 64
 PAIR = 2 * HEAD_DIM
-PAIRS = HEADS // 2
+QUAD = 2 * PAIR
+QUADS = HEADS // 4
 FF_BLOCK = 256
 LANE_PARTS = D // 128
 FACTOR = HEAD_DIM ** (-0.5)
@@ -98,14 +99,15 @@
     return total
 
 
-def enter_kernel(meta, tok, top, bot, pieces, kern, out, buf, ent):
+def enter_kernel(meta, tok, top, bot, lead, kern, out, buf, ent):
     latents = pl.num_programs(0)
     latent = pl.program_id(0)
     rows_here, cols = tok.shape[1], tok.shape[2]
     half = cols // 2
     row0 = meta[2 * latents]
-    shift = pieces[0, 0:1, :]
-    scale = 1.0 + pieces[0, 1:2, :]
+    shift = lead[pl.ds(latent, 1), :D]
+    scale = 1.0 + lead[pl.ds(latent, 1), D:]
+    taps = [kern[t : t + 1, :].astype(F32) for t in range(9)]
     for rr in range(rows_here + 2):
         source = top[0, 0] if rr == 0 else bot[0, 0] if rr == rows_here + 1 else tok[0, rr - 1]
         put_row(buf, rr, source.astype(F32))
@@ -118,14 +120,13 @@
             total = jnp.zeros((half, D), F32)
             for i in range(3):
                 for j in range(3):
-                    tap = 3 * i + j
-                    total = total + ent[row + i, parity + j] * kern[tap : tap + 1, :]
+                    total = total + ent[row + i, parity + j] * taps[3 * i + j]
             mixed = (ent[row + 1, 1 + parity] + total).astype(BF16)
             group = 2 * (row % 2) + parity
             out[0, group, (row // 2) * half : (row // 2 + 1) * half, :] = mixed
 
 
-def enter(meta, tokens, top, bot, pieces, kern):
+def enter(meta, tokens, top, bot, lead, kern):
     latents, rows_here, cols, _ = tokens.shape
     half = cols // 2
     per_group = rows_here // 2 * half
@@ -140,7 +141,7 @@
                 whole(1, rows_here, cols, D),
                 whole(1, 1, cols, D),
                 whole(1, 1, cols, D),
-                whole(1, 6, D),
+                pl.BlockSpec((latents, 2 * D), lambda l, m: (0, 0)),
                 pl.BlockSpec((9, D), lambda l, m: (0, 0)),
             ],
             out_specs=whole(1, 4, per_group, D),
@@ -152,7 +153,7 @@
         compiler_params=pltpu.CompilerParams(vmem_limit_bytes=VMEM_LIMIT),
         cost_estimate=pl.CostEstimate(flops=6_000_000_000, bytes_accessed=4_000_000, transcendentals=0),
         name="enter",
-    )(meta, tokens, top, bot, pieces, kern)
+    )(meta, tokens, top, bot, lead, kern)
 
 
 def cot_kernel(cot, pieces, ge_out, get_out, cot_out, buf):
@@ -271,7 +272,7 @@
     return jnp.where(values > 0.0, 1.0 - tail, tail), density
 
 
-def ffn_kernel(core, e2, e2t, ge, get, up, down, kern_in, exp_out, ge2_out, send_out, keep_out, kern_out, *scratch):
+def ffn_kernel(core, e2, e2t, ge, get, up, down, kern_in, exp_out, ge2_out, first_out, last_out, send_out, keep_out, kern_out, *scratch):
     latents = e2.shape[0]
     lifted, gact, gconv, act, graised = [scratch[k * latents : (k + 1) * latents] for k in range(5)]
     down_acc, up_acc = scratch[5 * latents :]
@@ -385,6 +386,11 @@
     lower(latents - 1)
     weigh_up(latents - 1)
 
+    @pl.when(step == pl.num_programs(0) - 1)
+    def _():
+        first_out[...] = ge2_out[:, : 2 * half].astype(BF16)
+        last_out[...] = ge2_out[:, 2 * half * (rows_here + 1) :].astype(BF16)
+
     size = down_acc.shape[0] // 4
     for which, acc in enumerate((down_acc, up_acc)):
         for y in range(2):
@@ -412,6 +418,8 @@
         out_shape=(
             jax.ShapeDtypeStruct((latents, own, D), F32),
             jax.ShapeDtypeStruct((latents, wide, D), F32),
+            jax.ShapeDtypeStruct((latents, cols, D), BF16),
+            jax.ShapeDtypeStruct((latents, cols, D), BF16),
             parts,
             parts,
             jax.ShapeDtypeStruct((9, hidden), F32),
@@ -431,6 +439,8 @@
             out_specs=(
                 fixed(latents, own, D),
                 fixed(latents, wide, D),
+                fixed(latents, cols, D),
+                fixed(latents, cols, D),
                 parts_spec,
                 parts_spec,
                 pl.BlockSpec((9, FF_BLOCK), lambda f, c: (0, f)),
@@ -561,7 +571,7 @@
     )(meta, ge2, low, high, after, branch, cot, pieces, proj)
 
 
-def leave_kernel(meta, gm, tok, top, bot, after_grad, pieces, kern, out, kern_out, sums_out, buf, ent, gmx, obuf, nbuf, sbuf):
+def leave_kernel(meta, gm, tok, top, bot, after_grad, pieces, kern, out, kern_out, sums_out, buf, ent, gmx, obuf, nbuf, sbuf, tot):
     latents = pl.num_programs(0)
     latent = pl.program_id(0)
     rows_here, cols = tok.shape[1], tok.shape[2]
@@ -569,23 +579,28 @@
     row0 = meta[2 * latents]
     shift = pieces[0, 0:1, :]
     scale = 1.0 + pieces[0, 1:2, :]
-    taps = [kern[t : t + 1, :] for t in range(9)]
-    for rr in range(rows_here + 2):
-        source = top[0, 0] if rr == 0 else bot[0, 0] if rr == rows_here + 1 else tok[0, rr - 1]
-        put_row(buf, rr, source.astype(F32))
+    taps = [kern[t : t + 1, :].astype(F32) for t in range(9)]
+    put_row(buf, 0, top[0, 0].astype(F32))
+    for row in range(rows_here):
+        put_row(buf, row + 1, tok[0, row].astype(F32))
+    put_row(buf, rows_here + 1, bot[0, 0].astype(F32))
+
+    def take(rr, carry):
+        at = pl.multiple_of(rr // 2 * half, half)
         for parity in range(2):
             normed, scaled = normalize(get_columns(buf, rr, parity))
-            if 1 <= rr <= rows_here:
-                nbuf[rr - 1, parity] = normed
-                sbuf[rr - 1, parity] = jnp.broadcast_to(scaled, (half, 128))
+            nbuf[rr, parity] = normed
+            sbuf[rr, parity] = jnp.broadcast_to(scaled, (half, 128))
             ok = usable_of(meta, latents, latent, row0 + rr - 1, parity, half)
-            put_shifts(ent, rr, parity, ((normed * scale + shift) * ok).astype(BF16).astype(F32))
+            put_shifts(ent, rr, parity, (normed * scale + shift) * ok)
             group = 2 * ((rr + 1) % 2) + parity
-            at = (rr // 2) * half
-            put_shifts(gmx, rr, parity, gm[group, at : at + half, :].astype(F32))
-    sums = [jnp.zeros((8, D), F32) for _ in range(2)]
-    tap_sums = [jnp.zeros((8, D), F32) for _ in range(9)]
-    for row in range(rows_here):
+            put_shifts(gmx, rr, parity, gm[group, pl.ds(at, half), :].astype(F32))
+        return carry
+
+    lax.fori_loop(0, rows_here + 2, take, 0)
+    tot[...] = jnp.zeros_like(tot)
+
+    def give(row, carry):
         for parity in range(2):
             here = gmx[row + 1, 1 + parity]
             total = here
@@ -593,20 +608,23 @@
                 for j in range(3):
                     t = 3 * i + j
                     total = total + gmx[row + 2 - i, parity + 2 - j] * taps[t]
-                    tap_sums[t] = tap_sums[t] + sum8(ent[row + i, parity + j] * here)
+                    tot[t] += sum8(ent[row + i, parity + j] * here)
             ok = usable_of(meta, latents, latent, row0 + row, parity, half)
             grad = total * ok
-            normed, scaled = nbuf[row, parity], sbuf[row, parity, :, 0:1]
-            sums[0] = sums[0] + sum8(grad)
-            sums[1] = sums[1] + sum8(grad * normed)
-            at = (2 * row + parity) * half
-            back = after_grad[0, at : at + half, :] + norm_back(grad * scale, normed, scaled)
+            normed, scaled = nbuf[row + 1, parity], sbuf[row + 1, parity, :, 0:1]
+            tot[9] += sum8(grad)
+            tot[10] += sum8(grad * normed)
+            at = pl.multiple_of((2 * row + parity) * half, half)
+            back = after_grad[0, pl.ds(at, half), :] + norm_back(grad * scale, normed, scaled)
             put_columns(obuf, row, parity, back)
         out[0, row] = get_row(obuf, row)
+        return carry
+
+    lax.fori_loop(0, rows_here, give, 0)
+    for t in range(9):
+        kern_out[0, t : t + 1, :] = jnp.sum(tot[t], axis=0, keepdims=True)
     for k in range(2):
-        sums_out[0, k : k + 1, :] = jnp.sum(sums[k], axis=0, keepdims=True)
-    for t in range(9):
-        kern_out[0, t : t + 1, :] = jnp.sum(tap_sums[t], axis=0, keepdims=True)
+        sums_out[0, k : k + 1, :] = jnp.sum(tot[9 + k], axis=0, keepdims=True)
 
 
 def leave(meta, gm, tokens, top, bot, after_grad, pieces, kern):
@@ -640,8 +658,9 @@
                 pltpu.VMEM((rows_here + 2, 4, half, D), F32),
                 pltpu.VMEM((rows_here + 2, 4, half, D), F32),
                 pltpu.VMEM((rows_here, LANE_PARTS, cols, 128), F32),
-                pltpu.VMEM((rows_here, 2, half, D), F32),
-                pltpu.VMEM((rows_here, 2, half, 128), F32),
+                pltpu.VMEM((rows_here + 2, 2, half, D), F32),
+                pltpu.VMEM((rows_here + 2, 2, half, 128), F32),
+                pltpu.VMEM((11, 8, D), F32),
             ],
         ),
         compiler_params=pltpu.CompilerParams(vmem_limit_bytes=VMEM_LIMIT),
@@ -667,17 +686,25 @@
     key = mm(m, wk[...]).astype(BF16)
     value_t = mm(wvt[...], m, NT).astype(BF16)
     keep = jnp.tile(bias[...], (1, tokens // 128))
-    scores = [mm(key_e, query, NT) + keep for key_e in pair_parts(key)]
+
+    def score(h):
+        cut = slice(h // 2 * PAIR, (h // 2 + 1) * PAIR)
+        return mm(pair_parts(key[:, cut])[h % 2], query[:, cut], NT)
+
+    scores = {0: score(0), 1: score(1)}
     parts = []
-    for e in range(2):
-        peak = jnp.max(scores[e], axis=0, keepdims=True)
-        raw = jnp.exp(scores[e] - peak)
+    for h in range(4):
+        masked = scores.pop(h) + keep
+        peak = jnp.max(masked, axis=0, keepdims=True)
+        raw = jnp.exp(masked - peak)
+        if h + 2 < 4:
+            scores[h + 2] = score(h + 2)
         total = jnp.sum(raw, axis=0, keepdims=True)
         prob = (raw * (1.0 / total)).astype(BF16)
-        parts.append(mm(value_t[e * HEAD_DIM : (e + 1) * HEAD_DIM], prob))
-        lse_out[0, e : e + 1, :] = peak + jnp.log(total)
-    padded[0:margin] = jnp.zeros((margin, PAIR), F32)
-    padded[margin + tokens :] = jnp.zeros((margin, PAIR), F32)
+        parts.append(mm(value_t[h * HEAD_DIM : (h + 1) * HEAD_DIM], prob))
+        lse_out[0, h : h + 1, :] = peak + jnp.log(total)
+    padded[0:margin] = jnp.zeros((margin, QUAD), F32)
+    padded[margin + tokens :] = jnp.zeros((margin, QUAD), F32)
     padded[margin : margin + tokens] = jnp.concatenate(parts, axis=0).T
     for s in range(strips):
         start = pl.multiple_of(offset[0] + s * step, 8)
@@ -691,23 +718,23 @@
         attend_kernel,
         out_shape=(
             jax.ShapeDtypeStruct((strips, window, D), BF16),
-            jax.ShapeDtypeStruct((PAIRS, 2, tokens), F32),
+            jax.ShapeDtypeStruct((QUADS, 4, tokens), F32),
         ),
         grid_spec=pltpu.PrefetchScalarGridSpec(
             num_scalar_prefetch=1,
-            grid=(PAIRS,),
+            grid=(QUADS,),
             in_specs=[
                 pl.BlockSpec((tokens, D), lambda p, o: (0, 0)),
-                pl.BlockSpec((D, PAIR), lambda p, o: (0, p)),
-                pl.BlockSpec((D, PAIR), lambda p, o: (0, PAIRS + p)),
-                pl.BlockSpec((PAIR, D), lambda p, o: (2 * PAIRS + p, 0)),
+                pl.BlockSpec((D, QUAD), lambda p, o: (0, p)),
+                pl.BlockSpec((D, QUAD), lambda p, o: (0, QUADS + p)),
+                pl.BlockSpec((QUAD, D), lambda p, o: (2 * QUADS + p, 0)),
                 pl.BlockSpec((tokens, 128), lambda p, o: (0, 0)),
             ],
             out_specs=(
-                pl.BlockSpec((strips, window, PAIR), lambda p, o: (0, 0, p)),
-                pl.BlockSpec((1, 2, tokens), lambda p, o: (p, 0, 0)),
+                pl.BlockSpec((strips, window, QUAD), lambda p, o: (0, 0, p)),
+                pl.BlockSpec((1, 4, tokens), lambda p, o: (p, 0, 0)),
             ),
-            scratch_shapes=[pltpu.VMEM((tokens + 2 * margin, PAIR), F32)],
+            scratch_shapes=[pltpu.VMEM((tokens + 2 * margin, QUAD), F32)],
         ),
         compiler_params=pltpu.CompilerParams(vmem_limit_bytes=VMEM_LIMIT),
         cost_estimate=pl.CostEstimate(flops=16_000_000_000, bytes_accessed=4_000_000, transcendentals=0),
@@ -721,33 +748,44 @@
     step = tokens // strips
     margin = window - step
     p = pl.program_id(0)
-    q = query[...]
     keep = jnp.tile(bias[...], (1, tokens // 128))
-    queries = pair_parts(q)
-    keys = pair_parts(key[...])
-    values = pair_parts(value[...])
-    grads = pair_parts(gatt[...])
-    scores = [mm(keys[e], q, NT) for e in range(2)]
-    grad_probs = [mm(values[e], gatt[...], NT) for e in range(2)]
-    parts, probs, grad_scores = [], [], []
-    for e in range(2):
-        prob = jnp.exp(scores[e] * FACTOR + keep - lse[0, e : e + 1, :])
-        delta = jnp.sum(prob * grad_probs[e], axis=0, keepdims=True)
-        probs.append(prob.astype(BF16))
-        grad_scores.append((prob * (grad_probs[e] - delta)).astype(BF16))
-        parts.append(mm(key_t[e * HEAD_DIM : (e + 1) * HEAD_DIM], grad_scores[e]))
-    dv = mm(jnp.concatenate(probs, axis=1), jnp.concatenate(grads, axis=0))
-    dk = mm(jnp.concatenate(grad_scores, axis=1), jnp.concatenate(queries, axis=0))
-    dq = jnp.concatenate(parts, axis=0).T * FACTOR
-    dk = dk * FACTOR
-    all_three = jnp.concatenate([dq.astype(BF16), dk.astype(BF16), dv.astype(BF16)], axis=1)
+
+    def pair(k):
+        cut = slice(k * PAIR, (k + 1) * PAIR)
+        q, grad = query[:, cut], gatt[:, cut]
+        keys, values = pair_parts(key[:, cut]), pair_parts(value[:, cut])
+        return [(mm(keys[e], q, NT), mm(values[e], grad, NT)) for e in range(2)]
+
+    def soften(k, e, score, grad_prob):
+        h = 2 * k + e
+        prob = jnp.exp(score * FACTOR + keep - lse[0, h : h + 1, :])
+        delta = jnp.sum(prob * grad_prob, axis=0, keepdims=True)
+        return prob.astype(BF16), (prob * (grad_prob - delta)).astype(BF16)
+
+    def finish(k, probs, grad_scores):
+        cut = slice(k * PAIR, (k + 1) * PAIR)
+        queries, grads = pair_parts(query[:, cut]), pair_parts(gatt[:, cut])
+        dv = mm(jnp.concatenate(probs, axis=1), jnp.concatenate(grads, axis=0))
+        dk = mm(jnp.concatenate(grad_scores, axis=1), jnp.concatenate(queries, axis=0)) * FACTOR
+        rows = [key_t[(2 * k + e) * HEAD_DIM : (2 * k + e + 1) * HEAD_DIM] for e in range(2)]
+        parts = [mm(rows[e], grad_scores[e]) for e in range(2)]
+        dq = jnp.concatenate(parts, axis=0).T * FACTOR
+        return dq.astype(BF16), dk.astype(BF16), dv.astype(BF16)
+
+    first = pair(0)
+    soft = [soften(0, e, *first[e]) for e in range(2)]
+    then = pair(1)
+    one = finish(0, [v[0] for v in soft], [v[1] for v in soft])
+    soft = [soften(1, e, *then[e]) for e in range(2)]
+    two = finish(1, [v[0] for v in soft], [v[1] for v in soft])
+    all_three = jnp.concatenate([v for k in range(3) for v in (one[k], two[k])], axis=1)
     part[...] = mm(mixed_t[...], all_three)
     size = D // 4
     for y in range(2):
         mine = pl.multiple_of((2 * y + offset[1]) * size, 8)
         other = pl.multiple_of((2 * y + 1 - offset[1]) * size, 8)
         for k in range(3):
-            cut = slice(k * PAIR, (k + 1) * PAIR)
+            cut = slice(k * QUAD, (k + 1) * QUAD)
             keep_out[k, y] = part[pl.ds(mine, size), cut].astype(BF16)
             send_out[k, y] = part[pl.ds(other, size), cut].astype(BF16)
     total = mm(all_three, jnp.concatenate([wq[...], wk[...], wv[...]], axis=1), NT)
@@ -772,10 +810,10 @@
 def attend_back(offset, triple, key_t, bias, lse, gatt, weight, mixed_t, strips, window):
     tokens = triple.shape[0]
     margin = window - tokens // strips
-    part = lambda k: pl.BlockSpec((tokens, PAIR), lambda p, o: (0, k * PAIRS + p))
-    slab = lambda k: pl.BlockSpec((D, PAIR), lambda p, o: (0, k * PAIRS + p))
+    part = lambda k: pl.BlockSpec((tokens, QUAD), lambda p, o: (0, k * QUADS + p))
+    slab = lambda k: pl.BlockSpec((D, QUAD), lambda p, o: (0, k * QUADS + p))
     parts = jax.ShapeDtypeStruct((3, 2, D // 4, D), BF16)
-    parts_spec = pl.BlockSpec((3, 2, D // 4, PAIR), lambda p, o: (0, 0, 0, p))
+    parts_spec = pl.BlockSpec((3, 2, D // 4, QUAD), lambda p, o: (0, 0, 0, p))
     return pl.pallas_call(
         attend_back_kernel,
         out_shape=(
@@ -785,14 +823,14 @@
         ),
         grid_spec=pltpu.PrefetchScalarGridSpec(
             num_scalar_prefetch=1,
-            grid=(PAIRS,),
+            grid=(QUADS,),
             in_specs=[
                 part(0),
                 part(1),
                 part(2),
-                pl.BlockSpec((PAIR, tokens), lambda p, o: (p, 0)),
+                pl.BlockSpec((QUAD, tokens), lambda p, o: (p, 0)),
                 pl.BlockSpec((tokens, 128), lambda p, o: (0, 0)),
-                pl.BlockSpec((1, 2, tokens), lambda p, o: (p, 0, 0)),
+                pl.BlockSpec((1, 4, tokens), lambda p, o: (p, 0, 0)),
                 part(0),
                 slab(0),
                 slab(1),
@@ -806,7 +844,7 @@
             ),
             scratch_shapes=[
                 pltpu.VMEM((tokens + 2 * margin, D), F32),
-                pltpu.VMEM((D, 3 * PAIR), F32),
+                pltpu.VMEM((D, 3 * QUAD), F32),
             ],
         ),
         compiler_params=pltpu.CompilerParams(vmem_limit_bytes=VMEM_LIMIT),
@@ -871,26 +909,29 @@
     return lax.psum_scatter(values, ("batch", "seq"), scatter_dimension=0, tiled=True).astype(F32)
 
 
-def sum_and_gather(common, sliced):
+def payload_of(common, sliced):
     seq_count, batch_count = lax.axis_size("seq"), lax.axis_size("batch")
-    batch_place = lax.axis_index("batch")
     flat = common.reshape(1, -1)
     pieces = [jnp.broadcast_to(flat, (seq_count, flat.shape[1]))]
     for values in sliced:
         cut = values.reshape(values.shape[0], batch_count, seq_count, -1).transpose(2, 1, 0, 3)
         pieces.append(cut.reshape(seq_count, -1))
     whole = jnp.concatenate(pieces, axis=1)
-    whole = jnp.pad(whole, ((0, 0), (0, -whole.shape[1] % 1024))).reshape(seq_count, -1, 128)
-    summed = jnp.sum(swap(whole), axis=0)
-    gathered = lax.all_gather(summed, "batch", axis=0).reshape(batch_count, -1)
-    common_all = gathered[:, : flat.shape[1]].reshape((batch_count,) + common.shape)
-    at = flat.shape[1]
+    return jnp.pad(whole, ((0, 0), (0, -whole.shape[1] % 1024))).reshape(seq_count, -1, 128)
+
+
+def unpack(gathered, common, sliced):
+    seq_count, batch_count = lax.axis_size("seq"), lax.axis_size("batch")
+    gathered = gathered.reshape(batch_count, -1)
+    at = common.size
+    common_all = gathered[:, :at].reshape((batch_count,) + common.shape)
     own = []
-    for values, piece in zip(sliced, pieces[1:]):
-        part = jnp.sum(gathered[:, at : at + piece.shape[1]], axis=0)
+    for values in sliced:
+        size = values.size // seq_count
+        part = jnp.sum(gathered[:, at : at + size], axis=0)
         part = part.reshape(batch_count, values.shape[0], -1)
-        own.append(lax.dynamic_index_in_dim(part, batch_place, 0, keepdims=False))
-        at += piece.shape[1]
+        own.append(lax.dynamic_index_in_dim(part, lax.axis_index("batch"), 0, keepdims=False))
+        at += size
     return common_all, own
 
 
@@ -972,14 +1013,16 @@
     condition = mm(embedding, time_weight) + mm(one_hot, class_table)
     logistic = jax.nn.sigmoid(condition)
     activated_cond = (condition * logistic).astype(BF16)
-    pieces = (mm(activated_cond, ada_weight) + ada_bias).reshape(latents, 6, D)
+    lead = mm(activated_cond, ada_weight[:, : 2 * D]) + ada_bias[: 2 * D]
     meta = jnp.concatenate(
         [heights, widths, jnp.reshape(seq_place * rows_here, (1,))]
     ).astype(jnp.int32)
-    kern_attn = conv_attn.astype(F32)
     core = jnp.reshape(batch_place % 2, (1,)).astype(jnp.int32)
 
-    mixed = enter(meta, tokens, top, bot, pieces, kern_attn)
+    mixed = enter(meta, tokens, top, bot, lead, conv_attn)
+    late_cond = after(activated_cond, mixed)
+    pieces = mm(late_cond, ada_weight[:, 2 * D :]) + ada_bias[2 * D :]
+    pieces = jnp.concatenate([lead, pieces], axis=1).reshape(latents, 6, D)
     sent = mixed.reshape(blocks, 1, per_group, D)
     sent = jnp.broadcast_to(sent, (blocks, share, per_group, D)).reshape(seq_count, per_group, D)
     grouped = swap(sent).reshape(group_tokens, D)
@@ -1031,14 +1074,14 @@
     e2, e2t, after_attn, branch = second(
         meta, attended, tokens, top, bot, pieces, proj_weight
     )
-    expanded, grad_e2, send_c, keep_c, conv_ffn_part = ffn(
+    expanded, grad_e2, edge_first, edge_last, send_c, keep_c, conv_ffn_part = ffn(
         core, e2, e2t, ge, get, up_weight, down_weight, conv_ffn, cols
     )
     halving = batch_count == 4 and seq_count == 8
     if halving:
         got_c = hop(send_c, "c")
-    low = from_before(grad_e2[:, cols * (rows_here + 1) :].astype(BF16), "seq")
-    high = from_after(grad_e2[:, :cols].astype(BF16), "seq")
+    low = from_before(edge_last, "seq")
+    high = from_after(edge_first, "seq")
     output, gate_sums = finish_output(expanded, after_attn, cot_split, pieces, rows_here, cols)
     grad_after, grad_branch, grad_attended, mid_sums = middle(
         meta, grad_e2, low, high, after_attn, branch, cot_split, pieces, proj_weight
@@ -1096,6 +1139,11 @@
         gm = after(gm, send_a, send_b)
         got_a, got_b = hop(send_a, "x"), hop(send_b, "y")
         got_one, got_two = hop(send_one, "y"), hop(send_two, "x")
+        gm, got_a, got_b = lax.optimization_barrier((gm, got_a, got_b))
+        pair = jnp.stack([add(keep_a, got_a), add(keep_b, got_b)]).astype(BF16)
+        send_l, keep_l, dims_l = split(pair, dims_a, "l")
+        gm = after(gm, send_l)
+        got_l = hop(send_l, "l")
     total = batch_count * latents
 
     here = batch_place * seq_count + seq_place
@@ -1116,25 +1164,31 @@
         return product[:total] + product[total : 2 * total] + product[2 * total :]
 
     token_grad, conv_attn_part, end_sums = leave(
-        meta, gm, tokens, top, bot, grad_after, pieces, kern_attn
+        meta, gm, tokens, top, bot, grad_after, pieces, conv_attn
     )
 
-    all_sums, (conv_attn_grad, conv_ffn_grad) = sum_and_gather(
-        jnp.concatenate([end_sums, mid_sums, gate_sums], axis=1),
-        (jnp.sum(conv_attn_part, axis=0), conv_ffn_part),
-    )
+    common = jnp.concatenate([end_sums, mid_sums, gate_sums], axis=1)
+    sliced = (jnp.sum(conv_attn_part, axis=0), conv_ffn_part)
+    message = payload_of(common, sliced)
     if halving:
-        keep_a, keep_b, keep_one, keep_two, end_sums = lax.optimization_barrier(
-            (keep_a, keep_b, keep_one, keep_two, end_sums)
+        message, keep_l, got_l, keep_one, keep_two = lax.optimization_barrier(
+            (message, keep_l, got_l, keep_one, keep_two)
         )
-        pair = jnp.stack([add(keep_a, got_a), add(keep_b, got_b)])
-        pair = reduce_rest(pair, dims_a, "lh")
-        down_rows, up_rows = pair[0], pair[1]
+        send_h, keep_h, _ = split(add(keep_l, got_l).astype(BF16), dims_l, "h")
+        got_h = hop(send_h, "h")
         send_one, keep_one, dims_one = split(add(keep_one, got_one).astype(BF16), dims_one, "x")
         send_two, keep_two, dims_two = split(add(keep_two, got_two).astype(BF16), dims_two, "y")
         got_one, got_two = hop(send_one, "x"), hop(send_two, "y")
+    gathered = lax.all_gather(jnp.sum(swap(message), axis=0), "batch", axis=0)
+    if halving:
+        gathered, keep_one, keep_two, keep_h = lax.optimization_barrier(
+            (gathered, keep_one, keep_two, keep_h)
+        )
+        pair = add(keep_h, got_h)
+        down_rows, up_rows = pair[0], pair[1]
         rest_rows = jnp.concatenate([add(keep_one, got_one), add(keep_two, got_two)])
-        rest_rows = reduce_rest(rest_rows, dims_one, "lh")
+        send_l, keep_l, dims_l = split(rest_rows.astype(BF16), dims_one, "l")
+        got_l = hop(send_l, "l")
     else:
         whole = jnp.stack([keep_c, send_c])
         whole = jnp.where(core[0] == 0, whole, whole[::-1]).transpose(1, 2, 0, 3, 4)
@@ -1146,11 +1200,15 @@
             proj_grad = mm(att_own, flat_branch, (((0,), (0,)), ((), ()))).astype(BF16)
             rest = jnp.concatenate([rest, proj_grad], axis=1)
         rest_rows = scatter_rows(rest).reshape(own_cols, 4, D).transpose(1, 0, 2)
+    all_sums, (conv_attn_grad, conv_ffn_grad) = unpack(gathered, common, sliced)
+
+    grad_pieces = all_sums.reshape(total, 6 * D)
+    grad_silu = back_through(grad_pieces)
+    if halving:
+        grad_silu, got_l = lax.optimization_barrier((grad_silu, got_l))
+        rest_rows = reduce_rest(add(keep_l, got_l), dims_l, "h")
     qkv_rows = jnp.concatenate([rest_rows[0], rest_rows[1], rest_rows[2]], axis=1)
     proj_rows = rest_rows[3]
-
-    grad_pieces = all_sums.reshape(total, 6 * D)
-    grad_silu = back_through(grad_pieces)
     cond_all = grad_silu * slope_all
     cond_grad = lax.dynamic_slice_in_dim(cond_all, batch_place * latents, latents)
     cond_cols = lax.dynamic_slice_in_dim(cond_all, here * own_cols, own_cols, axis=1)

time: 328 us -> 322 us (0.982)
  starting transfers between devices: 54.6 us -> 49.7 us
  waiting for transfers between devices: 71.1 us -> 67.6 us
    ppermute x15, waiting for transfers between devices: 20.8 us -> 9.35 us  [hop(): return lax.ppermute(values, axis, [(i, i ^ mask) for i in range(count)])]
    all_to_all x5, waiting for transfers between devices: 47 us -> 52.7 us  [swap(): return lax.all_to_all(values, 'seq', 0, 0, tiled=False)]
    squeeze x5 -> x7, local copies, waits for them, and re-layouts: 1.1 us -> 5.28 us  [split(): send = lax.dynamic_index_in_dim(values, 1 - mine, at, keepdims=False)]
    ppermute x15, starting transfers between devices: 18.2 us -> 14.6 us  [hop(): return lax.ppermute(values, axis, [(i, i ^ mask) for i in range(count)])]
    dot_general x7 -> x8, matrix products: 17.8 us -> 19.5 us  [mm(): return lax.dot_general(left, right, dims, preferred_element_type=F32)]
    unnamed x64 -> x71, local copies, waits for them, and re-layouts: 12.5 us -> 11.8 us
  transfers between devices with their start and end apart: 24 -> 24, of which waited for: 12 -> 11; matrix products, arithmetic and copies ran while one was open for 21% -> 23% of each run, Pallas kernels for 14% -> 14%
where the time goes in v5:
time: 322 us; the launch traced here: 320 us
  Pallas kernels  109 us (34%)
  waiting for transfers between devices  67.6 us (21%)
  starting transfers between devices  49.7 us (15%)
  local copies, waits for them, and re-layouts  31.1 us (10%)
  other arithmetic  28.1 us (9%)
  matrix products  22.6 us (7%)
  blocking collectives  10.9 us (3%)
    all_to_all x5, waiting for transfers between devices, swap(): return lax.all_to_all(values, 'seq', 0, 0, tiled=False)  52.7 us
    pallas_call x1, Pallas kernels, ffn(): pl.pallas_call(ffn_kernel, out_shape=(jax.ShapeDtypeStruct((latents, own,...  40.4 us
    all_to_all x5, starting transfers between devices, swap(): return lax.all_to_all(values, 'seq', 0, 0, tiled=False)  24.3 us
    pallas_call x1, Pallas kernels, attend_back(): pl.pallas_call(attend_back_kernel, out_shape=(parts, parts, jax.ShapeDtyp...  20.1 us
    dot_general x8, matrix products, mm(): return lax.dot_general(left, right, dims, preferred_element_type=F32)  19.5 us
    ppermute x15, starting transfers between devices, hop(): return lax.ppermute(values, axis, [(i, i ^ mask) for i in range(count)])  14.6 us
    pallas_call x1, Pallas kernels, attend(): pl.pallas_call(attend_kernel, out_shape=(jax.ShapeDtypeStruct((strips, wi...  12.6 us
    unnamed x71, local copies, waits for them, and re-layouts  11.8 us
  transfers between devices with their start and end apart: 24, of which 11 were waited for; matrix products, arithmetic and copies ran while one was open for 23% of the time, Pallas kernels for 14%

profile of v5, /device:TPU:0, one launch (start us, length us, event | category | flops | bytes accessed | tf_op | source)
XLA Modules:
  0.0 320.1 jit_solution(129232678426366386)
XLA Ops:
  1.9 4.9 %collective-permute-start = (bf16[2,1,64,768]{3,2,1,0:T(8,128)(2,1)S(1)}, bf16[2,1,64,768]{3,2,1,0:T(8,128)(2,1)S(1)}, u32[]{:S(2)}, u32[]{:S(2)}) collective-permute-start(bf16[2,1,64,768]{3,2,1,0:T(8,128)(2,1)S(1)} %get-tuple-element.152), channel_id=1, source_target_pairs={{0,1},{1,2},{2,3},{3,4},{4,5},{5,6},{6,7},{8,9},{9,10},{10,11},{11... | collective-permute-start | bytes 589832 | tf_op jit(solution)/shard_map/ppermute | solution.py:858
  10.4 2.7 fusion.7.lead
  15.7 5.0 %enter.1 = bf16[2,4,64,768]{3,2,1,0:T(8,128)(2,1)} custom-call(s32[5]{0:T(128)} %pad_add_fusion.meta, bf16[2,4,64,768]{3,2,1,0:T(8,128)(2,1)} %tok.5, bf16[2,1,64,768]{3,2,1,0:T(8,128)(2,1)} %copy-done.25, bf16[2,1,64,768]{3,2,1,0:T(8,128)(2,1)} %copy-done.26, f32[2,1536]{1,0:T(2,128)} %fusion.7.lead, bf16[9,768]{1,0:T(8,128)(2,1)} %kern.3), custom_call_target="tpu_custom_call" | custom-call | flops 6000000000 | bytes 4000000 | tf_op jit(solution)/shard_map/enter/pallas_call | solution.py:134
  20.7 7.0 %all-to-all-start = ((bf16[8,64,768]{2,1,0:T(8,128)(2,1)}), bf16[8,64,768]{2,1,0:T(8,128)(2,1)S(1)}, u32[]{:S(2)}, u32[]{:S(2)}) async-start(bf16[8,64,768]{2,1,0:T(8,128)(2,1)} %bitcast.171), calls=%async_computation | async-start | bytes 1572864 | tf_op jit(solution)/shard_map/all_to_all | solution.py:867
  28.8 5.7 %copy.70 = bf16[768,2304]{0,1:T(8,128)(2,1)} copy(bf16[768,2304]{1,0:T(8,128)(2,1)} %wv.1) | data formatting | bytes 7077888 | tf_op args[11]
  34.7 5.2 %all-gather.2 = f32[4,2,1025]{2,1,0:T(2,128)S(1)} all-gather(f32[1,2,1025]{2,1,0:T(2,128)S(1)} %maximum_bitcast_fusion), channel_id=2, replica_groups=mesh['batch'=4,'seq'=8] {'batch'}, dimensions={0}, use_global_device_ids=true | all-gather | bytes 41000 | tf_op jit(solution)/shard_map/all_gather | solution.py:1062
  41.8 6.3 %all-to-all-done = bf16[8,64,768]{2,1,0:T(8,128)(2,1)S(1)} async-done(((bf16[8,64,768]{2,1,0:T(8,128)(2,1)}), bf16[8,64,768]{2,1,0:T(8,128)(2,1)S(1)}, u32[]{:S(2)}, u32[]{:S(2)}) %all-to-all-start) | async-done | bytes 786464 | tf_op jit(solution)/shard_map/all_to_all | solution.py:867
  49.0 12.6 %attend.1 = (bf16[8,96,768]{2,1,0:T(8,128)(2,1)}, f32[3,4,512]{2,1,0:T(4,128)}) custom-call(s32[2]{0:T(128)} %pad_add_fusion.1.offset, bf16[512,768]{1,0:T(8,128)(2,1)} %bitcast.159, bf16[768,2304]{1,0:T(8,128)(2,1)} %wv.1, bf16[768,2304]{1,0:T(8,128)(2,1)} %wv.1, bf16[2304,768]{1,0:T(8,128)(2,1)} %bitcast.157, f32[512,128]{1,0:T(8,128)} %broadcast_in_dim.18.bias), custom_call_target="tpu_custom_call" | custom-call | flops 16000000000 | bytes 4000000 | tf_op jit(solution)/shard_map/attend/pallas_call | solution.py:717
  61.6 3.7 %all-to-all-start.1 = ((bf16[8,96,768]{2,1,0:T(8,128)(2,1)}), bf16[8,96,768]{2,1,0:T(8,128)(2,1)S(1)}, u32[]{:S(2)}, u32[]{:S(2)}) async-start(bf16[8,96,768]{2,1,0:T(8,128)(2,1)} %get-tuple-element.75), calls=%async_computation.1 | async-start | bytes 2359296 | tf_op jit(solution)/shard_map/all_to_all | solution.py:867
  65.4 3.1 fusion.2
  69.1 2.6 prepare_cot.1
  73.0 3.1 fusion.10.key_t
  76.1 3.4 %convolution_convert_fusion.query.key.value = bf16[512,2304]{1,0:T(8,128)(2,1)} fusion(bf16[512,768]{1,0:T(8,128)(2,1)S(1)} %bitcast.162, bf16[768,2304]{1,0:T(8,128)(2,1)S(1)} %copy-done.7), kind=kOutput, calls=%fused_computation.3 | convolution fusion | flops 1813118976 | bytes 6684672 | tf_op jit(solution)/shard_map/dot_general | solution.py:30
  79.5 14.5 %all-to-all-done.1.att = bf16[8,96,768]{2,1,0:T(8,128)(2,1)S(1)} async-done(((bf16[8,96,768]{2,1,0:T(8,128)(2,1)}), bf16[8,96,768]{2,1,0:T(8,128)(2,1)S(1)}, u32[]{:S(2)}, u32[]{:S(2)}) %all-to-all-start.1) | async-done | bytes 1179680 | tf_op jit(solution)/shard_map/all_to_all | solution.py:867
  95.1 6.5 %second.1 = (bf16[2,384,768]{2,1,0:T(8,128)(2,1)}, bf16[2,768,384]{2,1,0:T(8,128)(2,1)}, f32[2,256,768]{2,1,0:T(8,128)}, f32[2,256,768]{2,1,0:T(8,128)}) custom-call(s32[5]{0:T(128)} %pad_add_fusion.meta, bf16[8,96,768]{2,1,0:T(8,128)(2,1)} %copy-done.8, bf16[2,4,64,768]{3,2,1,0:T(8,128)(2,1)} %tok.5, bf16[2,1,64,768]{3,2,1,0:T(8,128)(2,1)} %copy-done.25, ...), custom_call_target="tpu_custom_call" | custom-call | flops 7000000000 | bytes 4000000 | tf_op jit(solution)/shard_map/second/pallas_call | solution.py:228
  101.6 40.4 %ffn.1 = (f32[2,256,768]{2,1,0:T(8,128)}, f32[2,384,768]{2,1,0:T(8,128)}, bf16[2,64,768]{2,1,0:T(8,128)(2,1)}, bf16[2,64,768]{2,1,0:T(8,128)(2,1)}, bf16[2,2,192...) custom-call(s32[1]{0:T(128)} %bitcast.core, ...), custom_call_target="tpu_custom_call" | custom-call | flops 35000000512 | bytes 4000000 | tf_op jit(solution)/shard_map/ffn/pallas_call | solution.py:416
  142.2 3.3 %collective-permute-start.2 = (bf16[2,64,768]{2,1,0:T(8,128)(2,1)}, bf16[2,64,768]{2,1,0:T(8,128)(2,1)S(1)}, u32[]{:S(2)}, u32[]{:S(2)}) collective-permute-start(bf16[2,64,768]{2,1,0:T(8,128)(2,1)} %get-tuple-element.91), channel_id=1, source_target_pairs={{0,1},{1,2},{2,3},{3,4},{4,5},{5,6},{6,7},{8,9},{9,10},{10,11},{11... | collective-permute-start | bytes 589832 | tf_op jit(solution)/shard_map/ppermute | solution.py:858
  146.8 3.1 finish_output.1
  150.4 4.3 %collective-permute-done.2.low = bf16[2,64,768]{2,1,0:T(8,128)(2,1)S(1)} collective-permute-done((bf16[2,64,768]{2,1,0:T(8,128)(2,1)}, bf16[2,64,768]{2,1,0:T(8,128)(2,1)S(1)}, u32[]{:S(2)}, u32[]{:S(2)}) %collective-permute-start.2) | collective-permute-done | bytes 196640 | tf_op jit(solution)/shard_map/ppermute | solution.py:858
  155.4 8.4 %middle.1 = (f32[2,256,768]{2,1,0:T(8,128)}, bf16[2,4,64,768]{3,2,1,0:T(8,128)(2,1)}, bf16[2,4,64,768]{3,2,1,0:T(8,128)(2,1)}, f32[2,3,768]{2,1,0:T(4,128)}) custom-call(s32[5]{0:T(128)} %pad_add_fusion.meta, f32[2,384,768]{2,1,0:T(8,128)} %get-tuple-element.90.ge2, bf16[2,64,768]{2,1,0:T(8,128)(2,1)} %copy-done.27, bf16[2,64,768]{2,1,0:T(8,128)(2,1)} %copy-done.28, ...), custom_call_target="tpu_custom_call" | custom-call | flops 8000000000 | bytes 4000000 | tf_op jit(solution)/shard_map/middle/pallas_call | solution.py:540
  163.8 4.8 %all-to-all-start.2 = ((bf16[8,64,768]{2,1,0:T(8,128)(2,1)}), bf16[8,64,768]{2,1,0:T(8,128)(2,1)}, u32[]{:S(2)}, u32[]{:S(2)}) async-start(bf16[8,64,768]{2,1,0:T(8,128)(2,1)} %bitcast.172), calls=%async_computation.2 | async-start | bytes 1572864 | tf_op jit(solution)/shard_map/all_to_all | solution.py:867
  171.5 5.7 %add_convert_fusion = bf16[2,2,192,3072]{3,2,1,0:T(8,128)(2,1)S(1)} fusion(bf16[2,2,192,3072]{3,2,1,0:T(8,128)(2,1)} %collective-permute-done.4, bf16[2,2,192,3072]{3,2,1,0:T(8,128)(2,1)} %get-tuple-element.96), kind=kLoop, calls=%fused_computation | loop fusion | flops 9437184 | bytes 14155776 | tf_op jit(solution)/shard_map/convert_element_type | solution.py:1099
  180.0 9.1 %all-to-all-done.2 = bf16[8,64,768]{2,1,0:T(8,128)(2,1)} async-done(((bf16[8,64,768]{2,1,0:T(8,128)(2,1)}), bf16[8,64,768]{2,1,0:T(8,128)(2,1)}, u32[]{:S(2)}, u32[]{:S(2)}) %all-to-all-start.2) | async-done | bytes 786464 | tf_op jit(solution)/shard_map/all_to_all | solution.py:867
  191.9 20.1 %attend_back.1 = (bf16[3,2,192,768]{3,2,1,0:T(8,128)(2,1)}, bf16[3,2,192,768]{3,2,1,0:T(8,128)(2,1)}, bf16[8,96,768]{2,1,0:T(8,128)(2,1)}) custom-call(s32[2]{0:T(128)} %pad_add_fusion.1.offset, bf16[512,2304]{1,0:T(8,128)(2,1)} %convolution_convert_fusion.query.key.value, bf16[512,2304]{1,0:T(8,128)(2,1)} %convolution_convert_fusion.query.key.value, ...), custom_call_target="tpu_custom_call" | custom-call | flops 23000000512 | bytes 4000000 | tf_op jit(solution)/shard_map/attend_back/pallas_call | solution.py:817
  217.2 4.7 %all-to-all-start.3 = ((bf16[8,96,768]{2,1,0:T(8,128)(2,1)}), bf16[8,96,768]{2,1,0:T(8,128)(2,1)}, u32[]{:S(2)}, u32[]{:S(2)}) async-start(bf16[8,96,768]{2,1,0:T(8,128)(2,1)} %get-tuple-element.106), calls=%async_computation.3 | async-start | bytes 2359296 | tf_op jit(solution)/shard_map/all_to_all | solution.py:867
  237.2 12.4 %all-to-all-done.3.gm = bf16[8,96,768]{2,1,0:T(8,128)(2,1)} async-done(((bf16[8,96,768]{2,1,0:T(8,128)(2,1)}), bf16[8,96,768]{2,1,0:T(8,128)(2,1)}, u32[]{:S(2)}, u32[]{:S(2)}) %all-to-all-start.3) | async-done | bytes 1179680 | tf_op jit(solution)/shard_map/all_to_all | solution.py:867
  255.3 10.0 %leave.1 = (f32[2,4,64,768]{3,2,1,0:T(8,128)}, f32[2,9,768]{2,1,0:T(8,128)}, f32[2,2,768]{2,1,0:T(2,128)}) custom-call(s32[5]{0:T(128)} %pad_add_fusion.meta, bf16[8,96,768]{2,1,0:T(8,128)(2,1)} %all-to-all-done.3.gm, bf16[2,4,64,768]{3,2,1,0:T(8,128)(2,1)} %tok.5, bf16[2,1,64,768]{3,2,1,0:T(8,128)(2,1)} %copy-done.25, bf16[2,1,64,768]{3,2,1,0:T(8,128)(2,1)} %copy-done.26, ...), custom_call_target="tpu_custom_call" | custom-call | flops 10000000000 | bytes 4000000 | tf_op jit(solution)/shard_map/leave/pallas_call | solution.py:636
  268.4 4.1 %all-to-all-start.4 = ((f32[8,112,128]{2,1,0:T(8,128)}), f32[8,112,128]{2,1,0:T(8,128)}, u32[]{:S(2)}, u32[]{:S(2)}) async-start(f32[8,112,128]{2,1,0:T(8,128)} %bitcast.151), calls=%async_computation.4 | async-start | bytes 917504 | tf_op jit(solution)/shard_map/all_to_all | solution.py:867
  281.5 10.4 %all-to-all-done.4 = f32[8,112,128]{2,1,0:T(8,128)} async-done(((f32[8,112,128]{2,1,0:T(8,128)}), f32[8,112,128]{2,1,0:T(8,128)}, u32[]{:S(2)}, u32[]{:S(2)}) %all-to-all-start.4) | async-done | bytes 458784 | tf_op jit(solution)/shard_map/all_to_all | solution.py:867
  292.9 5.7 %all-gather.1 = f32[448,128]{1,0:T(8,128)S(1)} all-gather(f32[112,128]{1,0:T(8,128)S(1)} %reduce_sum.46), channel_id=3, replica_groups=mesh['batch'=4,'seq'=8] {'batch'}, dimensions={0}, use_global_device_ids=true | all-gather | bytes 286720 | tf_op jit(solution)/shard_map/all_gather | solution.py:1182
  303.1 4.9 %fusion.31 = f32[24,768]{1,0:T(8,128)S(1)} fusion(bf16[768,4608]{1,0:T(8,128)(2,1)} %param.24, bf16[8,4608]{1,0:T(8,128)(2,1)S(1)} %get-tuple-element.166, bf16[8,4608]{1,0:T(8,128)(2,1)S(1)} %get-tuple-element.167, bf16[8,4608]{1,0:T(8,128)(2,1)S(1)} %get-tuple-element.165), kind=kOutput, calls=%fused_computation.80 | convolution fusion | flops 170532864 | bytes 7372800 | tf_op jit(solution)/shard_map/dot_general | solution.py:30
  313.1 5.6 %collective-permute-done.17 = bf16[4,24,768]{2,1,0:T(8,128)(2,1)S(1)} collective-permute-done((bf16[4,24,768]{2,1,0:T(8,128)(2,1)S(1)}, bf16[4,24,768]{2,1,0:T(8,128)(2,1)S(1)}, u32[]{:S(2)}, u32[]{:S(2)}) %collective-permute-start.17) | collective-permute-done | bytes 147488 | tf_op jit(solution)/shard_map/ppermute | solution.py:890
  (192 shorter events, 75.4 us)
Async XLA Ops:
  0.6 9.3 %copy-start = (bf16[1000,768]{1,0:T(8,128)(2,1)S(1)}, bf16[1000,768]{1,0:T(8,128)(2,1)}, u32[]{:S(2)}) copy-start(bf16[1000,768]{1,0:T(8,128)(2,1)} %param.23) | copy-start | bytes 4608004
  0.7 9.3 %copy-start.22 = (s32[2]{0:T(128)S(1)}, s32[2]{0:T(128)}, u32[]{:S(2)}) copy-start(s32[2]{0:T(128)} %param.19) | copy-start | bytes 28
  1.8 8.5 %slice-start.1 = ((f32[4608]{0:T(1024)}), f32[1536]{0:T(1024)S(1)}, s32[]{:S(2)}) async-start(f32[4608]{0:T(1024)} %param.25), calls=%async_computation.6 | async-start | bytes 16384 | tf_op jit(solution)/shard_map/slice | solution.py:1016
  1.9 11.8 %collective-permute-start = (bf16[2,1,64,768]{3,2,1,0:T(8,128)(2,1)S(1)}, bf16[2,1,64,768]{3,2,1,0:T(8,128)(2,1)S(1)}, u32[]{:S(2)}, u32[]{:S(2)}) collective-permute-start(bf16[2,1,64,768]{3,2,1,0:T(8,128)(2,1)S(1)} %get-tuple-element.152), channel_id=1, source_target_pairs={{0,1},{1,2},{2,3},{3,4},{4,5},{5,6},{6,7},{8,9},{9,10},{10,11},{11... | collective-permute-start | bytes 589832 | tf_op jit(solution)/shard_map/ppermute | solution.py:858
  6.7 8.3 %collective-permute-start.1 = (bf16[2,1,64,768]{3,2,1,0:T(8,128)(2,1)S(1)}, bf16[2,1,64,768]{3,2,1,0:T(8,128)(2,1)S(1)}, u32[]{:S(2)}, u32[]{:S(2)}) collective-permute-start(bf16[2,1,64,768]{3,2,1,0:T(8,128)(2,1)S(1)} %get-tuple-element.151), channel_id=1, source_target_pairs={{1,0},{2,1},{3,2},{4,3},{5,4},{6,5},{7,6},{9,8},{10,9},{11,10},{12... | collective-permute-start | bytes 589832 | tf_op jit(solution)/shard_map/ppermute | solution.py:863
  20.7 27.4 %all-to-all-start = ((bf16[8,64,768]{2,1,0:T(8,128)(2,1)}), bf16[8,64,768]{2,1,0:T(8,128)(2,1)S(1)}, u32[]{:S(2)}, u32[]{:S(2)}) async-start(bf16[8,64,768]{2,1,0:T(8,128)(2,1)} %bitcast.171), calls=%async_computation | async-start | bytes 1572864 | tf_op jit(solution)/shard_map/all_to_all | solution.py:867
  61.6 32.4 %all-to-all-start.1 = ((bf16[8,96,768]{2,1,0:T(8,128)(2,1)}), bf16[8,96,768]{2,1,0:T(8,128)(2,1)S(1)}, u32[]{:S(2)}, u32[]{:S(2)}) async-start(bf16[8,96,768]{2,1,0:T(8,128)(2,1)} %get-tuple-element.75), calls=%async_computation.1 | async-start | bytes 2359296 | tf_op jit(solution)/shard_map/all_to_all | solution.py:867
  142.0 26.7 %collective-permute-start.4 = (bf16[2,2,192,3072]{3,2,1,0:T(8,128)(2,1)}, bf16[2,2,192,3072]{3,2,1,0:T(8,128)(2,1)}, u32[]{:S(2)}, u32[]{:S(2)}) collective-permute-start(bf16[2,2,192,3072]{3,2,1,0:T(8,128)(2,1)} %get-tuple-element.97), channel_id=1, source_target_pairs={{0,8},{8,0},{16,24},{24,16},{1,9},{9,1},{17,25},{25,17},{2,10},{10... | collective-permute-start | bytes 14155784 | tf_op jit(solution)/shard_map/ppermute | solution.py:890
  142.2 12.5 %collective-permute-start.2 = (bf16[2,64,768]{2,1,0:T(8,128)(2,1)}, bf16[2,64,768]{2,1,0:T(8,128)(2,1)S(1)}, u32[]{:S(2)}, u32[]{:S(2)}) collective-permute-start(bf16[2,64,768]{2,1,0:T(8,128)(2,1)} %get-tuple-element.91), channel_id=1, source_target_pairs={{0,1},{1,2},{2,3},{3,4},{4,5},{5,6},{6,7},{8,9},{9,10},{10,11},{11... | collective-permute-start | bytes 589832 | tf_op jit(solution)/shard_map/ppermute | solution.py:858
  145.5 9.2 %collective-permute-start.3 = (bf16[2,64,768]{2,1,0:T(8,128)(2,1)}, bf16[2,64,768]{2,1,0:T(8,128)(2,1)S(1)}, u32[]{:S(2)}, u32[]{:S(2)}) collective-permute-start(bf16[2,64,768]{2,1,0:T(8,128)(2,1)} %get-tuple-element.92), channel_id=1, source_target_pairs={{1,0},{2,1},{3,2},{4,3},{5,4},{6,5},{7,6},{9,8},{10,9},{11,10},{12... | collective-permute-start | bytes 589832 | tf_op jit(solution)/shard_map/ppermute | solution.py:863
  163.8 25.3 %all-to-all-start.2 = ((bf16[8,64,768]{2,1,0:T(8,128)(2,1)}), bf16[8,64,768]{2,1,0:T(8,128)(2,1)}, u32[]{:S(2)}, u32[]{:S(2)}) async-start(bf16[8,64,768]{2,1,0:T(8,128)(2,1)} %bitcast.172), calls=%async_computation.2 | async-start | bytes 1572864 | tf_op jit(solution)/shard_map/all_to_all | solution.py:867
  171.5 40.6 %collective-permute-start.11 = (bf16[2,2,2,2,24,768]{5,4,2,1,0,3:T(8,128)(2,1)}, bf16[2,2,2,2,24,768]{5,4,2,1,0,3:T(8,128)(2,1)}, u32[]{:S(2)}, u32[]{:S(2)}) collective-permute-start(bf16[2,2,2,2,24,768]{5,4,2,1,0,3:T(8,128)(2,1)} %bitcast.150), channel_id=1, source_target_pairs={{0,8},{8,0},{16,24},{24,16},{1,9},{9,1},{17,25},{25,17},{2,10},{10... | collective-permute-start | bytes 1769480 | tf_op jit(solution)/shard_map/ppermute | solution.py:890
  189.1 26.9 %collective-permute-start.5 = (bf16[2,2,2,24,3072]{4,3,2,1,0:T(8,128)(2,1)}, bf16[2,2,2,24,3072]{4,3,2,1,0:T(8,128)(2,1)}, u32[]{:S(2)}, u32[]{:S(2)}) collective-permute-start(bf16[2,2,2,24,3072]{4,3,2,1,0:T(8,128)(2,1)} %get-tuple-element.104), channel_id=1, source_target_pairs={{0,16},{8,24},{16,0},{24,8},{1,17},{9,25},{17,1},{25,9},{2,18},{10... | collective-permute-start | bytes 3538952 | tf_op jit(solution)/shard_map/ppermute | solution.py:890
  190.6 26.6 %collective-permute-start.6 = (bf16[2,2,2,24,3072]{4,3,2,1,0:T(8,128)(2,1)}, bf16[2,2,2,24,3072]{4,3,2,1,0:T(8,128)(2,1)}, u32[]{:S(2)}, u32[]{:S(2)}) collective-permute-start(bf16[2,2,2,24,3072]{4,3,2,1,0:T(8,128)(2,1)} %get-tuple-element.105), channel_id=1, source_target_pairs={{0,1},{1,0},{2,3},{3,2},{4,5},{5,4},{6,7},{7,6},{8,9},{9,8},{10,11... | collective-permute-start | bytes 3538952 | tf_op jit(solution)/shard_map/ppermute | solution.py:890
  212.1 17.7 %collective-permute-start.10 = (bf16[3,2,192,768]{3,2,1,0:T(8,128)(2,1)}, bf16[3,2,192,768]{3,2,1,0:T(8,128)(2,1)}, u32[]{:S(2)}, u32[]{:S(2)}) collective-permute-start(bf16[3,2,192,768]{3,2,1,0:T(8,128)(2,1)} %get-tuple-element.124), channel_id=1, source_target_pairs={{0,8},{8,0},{16,24},{24,16},{1,9},{9,1},{17,25},{25,17},{2,10},{10... | collective-permute-start | bytes 5308424 | tf_op jit(solution)/shard_map/ppermute | solution.py:890
  217.2 32.5 %all-to-all-start.3 = ((bf16[8,96,768]{2,1,0:T(8,128)(2,1)}), bf16[8,96,768]{2,1,0:T(8,128)(2,1)}, u32[]{:S(2)}, u32[]{:S(2)}) async-start(bf16[8,96,768]{2,1,0:T(8,128)(2,1)} %get-tuple-element.106), calls=%async_computation.3 | async-start | bytes 2359296 | tf_op jit(solution)/shard_map/all_to_all | solution.py:867
  224.5 25.9 %collective-permute-start.7 = (bf16[2,2,24,3072]{3,2,1,0:T(8,128)(2,1)}, bf16[2,2,24,3072]{3,2,1,0:T(8,128)(2,1)}, u32[]{:S(2)}, u32[]{:S(2)}) collective-permute-start(bf16[2,2,24,3072]{3,2,1,0:T(8,128)(2,1)} %dynamic-slice_bitcast_fusion.7), channel_id=1, source_target_pairs={{0,1},{1,0},{2,3},{3,2},{4,5},{5,4},{6,7},{7,6},{8,9},{9,8},{10,11... | collective-permute-start | bytes 1769480 | tf_op jit(solution)/shard_map/ppermute | solution.py:890
  229.2 21.2 %collective-permute-start.8 = (bf16[2,2,24,3072]{3,2,1,0:T(8,128)(2,1)}, bf16[2,2,24,3072]{3,2,1,0:T(8,128)(2,1)}, u32[]{:S(2)}, u32[]{:S(2)}) collective-permute-start(bf16[2,2,24,3072]{3,2,1,0:T(8,128)(2,1)} %dynamic-slice_bitcast_fusion.6), channel_id=1, source_target_pairs={{0,16},{8,24},{16,0},{24,8},{1,17},{9,25},{17,1},{25,9},{2,18},{10... | collective-permute-start | bytes 1769480 | tf_op jit(solution)/shard_map/ppermute | solution.py:890
  234.0 38.5 %collective-permute-start.13 = (bf16[2,2,2,2,24,768]{5,4,3,2,1,0:T(8,128)(2,1)}, bf16[2,2,2,2,24,768]{5,4,3,2,1,0:T(8,128)(2,1)}, u32[]{:S(2)}, u32[]{:S(2)}) collective-permute-start(bf16[2,2,2,2,24,768]{5,4,3,2,1,0:T(8,128)(2,1)} %get-tuple-element.143), channel_id=1, source_target_pairs={{0,1},{1,0},{2,3},{3,2},{4,5},{5,4},{6,7},{7,6},{8,9},{9,8},{10,11... | collective-permute-start | bytes 1769480 | tf_op jit(solution)/shard_map/ppermute | solution.py:890
  234.6 15.8 %copy-start.4 = (bf16[2,2,2,24,3072]{4,3,2,1,0:T(8,128)(2,1)S(1)}, bf16[2,2,2,24,3072]{4,3,2,1,0:T(8,128)(2,1)}, u32[]{:S(2)}) copy-start(bf16[2,2,2,24,3072]{4,3,2,1,0:T(8,128)(2,1)} %copy-done.3) | copy-start | bytes 3538948
  235.7 15.9 %copy-start.6 = (bf16[2,2,2,24,3072]{4,3,2,1,0:T(8,128)(2,1)S(1)}, bf16[2,2,2,24,3072]{4,3,2,1,0:T(8,128)(2,1)}, u32[]{:S(2)}) copy-start(bf16[2,2,2,24,3072]{4,3,2,1,0:T(8,128)(2,1)} %copy-done.5) | copy-start | bytes 3538948
  235.7 36.8 %collective-permute-start.12 = (bf16[2,2,2,2,24,768]{5,4,3,2,1,0:T(8,128)(2,1)}, bf16[2,2,2,2,24,768]{5,4,3,2,1,0:T(8,128)(2,1)}, u32[]{:S(2)}, u32[]{:S(2)}) collective-permute-start(bf16[2,2,2,2,24,768]{5,4,3,2,1,0:T(8,128)(2,1)} %get-tuple-element.145), channel_id=1, source_target_pairs={{0,16},{8,24},{16,0},{24,8},{1,17},{9,25},{17,1},{25,9},{2,18},{10... | collective-permute-start | bytes 1769480 | tf_op jit(solution)/shard_map/ppermute | solution.py:890
  253.8 14.6 %collective-permute-start.9 = (bf16[2,2,24,3072]{3,2,1,0:T(8,128)(2,1)}, bf16[2,2,24,3072]{3,2,1,0:T(8,128)(2,1)S(1)}, u32[]{:S(2)}, u32[]{:S(2)}) collective-permute-start(bf16[2,2,24,3072]{3,2,1,0:T(8,128)(2,1)} %get-tuple-element.150), channel_id=1, source_target_pairs={{0,2},{1,3},{2,0},{3,1},{4,6},{5,7},{6,4},{7,5},{8,10},{9,11},{10,... | collective-permute-start | bytes 1769480 | tf_op jit(solution)/shard_map/ppermute | solution.py:890
  255.2 10.0 %copy-start.20 = (f32[2,3,768]{2,1,0:T(4,128)S(1)}, f32[2,3,768]{2,1,0:T(4,128)}, u32[]{:S(2)}) copy-start(f32[2,3,768]{2,1,0:T(4,128)} %get-tuple-element.120) | copy-start | bytes 55300
  255.3 10.0 %copy-start.21 = (f32[2,1,768]{2,1,0:T(1,128)S(1)}, f32[2,1,768]{2,1,0:T(1,128)}, u32[]{:S(2)}) copy-start(f32[2,1,768]{2,1,0:T(1,128)} %get-tuple-element.121) | copy-start | bytes 18436
  268.4 23.5 %all-to-all-start.4 = ((f32[8,112,128]{2,1,0:T(8,128)}), f32[8,112,128]{2,1,0:T(8,128)}, u32[]{:S(2)}, u32[]{:S(2)}) async-start(f32[8,112,128]{2,1,0:T(8,128)} %bitcast.151), calls=%async_computation.4 | async-start | bytes 917504 | tf_op jit(solution)/shard_map/all_to_all | solution.py:867
  275.7 23.1 %collective-permute-start.14 = (bf16[2,2,2,24,768]{4,3,2,1,0:T(8,128)(2,1)}, bf16[2,2,2,24,768]{4,3,2,1,0:T(8,128)(2,1)S(1)}, u32[]{:S(2)}, u32[]{:S(2)}) collective-permute-start(bf16[2,2,2,24,768]{4,3,2,1,0:T(8,128)(2,1)} %get-tuple-element.159), channel_id=1, source_target_pairs={{0,1},{1,0},{2,3},{3,2},{4,5},{5,4},{6,7},{7,6},{8,9},{9,8},{10,11... | collective-permute-start | bytes 884744 | tf_op jit(solution)/shard_map/ppermute | solution.py:890
  277.6 21.4 %collective-permute-start.15 = (bf16[2,2,2,24,768]{4,3,2,1,0:T(8,128)(2,1)}, bf16[2,2,2,24,768]{4,3,2,1,0:T(8,128)(2,1)S(1)}, u32[]{:S(2)}, u32[]{:S(2)}) collective-permute-start(bf16[2,2,2,24,768]{4,3,2,1,0:T(8,128)(2,1)} %get-tuple-element.157), channel_id=1, source_target_pairs={{0,16},{8,24},{16,0},{24,8},{1,17},{9,25},{17,1},{25,9},{2,18},{10... | collective-permute-start | bytes 884744 | tf_op jit(solution)/shard_map/ppermute | solution.py:890
  279.1 21.4 %collective-permute-start.18 = (bf16[2,24,3072]{2,1,0:T(8,128)(2,1)}, bf16[2,24,3072]{2,1,0:T(8,128)(2,1)}, u32[]{:S(2)}, u32[]{:S(2)}) collective-permute-start(bf16[2,24,3072]{2,1,0:T(8,128)(2,1)} %get-tuple-element.155), channel_id=1, source_target_pairs={{0,4},{1,5},{2,6},{3,7},{4,0},{5,1},{6,2},{7,3},{8,12},{9,13},{10,... | collective-permute-start | bytes 884744 | tf_op jit(solution)/shard_map/ppermute | solution.py:890
  299.1 9.6 %collective-permute-start.16 = (bf16[4,2,24,768]{3,2,1,0:T(8,128)(2,1)S(1)}, bf16[4,2,24,768]{3,2,1,0:T(8,128)(2,1)S(1)}, u32[]{:S(2)}, u32[]{:S(2)}) collective-permute-start(bf16[4,2,24,768]{3,2,1,0:T(8,128)(2,1)S(1)} %fusion.30), channel_id=1, source_target_pairs={{0,2},{1,3},{2,0},{3,1},{4,6},{5,7},{6,4},{7,5},{8,10},{9,11},{10,... | collective-permute-start | bytes 884744 | tf_op jit(solution)/shard_map/ppermute | solution.py:890
  308.8 9.9 %collective-permute-start.17 = (bf16[4,24,768]{2,1,0:T(8,128)(2,1)S(1)}, bf16[4,24,768]{2,1,0:T(8,128)(2,1)S(1)}, u32[]{:S(2)}, u32[]{:S(2)}) collective-permute-start(bf16[4,24,768]{2,1,0:T(8,128)(2,1)S(1)} %dynamic-slice_bitcast_fusion.14), channel_id=1, source_target_pairs={{0,4},{1,5},{2,6},{3,7},{4,0},{5,1},{6,2},{7,3},{8,12},{9,13},{10,... | collective-permute-start | bytes 442376 | tf_op jit(solution)/shard_map/ppermute | solution.py:890
  309.5 10.7 %copy-start.1 = (bf16[1000,768]{1,0:T(8,128)(2,1)S(1)}, bf16[1000,768]{1,0:T(8,128)(2,1)}, u32[]{:S(2)}) copy-start(bf16[1000,768]{1,0:T(8,128)(2,1)} %param.23) | copy-start | bytes 4608004
  (24 other events, 63.6 us)

commit v6 on v5

--- a/solution.py
+++ b/solution.py
@@ -898,6 +898,22 @@
     return lax.optimization_barrier((values,) + others)[0]
 
 
+STEPS = ("yxl", "xly", "lyx")
+
+
+def step_of(parts, dims, step):
+    cut = [split(part, left, order[step]) for part, left, order in zip(parts, dims, STEPS)]
+    return tuple(c[0] for c in cut), tuple(c[1] for c in cut), [c[2] for c in cut]
+
+
+def hops_of(sends, step):
+    return tuple(hop(send, order[step]) for send, order in zip(sends, STEPS))
+
+
+def fold_of(keeps, gots):
+    return [add(keep, got).astype(BF16) for keep, got in zip(keeps, gots)]
+
+
 def reduce_rest(values, dims, order):
     for bit in order:
         send, keep, dims = split(values.astype(BF16), dims, bit)
@@ -1097,20 +1113,21 @@
         if halving:
             keep_c = after(keep_c, grad_attended)
             sums = add(keep_c, got_c).astype(BF16).reshape(2, 2, 2, 2, 2, D // devices, hidden)
-            send_a, keep_a, dims_a = split(sums[0], "yhlx", "y")
-            send_b, keep_b, dims_b = split(sums[1], "yhlx", "x")
+            third = hidden // 3
+            cuts = [sums[..., k * third : (k + 1) * third] for k in range(3)]
+            sends, keeps, dims = step_of(cuts, ["yhlx"] * 3, 0)
             late_branch = after(flat_branch, got_c)
             proj_grad = mm(att_own, late_branch, (((0,), (0,)), ((), ()))).astype(BF16)
             send_p, keep_p, _ = split(blocks_of(proj_grad), ORDER, "c")
             got_p = hop(send_p, "c")
-            gatt, send_a, send_b, send_p = lax.optimization_barrier((gatt, send_a, send_b, send_p))
-            got_a, got_b = hop(send_a, "y"), hop(send_b, "x")
+            gatt, sends, send_p, gate_sums = lax.optimization_barrier((gatt, sends, send_p, gate_sums))
+            gots = hops_of(sends, 0)
         send_r, keep_r, gm_windows = attend_back(
             offset, triple, key_t, bias, lse, gatt, qkv_weight, grouped_t, seq_count, tall
         )
         gm = swap(gm_windows)
         if halving:
-            gm_windows, got_a, got_b = lax.optimization_barrier((gm_windows, got_a, got_b))
+            gm_windows, gots = lax.optimization_barrier((gm_windows, gots))
         gm = swap(gm_windows)
     else:
         sent = grad_attended.reshape(blocks, per_group, share, wide).transpose(0, 2, 1, 3)
@@ -1129,21 +1146,15 @@
 
     if halving:
         got_r = hop(send_r, "c")
-        keep_a, keep_b = after(keep_a, keep_r), after(keep_b, keep_r)
-        send_a, keep_a, dims_a = split(add(keep_a, got_a).astype(BF16), dims_a, "x")
-        send_b, keep_b, dims_b = split(add(keep_b, got_b).astype(BF16), dims_b, "y")
+        keeps = lax.optimization_barrier((keeps, keep_r))[0]
+        sends, keeps, dims = step_of(fold_of(keeps, gots), dims, 1)
         sums = add(keep_r, got_r).astype(BF16).reshape(3, 2, 2, 2, 2, D // devices, D)
         sums_p = add(keep_p, got_p).astype(BF16)
         send_one, keep_one, dims_one = split(sums[:2], "yhlx", "y")
         send_two, keep_two, dims_two = split(jnp.stack([sums[2], sums_p]), "yhlx", "x")
-        gm = after(gm, send_a, send_b)
-        got_a, got_b = hop(send_a, "x"), hop(send_b, "y")
+        gm = after(gm, *sends)
+        gots = hops_of(sends, 1)
         got_one, got_two = hop(send_one, "y"), hop(send_two, "x")
-        gm, got_a, got_b = lax.optimization_barrier((gm, got_a, got_b))
-        pair = jnp.stack([add(keep_a, got_a), add(keep_b, got_b)]).astype(BF16)
-        send_l, keep_l, dims_l = split(pair, dims_a, "l")
-        gm = after(gm, send_l)
-        got_l = hop(send_l, "l")
     total = batch_count * latents
 
     here = batch_place * seq_count + seq_place
@@ -1171,10 +1182,13 @@
     sliced = (jnp.sum(conv_attn_part, axis=0), conv_ffn_part)
     message = payload_of(common, sliced)
     if halving:
-        message, keep_l, got_l, keep_one, keep_two = lax.optimization_barrier(
-            (message, keep_l, got_l, keep_one, keep_two)
+        message, keeps, gots, keep_one, keep_two = lax.optimization_barrier(
+            (message, keeps, gots, keep_one, keep_two)
         )
-        send_h, keep_h, _ = split(add(keep_l, got_l).astype(BF16), dims_l, "h")
+        sends, keeps, dims = step_of(fold_of(keeps, gots), dims, 2)
+        gots = hops_of(sends, 2)
+        pair = jnp.concatenate(fold_of(keeps, gots), axis=-1)
+        send_h, keep_h, _ = split(pair, dims[0], "h")
         got_h = hop(send_h, "h")
         send_one, keep_one, dims_one = split(add(keep_one, got_one).astype(BF16), dims_one, "x")
         send_two, keep_two, dims_two = split(add(keep_two, got_two).astype(BF16), dims_two, "y")

time: 322 us -> 315 us (0.978)
  waiting for transfers between devices: 67.6 us -> 58.1 us
  starting transfers between devices: 49.7 us -> 53.5 us
    all_to_all x5, waiting for transfers between devices: 52.7 us -> 40.8 us  [swap(): return lax.all_to_all(values, 'seq', 0, 0, tiled=False)]
    convert_element_type x3 -> x9, other arithmetic: 3.5 us -> 8.26 us  [the longest x8 7.01 us: fold_of(): return [add(keep, got).astype(BF16) for keep, got in zip(keeps, gots)]]
    ppermute x15 -> x19, starting transfers between devices: 14.6 us -> 19 us  [hop(): return lax.ppermute(values, axis, [(i, i ^ mask) for i in range(count)])]
    ppermute x15 -> x19, waiting for transfers between devices: 9.35 us -> 11.8 us  [hop(): return lax.ppermute(values, axis, [(i, i ^ mask) for i in range(count)])]
    unnamed x71 -> x57, local copies, waits for them, and re-layouts: 11.8 us -> 11.3 us
  transfers between devices with their start and end apart: 24 -> 28, of which waited for: 11 -> 9; matrix products, arithmetic and copies ran while one was open for 23% -> 23% of each run, Pallas kernels for 14% -> 14%
where the time goes in v6:
time: 315 us; the launch traced here: 313 us
  Pallas kernels  109 us (35%)
  waiting for transfers between devices  58.1 us (18%)
  starting transfers between devices  53.5 us (17%)
  local copies, waits for them, and re-layouts  31.7 us (10%)
  other arithmetic  25.2 us (8%)
  matrix products  23.3 us (7%)
  blocking collectives  10.9 us (3%)
    all_to_all x5, waiting for transfers between devices, swap(): return lax.all_to_all(values, 'seq', 0, 0, tiled=False)  40.8 us
    pallas_call x1, Pallas kernels, ffn(): pl.pallas_call(ffn_kernel, out_shape=(jax.ShapeDtypeStruct((latents, own,...  40.4 us
    all_to_all x5, starting transfers between devices, swap(): return lax.all_to_all(values, 'seq', 0, 0, tiled=False)  23.8 us
    dot_general x8, matrix products, mm(): return lax.dot_general(left, right, dims, preferred_element_type=F32)  20.2 us
    pallas_call x1, Pallas kernels, attend_back(): pl.pallas_call(attend_back_kernel, out_shape=(parts, parts, jax.ShapeDtyp...  20.1 us
    ppermute x19, starting transfers between devices, hop(): return lax.ppermute(values, axis, [(i, i ^ mask) for i in range(count)])  19 us
    pallas_call x1, Pallas kernels, attend(): pl.pallas_call(attend_kernel, out_shape=(jax.ShapeDtypeStruct((strips, wi...  12.6 us
    ppermute x19, waiting for transfers between devices, hop(): return lax.ppermute(values, axis, [(i, i ^ mask) for i in range(count)])  11.8 us
  transfers between devices with their start and end apart: 28, of which 9 were waited for; matrix products, arithmetic and copies ran while one was open for 23% of the time, Pallas kernels for 14%

profile of v6, /device:TPU:0, one launch (start us, length us, event | category | flops | bytes accessed | tf_op | source)
XLA Modules:
  0.0 313.0 jit_solution(16707540840537055385)
XLA Ops:
  1.8 4.9 %collective-permute-start = (bf16[2,1,64,768]{3,2,1,0:T(8,128)(2,1)S(1)}, bf16[2,1,64,768]{3,2,1,0:T(8,128)(2,1)S(1)}, u32[]{:S(2)}, u32[]{:S(2)}) collective-permute-start(bf16[2,1,64,768]{3,2,1,0:T(8,128)(2,1)S(1)} %get-tuple-element.167), channel_id=1, source_target_pairs={{0,1},{1,2},{2,3},{3,4},{4,5},{5,6},{6,7},{8,9},{9,10},{10,11},{11... | collective-permute-start | bytes 589832 | tf_op jit(solution)/shard_map/ppermute | solution.py:858
  11.0 2.7 fusion.7.lead
  15.7 5.0 %enter.1 = bf16[2,4,64,768]{3,2,1,0:T(8,128)(2,1)} custom-call(s32[5]{0:T(128)} %pad_add_fusion.meta, bf16[2,4,64,768]{3,2,1,0:T(8,128)(2,1)} %tok.5, bf16[2,1,64,768]{3,2,1,0:T(8,128)(2,1)} %copy-done.18, bf16[2,1,64,768]{3,2,1,0:T(8,128)(2,1)} %copy-done.19, f32[2,1536]{1,0:T(2,128)} %fusion.7.lead, bf16[9,768]{1,0:T(8,128)(2,1)} %kern.3), custom_call_target="tpu_custom_call" | custom-call | flops 6000000000 | bytes 4000000 | tf_op jit(solution)/shard_map/enter/pallas_call | solution.py:134
  20.7 7.1 %all-to-all-start = ((bf16[8,64,768]{2,1,0:T(8,128)(2,1)}), bf16[8,64,768]{2,1,0:T(8,128)(2,1)S(1)}, u32[]{:S(2)}, u32[]{:S(2)}) async-start(bf16[8,64,768]{2,1,0:T(8,128)(2,1)} %bitcast.191), calls=%async_computation | async-start | bytes 1572864 | tf_op jit(solution)/shard_map/all_to_all | solution.py:867
  29.0 5.7 %copy.92 = bf16[768,2304]{0,1:T(8,128)(2,1)} copy(bf16[768,2304]{1,0:T(8,128)(2,1)} %wv.1) | data formatting | bytes 7077888 | tf_op args[11]
  34.8 5.2 %all-gather.2 = f32[4,2,1025]{2,1,0:T(2,128)S(1)} all-gather(f32[1,2,1025]{2,1,0:T(2,128)S(1)} %maximum_bitcast_fusion), channel_id=2, replica_groups=mesh['batch'=4,'seq'=8] {'batch'}, dimensions={0}, use_global_device_ids=true | all-gather | bytes 41000 | tf_op jit(solution)/shard_map/all_gather | solution.py:1078
  41.9 6.1 %all-to-all-done = bf16[8,64,768]{2,1,0:T(8,128)(2,1)S(1)} async-done(((bf16[8,64,768]{2,1,0:T(8,128)(2,1)}), bf16[8,64,768]{2,1,0:T(8,128)(2,1)S(1)}, u32[]{:S(2)}, u32[]{:S(2)}) %all-to-all-start) | async-done | bytes 786464 | tf_op jit(solution)/shard_map/all_to_all | solution.py:867
  49.0 12.6 %attend.1 = (bf16[8,96,768]{2,1,0:T(8,128)(2,1)}, f32[3,4,512]{2,1,0:T(4,128)}) custom-call(s32[2]{0:T(128)} %pad_add_fusion.1.offset, bf16[512,768]{1,0:T(8,128)(2,1)} %bitcast.177, bf16[768,2304]{1,0:T(8,128)(2,1)} %wv.1, bf16[768,2304]{1,0:T(8,128)(2,1)} %wv.1, bf16[2304,768]{1,0:T(8,128)(2,1)} %bitcast.175, f32[512,128]{1,0:T(8,128)} %broadcast_in_dim.18.bias), custom_call_target="tpu_custom_call" | custom-call | flops 16000000000 | bytes 4000000 | tf_op jit(solution)/shard_map/attend/pallas_call | solution.py:717
  61.6 3.7 %all-to-all-start.1 = ((bf16[8,96,768]{2,1,0:T(8,128)(2,1)}), bf16[8,96,768]{2,1,0:T(8,128)(2,1)S(1)}, u32[]{:S(2)}, u32[]{:S(2)}) async-start(bf16[8,96,768]{2,1,0:T(8,128)(2,1)} %get-tuple-element.79), calls=%async_computation.1 | async-start | bytes 2359296 | tf_op jit(solution)/shard_map/all_to_all | solution.py:867
  65.3 3.1 fusion.2
  69.1 2.6 prepare_cot.1
  72.9 3.1 fusion.10.key_t
  76.0 3.4 %convolution_convert_fusion.query.key.value = bf16[512,2304]{1,0:T(8,128)(2,1)} fusion(bf16[512,768]{1,0:T(8,128)(2,1)S(1)} %bitcast.180, bf16[768,2304]{1,0:T(8,128)(2,1)S(1)} %copy-done.4), kind=kOutput, calls=%fused_computation.3 | convolution fusion | flops 1813118976 | bytes 6684672 | tf_op jit(solution)/shard_map/dot_general | solution.py:30
  79.4 14.5 %all-to-all-done.1.att = bf16[8,96,768]{2,1,0:T(8,128)(2,1)S(1)} async-done(((bf16[8,96,768]{2,1,0:T(8,128)(2,1)}), bf16[8,96,768]{2,1,0:T(8,128)(2,1)S(1)}, u32[]{:S(2)}, u32[]{:S(2)}) %all-to-all-start.1) | async-done | bytes 1179680 | tf_op jit(solution)/shard_map/all_to_all | solution.py:867
  95.0 6.5 %second.1 = (bf16[2,384,768]{2,1,0:T(8,128)(2,1)}, bf16[2,768,384]{2,1,0:T(8,128)(2,1)}, f32[2,256,768]{2,1,0:T(8,128)}, f32[2,256,768]{2,1,0:T(8,128)}) custom-call(s32[5]{0:T(128)} %pad_add_fusion.meta, bf16[8,96,768]{2,1,0:T(8,128)(2,1)} %copy-done.5, bf16[2,4,64,768]{3,2,1,0:T(8,128)(2,1)} %tok.5, bf16[2,1,64,768]{3,2,1,0:T(8,128)(2,1)} %copy-done.18, ...), custom_call_target="tpu_custom_call" | custom-call | flops 7000000000 | bytes 4000000 | tf_op jit(solution)/shard_map/second/pallas_call | solution.py:228
  101.5 40.4 %ffn.1 = (f32[2,256,768]{2,1,0:T(8,128)}, f32[2,384,768]{2,1,0:T(8,128)}, bf16[2,64,768]{2,1,0:T(8,128)(2,1)}, bf16[2,64,768]{2,1,0:T(8,128)(2,1)}, bf16[2,2,192...) custom-call(s32[1]{0:T(128)} %bitcast.core, ...), custom_call_target="tpu_custom_call" | custom-call | flops 35000000512 | bytes 4000000 | tf_op jit(solution)/shard_map/ffn/pallas_call | solution.py:416
  142.1 3.3 %collective-permute-start.2 = (bf16[2,64,768]{2,1,0:T(8,128)(2,1)}, bf16[2,64,768]{2,1,0:T(8,128)(2,1)S(1)}, u32[]{:S(2)}, u32[]{:S(2)}) collective-permute-start(bf16[2,64,768]{2,1,0:T(8,128)(2,1)} %get-tuple-element.95), channel_id=1, source_target_pairs={{0,1},{1,2},{2,3},{3,4},{4,5},{5,6},{6,7},{8,9},{9,10},{10,11},{11... | collective-permute-start | bytes 589832 | tf_op jit(solution)/shard_map/ppermute | solution.py:858
  146.7 3.1 finish_output.1
  149.8 4.9 %collective-permute-done.2.low = bf16[2,64,768]{2,1,0:T(8,128)(2,1)S(1)} collective-permute-done((bf16[2,64,768]{2,1,0:T(8,128)(2,1)}, bf16[2,64,768]{2,1,0:T(8,128)(2,1)S(1)}, u32[]{:S(2)}, u32[]{:S(2)}) %collective-permute-start.2) | collective-permute-done | bytes 196640 | tf_op jit(solution)/shard_map/ppermute | solution.py:858
  155.4 8.4 %middle.1 = (f32[2,256,768]{2,1,0:T(8,128)}, bf16[2,4,64,768]{3,2,1,0:T(8,128)(2,1)}, bf16[2,4,64,768]{3,2,1,0:T(8,128)(2,1)}, f32[2,3,768]{2,1,0:T(4,128)}) custom-call(s32[5]{0:T(128)} %pad_add_fusion.meta, f32[2,384,768]{2,1,0:T(8,128)} %get-tuple-element.94.ge2, bf16[2,64,768]{2,1,0:T(8,128)(2,1)} %copy-done.20, bf16[2,64,768]{2,1,0:T(8,128)(2,1)} %copy-done.21, ...), custom_call_target="tpu_custom_call" | custom-call | flops 8000000000 | bytes 4000000 | tf_op jit(solution)/shard_map/middle/pallas_call | solution.py:540
  163.8 4.8 %all-to-all-start.2 = ((bf16[8,64,768]{2,1,0:T(8,128)(2,1)}), bf16[8,64,768]{2,1,0:T(8,128)(2,1)}, u32[]{:S(2)}, u32[]{:S(2)}) async-start(bf16[8,64,768]{2,1,0:T(8,128)(2,1)} %bitcast.192), calls=%async_computation.2 | async-start | bytes 1572864 | tf_op jit(solution)/shard_map/all_to_all | solution.py:867
  171.4 3.8 %add_convert_fusion = bf16[2,2,192,3072]{3,2,1,0:T(8,128)(2,1)S(1)} fusion(bf16[2,2,192,3072]{3,2,1,0:T(8,128)(2,1)} %collective-permute-done.4, bf16[2,2,192,3072]{3,2,1,0:T(8,128)(2,1)S(1)} %copy-done.3), kind=kLoop, calls=%fused_computation | loop fusion | flops 9437184 | bytes 14155776 | tf_op jit(solution)/shard_map/convert_element_type | solution.py:1115
  178.8 10.4 %all-to-all-done.2 = bf16[8,64,768]{2,1,0:T(8,128)(2,1)} async-done(((bf16[8,64,768]{2,1,0:T(8,128)(2,1)}), bf16[8,64,768]{2,1,0:T(8,128)(2,1)}, u32[]{:S(2)}, u32[]{:S(2)}) %all-to-all-start.2) | async-done | bytes 786464 | tf_op jit(solution)/shard_map/all_to_all | solution.py:867
  192.1 20.1 %attend_back.1 = (bf16[3,2,192,768]{3,2,1,0:T(8,128)(2,1)}, bf16[3,2,192,768]{3,2,1,0:T(8,128)(2,1)}, bf16[8,96,768]{2,1,0:T(8,128)(2,1)}) custom-call(s32[2]{0:T(128)} %pad_add_fusion.1.offset, bf16[512,2304]{1,0:T(8,128)(2,1)} %convolution_convert_fusion.query.key.value, bf16[512,2304]{1,0:T(8,128)(2,1)} %convolution_convert_fusion.query.key.value, ...), custom_call_target="tpu_custom_call" | custom-call | flops 23000000512 | bytes 4000000 | tf_op jit(solution)/shard_map/attend_back/pallas_call | solution.py:817
  212.4 4.5 %all-to-all-start.3 = ((bf16[8,96,768]{2,1,0:T(8,128)(2,1)}), bf16[8,96,768]{2,1,0:T(8,128)(2,1)}, u32[]{:S(2)}, u32[]{:S(2)}) async-start(bf16[8,96,768]{2,1,0:T(8,128)(2,1)} %get-tuple-element.112), calls=%async_computation.3 | async-start | bytes 2359296 | tf_op jit(solution)/shard_map/all_to_all | solution.py:867
  236.5 9.8 %all-to-all-done.3.gm = bf16[8,96,768]{2,1,0:T(8,128)(2,1)} async-done(((bf16[8,96,768]{2,1,0:T(8,128)(2,1)}), bf16[8,96,768]{2,1,0:T(8,128)(2,1)}, u32[]{:S(2)}, u32[]{:S(2)}) %all-to-all-start.3) | async-done | bytes 1179680 | tf_op jit(solution)/shard_map/all_to_all | solution.py:867
  246.3 10.0 %leave.1 = (f32[2,4,64,768]{3,2,1,0:T(8,128)}, f32[2,9,768]{2,1,0:T(8,128)}, f32[2,2,768]{2,1,0:T(2,128)}) custom-call(s32[5]{0:T(128)} %pad_add_fusion.meta, bf16[8,96,768]{2,1,0:T(8,128)(2,1)} %all-to-all-done.3.gm, bf16[2,4,64,768]{3,2,1,0:T(8,128)(2,1)} %tok.5, bf16[2,1,64,768]{3,2,1,0:T(8,128)(2,1)} %copy-done.18, bf16[2,1,64,768]{3,2,1,0:T(8,128)(2,1)} %copy-done.19, ...), custom_call_target="tpu_custom_call" | custom-call | flops 10000000000 | bytes 4000000 | tf_op jit(solution)/shard_map/leave/pallas_call | solution.py:636
  259.4 3.6 %all-to-all-start.4 = ((f32[8,112,128]{2,1,0:T(8,128)}), f32[8,112,128]{2,1,0:T(8,128)S(1)}, u32[]{:S(2)}, u32[]{:S(2)}) async-start(f32[8,112,128]{2,1,0:T(8,128)} %bitcast.163), calls=%async_computation.4 | async-start | bytes 917504 | tf_op jit(solution)/shard_map/all_to_all | solution.py:867
  280.4 5.7 %all-gather.1 = f32[448,128]{1,0:T(8,128)S(1)} all-gather(f32[112,128]{1,0:T(8,128)S(1)} %reduce_sum.46), channel_id=3, replica_groups=mesh['batch'=4,'seq'=8] {'batch'}, dimensions={0}, use_global_device_ids=true | all-gather | bytes 286720 | tf_op jit(solution)/shard_map/all_gather | solution.py:1196
  289.0 4.7 %collective-permute-done.22 = bf16[2,24,3072]{2,1,0:T(8,128)(2,1)} collective-permute-done((bf16[2,24,3072]{2,1,0:T(8,128)(2,1)}, bf16[2,24,3072]{2,1,0:T(8,128)(2,1)}, u32[]{:S(2)}, u32[]{:S(2)}) %collective-permute-start.22) | collective-permute-done | bytes 294944 | tf_op jit(solution)/shard_map/ppermute | solution.py:890
  296.3 4.9 %fusion.26 = f32[24,768]{1,0:T(8,128)S(1)} fusion(bf16[768,4608]{1,0:T(8,128)(2,1)} %param.24, bf16[8,4608]{1,0:T(8,128)(2,1)S(1)} %get-tuple-element.181, bf16[8,4608]{1,0:T(8,128)(2,1)S(1)} %get-tuple-element.182, bf16[8,4608]{1,0:T(8,128)(2,1)S(1)} %get-tuple-element.180), kind=kOutput, calls=%fused_computation.82 | convolution fusion | flops 170532864 | bytes 7372800 | tf_op jit(solution)/shard_map/dot_general | solution.py:30
  305.7 5.9 %collective-permute-done.21 = bf16[4,24,768]{2,1,0:T(8,128)(2,1)S(1)} collective-permute-done((bf16[4,24,768]{2,1,0:T(8,128)(2,1)S(1)}, bf16[4,24,768]{2,1,0:T(8,128)(2,1)S(1)}, u32[]{:S(2)}, u32[]{:S(2)}) %collective-permute-start.21) | collective-permute-done | bytes 147488 | tf_op jit(solution)/shard_map/ppermute | solution.py:890
  (201 shorter events, 76.9 us)
Async XLA Ops:
  0.7 10.4 %slice-start.1 = ((f32[4608]{0:T(1024)}), f32[1536]{0:T(1024)S(1)}, s32[]{:S(2)}) async-start(f32[4608]{0:T(1024)} %param.25), calls=%async_computation.6 | async-start | bytes 16384 | tf_op jit(solution)/shard_map/slice | solution.py:1032
  1.8 12.5 %collective-permute-start = (bf16[2,1,64,768]{3,2,1,0:T(8,128)(2,1)S(1)}, bf16[2,1,64,768]{3,2,1,0:T(8,128)(2,1)S(1)}, u32[]{:S(2)}, u32[]{:S(2)}) collective-permute-start(bf16[2,1,64,768]{3,2,1,0:T(8,128)(2,1)S(1)} %get-tuple-element.167), channel_id=1, source_target_pairs={{0,1},{1,2},{2,3},{3,4},{4,5},{5,6},{6,7},{8,9},{9,10},{10,11},{11... | collective-permute-start | bytes 589832 | tf_op jit(solution)/shard_map/ppermute | solution.py:858
  6.7 8.3 %collective-permute-start.1 = (bf16[2,1,64,768]{3,2,1,0:T(8,128)(2,1)S(1)}, bf16[2,1,64,768]{3,2,1,0:T(8,128)(2,1)S(1)}, u32[]{:S(2)}, u32[]{:S(2)}) collective-permute-start(bf16[2,1,64,768]{3,2,1,0:T(8,128)(2,1)S(1)} %get-tuple-element.166), channel_id=1, source_target_pairs={{1,0},{2,1},{3,2},{4,3},{5,4},{6,5},{7,6},{9,8},{10,9},{11,10},{12... | collective-permute-start | bytes 589832 | tf_op jit(solution)/shard_map/ppermute | solution.py:863
  20.7 27.3 %all-to-all-start = ((bf16[8,64,768]{2,1,0:T(8,128)(2,1)}), bf16[8,64,768]{2,1,0:T(8,128)(2,1)S(1)}, u32[]{:S(2)}, u32[]{:S(2)}) async-start(bf16[8,64,768]{2,1,0:T(8,128)(2,1)} %bitcast.191), calls=%async_computation | async-start | bytes 1572864 | tf_op jit(solution)/shard_map/all_to_all | solution.py:867
  61.6 32.4 %all-to-all-start.1 = ((bf16[8,96,768]{2,1,0:T(8,128)(2,1)}), bf16[8,96,768]{2,1,0:T(8,128)(2,1)S(1)}, u32[]{:S(2)}, u32[]{:S(2)}) async-start(bf16[8,96,768]{2,1,0:T(8,128)(2,1)} %get-tuple-element.79), calls=%async_computation.1 | async-start | bytes 2359296 | tf_op jit(solution)/shard_map/all_to_all | solution.py:867
  141.9 26.9 %collective-permute-start.4 = (bf16[2,2,192,3072]{3,2,1,0:T(8,128)(2,1)}, bf16[2,2,192,3072]{3,2,1,0:T(8,128)(2,1)}, u32[]{:S(2)}, u32[]{:S(2)}) collective-permute-start(bf16[2,2,192,3072]{3,2,1,0:T(8,128)(2,1)} %get-tuple-element.101), channel_id=1, source_target_pairs={{0,8},{8,0},{16,24},{24,16},{1,9},{9,1},{17,25},{25,17},{2,10},{10... | collective-permute-start | bytes 14155784 | tf_op jit(solution)/shard_map/ppermute | solution.py:890
  142.1 12.6 %collective-permute-start.2 = (bf16[2,64,768]{2,1,0:T(8,128)(2,1)}, bf16[2,64,768]{2,1,0:T(8,128)(2,1)S(1)}, u32[]{:S(2)}, u32[]{:S(2)}) collective-permute-start(bf16[2,64,768]{2,1,0:T(8,128)(2,1)} %get-tuple-element.95), channel_id=1, source_target_pairs={{0,1},{1,2},{2,3},{3,4},{4,5},{5,6},{6,7},{8,9},{9,10},{10,11},{11... | collective-permute-start | bytes 589832 | tf_op jit(solution)/shard_map/ppermute | solution.py:858
  145.4 9.3 %collective-permute-start.3 = (bf16[2,64,768]{2,1,0:T(8,128)(2,1)}, bf16[2,64,768]{2,1,0:T(8,128)(2,1)S(1)}, u32[]{:S(2)}, u32[]{:S(2)}) collective-permute-start(bf16[2,64,768]{2,1,0:T(8,128)(2,1)} %get-tuple-element.96), channel_id=1, source_target_pairs={{1,0},{2,1},{3,2},{4,3},{5,4},{6,5},{7,6},{9,8},{10,9},{11,10},{12... | collective-permute-start | bytes 589832 | tf_op jit(solution)/shard_map/ppermute | solution.py:863
  163.8 25.3 %all-to-all-start.2 = ((bf16[8,64,768]{2,1,0:T(8,128)(2,1)}), bf16[8,64,768]{2,1,0:T(8,128)(2,1)}, u32[]{:S(2)}, u32[]{:S(2)}) async-start(bf16[8,64,768]{2,1,0:T(8,128)(2,1)} %bitcast.192), calls=%async_computation.2 | async-start | bytes 1572864 | tf_op jit(solution)/shard_map/all_to_all | solution.py:867
  170.6 46.8 %collective-permute-start.12 = (bf16[2,2,2,2,24,768]{5,4,2,1,0,3:T(8,128)(2,1)}, bf16[2,2,2,2,24,768]{5,4,2,1,0,3:T(8,128)(2,1)}, u32[]{:S(2)}, u32[]{:S(2)}) collective-permute-start(bf16[2,2,2,2,24,768]{5,4,2,1,0,3:T(8,128)(2,1)} %bitcast.162), channel_id=1, source_target_pairs={{0,8},{8,0},{16,24},{24,16},{1,9},{9,1},{17,25},{25,17},{2,10},{10... | collective-permute-start | bytes 1769480 | tf_op jit(solution)/shard_map/ppermute | solution.py:890
  189.2 23.2 %collective-permute-start.5 = (bf16[2,2,2,2,24,1024]{5,4,3,2,1,0:T(8,128)(2,1)}, bf16[2,2,2,2,24,1024]{5,4,3,2,1,0:T(8,128)(2,1)}, u32[]{:S(2)}, u32[]{:S(2)}) collective-permute-start(bf16[2,2,2,2,24,1024]{5,4,3,2,1,0:T(8,128)(2,1)} %get-tuple-element.109), channel_id=1, source_target_pairs={{0,16},{8,24},{16,0},{24,8},{1,17},{9,25},{17,1},{25,9},{2,18},{10... | collective-permute-start | bytes 2359304 | tf_op jit(solution)/shard_map/ppermute | solution.py:890
  190.7 21.7 %collective-permute-start.6 = (bf16[2,2,2,2,24,1024]{5,4,3,2,1,0:T(8,128)(2,1)}, bf16[2,2,2,2,24,1024]{5,4,3,2,1,0:T(8,128)(2,1)}, u32[]{:S(2)}, u32[]{:S(2)}) collective-permute-start(bf16[2,2,2,2,24,1024]{5,4,3,2,1,0:T(8,128)(2,1)} %get-tuple-element.110), channel_id=1, source_target_pairs={{0,1},{1,0},{2,3},{3,2},{4,5},{5,4},{6,7},{7,6},{8,9},{9,8},{10,11... | collective-permute-start | bytes 2359304 | tf_op jit(solution)/shard_map/ppermute | solution.py:890
  192.1 20.3 %collective-permute-start.7 = (bf16[2,2,2,2,24,1024]{5,4,3,2,1,0:T(8,128)(2,1)}, bf16[2,2,2,2,24,1024]{5,4,3,2,1,0:T(8,128)(2,1)}, u32[]{:S(2)}, u32[]{:S(2)}) collective-permute-start(bf16[2,2,2,2,24,1024]{5,4,3,2,1,0:T(8,128)(2,1)} %get-tuple-element.111), channel_id=1, source_target_pairs={{0,2},{1,3},{2,0},{3,1},{4,6},{5,7},{6,4},{7,5},{8,10},{9,11},{10,... | collective-permute-start | bytes 2359304 | tf_op jit(solution)/shard_map/ppermute | solution.py:890
  212.2 16.9 %collective-permute-start.11 = (bf16[3,2,192,768]{3,2,1,0:T(8,128)(2,1)}, bf16[3,2,192,768]{3,2,1,0:T(8,128)(2,1)}, u32[]{:S(2)}, u32[]{:S(2)}) collective-permute-start(bf16[3,2,192,768]{3,2,1,0:T(8,128)(2,1)} %get-tuple-element.128), channel_id=1, source_target_pairs={{0,8},{8,0},{16,24},{24,16},{1,9},{9,1},{17,25},{25,17},{2,10},{10... | collective-permute-start | bytes 5308424 | tf_op jit(solution)/shard_map/ppermute | solution.py:890
  212.4 33.9 %all-to-all-start.3 = ((bf16[8,96,768]{2,1,0:T(8,128)(2,1)}), bf16[8,96,768]{2,1,0:T(8,128)(2,1)}, u32[]{:S(2)}, u32[]{:S(2)}) async-start(bf16[8,96,768]{2,1,0:T(8,128)(2,1)} %get-tuple-element.112), calls=%async_computation.3 | async-start | bytes 2359296 | tf_op jit(solution)/shard_map/all_to_all | solution.py:867
  225.5 33.9 %collective-permute-start.8 = (bf16[2,2,2,24,1024]{4,3,0,1,2:T(8,128)(2,1)}, bf16[2,2,2,24,1024]{4,3,0,1,2:T(8,128)(2,1)}, u32[]{:S(2)}, u32[]{:S(2)}) collective-permute-start(bf16[2,2,2,24,1024]{4,3,0,1,2:T(8,128)(2,1)} %bitcast.169), channel_id=1, source_target_pairs={{0,1},{1,0},{2,3},{3,2},{4,5},{5,4},{6,7},{7,6},{8,9},{9,8},{10,11... | collective-permute-start | bytes 1179656 | tf_op jit(solution)/shard_map/ppermute | solution.py:890
  227.1 32.3 %collective-permute-start.9 = (bf16[2,2,2,24,1024]{4,3,0,2,1:T(8,128)(2,1)}, bf16[2,2,2,24,1024]{4,3,0,2,1:T(8,128)(2,1)}, u32[]{:S(2)}, u32[]{:S(2)}) collective-permute-start(bf16[2,2,2,24,1024]{4,3,0,2,1:T(8,128)(2,1)} %bitcast.168), channel_id=1, source_target_pairs={{0,2},{1,3},{2,0},{3,1},{4,6},{5,7},{6,4},{7,5},{8,10},{9,11},{10,... | collective-permute-start | bytes 1179656 | tf_op jit(solution)/shard_map/ppermute | solution.py:890
  228.6 30.8 %collective-permute-start.10 = (bf16[2,2,2,24,1024]{4,3,0,1,2:T(8,128)(2,1)}, bf16[2,2,2,24,1024]{4,3,0,1,2:T(8,128)(2,1)}, u32[]{:S(2)}, u32[]{:S(2)}) collective-permute-start(bf16[2,2,2,24,1024]{4,3,0,1,2:T(8,128)(2,1)} %bitcast.167), channel_id=1, source_target_pairs={{0,16},{8,24},{16,0},{24,8},{1,17},{9,25},{17,1},{25,9},{2,18},{10... | collective-permute-start | bytes 1179656 | tf_op jit(solution)/shard_map/ppermute | solution.py:890
  233.1 37.7 %collective-permute-start.13 = (bf16[2,2,2,2,24,768]{5,4,3,2,1,0:T(8,128)(2,1)}, bf16[2,2,2,2,24,768]{5,4,3,2,1,0:T(8,128)(2,1)}, u32[]{:S(2)}, u32[]{:S(2)}) collective-permute-start(bf16[2,2,2,2,24,768]{5,4,3,2,1,0:T(8,128)(2,1)} %get-tuple-element.156), channel_id=1, source_target_pairs={{0,16},{8,24},{16,0},{24,8},{1,17},{9,25},{17,1},{25,9},{2,18},{10... | collective-permute-start | bytes 1769480 | tf_op jit(solution)/shard_map/ppermute | solution.py:890
  235.6 37.2 %collective-permute-start.14 = (bf16[2,2,2,2,24,768]{5,4,3,2,1,0:T(8,128)(2,1)}, bf16[2,2,2,2,24,768]{5,4,3,2,1,0:T(8,128)(2,1)}, u32[]{:S(2)}, u32[]{:S(2)}) collective-permute-start(bf16[2,2,2,2,24,768]{5,4,3,2,1,0:T(8,128)(2,1)} %get-tuple-element.154), channel_id=1, source_target_pairs={{0,1},{1,0},{2,3},{3,2},{4,5},{5,4},{6,7},{7,6},{8,9},{9,8},{10,11... | collective-permute-start | bytes 1769480 | tf_op jit(solution)/shard_map/ppermute | solution.py:890
  246.3 10.0 %copy-start.13 = (f32[2,3,768]{2,1,0:T(4,128)S(1)}, f32[2,3,768]{2,1,0:T(4,128)}, u32[]{:S(2)}) copy-start(f32[2,3,768]{2,1,0:T(4,128)} %get-tuple-element.124) | copy-start | bytes 55300
  246.3 10.0 %copy-start.14 = (f32[2,1,768]{2,1,0:T(1,128)S(1)}, f32[2,1,768]{2,1,0:T(1,128)}, u32[]{:S(2)}) copy-start(f32[2,1,768]{2,1,0:T(1,128)} %get-tuple-element.125) | copy-start | bytes 18436
  259.4 21.0 %all-to-all-start.4 = ((f32[8,112,128]{2,1,0:T(8,128)}), f32[8,112,128]{2,1,0:T(8,128)S(1)}, u32[]{:S(2)}, u32[]{:S(2)}) async-start(f32[8,112,128]{2,1,0:T(8,128)} %bitcast.163), calls=%async_computation.4 | async-start | bytes 917504 | tf_op jit(solution)/shard_map/all_to_all | solution.py:867
  264.3 12.0 %collective-permute-start.17 = (bf16[2,2,24,1024]{3,2,0,1:T(8,128)(2,1)S(1)}, bf16[2,2,24,1024]{3,2,0,1:T(8,128)(2,1)S(1)}, u32[]{:S(2)}, u32[]{:S(2)}) collective-permute-start(bf16[2,2,24,1024]{3,2,0,1:T(8,128)(2,1)S(1)} %dynamic-slice_bitcast_fusion.14), channel_id=1, source_target_pairs={{0,1},{1,0},{2,3},{3,2},{4,5},{5,4},{6,7},{7,6},{8,9},{9,8},{10,11... | collective-permute-start | bytes 589832 | tf_op jit(solution)/shard_map/ppermute | solution.py:890
  267.5 8.8 %collective-permute-start.16 = (bf16[2,2,24,1024]{3,2,0,1:T(8,128)(2,1)S(1)}, bf16[2,2,24,1024]{3,2,0,1:T(8,128)(2,1)S(1)}, u32[]{:S(2)}, u32[]{:S(2)}) collective-permute-start(bf16[2,2,24,1024]{3,2,0,1:T(8,128)(2,1)S(1)} %dynamic-slice_bitcast_fusion.15), channel_id=1, source_target_pairs={{0,16},{8,24},{16,0},{24,8},{1,17},{9,25},{17,1},{25,9},{2,18},{10... | collective-permute-start | bytes 589832 | tf_op jit(solution)/shard_map/ppermute | solution.py:890
  269.3 8.3 %collective-permute-start.15 = (bf16[2,2,24,1024]{3,2,0,1:T(8,128)(2,1)S(1)}, bf16[2,2,24,1024]{3,2,0,1:T(8,128)(2,1)S(1)}, u32[]{:S(2)}, u32[]{:S(2)}) collective-permute-start(bf16[2,2,24,1024]{3,2,0,1:T(8,128)(2,1)S(1)} %dynamic-slice_bitcast_fusion.16), channel_id=1, source_target_pairs={{0,2},{1,3},{2,0},{3,1},{4,6},{5,7},{6,4},{7,5},{8,10},{9,11},{10,... | collective-permute-start | bytes 589832 | tf_op jit(solution)/shard_map/ppermute | solution.py:890
  272.1 14.2 %collective-permute-start.18 = (bf16[2,2,2,24,768]{4,3,2,1,0:T(8,128)(2,1)S(1)}, bf16[2,2,2,24,768]{4,3,2,1,0:T(8,128)(2,1)S(1)}, u32[]{:S(2)}, u32[]{:S(2)}) collective-permute-start(bf16[2,2,2,24,768]{4,3,2,1,0:T(8,128)(2,1)S(1)} %get-tuple-element.174), channel_id=1, source_target_pairs={{0,1},{1,0},{2,3},{3,2},{4,5},{5,4},{6,7},{7,6},{8,9},{9,8},{10,11... | collective-permute-start | bytes 884744 | tf_op jit(solution)/shard_map/ppermute | solution.py:890
  274.7 11.7 %collective-permute-start.19 = (bf16[2,2,2,24,768]{4,3,2,1,0:T(8,128)(2,1)}, bf16[2,2,2,24,768]{4,3,2,1,0:T(8,128)(2,1)S(1)}, u32[]{:S(2)}, u32[]{:S(2)}) collective-permute-start(bf16[2,2,2,24,768]{4,3,2,1,0:T(8,128)(2,1)} %get-tuple-element.172), channel_id=1, source_target_pairs={{0,16},{8,24},{16,0},{24,8},{1,17},{9,25},{17,1},{25,9},{2,18},{10... | collective-permute-start | bytes 884744 | tf_op jit(solution)/shard_map/ppermute | solution.py:890
  278.4 15.3 %collective-permute-start.22 = (bf16[2,24,3072]{2,1,0:T(8,128)(2,1)}, bf16[2,24,3072]{2,1,0:T(8,128)(2,1)}, u32[]{:S(2)}, u32[]{:S(2)}) collective-permute-start(bf16[2,24,3072]{2,1,0:T(8,128)(2,1)} %get-tuple-element.170), channel_id=1, source_target_pairs={{0,4},{1,5},{2,6},{3,7},{4,0},{5,1},{6,2},{7,3},{8,12},{9,13},{10,... | collective-permute-start | bytes 884744 | tf_op jit(solution)/shard_map/ppermute | solution.py:890
  286.6 15.3 %collective-permute-start.20 = (bf16[4,2,24,768]{3,2,1,0:T(8,128)(2,1)S(1)}, bf16[4,2,24,768]{3,2,1,0:T(8,128)(2,1)S(1)}, u32[]{:S(2)}, u32[]{:S(2)}) collective-permute-start(bf16[4,2,24,768]{3,2,1,0:T(8,128)(2,1)S(1)} %fusion.25), channel_id=1, source_target_pairs={{0,2},{1,3},{2,0},{3,1},{4,6},{5,7},{6,4},{7,5},{8,10},{9,11},{10,... | collective-permute-start | bytes 884744 | tf_op jit(solution)/shard_map/ppermute | solution.py:890
  301.8 11.1 %copy-start.1 = (bf16[1000,768]{1,0:T(8,128)(2,1)S(1)}, bf16[1000,768]{1,0:T(8,128)(2,1)}, u32[]{:S(2)}) copy-start(bf16[1000,768]{1,0:T(8,128)(2,1)} %param.23) | copy-start | bytes 4608004
  302.0 9.6 %collective-permute-start.21 = (bf16[4,24,768]{2,1,0:T(8,128)(2,1)S(1)}, bf16[4,24,768]{2,1,0:T(8,128)(2,1)S(1)}, u32[]{:S(2)}, u32[]{:S(2)}) collective-permute-start(bf16[4,24,768]{2,1,0:T(8,128)(2,1)S(1)} %dynamic-slice_bitcast_fusion.17), channel_id=1, source_target_pairs={{0,4},{1,5},{2,6},{3,7},{4,0},{5,1},{6,2},{7,3},{8,12},{9,13},{10,... | collective-permute-start | bytes 442376 | tf_op jit(solution)/shard_map/ppermute | solution.py:890
  (21 other events, 68.5 us)

commit v7 on v6

--- a/solution.py
+++ b/solution.py
@@ -1217,9 +1217,10 @@
     all_sums, (conv_attn_grad, conv_ffn_grad) = unpack(gathered, common, sliced)
 
     grad_pieces = all_sums.reshape(total, 6 * D)
+    if halving:
+        grad_pieces, got_l = lax.optimization_barrier((grad_pieces, got_l))
     grad_silu = back_through(grad_pieces)
     if halving:
-        grad_silu, got_l = lax.optimization_barrier((grad_silu, got_l))
         rest_rows = reduce_rest(add(keep_l, got_l), dims_l, "h")
     qkv_rows = jnp.concatenate([rest_rows[0], rest_rows[1], rest_rows[2]], axis=1)
     proj_rows = rest_rows[3]

time: 315 us -> 318 us (level)
  transfers between devices with their start and end apart: 28 -> 28, of which waited for: 9 -> 11; matrix products, arithmetic and copies ran while one was open for 23% -> 21% of each run, Pallas kernels for 14% -> 14%
where the time goes in v7:
time: 318 us; the launch traced here: 316 us
  Pallas kernels  109 us (34%)
  waiting for transfers between devices  61.2 us (19%)
  starting transfers between devices  54.6 us (17%)
  local copies, waits for them, and re-layouts  30.9 us (10%)
  other arithmetic  25.2 us (8%)
  matrix products  23.3 us (7%)
  blocking collectives  10.9 us (3%)
    all_to_all x5, waiting for transfers between devices, swap(): return lax.all_to_all(values, 'seq', 0, 0, tiled=False)  40.8 us
    pallas_call x1, Pallas kernels, ffn(): pl.pallas_call(ffn_kernel, out_shape=(jax.ShapeDtypeStruct((latents, own,...  40.4 us
    all_to_all x5, starting transfers between devices, swap(): return lax.all_to_all(values, 'seq', 0, 0, tiled=False)  23.8 us
    dot_general x8, matrix products, mm(): return lax.dot_general(left, right, dims, preferred_element_type=F32)  20.2 us
    pallas_call x1, Pallas kernels, attend_back(): pl.pallas_call(attend_back_kernel, out_shape=(parts, parts, jax.ShapeDtyp...  20.1 us
    ppermute x19, starting transfers between devices, hop(): return lax.ppermute(values, axis, [(i, i ^ mask) for i in range(count)])  20 us
    ppermute x19, waiting for transfers between devices, hop(): return lax.ppermute(values, axis, [(i, i ^ mask) for i in range(count)])  14.9 us
    pallas_call x1, Pallas kernels, attend(): pl.pallas_call(attend_kernel, out_shape=(jax.ShapeDtypeStruct((strips, wi...  12.6 us
  transfers between devices with their start and end apart: 28, of which 11 were waited for; matrix products, arithmetic and copies ran while one was open for 21% of the time, Pallas kernels for 14%

profile of v7, /device:TPU:0, one launch (start us, length us, event | category | flops | bytes accessed | tf_op | source)
XLA Modules:
  0.0 316.3 jit_solution(9954868632030159043)
XLA Ops:
  1.8 4.9 %collective-permute-start = (bf16[2,1,64,768]{3,2,1,0:T(8,128)(2,1)S(1)}, bf16[2,1,64,768]{3,2,1,0:T(8,128)(2,1)S(1)}, u32[]{:S(2)}, u32[]{:S(2)}) collective-permute-start(bf16[2,1,64,768]{3,2,1,0:T(8,128)(2,1)S(1)} %get-tuple-element.167), channel_id=1, source_target_pairs={{0,1},{1,2},{2,3},{3,4},{4,5},{5,6},{6,7},{8,9},{9,10},{10,11},{11... | collective-permute-start | bytes 589832 | tf_op jit(solution)/shard_map/ppermute | solution.py:858
  11.0 2.7 fusion.7.lead
  15.7 5.0 %enter.1 = bf16[2,4,64,768]{3,2,1,0:T(8,128)(2,1)} custom-call(s32[5]{0:T(128)} %pad_add_fusion.meta, bf16[2,4,64,768]{3,2,1,0:T(8,128)(2,1)} %tok.5, bf16[2,1,64,768]{3,2,1,0:T(8,128)(2,1)} %copy-done.18, bf16[2,1,64,768]{3,2,1,0:T(8,128)(2,1)} %copy-done.19, f32[2,1536]{1,0:T(2,128)} %fusion.7.lead, bf16[9,768]{1,0:T(8,128)(2,1)} %kern.3), custom_call_target="tpu_custom_call" | custom-call | flops 6000000000 | bytes 4000000 | tf_op jit(solution)/shard_map/enter/pallas_call | solution.py:134
  20.7 7.1 %all-to-all-start = ((bf16[8,64,768]{2,1,0:T(8,128)(2,1)}), bf16[8,64,768]{2,1,0:T(8,128)(2,1)S(1)}, u32[]{:S(2)}, u32[]{:S(2)}) async-start(bf16[8,64,768]{2,1,0:T(8,128)(2,1)} %bitcast.191), calls=%async_computation | async-start | bytes 1572864 | tf_op jit(solution)/shard_map/all_to_all | solution.py:867
  29.0 5.7 %copy.92 = bf16[768,2304]{0,1:T(8,128)(2,1)} copy(bf16[768,2304]{1,0:T(8,128)(2,1)} %wv.1) | data formatting | bytes 7077888 | tf_op args[11]
  34.8 5.2 %all-gather.2 = f32[4,2,1025]{2,1,0:T(2,128)S(1)} all-gather(f32[1,2,1025]{2,1,0:T(2,128)S(1)} %maximum_bitcast_fusion), channel_id=2, replica_groups=mesh['batch'=4,'seq'=8] {'batch'}, dimensions={0}, use_global_device_ids=true | all-gather | bytes 41000 | tf_op jit(solution)/shard_map/all_gather | solution.py:1078
  41.9 6.1 %all-to-all-done = bf16[8,64,768]{2,1,0:T(8,128)(2,1)S(1)} async-done(((bf16[8,64,768]{2,1,0:T(8,128)(2,1)}), bf16[8,64,768]{2,1,0:T(8,128)(2,1)S(1)}, u32[]{:S(2)}, u32[]{:S(2)}) %all-to-all-start) | async-done | bytes 786464 | tf_op jit(solution)/shard_map/all_to_all | solution.py:867
  49.0 12.6 %attend.1 = (bf16[8,96,768]{2,1,0:T(8,128)(2,1)}, f32[3,4,512]{2,1,0:T(4,128)}) custom-call(s32[2]{0:T(128)} %pad_add_fusion.1.offset, bf16[512,768]{1,0:T(8,128)(2,1)} %bitcast.177, bf16[768,2304]{1,0:T(8,128)(2,1)} %wv.1, bf16[768,2304]{1,0:T(8,128)(2,1)} %wv.1, bf16[2304,768]{1,0:T(8,128)(2,1)} %bitcast.175, f32[512,128]{1,0:T(8,128)} %broadcast_in_dim.18.bias), custom_call_target="tpu_custom_call" | custom-call | flops 16000000000 | bytes 4000000 | tf_op jit(solution)/shard_map/attend/pallas_call | solution.py:717
  61.6 3.7 %all-to-all-start.1 = ((bf16[8,96,768]{2,1,0:T(8,128)(2,1)}), bf16[8,96,768]{2,1,0:T(8,128)(2,1)S(1)}, u32[]{:S(2)}, u32[]{:S(2)}) async-start(bf16[8,96,768]{2,1,0:T(8,128)(2,1)} %get-tuple-element.79), calls=%async_computation.1 | async-start | bytes 2359296 | tf_op jit(solution)/shard_map/all_to_all | solution.py:867
  65.3 3.1 fusion.2
  72.9 3.1 fusion.10.key_t
  76.0 3.4 %convolution_convert_fusion.query.key.value = bf16[512,2304]{1,0:T(8,128)(2,1)} fusion(bf16[512,768]{1,0:T(8,128)(2,1)S(1)} %bitcast.180, bf16[768,2304]{1,0:T(8,128)(2,1)S(1)} %copy-done.4), kind=kOutput, calls=%fused_computation.3 | convolution fusion | flops 1813118976 | bytes 6684672 | tf_op jit(solution)/shard_map/dot_general | solution.py:30
  79.4 14.5 %all-to-all-done.1.att = bf16[8,96,768]{2,1,0:T(8,128)(2,1)S(1)} async-done(((bf16[8,96,768]{2,1,0:T(8,128)(2,1)}), bf16[8,96,768]{2,1,0:T(8,128)(2,1)S(1)}, u32[]{:S(2)}, u32[]{:S(2)}) %all-to-all-start.1) | async-done | bytes 1179680 | tf_op jit(solution)/shard_map/all_to_all | solution.py:867
  95.0 6.5 %second.1 = (bf16[2,384,768]{2,1,0:T(8,128)(2,1)}, bf16[2,768,384]{2,1,0:T(8,128)(2,1)}, f32[2,256,768]{2,1,0:T(8,128)}, f32[2,256,768]{2,1,0:T(8,128)}) custom-call(s32[5]{0:T(128)} %pad_add_fusion.meta, bf16[8,96,768]{2,1,0:T(8,128)(2,1)} %copy-done.5, bf16[2,4,64,768]{3,2,1,0:T(8,128)(2,1)} %tok.5, bf16[2,1,64,768]{3,2,1,0:T(8,128)(2,1)} %copy-done.18, ...), custom_call_target="tpu_custom_call" | custom-call | flops 7000000000 | bytes 4000000 | tf_op jit(solution)/shard_map/second/pallas_call | solution.py:228
  101.5 40.4 %ffn.1 = (f32[2,256,768]{2,1,0:T(8,128)}, f32[2,384,768]{2,1,0:T(8,128)}, bf16[2,64,768]{2,1,0:T(8,128)(2,1)}, bf16[2,64,768]{2,1,0:T(8,128)(2,1)}, bf16[2,2,192...) custom-call(s32[1]{0:T(128)} %bitcast.core, ...), custom_call_target="tpu_custom_call" | custom-call | flops 35000000512 | bytes 4000000 | tf_op jit(solution)/shard_map/ffn/pallas_call | solution.py:416
  142.1 3.3 %collective-permute-start.2 = (bf16[2,64,768]{2,1,0:T(8,128)(2,1)}, bf16[2,64,768]{2,1,0:T(8,128)(2,1)S(1)}, u32[]{:S(2)}, u32[]{:S(2)}) collective-permute-start(bf16[2,64,768]{2,1,0:T(8,128)(2,1)} %get-tuple-element.95), channel_id=1, source_target_pairs={{0,1},{1,2},{2,3},{3,4},{4,5},{5,6},{6,7},{8,9},{9,10},{10,11},{11... | collective-permute-start | bytes 589832 | tf_op jit(solution)/shard_map/ppermute | solution.py:858
  146.7 3.1 finish_output.1
  149.8 4.9 %collective-permute-done.2.low = bf16[2,64,768]{2,1,0:T(8,128)(2,1)S(1)} collective-permute-done((bf16[2,64,768]{2,1,0:T(8,128)(2,1)}, bf16[2,64,768]{2,1,0:T(8,128)(2,1)S(1)}, u32[]{:S(2)}, u32[]{:S(2)}) %collective-permute-start.2) | collective-permute-done | bytes 196640 | tf_op jit(solution)/shard_map/ppermute | solution.py:858
  155.4 8.4 %middle.1 = (f32[2,256,768]{2,1,0:T(8,128)}, bf16[2,4,64,768]{3,2,1,0:T(8,128)(2,1)}, bf16[2,4,64,768]{3,2,1,0:T(8,128)(2,1)}, f32[2,3,768]{2,1,0:T(4,128)}) custom-call(s32[5]{0:T(128)} %pad_add_fusion.meta, f32[2,384,768]{2,1,0:T(8,128)} %get-tuple-element.94.ge2, bf16[2,64,768]{2,1,0:T(8,128)(2,1)} %copy-done.20, bf16[2,64,768]{2,1,0:T(8,128)(2,1)} %copy-done.21, ...), custom_call_target="tpu_custom_call" | custom-call | flops 8000000000 | bytes 4000000 | tf_op jit(solution)/shard_map/middle/pallas_call | solution.py:540
  163.8 4.8 %all-to-all-start.2 = ((bf16[8,64,768]{2,1,0:T(8,128)(2,1)}), bf16[8,64,768]{2,1,0:T(8,128)(2,1)}, u32[]{:S(2)}, u32[]{:S(2)}) async-start(bf16[8,64,768]{2,1,0:T(8,128)(2,1)} %bitcast.192), calls=%async_computation.2 | async-start | bytes 1572864 | tf_op jit(solution)/shard_map/all_to_all | solution.py:867
  171.4 3.8 %add_convert_fusion = bf16[2,2,192,3072]{3,2,1,0:T(8,128)(2,1)S(1)} fusion(bf16[2,2,192,3072]{3,2,1,0:T(8,128)(2,1)} %collective-permute-done.4, bf16[2,2,192,3072]{3,2,1,0:T(8,128)(2,1)S(1)} %copy-done.3), kind=kLoop, calls=%fused_computation | loop fusion | flops 9437184 | bytes 14155776 | tf_op jit(solution)/shard_map/convert_element_type | solution.py:1115
  178.8 10.4 %all-to-all-done.2 = bf16[8,64,768]{2,1,0:T(8,128)(2,1)} async-done(((bf16[8,64,768]{2,1,0:T(8,128)(2,1)}), bf16[8,64,768]{2,1,0:T(8,128)(2,1)}, u32[]{:S(2)}, u32[]{:S(2)}) %all-to-all-start.2) | async-done | bytes 786464 | tf_op jit(solution)/shard_map/all_to_all | solution.py:867
  192.1 20.1 %attend_back.1 = (bf16[3,2,192,768]{3,2,1,0:T(8,128)(2,1)}, bf16[3,2,192,768]{3,2,1,0:T(8,128)(2,1)}, bf16[8,96,768]{2,1,0:T(8,128)(2,1)}) custom-call(s32[2]{0:T(128)} %pad_add_fusion.1.offset, bf16[512,2304]{1,0:T(8,128)(2,1)} %convolution_convert_fusion.query.key.value, bf16[512,2304]{1,0:T(8,128)(2,1)} %convolution_convert_fusion.query.key.value, ...), custom_call_target="tpu_custom_call" | custom-call | flops 23000000512 | bytes 4000000 | tf_op jit(solution)/shard_map/attend_back/pallas_call | solution.py:817
  212.4 4.5 %all-to-all-start.3 = ((bf16[8,96,768]{2,1,0:T(8,128)(2,1)}), bf16[8,96,768]{2,1,0:T(8,128)(2,1)}, u32[]{:S(2)}, u32[]{:S(2)}) async-start(bf16[8,96,768]{2,1,0:T(8,128)(2,1)} %get-tuple-element.112), calls=%async_computation.3 | async-start | bytes 2359296 | tf_op jit(solution)/shard_map/all_to_all | solution.py:867
  236.5 9.8 %all-to-all-done.3.gm = bf16[8,96,768]{2,1,0:T(8,128)(2,1)} async-done(((bf16[8,96,768]{2,1,0:T(8,128)(2,1)}), bf16[8,96,768]{2,1,0:T(8,128)(2,1)}, u32[]{:S(2)}, u32[]{:S(2)}) %all-to-all-start.3) | async-done | bytes 1179680 | tf_op jit(solution)/shard_map/all_to_all | solution.py:867
  246.3 10.0 %leave.1 = (f32[2,4,64,768]{3,2,1,0:T(8,128)}, f32[2,9,768]{2,1,0:T(8,128)}, f32[2,2,768]{2,1,0:T(2,128)}) custom-call(s32[5]{0:T(128)} %pad_add_fusion.meta, bf16[8,96,768]{2,1,0:T(8,128)(2,1)} %all-to-all-done.3.gm, bf16[2,4,64,768]{3,2,1,0:T(8,128)(2,1)} %tok.5, bf16[2,1,64,768]{3,2,1,0:T(8,128)(2,1)} %copy-done.18, bf16[2,1,64,768]{3,2,1,0:T(8,128)(2,1)} %copy-done.19, ...), custom_call_target="tpu_custom_call" | custom-call | flops 10000000000 | bytes 4000000 | tf_op jit(solution)/shard_map/leave/pallas_call | solution.py:636
  259.4 3.6 %all-to-all-start.4 = ((f32[8,112,128]{2,1,0:T(8,128)}), f32[8,112,128]{2,1,0:T(8,128)S(1)}, u32[]{:S(2)}, u32[]{:S(2)}) async-start(f32[8,112,128]{2,1,0:T(8,128)} %bitcast.163), calls=%async_computation.4 | async-start | bytes 917504 | tf_op jit(solution)/shard_map/all_to_all | solution.py:867
  280.4 5.7 %all-gather.1 = f32[448,128]{1,0:T(8,128)S(1)} all-gather(f32[112,128]{1,0:T(8,128)S(1)} %reduce_sum.46), channel_id=3, replica_groups=mesh['batch'=4,'seq'=8] {'batch'}, dimensions={0}, use_global_device_ids=true | all-gather | bytes 286720 | tf_op jit(solution)/shard_map/all_gather | solution.py:1196
  288.1 5.6 %collective-permute-done.22 = bf16[2,24,3072]{2,1,0:T(8,128)(2,1)} collective-permute-done((bf16[2,24,3072]{2,1,0:T(8,128)(2,1)}, bf16[2,24,3072]{2,1,0:T(8,128)(2,1)}, u32[]{:S(2)}, u32[]{:S(2)}) %collective-permute-start.22) | collective-permute-done | bytes 294944 | tf_op jit(solution)/shard_map/ppermute | solution.py:890
  297.0 2.8 collective-permute-done.20
  299.8 4.9 %fusion.26 = f32[24,768]{1,0:T(8,128)S(1)} fusion(bf16[768,4608]{1,0:T(8,128)(2,1)} %param.24, bf16[8,4608]{1,0:T(8,128)(2,1)S(1)} %get-tuple-element.181, bf16[8,4608]{1,0:T(8,128)(2,1)S(1)} %get-tuple-element.182, bf16[8,4608]{1,0:T(8,128)(2,1)S(1)} %get-tuple-element.180), kind=kOutput, calls=%fused_computation.82 | convolution fusion | flops 170532864 | bytes 7372800 | tf_op jit(solution)/shard_map/dot_general | solution.py:30
  310.3 4.6 %collective-permute-done.21 = bf16[4,24,768]{2,1,0:T(8,128)(2,1)S(1)} collective-permute-done((bf16[4,24,768]{2,1,0:T(8,128)(2,1)S(1)}, bf16[4,24,768]{2,1,0:T(8,128)(2,1)S(1)}, u32[]{:S(2)}, u32[]{:S(2)}) %collective-permute-start.21) | collective-permute-done | bytes 147488 | tf_op jit(solution)/shard_map/ppermute | solution.py:890
  (200 shorter events, 80.4 us)
Async XLA Ops:
  0.7 10.4 %slice-start.1 = ((f32[4608]{0:T(1024)}), f32[1536]{0:T(1024)S(1)}, s32[]{:S(2)}) async-start(f32[4608]{0:T(1024)} %param.25), calls=%async_computation.6 | async-start | bytes 16384 | tf_op jit(solution)/shard_map/slice | solution.py:1032
  1.8 12.5 %collective-permute-start = (bf16[2,1,64,768]{3,2,1,0:T(8,128)(2,1)S(1)}, bf16[2,1,64,768]{3,2,1,0:T(8,128)(2,1)S(1)}, u32[]{:S(2)}, u32[]{:S(2)}) collective-permute-start(bf16[2,1,64,768]{3,2,1,0:T(8,128)(2,1)S(1)} %get-tuple-element.167), channel_id=1, source_target_pairs={{0,1},{1,2},{2,3},{3,4},{4,5},{5,6},{6,7},{8,9},{9,10},{10,11},{11... | collective-permute-start | bytes 589832 | tf_op jit(solution)/shard_map/ppermute | solution.py:858
  6.7 8.3 %collective-permute-start.1 = (bf16[2,1,64,768]{3,2,1,0:T(8,128)(2,1)S(1)}, bf16[2,1,64,768]{3,2,1,0:T(8,128)(2,1)S(1)}, u32[]{:S(2)}, u32[]{:S(2)}) collective-permute-start(bf16[2,1,64,768]{3,2,1,0:T(8,128)(2,1)S(1)} %get-tuple-element.166), channel_id=1, source_target_pairs={{1,0},{2,1},{3,2},{4,3},{5,4},{6,5},{7,6},{9,8},{10,9},{11,10},{12... | collective-permute-start | bytes 589832 | tf_op jit(solution)/shard_map/ppermute | solution.py:863
  20.7 27.3 %all-to-all-start = ((bf16[8,64,768]{2,1,0:T(8,128)(2,1)}), bf16[8,64,768]{2,1,0:T(8,128)(2,1)S(1)}, u32[]{:S(2)}, u32[]{:S(2)}) async-start(bf16[8,64,768]{2,1,0:T(8,128)(2,1)} %bitcast.191), calls=%async_computation | async-start | bytes 1572864 | tf_op jit(solution)/shard_map/all_to_all | solution.py:867
  61.6 32.4 %all-to-all-start.1 = ((bf16[8,96,768]{2,1,0:T(8,128)(2,1)}), bf16[8,96,768]{2,1,0:T(8,128)(2,1)S(1)}, u32[]{:S(2)}, u32[]{:S(2)}) async-start(bf16[8,96,768]{2,1,0:T(8,128)(2,1)} %get-tuple-element.79), calls=%async_computation.1 | async-start | bytes 2359296 | tf_op jit(solution)/shard_map/all_to_all | solution.py:867
  141.9 26.9 %collective-permute-start.4 = (bf16[2,2,192,3072]{3,2,1,0:T(8,128)(2,1)}, bf16[2,2,192,3072]{3,2,1,0:T(8,128)(2,1)}, u32[]{:S(2)}, u32[]{:S(2)}) collective-permute-start(bf16[2,2,192,3072]{3,2,1,0:T(8,128)(2,1)} %get-tuple-element.101), channel_id=1, source_target_pairs={{0,8},{8,0},{16,24},{24,16},{1,9},{9,1},{17,25},{25,17},{2,10},{10... | collective-permute-start | bytes 14155784 | tf_op jit(solution)/shard_map/ppermute | solution.py:890
  142.1 12.6 %collective-permute-start.2 = (bf16[2,64,768]{2,1,0:T(8,128)(2,1)}, bf16[2,64,768]{2,1,0:T(8,128)(2,1)S(1)}, u32[]{:S(2)}, u32[]{:S(2)}) collective-permute-start(bf16[2,64,768]{2,1,0:T(8,128)(2,1)} %get-tuple-element.95), channel_id=1, source_target_pairs={{0,1},{1,2},{2,3},{3,4},{4,5},{5,6},{6,7},{8,9},{9,10},{10,11},{11... | collective-permute-start | bytes 589832 | tf_op jit(solution)/shard_map/ppermute | solution.py:858
  145.4 9.3 %collective-permute-start.3 = (bf16[2,64,768]{2,1,0:T(8,128)(2,1)}, bf16[2,64,768]{2,1,0:T(8,128)(2,1)S(1)}, u32[]{:S(2)}, u32[]{:S(2)}) collective-permute-start(bf16[2,64,768]{2,1,0:T(8,128)(2,1)} %get-tuple-element.96), channel_id=1, source_target_pairs={{1,0},{2,1},{3,2},{4,3},{5,4},{6,5},{7,6},{9,8},{10,9},{11,10},{12... | collective-permute-start | bytes 589832 | tf_op jit(solution)/shard_map/ppermute | solution.py:863
  163.8 25.3 %all-to-all-start.2 = ((bf16[8,64,768]{2,1,0:T(8,128)(2,1)}), bf16[8,64,768]{2,1,0:T(8,128)(2,1)}, u32[]{:S(2)}, u32[]{:S(2)}) async-start(bf16[8,64,768]{2,1,0:T(8,128)(2,1)} %bitcast.192), calls=%async_computation.2 | async-start | bytes 1572864 | tf_op jit(solution)/shard_map/all_to_all | solution.py:867
  170.6 46.8 %collective-permute-start.12 = (bf16[2,2,2,2,24,768]{5,4,2,1,0,3:T(8,128)(2,1)}, bf16[2,2,2,2,24,768]{5,4,2,1,0,3:T(8,128)(2,1)}, u32[]{:S(2)}, u32[]{:S(2)}) collective-permute-start(bf16[2,2,2,2,24,768]{5,4,2,1,0,3:T(8,128)(2,1)} %bitcast.162), channel_id=1, source_target_pairs={{0,8},{8,0},{16,24},{24,16},{1,9},{9,1},{17,25},{25,17},{2,10},{10... | collective-permute-start | bytes 1769480 | tf_op jit(solution)/shard_map/ppermute | solution.py:890
  189.2 23.2 %collective-permute-start.5 = (bf16[2,2,2,2,24,1024]{5,4,3,2,1,0:T(8,128)(2,1)}, bf16[2,2,2,2,24,1024]{5,4,3,2,1,0:T(8,128)(2,1)}, u32[]{:S(2)}, u32[]{:S(2)}) collective-permute-start(bf16[2,2,2,2,24,1024]{5,4,3,2,1,0:T(8,128)(2,1)} %get-tuple-element.109), channel_id=1, source_target_pairs={{0,16},{8,24},{16,0},{24,8},{1,17},{9,25},{17,1},{25,9},{2,18},{10... | collective-permute-start | bytes 2359304 | tf_op jit(solution)/shard_map/ppermute | solution.py:890
  190.7 21.7 %collective-permute-start.6 = (bf16[2,2,2,2,24,1024]{5,4,3,2,1,0:T(8,128)(2,1)}, bf16[2,2,2,2,24,1024]{5,4,3,2,1,0:T(8,128)(2,1)}, u32[]{:S(2)}, u32[]{:S(2)}) collective-permute-start(bf16[2,2,2,2,24,1024]{5,4,3,2,1,0:T(8,128)(2,1)} %get-tuple-element.110), channel_id=1, source_target_pairs={{0,1},{1,0},{2,3},{3,2},{4,5},{5,4},{6,7},{7,6},{8,9},{9,8},{10,11... | collective-permute-start | bytes 2359304 | tf_op jit(solution)/shard_map/ppermute | solution.py:890
  192.1 20.3 %collective-permute-start.7 = (bf16[2,2,2,2,24,1024]{5,4,3,2,1,0:T(8,128)(2,1)}, bf16[2,2,2,2,24,1024]{5,4,3,2,1,0:T(8,128)(2,1)}, u32[]{:S(2)}, u32[]{:S(2)}) collective-permute-start(bf16[2,2,2,2,24,1024]{5,4,3,2,1,0:T(8,128)(2,1)} %get-tuple-element.111), channel_id=1, source_target_pairs={{0,2},{1,3},{2,0},{3,1},{4,6},{5,7},{6,4},{7,5},{8,10},{9,11},{10,... | collective-permute-start | bytes 2359304 | tf_op jit(solution)/shard_map/ppermute | solution.py:890
  212.2 16.9 %collective-permute-start.11 = (bf16[3,2,192,768]{3,2,1,0:T(8,128)(2,1)}, bf16[3,2,192,768]{3,2,1,0:T(8,128)(2,1)}, u32[]{:S(2)}, u32[]{:S(2)}) collective-permute-start(bf16[3,2,192,768]{3,2,1,0:T(8,128)(2,1)} %get-tuple-element.128), channel_id=1, source_target_pairs={{0,8},{8,0},{16,24},{24,16},{1,9},{9,1},{17,25},{25,17},{2,10},{10... | collective-permute-start | bytes 5308424 | tf_op jit(solution)/shard_map/ppermute | solution.py:890
  212.4 33.9 %all-to-all-start.3 = ((bf16[8,96,768]{2,1,0:T(8,128)(2,1)}), bf16[8,96,768]{2,1,0:T(8,128)(2,1)}, u32[]{:S(2)}, u32[]{:S(2)}) async-start(bf16[8,96,768]{2,1,0:T(8,128)(2,1)} %get-tuple-element.112), calls=%async_computation.3 | async-start | bytes 2359296 | tf_op jit(solution)/shard_map/all_to_all | solution.py:867
  225.5 33.9 %collective-permute-start.8 = (bf16[2,2,2,24,1024]{4,3,0,1,2:T(8,128)(2,1)}, bf16[2,2,2,24,1024]{4,3,0,1,2:T(8,128)(2,1)}, u32[]{:S(2)}, u32[]{:S(2)}) collective-permute-start(bf16[2,2,2,24,1024]{4,3,0,1,2:T(8,128)(2,1)} %bitcast.169), channel_id=1, source_target_pairs={{0,1},{1,0},{2,3},{3,2},{4,5},{5,4},{6,7},{7,6},{8,9},{9,8},{10,11... | collective-permute-start | bytes 1179656 | tf_op jit(solution)/shard_map/ppermute | solution.py:890
  227.1 32.3 %collective-permute-start.9 = (bf16[2,2,2,24,1024]{4,3,0,2,1:T(8,128)(2,1)}, bf16[2,2,2,24,1024]{4,3,0,2,1:T(8,128)(2,1)}, u32[]{:S(2)}, u32[]{:S(2)}) collective-permute-start(bf16[2,2,2,24,1024]{4,3,0,2,1:T(8,128)(2,1)} %bitcast.168), channel_id=1, source_target_pairs={{0,2},{1,3},{2,0},{3,1},{4,6},{5,7},{6,4},{7,5},{8,10},{9,11},{10,... | collective-permute-start | bytes 1179656 | tf_op jit(solution)/shard_map/ppermute | solution.py:890
  228.6 30.8 %collective-permute-start.10 = (bf16[2,2,2,24,1024]{4,3,0,1,2:T(8,128)(2,1)}, bf16[2,2,2,24,1024]{4,3,0,1,2:T(8,128)(2,1)}, u32[]{:S(2)}, u32[]{:S(2)}) collective-permute-start(bf16[2,2,2,24,1024]{4,3,0,1,2:T(8,128)(2,1)} %bitcast.167), channel_id=1, source_target_pairs={{0,16},{8,24},{16,0},{24,8},{1,17},{9,25},{17,1},{25,9},{2,18},{10... | collective-permute-start | bytes 1179656 | tf_op jit(solution)/shard_map/ppermute | solution.py:890
  233.1 37.7 %collective-permute-start.13 = (bf16[2,2,2,2,24,768]{5,4,3,2,1,0:T(8,128)(2,1)}, bf16[2,2,2,2,24,768]{5,4,3,2,1,0:T(8,128)(2,1)}, u32[]{:S(2)}, u32[]{:S(2)}) collective-permute-start(bf16[2,2,2,2,24,768]{5,4,3,2,1,0:T(8,128)(2,1)} %get-tuple-element.156), channel_id=1, source_target_pairs={{0,16},{8,24},{16,0},{24,8},{1,17},{9,25},{17,1},{25,9},{2,18},{10... | collective-permute-start | bytes 1769480 | tf_op jit(solution)/shard_map/ppermute | solution.py:890
  235.6 37.2 %collective-permute-start.14 = (bf16[2,2,2,2,24,768]{5,4,3,2,1,0:T(8,128)(2,1)}, bf16[2,2,2,2,24,768]{5,4,3,2,1,0:T(8,128)(2,1)}, u32[]{:S(2)}, u32[]{:S(2)}) collective-permute-start(bf16[2,2,2,2,24,768]{5,4,3,2,1,0:T(8,128)(2,1)} %get-tuple-element.154), channel_id=1, source_target_pairs={{0,1},{1,0},{2,3},{3,2},{4,5},{5,4},{6,7},{7,6},{8,9},{9,8},{10,11... | collective-permute-start | bytes 1769480 | tf_op jit(solution)/shard_map/ppermute | solution.py:890
  246.3 10.0 %copy-start.13 = (f32[2,3,768]{2,1,0:T(4,128)S(1)}, f32[2,3,768]{2,1,0:T(4,128)}, u32[]{:S(2)}) copy-start(f32[2,3,768]{2,1,0:T(4,128)} %get-tuple-element.124) | copy-start | bytes 55300
  246.3 10.0 %copy-start.14 = (f32[2,1,768]{2,1,0:T(1,128)S(1)}, f32[2,1,768]{2,1,0:T(1,128)}, u32[]{:S(2)}) copy-start(f32[2,1,768]{2,1,0:T(1,128)} %get-tuple-element.125) | copy-start | bytes 18436
  259.4 21.0 %all-to-all-start.4 = ((f32[8,112,128]{2,1,0:T(8,128)}), f32[8,112,128]{2,1,0:T(8,128)S(1)}, u32[]{:S(2)}, u32[]{:S(2)}) async-start(f32[8,112,128]{2,1,0:T(8,128)} %bitcast.163), calls=%async_computation.4 | async-start | bytes 917504 | tf_op jit(solution)/shard_map/all_to_all | solution.py:867
  264.3 11.6 %collective-permute-start.17 = (bf16[2,2,24,1024]{3,2,0,1:T(8,128)(2,1)S(1)}, bf16[2,2,24,1024]{3,2,0,1:T(8,128)(2,1)S(1)}, u32[]{:S(2)}, u32[]{:S(2)}) collective-permute-start(bf16[2,2,24,1024]{3,2,0,1:T(8,128)(2,1)S(1)} %dynamic-slice_bitcast_fusion.14), channel_id=1, source_target_pairs={{0,1},{1,0},{2,3},{3,2},{4,5},{5,4},{6,7},{7,6},{8,9},{9,8},{10,11... | collective-permute-start | bytes 589832 | tf_op jit(solution)/shard_map/ppermute | solution.py:890
  267.5 8.4 %collective-permute-start.16 = (bf16[2,2,24,1024]{3,2,0,1:T(8,128)(2,1)S(1)}, bf16[2,2,24,1024]{3,2,0,1:T(8,128)(2,1)S(1)}, u32[]{:S(2)}, u32[]{:S(2)}) collective-permute-start(bf16[2,2,24,1024]{3,2,0,1:T(8,128)(2,1)S(1)} %dynamic-slice_bitcast_fusion.15), channel_id=1, source_target_pairs={{0,16},{8,24},{16,0},{24,8},{1,17},{9,25},{17,1},{25,9},{2,18},{10... | collective-permute-start | bytes 589832 | tf_op jit(solution)/shard_map/ppermute | solution.py:890
  269.3 8.3 %collective-permute-start.15 = (bf16[2,2,24,1024]{3,2,0,1:T(8,128)(2,1)S(1)}, bf16[2,2,24,1024]{3,2,0,1:T(8,128)(2,1)S(1)}, u32[]{:S(2)}, u32[]{:S(2)}) collective-permute-start(bf16[2,2,24,1024]{3,2,0,1:T(8,128)(2,1)S(1)} %dynamic-slice_bitcast_fusion.16), channel_id=1, source_target_pairs={{0,2},{1,3},{2,0},{3,1},{4,6},{5,7},{6,4},{7,5},{8,10},{9,11},{10,... | collective-permute-start | bytes 589832 | tf_op jit(solution)/shard_map/ppermute | solution.py:890
  272.1 14.0 %collective-permute-start.18 = (bf16[2,2,2,24,768]{4,3,2,1,0:T(8,128)(2,1)S(1)}, bf16[2,2,2,24,768]{4,3,2,1,0:T(8,128)(2,1)S(1)}, u32[]{:S(2)}, u32[]{:S(2)}) collective-permute-start(bf16[2,2,2,24,768]{4,3,2,1,0:T(8,128)(2,1)S(1)} %get-tuple-element.174), channel_id=1, source_target_pairs={{0,1},{1,0},{2,3},{3,2},{4,5},{5,4},{6,7},{7,6},{8,9},{9,8},{10,11... | collective-permute-start | bytes 884744 | tf_op jit(solution)/shard_map/ppermute | solution.py:890
  274.0 12.2 %collective-permute-start.19 = (bf16[2,2,2,24,768]{4,3,2,1,0:T(8,128)(2,1)S(1)}, bf16[2,2,2,24,768]{4,3,2,1,0:T(8,128)(2,1)S(1)}, u32[]{:S(2)}, u32[]{:S(2)}) collective-permute-start(bf16[2,2,2,24,768]{4,3,2,1,0:T(8,128)(2,1)S(1)} %get-tuple-element.172), channel_id=1, source_target_pairs={{0,16},{8,24},{16,0},{24,8},{1,17},{9,25},{17,1},{25,9},{2,18},{10... | collective-permute-start | bytes 884744 | tf_op jit(solution)/shard_map/ppermute | solution.py:890
  278.4 15.3 %collective-permute-start.22 = (bf16[2,24,3072]{2,1,0:T(8,128)(2,1)}, bf16[2,24,3072]{2,1,0:T(8,128)(2,1)}, u32[]{:S(2)}, u32[]{:S(2)}) collective-permute-start(bf16[2,24,3072]{2,1,0:T(8,128)(2,1)} %get-tuple-element.170), channel_id=1, source_target_pairs={{0,4},{1,5},{2,6},{3,7},{4,0},{5,1},{6,2},{7,3},{8,12},{9,13},{10,... | collective-permute-start | bytes 884744 | tf_op jit(solution)/shard_map/ppermute | solution.py:890
  286.5 13.3 %collective-permute-start.20 = (bf16[4,2,24,768]{3,2,1,0:T(8,128)(2,1)S(1)}, bf16[4,2,24,768]{3,2,1,0:T(8,128)(2,1)S(1)}, u32[]{:S(2)}, u32[]{:S(2)}) collective-permute-start(bf16[4,2,24,768]{3,2,1,0:T(8,128)(2,1)S(1)} %fusion.25), channel_id=1, source_target_pairs={{0,2},{1,3},{2,0},{3,1},{4,6},{5,7},{6,4},{7,5},{8,10},{9,11},{10,... | collective-permute-start | bytes 884744 | tf_op jit(solution)/shard_map/ppermute | solution.py:890
  304.8 11.5 %copy-start.1 = (bf16[1000,768]{1,0:T(8,128)(2,1)S(1)}, bf16[1000,768]{1,0:T(8,128)(2,1)}, u32[]{:S(2)}) copy-start(bf16[1000,768]{1,0:T(8,128)(2,1)} %param.23) | copy-start | bytes 4608004
  305.0 9.9 %collective-permute-start.21 = (bf16[4,24,768]{2,1,0:T(8,128)(2,1)S(1)}, bf16[4,24,768]{2,1,0:T(8,128)(2,1)S(1)}, u32[]{:S(2)}, u32[]{:S(2)}) collective-permute-start(bf16[4,24,768]{2,1,0:T(8,128)(2,1)S(1)} %dynamic-slice_bitcast_fusion.17), channel_id=1, source_target_pairs={{0,4},{1,5},{2,6},{3,7},{4,0},{5,1},{6,2},{7,3},{8,12},{9,13},{10,... | collective-permute-start | bytes 442376 | tf_op jit(solution)/shard_map/ppermute | solution.py:890
  (21 other events, 68.5 us)
